TPU v7x, 32 devices: a whole 2x2x4 slice. The times are simulated.
32 devices in a mesh: grp: 2 (over y), energy: 4 (over z), atom: 2 (over x), kz: 2 (over core).
Axes of the slice: x: 2, y: 2, z: 4, core: 2. Of those that a mesh axis runs over, the one named last changes fastest.
Arguments:
- green: float32 [8, 32, 512, 512], P(('grp', 'kz'), 'energy', 'atom'), parts along dimension 0, may hold values from -6 to 6
- couplings: float32 [4, 512, 512], P('atom'), may hold values from -0.25 to 0.25
- occupation: float32 [3], replicated, may hold values from 0.05 to 2
- offsets: int32 [3], replicated, may hold values from 1 to 16, as said below
- owners: int32 [3], replicated, may hold values from 0 to 3
Outputs:
- sigma: float32 [1024, 32, 512], P(('grp', 'atom', 'kz'), 'energy'), parts along dimension 0
There are 2 independent parts, one for each index of `grp`. A program takes and returns all parts, laid end to end along the dimension named above; an argument that names none is the same for every part. Nothing has to cross between parts.
Inputs may be any that keep to these rules, and one draw needn't show every extreme that they name: `offsets`: one mode's offset is exactly 16.
All inputs are finite; a program needn't handle non-finite values.
Results may differ from a plain program's by a relative error of at most 0.0001.
Values sent between devices are 32-bit elements; how exact they have to be, the bound alone decides.
No kernel may reach another device: no remote copies, remote signals or barrier semaphores. Data moves between devices by JAX's collectives and lax.ppermute only.
A program may use at most 192 MiB of HBM per device.

v0:
```python
import functools

import jax
import jax.numpy as jnp
from jax import lax
from jax.experimental import pallas as pl
from jax.experimental.pallas import tpu as pltpu
from jax.sharding import PartitionSpec as P


MODES = 3
REACH = 2
PIECES = 2


def chunks_of(half):
    return [1, 1, half - 2] if half > 2 else [1] * half


def halves(x):
    high = lax.reduce_precision(x, exponent_bits=8, mantissa_bits=7)
    return high.astype(jnp.bfloat16), (x - high).astype(jnp.bfloat16)


def add_momenta(where, green, *refs):
    out = refs[-1]
    total = green[0, 0]
    for k in range(1, green.shape[0]):
        total = total + green[k, 0]
    for ref in refs[:-1]:
        total = total + ref[0]
    out[0] = total


def split_dot(n_groups, n_parts, n_atoms, momenta, base, grid_total, edev, far, line, steps, occupation, right_high, right_low, left, *refs):
    sources = [
        [refs[(g * 2 + h) * n_parts : (g * 2 + h + 1) * n_parts] for h in range(2)]
        for g in range(n_groups)
    ]
    outs = refs[n_groups * 2 * n_parts : -3]
    planes, inner, sems = refs[-3:]
    count, size = outs[0].shape[:2]
    rows = planes.shape[2]
    half_planes = edev // 2
    place, core, atom = (lax.axis_index(a) for a in ("energy", "kz", "atom"))
    blocks = grid_total // edev
    target = blocks - 1 - place if far else place
    base = base + core * half_planes

    def source_of(energy, mode, side):
        step = steps[mode] if side == 0 else -steps[mode]
        source = lax.rem(target * edev + base + energy + step + grid_total, grid_total)
        rel = lax.div(source, edev) - place
        if far:
            valid = rel == 0
        elif line:
            valid = jnp.abs(rel) <= REACH
        else:
            rel = lax.rem(rel + REACH + blocks, blocks) - REACH
            valid = rel <= REACH
        group = jnp.where(valid, rel + n_groups // 2, n_groups // 2)
        return valid, group, lax.rem(source, edev)

    def fetch(energy, buffer):
        for mode in range(MODES):
            for side in range(2):
                _, group, plane = source_of(energy, mode, side)
                other = jnp.where(lax.div(plane, half_planes) == core, 0, 1)
                at = lax.rem(plane, half_planes)
                slot = mode * 2 + side
                for g in range(n_groups):
                    for h in range(2):

                        @pl.when((group == g) & (other == h))
                        def _(g=g, h=h, at=at, slot=slot):
                            first = 0
                            for ref in sources[g][h]:
                                depth = ref.shape[1]
                                start = first
                                if far:
                                    per = rows // n_atoms
                                    start = pl.multiple_of(
                                        lax.rem(atom - first // per + n_atoms, n_atoms) * per + first % per, 8
                                    )
                                pltpu.make_async_copy(
                                    ref.at[at], planes.at[buffer, slot, pl.ds(start, depth)], sems.at[buffer, slot]
                                ).start()
                                first += depth

    fetch(0, 0)

    @pl.loop(0, count)
    def _(energy):
        buffer = lax.rem(energy, 2)

        @pl.when(energy + 1 < count)
        def _():
            fetch(energy + 1, 1 - buffer)

        dot = functools.partial(jnp.dot, preferred_element_type=jnp.float32)
        for mode in range(MODES):
            scales = []
            for side in range(2):
                slot = mode * 2 + side
                held = planes.at[buffer, slot]
                pltpu.make_async_copy(held, held, sems.at[buffer, slot]).wait()
                scales.append(jnp.where(source_of(energy, mode, side)[0], (occupation[mode] + (1.0 - side)) * (1.0 / momenta), 0.0))
            combined = scales[0] * planes[buffer, 2 * mode] + scales[1] * planes[buffer, 2 * mode + 1]
            high = combined.astype(jnp.bfloat16)
            low = (combined - high.astype(jnp.float32)).astype(jnp.bfloat16)
            product = dot(high, right_high[mode]) + dot(low, right_high[mode]) + dot(high, right_low[mode])
            high = product.astype(jnp.bfloat16)
            low = (product - high.astype(jnp.float32)).astype(jnp.bfloat16)
            inner[mode, pl.ds(0, rows)] = high
            inner[mode, pl.ds(rows, rows)] = low
            inner[mode, pl.ds(2 * rows, rows)] = high
        for index, out in enumerate(outs):
            s, t = index // 2, index % 2
            block = lax.rem(core + t, 2)
            if not far:
                block = block + 2 * lax.rem(atom + s, n_atoms)
            where = pl.ds(pl.multiple_of(block * size, 8), size)
            total = dot(left[0, where], inner[0])
            for mode in range(1, MODES):
                total = total + dot(left[mode, where], inner[mode])
            out[energy] = total


def sandwich(steps, occupation, right, left, groups, n_atoms, momenta, base, grid_total, edev, far, line, out_rows, count):
    order = right[0].shape[-1]
    flat = [part for group in groups for half in group for part in half]
    rows = sum(part.shape[1] for part in groups[0][0])
    n_out = left.shape[1] // out_rows
    flops = count * 2 * 3 * MODES * (rows * order * order + left.shape[1] * rows * order)
    return pl.pallas_call(
        functools.partial(split_dot, len(groups), len(groups[0][0]), n_atoms, momenta, base, grid_total, edev, far, line),
        out_shape=[jax.ShapeDtypeStruct((count, out_rows, order), jnp.float32)] * n_out,
        in_specs=[pl.BlockSpec(memory_space=pltpu.SMEM)] * 2
        + [pl.BlockSpec(memory_space=pltpu.VMEM)] * 3
        + [pl.BlockSpec(memory_space=pl.ANY)] * len(flat),
        out_specs=[pl.BlockSpec(memory_space=pltpu.VMEM)] * n_out,
        scratch_shapes=[
            pltpu.VMEM((2, 2 * MODES, rows, order), jnp.float32),
            pltpu.VMEM((MODES, 3 * rows, order), jnp.bfloat16),
            pltpu.SemaphoreType.DMA((2, 2 * MODES)),
        ],
        compiler_params=pltpu.CompilerParams(vmem_limit_bytes=40 << 20),
        cost_estimate=pl.CostEstimate(
            flops=flops,
            bytes_accessed=count * 4 * (2 * MODES * rows * order + left.shape[1] * order),
            transcendentals=0,
        ),
        name="far_sandwich" if far else "near_sandwich",
    )(steps, occupation, right[0], right[1], left, *flat)


def gather_up(layout, count, *refs):
    out = refs[-1]
    core = lax.axis_index("kz")
    for own in range(2):

        @pl.when(core == own)
        def _(own=own):
            at = 0
            for half, chunks in enumerate(layout):
                where = own if half == 0 else 1 - own
                terms = []
                for size in chunks:
                    rows = []
                    for _ in range(size):
                        rows.extend((at, k) for k in range(refs[at].shape[0]))
                        at += 1
                    terms.append(rows)
                for j in range(count):
                    total = None
                    for rows in terms:
                        ref, k = rows[j]
                        total = refs[ref][k] if total is None else total + refs[ref][k]
                    out[:, where * count + j, :] = total


def shards(green, couplings, occupation, offsets, owners):
    momenta_here, edev, brows, order = green.shape
    n, atoms, cores = lax.axis_size("energy"), lax.axis_size("atom"), lax.axis_size("kz")
    momenta = momenta_here * cores
    grid_total = n * edev
    _, atom, core = (lax.axis_index(a) for a in ("energy", "atom", "kz"))
    line = n == 2 * REACH
    half = edev // cores
    swap = [(i, (i + 1) % cores) for i in range(cores)]
    around = [[(i, (i + s) % atoms) for i in range(atoms)] for s in range(atoms)]

    size = brows // PIECES

    def summed(theirs, piece, *more):
        def first(e, where):
            return 0, where[0] * half + e, piece, 0

        where = ((core + 1) % cores if theirs else core).reshape(1)
        spec = pl.BlockSpec((1, size, order), lambda e, where: (e, 0, 0))
        return pl.pallas_call(
            add_momenta,
            out_shape=jax.ShapeDtypeStruct((half, size, order), jnp.float32),
            grid_spec=pltpu.PrefetchScalarGridSpec(
                num_scalar_prefetch=1,
                grid=(half,),
                in_specs=[pl.BlockSpec((momenta_here, 1, size, order), first)] + [spec] * len(more),
                out_specs=spec,
            ),
            cost_estimate=pl.CostEstimate(
                flops=momenta_here * half * size * order,
                bytes_accessed=4 * (momenta_here + 1 + len(more)) * half * size * order,
                transcendentals=0,
            ),
            name="add_momenta",
        )(where, green, *more)

    own = []
    for piece in range(PIECES):
        given = summed(True, piece)
        given = lax.ppermute(given, "kz", swap)
        own.append(summed(False, piece, given))

    if line:
        up = [[(i, i + 1) for i in range(d, n - 1)] for d in range(REACH)]
        down = [[(i, i - 1) for i in range(n - 1 - d, 0, -1)] for d in range(REACH)]
    else:
        up = [[(i, (i + 1) % n) for i in range(n)]] * REACH
        down = [[(i, (i - 1) % n) for i in range(n)]] * REACH
    streams = {0: own}
    for d in range(1, REACH + 1):
        streams[-d] = [lax.ppermute(x, "energy", up[d - 1]) for x in streams[1 - d]]
        streams[d] = [lax.ppermute(x, "energy", down[d - 1]) for x in streams[d - 1]]
    groups = [(streams[d], [lax.ppermute(x, "kz", swap) for x in streams[d]]) for d in range(-REACH, REACH + 1)]

    table_rows = couplings.shape[0]
    strip = order // cores
    mine = lax.dynamic_slice(couplings, (0, core * strip, 0), (table_rows, strip, order))
    others = []
    for s in range(1, atoms):
        got = lax.ppermute(mine, "atom", around[s])
        others.append((got, lax.ppermute(got, "kz", swap)))
    rows_of = lax.rem(owners, jnp.int32(table_rows))
    behind_of = lax.rem(atom - lax.div(owners, jnp.int32(table_rows)) + atoms, jnp.int32(atoms))

    def pick(m):
        row, behind = rows_of[m], behind_of[m]

        def at(table):
            return lax.dynamic_slice(table, (row, 0, 0), (1,) + table.shape[1:])[0]

        value = at(couplings)
        for s, (got, other) in enumerate(others, 1):
            first = jnp.where(core == 0, at(got), at(other))
            second = jnp.where(core == 0, at(other), at(got))
            value = jnp.where(behind == s, jnp.concatenate([first, second], 0), value)
        return value

    coupling = jnp.stack([pick(m) for m in range(MODES)], 0)
    right = halves(coupling.swapaxes(1, 2))
    out_rows = order // (atoms * cores)

    def left_of(x):
        high, low = halves(x)
        return jnp.concatenate([high, high, low], 2)

    left_near = left_of(lax.dynamic_slice(coupling, (0, 0, atom * brows), (MODES, order, brows)))

    beyond = []
    if line:
        left_far = left_of(lax.dynamic_slice(coupling, (0, atom * cores * out_rows, 0), (MODES, cores * out_rows, order)))
        got = [lax.ppermute(x, "atom", around[s]) for s in range(1, atoms) for x in own]
        got, right, left_far, left_near = lax.optimization_barrier((got, right, left_far, left_near))
        whole = (
            list(own) + got,
            groups[REACH][1] + [lax.ppermute(x, "kz", swap) for x in got],
        )
        sums = sandwich(
            offsets, occupation, right, left_far, [whole], atoms, momenta, 0, grid_total, edev, True, line, out_rows, half
        )
        for t in range(cores):
            pairs = [
                (a * cores + k, b * cores + (k + t) % cores)
                for a, b in ((0, n - 1), (n - 1, 0))
                for k in range(cores)
            ]
            beyond.append(lax.ppermute(sums[t], ("energy", "kz"), pairs))

    terms = [[[] for _ in range(atoms)] for _ in range(cores)]
    base = 0
    for count in chunks_of(half):
        sums = sandwich(
            offsets, occupation, right, left_near, groups, atoms, momenta, base, grid_total, edev, False, line, out_rows, count
        )
        base += count
        for s in range(atoms - 1, -1, -1):
            for t in range(cores):
                block = sums[s * cores + t]
                if s or t:
                    pairs = [
                        (i * cores + k, ((i + s) % atoms) * cores + (k + t) % cores)
                        for i in range(atoms)
                        for k in range(cores)
                    ]
                    block = lax.ppermute(block, ("atom", "kz"), pairs)
                terms[t][s].append(block)
    for t in range(cores):
        if beyond:
            terms[t].append([beyond[t]])
    flat = [x for t in range(cores) for term in terms[t] for x in term]
    layout = [[len(term) for term in terms[t]] for t in range(cores)]
    step = min(out_rows, 32)
    return pl.pallas_call(
        functools.partial(gather_up, layout, half),
        grid=(out_rows // step,),
        out_shape=jax.ShapeDtypeStruct((out_rows, edev, order), jnp.float32),
        in_specs=[pl.BlockSpec((x.shape[0], step, order), lambda i: (0, i, 0)) for x in flat],
        out_specs=pl.BlockSpec((step, edev, order), lambda i: (i, 0, 0)),
        name="gather_up",
    )(*flat)


def solution(mesh):
    return jax.shard_map(
        shards,
        mesh=mesh,
        in_specs=(P(("grp", "kz"), "energy", "atom", None), P("atom", None, None), P(), P(), P()),
        out_specs=P(("grp", "atom", "kz"), "energy", None),
        check_vma=False,
    )
```

profile of v0, /device:TPU:0, one launch (start us, length us, event | category | flops | bytes accessed | tf_op | source)
XLA Modules:
  0.0 278.9 jit_solution(13034530345244439612)
XLA Ops:
  0.0 1.3 constant_dynamic-slice_fusion
  1.3 3.0 %collective-permute-start.4 = (f32[2,256,512]{2,1,0:T(8,128)S(1)}, f32[2,256,512]{2,1,0:T(8,128)}, u32[]{:S(2)}, u32[]{:S(2)}) collective-permute-start(f32[2,256,512]{2,1,0:T(8,128)S(1)} %constant_dynamic-slice_fusion), channel_id=1, source_target_pairs={{0,2},{2,0},{1,3},{3,1},{4,6},{6,4},{5,7},{7,5},{8,10},{10,8},{9,1... | collective-permute-start | bytes 3145736 | tf_op jit(solution)/shard_map/ppermute | solution.py:241
  4.3 3.6 %add_momenta.6 = f32[4,128,512]{2,1,0:T(8,128)} custom-call(s32[1]{0:T(128)} %bitcast.1.where, f32[2,8,256,512]{3,2,1,0:T(8,128)} %green.7), custom_call_target="tpu_custom_call" | custom-call | flops 524288 | bytes 3145728 | tf_op jit(solution)/shard_map/add_momenta/pallas_call | solution.py:201
  7.9 3.6 %add_momenta.4 = f32[4,128,512]{2,1,0:T(8,128)} custom-call(s32[1]{0:T(128)} %bitcast.1.where, f32[2,8,256,512]{3,2,1,0:T(8,128)} %green.7), custom_call_target="tpu_custom_call" | custom-call | flops 524288 | bytes 3145728 | tf_op jit(solution)/shard_map/add_momenta/pallas_call | solution.py:201
  12.0 15.6 %collective-permute-done.4 = f32[2,256,512]{2,1,0:T(8,128)} collective-permute-done((f32[2,256,512]{2,1,0:T(8,128)S(1)}, f32[2,256,512]{2,1,0:T(8,128)}, u32[]{:S(2)}, u32[]{:S(2)}) %collective-permute-start.4) | collective-permute-done | bytes 1048608 | tf_op jit(solution)/shard_map/ppermute | solution.py:241
  28.6 3.8 %add_momenta.7.refs_9_.refs_1_ = f32[4,128,512]{2,1,0:T(8,128)} custom-call(s32[1]{0:T(128)} %bitcast.where, f32[2,8,256,512]{3,2,1,0:T(8,128)} %green.7, f32[4,128,512]{2,1,0:T(8,128)} %copy-done.37), custom_call_target="tpu_custom_call" | custom-call | flops 524288 | bytes 4194304 | tf_op jit(solution)/shard_map/add_momenta/pallas_call | solution.py:201
  32.3 1.7 collective-permute-start.3
  35.0 3.8 %add_momenta.5.refs_8_.refs_0_ = f32[4,128,512]{2,1,0:T(8,128)} custom-call(s32[1]{0:T(128)} %bitcast.where, f32[2,8,256,512]{3,2,1,0:T(8,128)} %green.7, f32[4,128,512]{2,1,0:T(8,128)} %copy-done.36), custom_call_target="tpu_custom_call" | custom-call | flops 524288 | bytes 4194304 | tf_op jit(solution)/shard_map/add_momenta/pallas_call | solution.py:201
  47.9 4.9 %collective-permute-start.8 = (f32[4,128,512]{2,1,0:T(8,128)S(1)}, f32[4,128,512]{2,1,0:T(8,128)}, u32[]{:S(2)}, u32[]{:S(2)}) collective-permute-start(f32[4,128,512]{2,1,0:T(8,128)S(1)} %copy-done.2), channel_id=1, source_target_pairs={{0,4},{4,8},{8,12},{1,5},{5,9},{9,13},{2,6},{6,10},{10,14},{3,7},{... | collective-permute-start | bytes 3145736 | tf_op jit(solution)/shard_map/ppermute | solution.py:232
  52.8 2.2 dynamic-slice_select_fusion.5
  55.8 2.8 collective-permute-done.3.refs_3_
  58.6 1.3 collective-permute-start.17
  59.9 20.7 %collective-permute-done.1.refs_2_ = f32[4,128,512]{2,1,0:T(8,128)S(1)} collective-permute-done((f32[4,128,512]{2,1,0:T(8,128)}, f32[4,128,512]{2,1,0:T(8,128)S(1)}, u32[]{:S(2)}, u32[]{:S(2)}) %collective-permute-start.1) | collective-permute-done | bytes 1048608 | tf_op jit(solution)/shard_map/ppermute | solution.py:272
  80.6 4.7 %collective-permute-start.6 = (f32[4,128,512]{2,1,0:T(8,128)S(1)}, f32[4,128,512]{2,1,0:T(8,128)}, u32[]{:S(2)}, u32[]{:S(2)}) collective-permute-start(f32[4,128,512]{2,1,0:T(8,128)S(1)} %copy-done.5), channel_id=1, source_target_pairs={{0,4},{4,8},{8,12},{1,5},{5,9},{9,13},{2,6},{6,10},{10,14},{3,7},{... | collective-permute-start | bytes 3145736 | tf_op jit(solution)/shard_map/ppermute | solution.py:232
  86.2 1.6 pad_maximum_fusion.2.left
  87.7 2.2 fusion
  90.0 1.6 pad_maximum_fusion.1.left
  92.5 1.3 collective-permute-start.16
  96.0 10.6 %collective-permute-done.6.refs_4_ = f32[4,128,512]{2,1,0:T(8,128)} collective-permute-done((f32[4,128,512]{2,1,0:T(8,128)S(1)}, f32[4,128,512]{2,1,0:T(8,128)}, u32[]{:S(2)}, u32[]{:S(2)}) %collective-permute-start.6) | collective-permute-done | bytes 1048608 | tf_op jit(solution)/shard_map/ppermute | solution.py:232
  106.6 1.3 collective-permute-start.21
  107.9 12.6 %collective-permute-done.16.refs_12_ = f32[4,128,512]{2,1,0:T(8,128)} collective-permute-done((f32[4,128,512]{2,1,0:T(8,128)S(1)}, f32[4,128,512]{2,1,0:T(8,128)}, u32[]{:S(2)}, u32[]{:S(2)}) %collective-permute-start.16) | collective-permute-done | bytes 1048608 | tf_op jit(solution)/shard_map/ppermute | solution.py:233
  120.5 1.6 collective-permute-start.7
  123.2 1.3 collective-permute-start.20
  125.9 16.9 %collective-permute-done.21.refs_17_ = f32[4,128,512]{2,1,0:T(8,128)S(1)} collective-permute-done((f32[4,128,512]{2,1,0:T(8,128)}, f32[4,128,512]{2,1,0:T(8,128)S(1)}, u32[]{:S(2)}, u32[]{:S(2)}) %collective-permute-start.21) | collective-permute-done | bytes 1048608 | tf_op jit(solution)/shard_map/ppermute | solution.py:233
  143.8 1.7 copy.6.right_high
  145.6 2.3 copy.7.right_low
  148.5 15.5 %collective-permute-done.20.refs_16_ = f32[4,128,512]{2,1,0:T(8,128)} collective-permute-done((f32[4,128,512]{2,1,0:T(8,128)}, f32[4,128,512]{2,1,0:T(8,128)}, u32[]{:S(2)}, u32[]{:S(2)}) %collective-permute-start.20) | collective-permute-done | bytes 1048608 | tf_op jit(solution)/shard_map/ppermute | solution.py:233
  165.0 1.2 copy-done.3
  166.2 1.2 copy-done.6
  167.4 1.2 copy-done.9
  168.7 1.2 copy-done.13
  169.9 1.2 copy-done.23
  171.1 1.2 copy-done.25
  172.3 1.2 copy-done.27
  173.6 1.2 copy-done.29
  174.8 21.7 %far_sandwich.1 = (f32[4,128,512]{2,1,0:T(8,128)S(1)}, f32[4,128,512]{2,1,0:T(8,128)S(1)}) custom-call(s32[3]{0:T(128)S(1)} %copy-done.20, f32[3]{0:T(128)S(1)} %copy-done.21, bf16[3,512,512]{2,1,0:T(8,128)(2,1)S(1)} %copy.6.right_high, bf16[3,512,512]{2,1,0:T(8,128)(2,1)S(1)} %copy.7.right_low, bf16[3,256,1536]{2,1,0:T(8,128)(2,1)} %pad_maximum_fusion.1.left, ...), custom_call_target="tpu_custom_call" | custom-call | flops 14495514624 | bytes 27262976 | tf_op jit(solution)/shard_map/far_sandwich/pallas_call | solution.py:135
  196.6 1.9 collective-permute-start.29
  198.5 5.1 %collective-permute-start.36 = (f32[4,128,512]{2,1,0:T(8,128)S(1)}, f32[4,128,512]{2,1,0:T(8,128)S(1)}, u32[]{:S(2)}, u32[]{:S(2)}) collective-permute-start(f32[4,128,512]{2,1,0:T(8,128)S(1)} %get-tuple-element.44), channel_id=1, source_target_pairs={{0,13},{1,12},{12,1},{13,0},{2,15},{3,14},{14,3},{15,2},{16,29},{1... | collective-permute-start | bytes 3145736 | tf_op jit(solution)/shard_map/ppermute | solution.py:287
  204.7 7.1 %near_sandwich.4 = (f32[1,128,512]{2,1,0:T(8,128)S(1)}, f32[1,128,512]{2,1,0:T(8,128)S(1)}, f32[1,128,512]{2,1,0:T(8,128)S(1)}, f32[1,128,512]{2,1,0:T(8,128)S(1)}) custom-call(s32[3]{0:T(128)S(1)} %copy-done.20, f32[3]{0:T(128)S(1)} %copy-done.21, bf16[3,512,512]{2,1,0:T(8,128)(2,1)} %copy-done, bf16[3,512,512]{2,1,0:T(8,128)(2,1)} %copy-done.1, ...), custom_call_target="tpu_custom_call" | custom-call | flops 2415919104 | bytes 4194304 | tf_op jit(solution)/shard_map/near_sandwich/pallas_call | solution.py:135
  212.5 1.5 collective-permute-start.25
  214.5 10.4 %near_sandwich.5 = (f32[2,128,512]{2,1,0:T(8,128)S(1)}, f32[2,128,512]{2,1,0:T(8,128)S(1)}, f32[2,128,512]{2,1,0:T(8,128)S(1)}, f32[2,128,512]{2,1,0:T(8,128)S(1)}) custom-call(s32[3]{0:T(128)S(1)} %copy-done.20, f32[3]{0:T(128)S(1)} %copy-done.21, bf16[3,512,512]{2,1,0:T(8,128)(2,1)} %copy-done, bf16[3,512,512]{2,1,0:T(8,128)(2,1)} %copy-done.1, ...), custom_call_target="tpu_custom_call" | custom-call | flops 4831838208 | bytes 8388608 | tf_op jit(solution)/shard_map/near_sandwich/pallas_call | solution.py:135
  225.6 7.2 %near_sandwich.3 = (f32[1,128,512]{2,1,0:T(8,128)S(1)}, f32[1,128,512]{2,1,0:T(8,128)S(1)}, f32[1,128,512]{2,1,0:T(8,128)S(1)}, f32[1,128,512]{2,1,0:T(8,128)S(1)}) custom-call(s32[3]{0:T(128)S(1)} %copy-done.20, f32[3]{0:T(128)S(1)} %copy-done.21, bf16[3,512,512]{2,1,0:T(8,128)(2,1)} %copy-done, bf16[3,512,512]{2,1,0:T(8,128)(2,1)} %copy-done.1, ...), custom_call_target="tpu_custom_call" | custom-call | flops 2415919104 | bytes 4194304 | tf_op jit(solution)/shard_map/near_sandwich/pallas_call | solution.py:135
  233.4 1.0 collective-permute-start.34
  234.5 12.5 %collective-permute-done.36.refs_13_ = f32[4,128,512]{2,1,0:T(8,128)S(1)} collective-permute-done((f32[4,128,512]{2,1,0:T(8,128)S(1)}, f32[4,128,512]{2,1,0:T(8,128)S(1)}, u32[]{:S(2)}, u32[]{:S(2)}) %collective-permute-start.36) | collective-permute-done | bytes 1048608 | tf_op jit(solution)/shard_map/ppermute | solution.py:287
  247.0 1.5 collective-permute-start.24
  249.6 6.6 %collective-permute-done.24.refs_3_ = f32[1,128,512]{2,1,0:T(8,128)S(1)} collective-permute-done((f32[1,128,512]{2,1,0:T(8,128)S(1)}, f32[1,128,512]{2,1,0:T(8,128)S(1)}, u32[]{:S(2)}, u32[]{:S(2)}) %collective-permute-start.24) | collective-permute-done | bytes 262176 | tf_op jit(solution)/shard_map/ppermute | solution.py:305
  256.9 15.6 %collective-permute-done.33.refs_10_ = f32[1,128,512]{2,1,0:T(8,128)S(1)} collective-permute-done((f32[1,128,512]{2,1,0:T(8,128)S(1)}, f32[1,128,512]{2,1,0:T(8,128)S(1)}, u32[]{:S(2)}, u32[]{:S(2)}) %collective-permute-start.33) | collective-permute-done | bytes 262176 | tf_op jit(solution)/shard_map/ppermute | solution.py:305
  273.8 4.9 %gather_up.1 = f32[128,8,512]{2,1,0:T(8,128)} custom-call(f32[1,128,512]{2,1,0:T(8,128)} %copy-done.19, f32[1,128,512]{2,1,0:T(8,128)} %copy-done.18, f32[2,128,512]{2,1,0:T(8,128)} %copy-done.17, f32[1,128,512]{2,1,0:T(8,128)} %copy-done.44, f32[1,128,512]{2,1,0:T(8,128)} %copy-done.41, f32[2,128,512]{2,1,0:T(8,128)} %copy-done.38, ...), custom_call_target="tpu_custom_call" | custom-call | tf_op jit(solution)/shard_map/gather_up/pallas_call | solution.py:313
  (144 shorter events, 20.6 us)
Async XLA Ops:
  1.3 26.3 %collective-permute-start.4 = (f32[2,256,512]{2,1,0:T(8,128)S(1)}, f32[2,256,512]{2,1,0:T(8,128)}, u32[]{:S(2)}, u32[]{:S(2)}) collective-permute-start(f32[2,256,512]{2,1,0:T(8,128)S(1)} %constant_dynamic-slice_fusion), channel_id=1, source_target_pairs={{0,2},{2,0},{1,3},{3,1},{4,6},{6,4},{5,7},{7,5},{8,10},{10,8},{9,1... | collective-permute-start | bytes 3145736 | tf_op jit(solution)/shard_map/ppermute | solution.py:241
  7.9 19.7 %collective-permute-start.2 = (f32[4,128,512]{2,1,0:T(8,128)}, f32[4,128,512]{2,1,0:T(8,128)S(1)}, u32[]{:S(2)}, u32[]{:S(2)}) collective-permute-start(f32[4,128,512]{2,1,0:T(8,128)} %add_momenta.6), channel_id=1, source_target_pairs={{0,1},{1,0},{2,3},{3,2},{4,5},{5,4},{6,7},{7,6},{8,9},{9,8},{10,11... | collective-permute-start | bytes 3145736 | tf_op jit(solution)/shard_map/ppermute | solution.py:221
  11.5 22.6 %collective-permute-start = (f32[4,128,512]{2,1,0:T(8,128)}, f32[4,128,512]{2,1,0:T(8,128)S(1)}, u32[]{:S(2)}, u32[]{:S(2)}) collective-permute-start(f32[4,128,512]{2,1,0:T(8,128)} %add_momenta.4), channel_id=1, source_target_pairs={{0,1},{1,0},{2,3},{3,2},{4,5},{5,4},{6,7},{7,6},{8,9},{9,8},{10,11... | collective-permute-start | bytes 3145736 | tf_op jit(solution)/shard_map/ppermute | solution.py:221
  27.6 20.3 %collective-permute-start.5 = (f32[2,256,512]{2,1,0:T(8,128)}, f32[2,256,512]{2,1,0:T(8,128)}, u32[]{:S(2)}, u32[]{:S(2)}) collective-permute-start(f32[2,256,512]{2,1,0:T(8,128)} %collective-permute-done.4), channel_id=1, source_target_pairs={{0,1},{1,0},{2,3},{3,2},{4,5},{5,4},{6,7},{7,6},{8,9},{9,8},{10,11... | collective-permute-start | bytes 3145736 | tf_op jit(solution)/shard_map/ppermute | solution.py:242
  32.3 26.2 %collective-permute-start.3 = (f32[4,128,512]{2,1,0:T(8,128)}, f32[4,128,512]{2,1,0:T(8,128)S(1)}, u32[]{:S(2)}, u32[]{:S(2)}) collective-permute-start(f32[4,128,512]{2,1,0:T(8,128)} %add_momenta.7.refs_9_.refs_1_), channel_id=1, source_target_pairs={{0,2},{2,0},{1,3},{3,1},{4,6},{6,4},{5,7},{7,5},{8,10},{10,8},{9,1... | collective-permute-start | bytes 3145736 | tf_op jit(solution)/shard_map/ppermute | solution.py:272
  38.8 41.8 %collective-permute-start.1 = (f32[4,128,512]{2,1,0:T(8,128)}, f32[4,128,512]{2,1,0:T(8,128)S(1)}, u32[]{:S(2)}, u32[]{:S(2)}) collective-permute-start(f32[4,128,512]{2,1,0:T(8,128)} %add_momenta.5.refs_8_.refs_0_), channel_id=1, source_target_pairs={{0,2},{2,0},{1,3},{3,1},{4,6},{6,4},{5,7},{7,5},{8,10},{10,8},{9,1... | collective-permute-start | bytes 3145736 | tf_op jit(solution)/shard_map/ppermute | solution.py:272
  47.3 44.2 %collective-permute-start.15 = (f32[4,128,512]{2,1,0:T(8,128)S(1)}, f32[4,128,512]{2,1,0:T(8,128)S(1)}, u32[]{:S(2)}, u32[]{:S(2)}) collective-permute-start(f32[4,128,512]{2,1,0:T(8,128)S(1)} %copy-done.2), channel_id=1, source_target_pairs={{0,1},{1,0},{2,3},{3,2},{4,5},{5,4},{6,7},{7,6},{8,9},{9,8},{10,11... | collective-permute-start | bytes 3145736 | tf_op jit(solution)/shard_map/ppermute | solution.py:234
  47.4 46.4 %collective-permute-start.14 = (f32[4,128,512]{2,1,0:T(8,128)}, f32[4,128,512]{2,1,0:T(8,128)S(1)}, u32[]{:S(2)}, u32[]{:S(2)}) collective-permute-start(f32[4,128,512]{2,1,0:T(8,128)} %add_momenta.5.refs_8_.refs_0_), channel_id=1, source_target_pairs={{0,1},{1,0},{2,3},{3,2},{4,5},{5,4},{6,7},{7,6},{8,9},{9,8},{10,11... | collective-permute-start | bytes 3145736 | tf_op jit(solution)/shard_map/ppermute | solution.py:234
  47.9 46.9 %collective-permute-start.8 = (f32[4,128,512]{2,1,0:T(8,128)S(1)}, f32[4,128,512]{2,1,0:T(8,128)}, u32[]{:S(2)}, u32[]{:S(2)}) collective-permute-start(f32[4,128,512]{2,1,0:T(8,128)S(1)} %copy-done.2), channel_id=1, source_target_pairs={{0,4},{4,8},{8,12},{1,5},{5,9},{9,13},{2,6},{6,10},{10,14},{3,7},{... | collective-permute-start | bytes 3145736 | tf_op jit(solution)/shard_map/ppermute | solution.py:232
  58.6 36.2 %copy-start.22 = (f32[4,128,512]{2,1,0:T(8,128)}, f32[4,128,512]{2,1,0:T(8,128)S(1)}, u32[]{:S(2)}) copy-start(f32[4,128,512]{2,1,0:T(8,128)S(1)} %collective-permute-done.3.refs_3_) | copy-start | bytes 3145732
  58.6 36.7 %collective-permute-start.17 = (f32[4,128,512]{2,1,0:T(8,128)S(1)}, f32[4,128,512]{2,1,0:T(8,128)}, u32[]{:S(2)}, u32[]{:S(2)}) collective-permute-start(f32[4,128,512]{2,1,0:T(8,128)S(1)} %copy-done.2), channel_id=1, source_target_pairs={{12,8},{8,4},{4,0},{13,9},{9,5},{5,1},{14,10},{10,6},{6,2},{15,11}... | collective-permute-start | bytes 3145736 | tf_op jit(solution)/shard_map/ppermute | solution.py:233
  80.6 26.0 %collective-permute-start.6 = (f32[4,128,512]{2,1,0:T(8,128)S(1)}, f32[4,128,512]{2,1,0:T(8,128)}, u32[]{:S(2)}, u32[]{:S(2)}) collective-permute-start(f32[4,128,512]{2,1,0:T(8,128)S(1)} %copy-done.5), channel_id=1, source_target_pairs={{0,4},{4,8},{8,12},{1,5},{5,9},{9,13},{2,6},{6,10},{10,14},{3,7},{... | collective-permute-start | bytes 3145736 | tf_op jit(solution)/shard_map/ppermute | solution.py:232
  91.5 73.5 %copy-start.20 = (s32[3]{0:T(128)S(1)}, s32[3]{0:T(128)}, u32[]{:S(2)}) copy-start(s32[3]{0:T(128)} %steps.7) | copy-start | bytes 40
  91.5 73.5 %copy-start.21 = (f32[3]{0:T(128)S(1)}, f32[3]{0:T(128)}, u32[]{:S(2)}) copy-start(f32[3]{0:T(128)} %occupation.7) | copy-start | bytes 40
  92.5 28.0 %collective-permute-start.16 = (f32[4,128,512]{2,1,0:T(8,128)S(1)}, f32[4,128,512]{2,1,0:T(8,128)}, u32[]{:S(2)}, u32[]{:S(2)}) collective-permute-start(f32[4,128,512]{2,1,0:T(8,128)S(1)} %copy-done.5), channel_id=1, source_target_pairs={{12,8},{8,4},{4,0},{13,9},{9,5},{5,1},{14,10},{10,6},{6,2},{15,11}... | collective-permute-start | bytes 3145736 | tf_op jit(solution)/shard_map/ppermute | solution.py:233
  94.8 27.4 %collective-permute-start.27 = (f32[4,128,512]{2,1,0:T(8,128)S(1)}, f32[4,128,512]{2,1,0:T(8,128)S(1)}, u32[]{:S(2)}, u32[]{:S(2)}) collective-permute-start(f32[4,128,512]{2,1,0:T(8,128)S(1)} %collective-permute-done.1.refs_2_), channel_id=1, source_target_pairs={{0,1},{1,0},{2,3},{3,2},{4,5},{5,4},{6,7},{7,6},{8,9},{9,8},{10,11... | collective-permute-start | bytes 3145736 | tf_op jit(solution)/shard_map/ppermute | solution.py:276
  94.8 29.6 %collective-permute-start.28 = (f32[4,128,512]{2,1,0:T(8,128)S(1)}, f32[4,128,512]{2,1,0:T(8,128)S(1)}, u32[]{:S(2)}, u32[]{:S(2)}) collective-permute-start(f32[4,128,512]{2,1,0:T(8,128)S(1)} %collective-permute-done.3.refs_3_), channel_id=1, source_target_pairs={{0,1},{1,0},{2,3},{3,2},{4,5},{5,4},{6,7},{7,6},{8,9},{9,8},{10,11... | collective-permute-start | bytes 3145736 | tf_op jit(solution)/shard_map/ppermute | solution.py:276
  95.3 30.1 %collective-permute-start.9 = (f32[4,128,512]{2,1,0:T(8,128)}, f32[4,128,512]{2,1,0:T(8,128)S(1)}, u32[]{:S(2)}, u32[]{:S(2)}) collective-permute-start(f32[4,128,512]{2,1,0:T(8,128)} %collective-permute-done.8.refs_5_), channel_id=1, source_target_pairs={{4,8},{8,12},{5,9},{9,13},{6,10},{10,14},{7,11},{11,15},{20,24},{2... | collective-permute-start | bytes 3145736 | tf_op jit(solution)/shard_map/ppermute | solution.py:232
  106.6 36.2 %collective-permute-start.21 = (f32[4,128,512]{2,1,0:T(8,128)}, f32[4,128,512]{2,1,0:T(8,128)S(1)}, u32[]{:S(2)}, u32[]{:S(2)}) collective-permute-start(f32[4,128,512]{2,1,0:T(8,128)} %collective-permute-done.17.refs_13_), channel_id=1, source_target_pairs={{8,4},{4,0},{9,5},{5,1},{10,6},{6,2},{11,7},{7,3},{24,20},{20,16},... | collective-permute-start | bytes 3145736 | tf_op jit(solution)/shard_map/ppermute | solution.py:233
  120.5 27.4 %collective-permute-start.7 = (f32[4,128,512]{2,1,0:T(8,128)}, f32[4,128,512]{2,1,0:T(8,128)}, u32[]{:S(2)}, u32[]{:S(2)}) collective-permute-start(f32[4,128,512]{2,1,0:T(8,128)} %collective-permute-done.6.refs_4_), channel_id=1, source_target_pairs={{4,8},{8,12},{5,9},{9,13},{6,10},{10,14},{7,11},{11,15},{20,24},{2... | collective-permute-start | bytes 3145736 | tf_op jit(solution)/shard_map/ppermute | solution.py:232
  123.2 40.8 %collective-permute-start.20 = (f32[4,128,512]{2,1,0:T(8,128)}, f32[4,128,512]{2,1,0:T(8,128)}, u32[]{:S(2)}, u32[]{:S(2)}) collective-permute-start(f32[4,128,512]{2,1,0:T(8,128)} %collective-permute-done.16.refs_12_), channel_id=1, source_target_pairs={{8,4},{4,0},{9,5},{5,1},{10,6},{6,2},{11,7},{7,3},{24,20},{20,16},... | collective-permute-start | bytes 3145736 | tf_op jit(solution)/shard_map/ppermute | solution.py:233
  125.4 38.5 %collective-permute-start.13 = (f32[4,128,512]{2,1,0:T(8,128)}, f32[4,128,512]{2,1,0:T(8,128)}, u32[]{:S(2)}, u32[]{:S(2)}) collective-permute-start(f32[4,128,512]{2,1,0:T(8,128)} %collective-permute-done.8.refs_5_), channel_id=1, source_target_pairs={{0,1},{1,0},{2,3},{3,2},{4,5},{5,4},{6,7},{7,6},{8,9},{9,8},{10,11... | collective-permute-start | bytes 3145736 | tf_op jit(solution)/shard_map/ppermute | solution.py:234
  125.4 39.0 %collective-permute-start.19 = (f32[4,128,512]{2,1,0:T(8,128)}, f32[4,128,512]{2,1,0:T(8,128)}, u32[]{:S(2)}, u32[]{:S(2)}) collective-permute-start(f32[4,128,512]{2,1,0:T(8,128)} %collective-permute-done.17.refs_13_), channel_id=1, source_target_pairs={{0,1},{1,0},{2,3},{3,2},{4,5},{5,4},{6,7},{7,6},{8,9},{9,8},{10,11... | collective-permute-start | bytes 3145736 | tf_op jit(solution)/shard_map/ppermute | solution.py:234
  143.8 20.7 %collective-permute-start.12 = (f32[4,128,512]{2,1,0:T(8,128)}, f32[4,128,512]{2,1,0:T(8,128)}, u32[]{:S(2)}, u32[]{:S(2)}) collective-permute-start(f32[4,128,512]{2,1,0:T(8,128)} %collective-permute-done.6.refs_4_), channel_id=1, source_target_pairs={{0,1},{1,0},{2,3},{3,2},{4,5},{5,4},{6,7},{7,6},{8,9},{9,8},{10,11... | collective-permute-start | bytes 3145736 | tf_op jit(solution)/shard_map/ppermute | solution.py:234
  145.6 51.0 %copy-start = (bf16[3,512,512]{2,1,0:T(8,128)(2,1)}, bf16[3,512,512]{2,1,0:T(8,128)(2,1)S(1)}, u32[]{:S(2)}) copy-start(bf16[3,512,512]{2,1,0:T(8,128)(2,1)S(1)} %copy.6.right_high) | copy-start | bytes 4718596
  147.9 48.7 %copy-start.1 = (bf16[3,512,512]{2,1,0:T(8,128)(2,1)}, bf16[3,512,512]{2,1,0:T(8,128)(2,1)S(1)}, u32[]{:S(2)}) copy-start(bf16[3,512,512]{2,1,0:T(8,128)(2,1)S(1)} %copy.7.right_low) | copy-start | bytes 4718596
  147.9 48.7 %collective-permute-start.18 = (f32[4,128,512]{2,1,0:T(8,128)}, f32[4,128,512]{2,1,0:T(8,128)S(1)}, u32[]{:S(2)}, u32[]{:S(2)}) collective-permute-start(f32[4,128,512]{2,1,0:T(8,128)} %collective-permute-done.16.refs_12_), channel_id=1, source_target_pairs={{0,1},{1,0},{2,3},{3,2},{4,5},{5,4},{6,7},{7,6},{8,9},{9,8},{10,11... | collective-permute-start | bytes 3145736 | tf_op jit(solution)/shard_map/ppermute | solution.py:234
  164.0 34.6 %collective-permute-start.11 = (f32[4,128,512]{2,1,0:T(8,128)}, f32[4,128,512]{2,1,0:T(8,128)S(1)}, u32[]{:S(2)}, u32[]{:S(2)}) collective-permute-start(f32[4,128,512]{2,1,0:T(8,128)} %copy-done.15), channel_id=1, source_target_pairs={{0,1},{1,0},{2,3},{3,2},{4,5},{5,4},{6,7},{7,6},{8,9},{9,8},{10,11... | collective-permute-start | bytes 3145736 | tf_op jit(solution)/shard_map/ppermute | solution.py:234
  164.0 39.7 %collective-permute-start.23 = (f32[4,128,512]{2,1,0:T(8,128)}, f32[4,128,512]{2,1,0:T(8,128)S(1)}, u32[]{:S(2)}, u32[]{:S(2)}) collective-permute-start(f32[4,128,512]{2,1,0:T(8,128)} %copy-done.30), channel_id=1, source_target_pairs={{0,1},{1,0},{2,3},{3,2},{4,5},{5,4},{6,7},{7,6},{8,9},{9,8},{10,11... | collective-permute-start | bytes 3145736 | tf_op jit(solution)/shard_map/ppermute | solution.py:234
  164.5 39.2 %collective-permute-start.10 = (f32[4,128,512]{2,1,0:T(8,128)}, f32[4,128,512]{2,1,0:T(8,128)S(1)}, u32[]{:S(2)}, u32[]{:S(2)}) collective-permute-start(f32[4,128,512]{2,1,0:T(8,128)} %collective-permute-done.7.refs_0_), channel_id=1, source_target_pairs={{0,1},{1,0},{2,3},{3,2},{4,5},{5,4},{6,7},{7,6},{8,9},{9,8},{10,11... | collective-permute-start | bytes 3145736 | tf_op jit(solution)/shard_map/ppermute | solution.py:234
  164.5 39.1 %collective-permute-start.22 = (f32[4,128,512]{2,1,0:T(8,128)}, f32[4,128,512]{2,1,0:T(8,128)}, u32[]{:S(2)}, u32[]{:S(2)}) collective-permute-start(f32[4,128,512]{2,1,0:T(8,128)} %collective-permute-done.20.refs_16_), channel_id=1, source_target_pairs={{0,1},{1,0},{2,3},{3,2},{4,5},{5,4},{6,7},{7,6},{8,9},{9,8},{10,11... | collective-permute-start | bytes 3145736 | tf_op jit(solution)/shard_map/ppermute | solution.py:234
  174.8 29.9 %copy-start.4 = (f32[4,128,512]{2,1,0:T(8,128)S(1)}, f32[4,128,512]{2,1,0:T(8,128)}, u32[]{:S(2)}) copy-start(f32[4,128,512]{2,1,0:T(8,128)} %add_momenta.7.refs_9_.refs_1_) | copy-start | bytes 3145732
  174.8 29.9 %copy-start.7 = (f32[4,128,512]{2,1,0:T(8,128)S(1)}, f32[4,128,512]{2,1,0:T(8,128)}, u32[]{:S(2)}) copy-start(f32[4,128,512]{2,1,0:T(8,128)} %add_momenta.5.refs_8_.refs_0_) | copy-start | bytes 3145732
  174.8 29.9 %copy-start.10 = (f32[4,128,512]{2,1,0:T(8,128)S(1)}, f32[4,128,512]{2,1,0:T(8,128)}, u32[]{:S(2)}) copy-start(f32[4,128,512]{2,1,0:T(8,128)} %copy-done.8) | copy-start | bytes 3145732
  174.8 29.9 %copy-start.14 = (f32[4,128,512]{2,1,0:T(8,128)S(1)}, f32[4,128,512]{2,1,0:T(8,128)}, u32[]{:S(2)}) copy-start(f32[4,128,512]{2,1,0:T(8,128)} %copy-done.12) | copy-start | bytes 3145732
  174.8 29.9 %copy-start.16 = (f32[4,128,512]{2,1,0:T(8,128)S(1)}, f32[4,128,512]{2,1,0:T(8,128)}, u32[]{:S(2)}) copy-start(f32[4,128,512]{2,1,0:T(8,128)} %copy-done.15) | copy-start | bytes 3145732
  196.6 36.8 %collective-permute-start.29 = (f32[4,128,512]{2,1,0:T(8,128)S(1)}, f32[4,128,512]{2,1,0:T(8,128)S(1)}, u32[]{:S(2)}, u32[]{:S(2)}) collective-permute-start(f32[4,128,512]{2,1,0:T(8,128)S(1)} %get-tuple-element.37), channel_id=1, source_target_pairs={{0,12},{1,13},{12,0},{13,1},{2,14},{3,15},{14,2},{15,3},{16,28},{1... | collective-permute-start | bytes 3145736 | tf_op jit(solution)/shard_map/ppermute | solution.py:287
  198.5 48.4 %collective-permute-start.36 = (f32[4,128,512]{2,1,0:T(8,128)S(1)}, f32[4,128,512]{2,1,0:T(8,128)S(1)}, u32[]{:S(2)}, u32[]{:S(2)}) collective-permute-start(f32[4,128,512]{2,1,0:T(8,128)S(1)} %get-tuple-element.44), channel_id=1, source_target_pairs={{0,13},{1,12},{12,1},{13,0},{2,15},{3,14},{14,3},{15,2},{16,29},{1... | collective-permute-start | bytes 3145736 | tf_op jit(solution)/shard_map/ppermute | solution.py:287
  212.5 35.9 %collective-permute-start.25 = (f32[1,128,512]{2,1,0:T(8,128)S(1)}, f32[1,128,512]{2,1,0:T(8,128)S(1)}, u32[]{:S(2)}, u32[]{:S(2)}) collective-permute-start(f32[1,128,512]{2,1,0:T(8,128)S(1)} %get-tuple-element.32), channel_id=1, source_target_pairs={{0,2},{1,3},{2,0},{3,1},{4,6},{5,7},{6,4},{7,5},{8,10},{9,11},{10,... | collective-permute-start | bytes 786440 | tf_op jit(solution)/shard_map/ppermute | solution.py:305
  214.0 34.9 %collective-permute-start.31 = (f32[1,128,512]{2,1,0:T(8,128)S(1)}, f32[1,128,512]{2,1,0:T(8,128)S(1)}, u32[]{:S(2)}, u32[]{:S(2)}) collective-permute-start(f32[1,128,512]{2,1,0:T(8,128)S(1)} %get-tuple-element.39), channel_id=1, source_target_pairs={{0,1},{1,0},{2,3},{3,2},{4,5},{5,4},{6,7},{7,6},{8,9},{9,8},{10,11... | collective-permute-start | bytes 786440 | tf_op jit(solution)/shard_map/ppermute | solution.py:305
  224.9 47.6 %collective-permute-start.26 = (f32[2,128,512]{2,1,0:T(8,128)S(1)}, f32[2,128,512]{2,1,0:T(8,128)S(1)}, u32[]{:S(2)}, u32[]{:S(2)}) collective-permute-start(f32[2,128,512]{2,1,0:T(8,128)S(1)} %get-tuple-element.33), channel_id=1, source_target_pairs={{0,2},{1,3},{2,0},{3,1},{4,6},{5,7},{6,4},{7,5},{8,10},{9,11},{10,... | collective-permute-start | bytes 1572872 | tf_op jit(solution)/shard_map/ppermute | solution.py:305
  233.4 40.0 %copy-start.34 = (f32[4,128,512]{2,1,0:T(8,128)}, f32[4,128,512]{2,1,0:T(8,128)S(1)}, u32[]{:S(2)}) copy-start(f32[4,128,512]{2,1,0:T(8,128)S(1)} %collective-permute-done.29.refs_6_) | copy-start | bytes 3145732
  233.4 15.7 %collective-permute-start.34 = (f32[1,128,512]{2,1,0:T(8,128)S(1)}, f32[1,128,512]{2,1,0:T(8,128)S(1)}, u32[]{:S(2)}, u32[]{:S(2)}) collective-permute-start(f32[1,128,512]{2,1,0:T(8,128)S(1)} %get-tuple-element.42), channel_id=1, source_target_pairs={{0,3},{1,2},{2,1},{3,0},{4,7},{5,6},{6,5},{7,4},{8,11},{9,10},{10,... | collective-permute-start | bytes 786440 | tf_op jit(solution)/shard_map/ppermute | solution.py:305
  247.0 9.2 %collective-permute-start.24 = (f32[1,128,512]{2,1,0:T(8,128)S(1)}, f32[1,128,512]{2,1,0:T(8,128)S(1)}, u32[]{:S(2)}, u32[]{:S(2)}) collective-permute-start(f32[1,128,512]{2,1,0:T(8,128)S(1)} %get-tuple-element.31), channel_id=1, source_target_pairs={{0,2},{1,3},{2,0},{3,1},{4,6},{5,7},{6,4},{7,5},{8,10},{9,11},{10,... | collective-permute-start | bytes 786440 | tf_op jit(solution)/shard_map/ppermute | solution.py:305
  248.5 24.1 %collective-permute-start.32 = (f32[2,128,512]{2,1,0:T(8,128)S(1)}, f32[2,128,512]{2,1,0:T(8,128)S(1)}, u32[]{:S(2)}, u32[]{:S(2)}) collective-permute-start(f32[2,128,512]{2,1,0:T(8,128)S(1)} %get-tuple-element.40), channel_id=1, source_target_pairs={{0,1},{1,0},{2,3},{3,2},{4,5},{5,4},{6,7},{7,6},{8,9},{9,8},{10,11... | collective-permute-start | bytes 1572872 | tf_op jit(solution)/shard_map/ppermute | solution.py:305
  248.9 23.6 %collective-permute-start.35 = (f32[2,128,512]{2,1,0:T(8,128)S(1)}, f32[2,128,512]{2,1,0:T(8,128)S(1)}, u32[]{:S(2)}, u32[]{:S(2)}) collective-permute-start(f32[2,128,512]{2,1,0:T(8,128)S(1)} %get-tuple-element.43), channel_id=1, source_target_pairs={{0,3},{1,2},{2,1},{3,0},{4,7},{5,6},{6,5},{7,4},{8,11},{9,10},{10,... | collective-permute-start | bytes 1572872 | tf_op jit(solution)/shard_map/ppermute | solution.py:305
  249.2 7.7 %collective-permute-start.30 = (f32[1,128,512]{2,1,0:T(8,128)S(1)}, f32[1,128,512]{2,1,0:T(8,128)S(1)}, u32[]{:S(2)}, u32[]{:S(2)}) collective-permute-start(f32[1,128,512]{2,1,0:T(8,128)S(1)} %get-tuple-element.38), channel_id=1, source_target_pairs={{0,1},{1,0},{2,3},{3,2},{4,5},{5,4},{6,7},{7,6},{8,9},{9,8},{10,11... | collective-permute-start | bytes 786440 | tf_op jit(solution)/shard_map/ppermute | solution.py:305
  256.2 16.4 %collective-permute-start.33 = (f32[1,128,512]{2,1,0:T(8,128)S(1)}, f32[1,128,512]{2,1,0:T(8,128)S(1)}, u32[]{:S(2)}, u32[]{:S(2)}) collective-permute-start(f32[1,128,512]{2,1,0:T(8,128)S(1)} %get-tuple-element.41), channel_id=1, source_target_pairs={{0,3},{1,2},{2,1},{3,0},{4,7},{5,6},{6,5},{7,4},{8,11},{9,10},{10,... | collective-permute-start | bytes 786440 | tf_op jit(solution)/shard_map/ppermute | solution.py:305
  (37 other events, 269.8 us)
where the time goes:
time: 280 us; the launch traced here: 279 us
  waiting for transfers between devices  130 us (46%)
  Pallas kernels  66 us (24%)
  starting transfers between devices  39.7 us (14%)
  local copies, waits for them, and re-layouts  26.3 us (9%)
  other arithmetic  9.19 us (3%)
  between operations  8.17 us (3%)
    pallas_call x4, Pallas kernels, sandwich(): pl.pallas_call(functools.partial(split_dot, len(groups), len(groups[0][0]...  46.4 us
    ppermute x4, waiting for transfers between devices, shards(): lax.ppermute(x, 'energy', down[d - 1])  45 us
    ppermute x2, waiting for transfers between devices, shards(): lax.ppermute(x, 'atom', around[s])  23.5 us
    ppermute x9, waiting for transfers between devices, shards(): block = lax.ppermute(block, ('atom', 'kz'), pairs)  22.2 us
    unnamed x96, local copies, waits for them, and re-layouts  20.3 us
    ppermute x1, waiting for transfers between devices, shards(): got = lax.ppermute(mine, 'atom', around[s])  15.6 us
    pallas_call x4, Pallas kernels, summed(): pl.pallas_call(add_momenta, out_shape=jax.ShapeDtypeStruct((half, size, o...  14.7 us
    ppermute x2, waiting for transfers between devices, shards(): beyond.append(lax.ppermute(sums[t], ('energy', 'kz'), pairs))  12.5 us
  transfers between devices with their start and end apart: 37, of which 10 were waited for; matrix products, arithmetic and copies ran while one was open for 5% of the time, Pallas kernels for 22%

commit v1 on v0

--- a/solution.py
+++ b/solution.py
@@ -22,14 +22,26 @@
     return high.astype(jnp.bfloat16), (x - high).astype(jnp.bfloat16)
 
 
-def add_momenta(where, green, *refs):
-    out = refs[-1]
-    total = green[0, 0]
-    for k in range(1, green.shape[0]):
-        total = total + green[k, 0]
-    for ref in refs[:-1]:
-        total = total + ref[0]
-    out[0] = total
+def add_momenta(theirs, first, green, *refs):
+    out, held, total, arrived, left = refs[-5:]
+    given = refs[:-5]
+    momenta, count, size = green.shape[0], held.shape[0], held.shape[2]
+    core = lax.axis_index("kz")
+    base = (1 - core if theirs else core) * count
+    for e in range(count):
+        for k in range(momenta):
+            pltpu.make_async_copy(green.at[k, base + e, pl.ds(first, size)], held.at[e, k], arrived.at[e]).start()
+        for ref in given:
+            pltpu.make_async_copy(ref.at[e], held.at[e, momenta], arrived.at[e]).start()
+    for e in range(count):
+        pltpu.make_async_copy(held.at[e], held.at[e], arrived.at[e]).wait()
+        value = held[e, 0]
+        for k in range(1, held.shape[1]):
+            value = value + held[e, k]
+        total[e] = value
+        pltpu.make_async_copy(total.at[e], out.at[e], left.at[e]).start()
+    for e in range(count):
+        pltpu.make_async_copy(total.at[e], out.at[e], left.at[e]).wait()
 
 
 def split_dot(n_groups, n_parts, n_atoms, momenta, base, grid_total, edev, far, line, steps, occupation, right_high, right_low, left, *refs):
@@ -193,27 +205,24 @@
     size = brows // PIECES
 
     def summed(theirs, piece, *more):
-        def first(e, where):
-            return 0, where[0] * half + e, piece, 0
-
-        where = ((core + 1) % cores if theirs else core).reshape(1)
-        spec = pl.BlockSpec((1, size, order), lambda e, where: (e, 0, 0))
         return pl.pallas_call(
-            add_momenta,
+            functools.partial(add_momenta, theirs, piece * size),
             out_shape=jax.ShapeDtypeStruct((half, size, order), jnp.float32),
-            grid_spec=pltpu.PrefetchScalarGridSpec(
-                num_scalar_prefetch=1,
-                grid=(half,),
-                in_specs=[pl.BlockSpec((momenta_here, 1, size, order), first)] + [spec] * len(more),
-                out_specs=spec,
-            ),
+            in_specs=[pl.BlockSpec(memory_space=pl.ANY)] * (1 + len(more)),
+            out_specs=pl.BlockSpec(memory_space=pl.ANY),
+            scratch_shapes=[
+                pltpu.VMEM((half, momenta_here + len(more), size, order), jnp.float32),
+                pltpu.VMEM((half, size, order), jnp.float32),
+                pltpu.SemaphoreType.DMA((half,)),
+                pltpu.SemaphoreType.DMA((half,)),
+            ],
             cost_estimate=pl.CostEstimate(
                 flops=momenta_here * half * size * order,
                 bytes_accessed=4 * (momenta_here + 1 + len(more)) * half * size * order,
                 transcendentals=0,
             ),
             name="add_momenta",
-        )(where, green, *more)
+        )(green, *more)
 
     own = []
     for piece in range(PIECES):
@@ -268,7 +277,9 @@
 
     beyond = []
     if line:
-        left_far = left_of(lax.dynamic_slice(coupling, (0, atom * cores * out_rows, 0), (MODES, cores * out_rows, order)))
+        left_far = left_of(
+            lax.dynamic_slice(coupling, (0, atom * cores * out_rows, 0), (MODES, cores * out_rows, order))
+        )
         got = [lax.ppermute(x, "atom", around[s]) for s in range(1, atoms) for x in own]
         got, right, left_far, left_near = lax.optimization_barrier((got, right, left_far, left_near))
         whole = (

time: 280 us -> 294 us (1.050)
  waiting for transfers between devices: 130 us -> 149 us
  Pallas kernels: 66 us -> 61.1 us
    ppermute x4, waiting for transfers between devices: 45 us -> 70.5 us  [shards(): lax.ppermute(x, 'energy', down[d - 1])]
    ppermute x4, waiting for transfers between devices: 10.6 us -> 3.56 us  [shards(): streams[-d] = [lax.ppermute(x, 'energy', up[d - 1]) for x in streams[1 - d]]]
    pallas_call x4, Pallas kernels: 14.7 us -> 9.87 us  [summed(): pl.pallas_call(functools.partial(add_momenta, theirs, piece * size), out_...]
    unnamed x96 -> x98, local copies, waits for them, and re-layouts: 20.3 us -> 20.3 us
  transfers between devices with their start and end apart: 37 -> 37, of which waited for: 10 -> 11; matrix products, arithmetic and copies ran while one was open for 5% -> 5% of each run, Pallas kernels for 22% -> 19%
where the time goes in v1:
time: 294 us; the launch traced here: 293 us
  waiting for transfers between devices  149 us (51%)
  Pallas kernels  61.1 us (21%)
  starting transfers between devices  39 us (13%)
  local copies, waits for them, and re-layouts  26.3 us (9%)
  other arithmetic  9.19 us (3%)
  between operations  8.1 us (3%)
    ppermute x4, waiting for transfers between devices, shards(): lax.ppermute(x, 'energy', down[d - 1])  70.5 us
    pallas_call x4, Pallas kernels, sandwich(): pl.pallas_call(functools.partial(split_dot, len(groups), len(groups[0][0]...  46.3 us
    ppermute x9, waiting for transfers between devices, shards(): block = lax.ppermute(block, ('atom', 'kz'), pairs)  22.3 us
    ppermute x2, waiting for transfers between devices, shards(): lax.ppermute(x, 'atom', around[s])  21.3 us
    unnamed x98, local copies, waits for them, and re-layouts  20.3 us
    ppermute x1, waiting for transfers between devices, shards(): got = lax.ppermute(mine, 'atom', around[s])  18 us
    ppermute x2, waiting for transfers between devices, shards(): beyond.append(lax.ppermute(sums[t], ('energy', 'kz'), pairs))  13.2 us
    ppermute x4, starting transfers between devices, shards(): streams[-d] = [lax.ppermute(x, 'energy', up[d - 1]) for x in streams[1 - d]]  11 us
  transfers between devices with their start and end apart: 37, of which 11 were waited for; matrix products, arithmetic and copies ran while one was open for 5% of the time, Pallas kernels for 19%

profile of v1, /device:TPU:0, one launch (start us, length us, event | category | flops | bytes accessed | tf_op | source)
XLA Modules:
  0.0 292.6 jit_solution(15255499328024068739)
XLA Ops:
  0.0 1.3 constant_dynamic-slice_fusion
  1.3 3.0 %collective-permute-start.4 = (f32[2,256,512]{2,1,0:T(8,128)S(1)}, f32[2,256,512]{2,1,0:T(8,128)}, u32[]{:S(2)}, u32[]{:S(2)}) collective-permute-start(f32[2,256,512]{2,1,0:T(8,128)S(1)} %constant_dynamic-slice_fusion), channel_id=1, source_target_pairs={{0,2},{2,0},{1,3},{3,1},{4,6},{6,4},{5,7},{7,5},{8,10},{10,8},{9,1... | collective-permute-start | bytes 3145736 | tf_op jit(solution)/shard_map/ppermute | solution.py:250
  4.3 2.3 add_momenta.4
  6.7 2.3 add_momenta.6
  9.6 18.0 %collective-permute-done.4 = f32[2,256,512]{2,1,0:T(8,128)} collective-permute-done((f32[2,256,512]{2,1,0:T(8,128)S(1)}, f32[2,256,512]{2,1,0:T(8,128)}, u32[]{:S(2)}, u32[]{:S(2)}) %collective-permute-start.4) | collective-permute-done | bytes 1048608 | tf_op jit(solution)/shard_map/ppermute | solution.py:250
  28.6 2.6 add_momenta.5.refs_8_.refs_0_
  31.2 1.8 collective-permute-start.1
  34.0 2.6 add_momenta.7.refs_9_.refs_1_
  45.6 4.9 %collective-permute-start.6 = (f32[4,128,512]{2,1,0:T(8,128)S(1)}, f32[4,128,512]{2,1,0:T(8,128)}, u32[]{:S(2)}, u32[]{:S(2)}) collective-permute-start(f32[4,128,512]{2,1,0:T(8,128)S(1)} %copy-done.2), channel_id=1, source_target_pairs={{0,4},{4,8},{8,12},{1,5},{5,9},{9,13},{2,6},{6,10},{10,14},{3,7},{... | collective-permute-start | bytes 3145736 | tf_op jit(solution)/shard_map/ppermute | solution.py:241
  50.5 2.2 dynamic-slice_select_fusion.5
  53.5 4.0 %collective-permute-done.1.refs_2_ = f32[4,128,512]{2,1,0:T(8,128)S(1)} collective-permute-done((f32[4,128,512]{2,1,0:T(8,128)}, f32[4,128,512]{2,1,0:T(8,128)S(1)}, u32[]{:S(2)}, u32[]{:S(2)}) %collective-permute-start.1) | collective-permute-done | bytes 1048608 | tf_op jit(solution)/shard_map/ppermute | solution.py:283
  57.5 4.7 %collective-permute-start.8 = (f32[4,128,512]{2,1,0:T(8,128)S(1)}, f32[4,128,512]{2,1,0:T(8,128)}, u32[]{:S(2)}, u32[]{:S(2)}) collective-permute-start(f32[4,128,512]{2,1,0:T(8,128)S(1)} %copy-done.5), channel_id=1, source_target_pairs={{0,4},{4,8},{8,12},{1,5},{5,9},{9,13},{2,6},{6,10},{10,14},{3,7},{... | collective-permute-start | bytes 3145736 | tf_op jit(solution)/shard_map/ppermute | solution.py:241
  62.3 17.3 %collective-permute-done.3.refs_3_ = f32[4,128,512]{2,1,0:T(8,128)S(1)} collective-permute-done((f32[4,128,512]{2,1,0:T(8,128)}, f32[4,128,512]{2,1,0:T(8,128)S(1)}, u32[]{:S(2)}, u32[]{:S(2)}) %collective-permute-start.3) | collective-permute-done | bytes 1048608 | tf_op jit(solution)/shard_map/ppermute | solution.py:283
  79.6 1.3 collective-permute-start.16
  81.7 1.5 pad_maximum_fusion.2.left
  83.3 2.2 fusion
  85.5 1.6 pad_maximum_fusion.1.left
  88.1 1.3 collective-permute-start.17
  90.9 3.6 %collective-permute-done.8.refs_5_ = f32[4,128,512]{2,1,0:T(8,128)} collective-permute-done((f32[4,128,512]{2,1,0:T(8,128)S(1)}, f32[4,128,512]{2,1,0:T(8,128)}, u32[]{:S(2)}, u32[]{:S(2)}) %collective-permute-start.8) | collective-permute-done | bytes 1048608 | tf_op jit(solution)/shard_map/ppermute | solution.py:241
  95.2 12.4 %collective-permute-done.16.refs_12_ = f32[4,128,512]{2,1,0:T(8,128)} collective-permute-done((f32[4,128,512]{2,1,0:T(8,128)S(1)}, f32[4,128,512]{2,1,0:T(8,128)}, u32[]{:S(2)}, u32[]{:S(2)}) %collective-permute-start.16) | collective-permute-done | bytes 1048608 | tf_op jit(solution)/shard_map/ppermute | solution.py:242
  108.3 20.6 %collective-permute-done.17.refs_13_ = f32[4,128,512]{2,1,0:T(8,128)} collective-permute-done((f32[4,128,512]{2,1,0:T(8,128)S(1)}, f32[4,128,512]{2,1,0:T(8,128)}, u32[]{:S(2)}, u32[]{:S(2)}) %collective-permute-start.17) | collective-permute-done | bytes 1048608 | tf_op jit(solution)/shard_map/ppermute | solution.py:242
  128.9 1.3 collective-permute-start.20
  131.2 1.3 collective-permute-start.21
  134.6 1.0 copy-done.17
  136.1 1.7 copy.6.right_high
  137.9 2.3 copy.7.right_low
  140.2 17.0 %collective-permute-done.20.refs_16_ = f32[4,128,512]{2,1,0:T(8,128)} collective-permute-done((f32[4,128,512]{2,1,0:T(8,128)}, f32[4,128,512]{2,1,0:T(8,128)}, u32[]{:S(2)}, u32[]{:S(2)}) %collective-permute-start.20) | collective-permute-done | bytes 1048608 | tf_op jit(solution)/shard_map/ppermute | solution.py:242
  157.2 20.5 %collective-permute-done.21.refs_17_ = f32[4,128,512]{2,1,0:T(8,128)} collective-permute-done((f32[4,128,512]{2,1,0:T(8,128)}, f32[4,128,512]{2,1,0:T(8,128)}, u32[]{:S(2)}, u32[]{:S(2)}) %collective-permute-start.21) | collective-permute-done | bytes 1048608 | tf_op jit(solution)/shard_map/ppermute | solution.py:242
  178.7 1.2 copy-done.3
  179.9 1.2 copy-done.6
  181.1 1.2 copy-done.9
  182.4 1.2 copy-done.12
  183.6 1.2 copy-done.25
  184.8 1.2 copy-done.27
  186.0 1.2 copy-done.29
  187.3 1.2 copy-done.31
  188.5 21.7 %far_sandwich.1 = (f32[4,128,512]{2,1,0:T(8,128)S(1)}, f32[4,128,512]{2,1,0:T(8,128)S(1)}) custom-call(s32[3]{0:T(128)S(1)} %copy-done.22, f32[3]{0:T(128)S(1)} %copy-done.23, bf16[3,512,512]{2,1,0:T(8,128)(2,1)S(1)} %copy.6.right_high, bf16[3,512,512]{2,1,0:T(8,128)(2,1)S(1)} %copy.7.right_low, bf16[3,256,1536]{2,1,0:T(8,128)(2,1)} %pad_maximum_fusion.1.left, ...), custom_call_target="tpu_custom_call" | custom-call | flops 14495514624 | bytes 27262976 | tf_op jit(solution)/shard_map/far_sandwich/pallas_call | solution.py:147
  210.3 1.9 collective-permute-start.29
  212.2 5.1 %collective-permute-start.36 = (f32[4,128,512]{2,1,0:T(8,128)S(1)}, f32[4,128,512]{2,1,0:T(8,128)S(1)}, u32[]{:S(2)}, u32[]{:S(2)}) collective-permute-start(f32[4,128,512]{2,1,0:T(8,128)S(1)} %get-tuple-element.44), channel_id=1, source_target_pairs={{0,13},{1,12},{12,1},{13,0},{2,15},{3,14},{14,3},{15,2},{16,29},{1... | collective-permute-start | bytes 3145736 | tf_op jit(solution)/shard_map/ppermute | solution.py:298
  218.4 7.2 %near_sandwich.4 = (f32[1,128,512]{2,1,0:T(8,128)S(1)}, f32[1,128,512]{2,1,0:T(8,128)S(1)}, f32[1,128,512]{2,1,0:T(8,128)S(1)}, f32[1,128,512]{2,1,0:T(8,128)S(1)}) custom-call(s32[3]{0:T(128)S(1)} %copy-done.22, f32[3]{0:T(128)S(1)} %copy-done.23, bf16[3,512,512]{2,1,0:T(8,128)(2,1)} %copy-done, bf16[3,512,512]{2,1,0:T(8,128)(2,1)} %copy-done.1, ...), custom_call_target="tpu_custom_call" | custom-call | flops 2415919104 | bytes 4194304 | tf_op jit(solution)/shard_map/near_sandwich/pallas_call | solution.py:147
  225.6 1.5 collective-permute-start.25
  227.6 10.3 %near_sandwich.5 = (f32[2,128,512]{2,1,0:T(8,128)S(1)}, f32[2,128,512]{2,1,0:T(8,128)S(1)}, f32[2,128,512]{2,1,0:T(8,128)S(1)}, f32[2,128,512]{2,1,0:T(8,128)S(1)}) custom-call(s32[3]{0:T(128)S(1)} %copy-done.22, f32[3]{0:T(128)S(1)} %copy-done.23, bf16[3,512,512]{2,1,0:T(8,128)(2,1)} %copy-done, bf16[3,512,512]{2,1,0:T(8,128)(2,1)} %copy-done.1, ...), custom_call_target="tpu_custom_call" | custom-call | flops 4831838208 | bytes 8388608 | tf_op jit(solution)/shard_map/near_sandwich/pallas_call | solution.py:147
  238.6 7.1 %near_sandwich.3 = (f32[1,128,512]{2,1,0:T(8,128)S(1)}, f32[1,128,512]{2,1,0:T(8,128)S(1)}, f32[1,128,512]{2,1,0:T(8,128)S(1)}, f32[1,128,512]{2,1,0:T(8,128)S(1)}) custom-call(s32[3]{0:T(128)S(1)} %copy-done.22, f32[3]{0:T(128)S(1)} %copy-done.23, bf16[3,512,512]{2,1,0:T(8,128)(2,1)} %copy-done, bf16[3,512,512]{2,1,0:T(8,128)(2,1)} %copy-done.1, ...), custom_call_target="tpu_custom_call" | custom-call | flops 2415919104 | bytes 4194304 | tf_op jit(solution)/shard_map/near_sandwich/pallas_call | solution.py:147
  247.4 13.2 %collective-permute-done.36.refs_13_ = f32[4,128,512]{2,1,0:T(8,128)S(1)} collective-permute-done((f32[4,128,512]{2,1,0:T(8,128)S(1)}, f32[4,128,512]{2,1,0:T(8,128)S(1)}, u32[]{:S(2)}, u32[]{:S(2)}) %collective-permute-start.36) | collective-permute-done | bytes 1048608 | tf_op jit(solution)/shard_map/ppermute | solution.py:298
  260.7 1.4 collective-permute-start.24
  263.3 6.6 %collective-permute-done.24.refs_3_ = f32[1,128,512]{2,1,0:T(8,128)S(1)} collective-permute-done((f32[1,128,512]{2,1,0:T(8,128)S(1)}, f32[1,128,512]{2,1,0:T(8,128)S(1)}, u32[]{:S(2)}, u32[]{:S(2)}) %collective-permute-start.24) | collective-permute-done | bytes 262176 | tf_op jit(solution)/shard_map/ppermute | solution.py:316
  270.5 15.7 %collective-permute-done.33.refs_10_ = f32[1,128,512]{2,1,0:T(8,128)S(1)} collective-permute-done((f32[1,128,512]{2,1,0:T(8,128)S(1)}, f32[1,128,512]{2,1,0:T(8,128)S(1)}, u32[]{:S(2)}, u32[]{:S(2)}) %collective-permute-start.33) | collective-permute-done | bytes 262176 | tf_op jit(solution)/shard_map/ppermute | solution.py:316
  287.5 4.9 %gather_up.1 = f32[128,8,512]{2,1,0:T(8,128)} custom-call(f32[1,128,512]{2,1,0:T(8,128)} %copy-done.21, f32[1,128,512]{2,1,0:T(8,128)} %copy-done.20, f32[2,128,512]{2,1,0:T(8,128)} %copy-done.19, f32[1,128,512]{2,1,0:T(8,128)} %copy-done.45, f32[1,128,512]{2,1,0:T(8,128)} %copy-done.42, f32[2,128,512]{2,1,0:T(8,128)} %copy-done.39, ...), custom_call_target="tpu_custom_call" | custom-call | tf_op jit(solution)/shard_map/gather_up/pallas_call | solution.py:324
  (146 shorter events, 21.4 us)
Async XLA Ops:
  1.3 26.3 %collective-permute-start.4 = (f32[2,256,512]{2,1,0:T(8,128)S(1)}, f32[2,256,512]{2,1,0:T(8,128)}, u32[]{:S(2)}, u32[]{:S(2)}) collective-permute-start(f32[2,256,512]{2,1,0:T(8,128)S(1)} %constant_dynamic-slice_fusion), channel_id=1, source_target_pairs={{0,2},{2,0},{1,3},{3,1},{4,6},{6,4},{5,7},{7,5},{8,10},{10,8},{9,1... | collective-permute-start | bytes 3145736 | tf_op jit(solution)/shard_map/ppermute | solution.py:250
  6.6 21.0 %collective-permute-start = (f32[4,128,512]{2,1,0:T(8,128)}, f32[4,128,512]{2,1,0:T(8,128)S(1)}, u32[]{:S(2)}, u32[]{:S(2)}) collective-permute-start(f32[4,128,512]{2,1,0:T(8,128)} %add_momenta.4), channel_id=1, source_target_pairs={{0,1},{1,0},{2,3},{3,2},{4,5},{5,4},{6,7},{7,6},{8,9},{9,8},{10,11... | collective-permute-start | bytes 3145736 | tf_op jit(solution)/shard_map/ppermute | solution.py:230
  9.0 24.0 %collective-permute-start.2 = (f32[4,128,512]{2,1,0:T(8,128)}, f32[4,128,512]{2,1,0:T(8,128)S(1)}, u32[]{:S(2)}, u32[]{:S(2)}) collective-permute-start(f32[4,128,512]{2,1,0:T(8,128)} %add_momenta.6), channel_id=1, source_target_pairs={{0,1},{1,0},{2,3},{3,2},{4,5},{5,4},{6,7},{7,6},{8,9},{9,8},{10,11... | collective-permute-start | bytes 3145736 | tf_op jit(solution)/shard_map/ppermute | solution.py:230
  27.6 18.0 %collective-permute-start.5 = (f32[2,256,512]{2,1,0:T(8,128)}, f32[2,256,512]{2,1,0:T(8,128)}, u32[]{:S(2)}, u32[]{:S(2)}) collective-permute-start(f32[2,256,512]{2,1,0:T(8,128)} %collective-permute-done.4), channel_id=1, source_target_pairs={{0,1},{1,0},{2,3},{3,2},{4,5},{5,4},{6,7},{7,6},{8,9},{9,8},{10,11... | collective-permute-start | bytes 3145736 | tf_op jit(solution)/shard_map/ppermute | solution.py:251
  31.2 26.3 %collective-permute-start.1 = (f32[4,128,512]{2,1,0:T(8,128)}, f32[4,128,512]{2,1,0:T(8,128)S(1)}, u32[]{:S(2)}, u32[]{:S(2)}) collective-permute-start(f32[4,128,512]{2,1,0:T(8,128)} %add_momenta.5.refs_8_.refs_0_), channel_id=1, source_target_pairs={{0,2},{2,0},{1,3},{3,1},{4,6},{6,4},{5,7},{7,5},{8,10},{10,8},{9,1... | collective-permute-start | bytes 3145736 | tf_op jit(solution)/shard_map/ppermute | solution.py:283
  36.7 42.9 %collective-permute-start.3 = (f32[4,128,512]{2,1,0:T(8,128)}, f32[4,128,512]{2,1,0:T(8,128)S(1)}, u32[]{:S(2)}, u32[]{:S(2)}) collective-permute-start(f32[4,128,512]{2,1,0:T(8,128)} %add_momenta.7.refs_9_.refs_1_), channel_id=1, source_target_pairs={{0,2},{2,0},{1,3},{3,1},{4,6},{6,4},{5,7},{7,5},{8,10},{10,8},{9,1... | collective-permute-start | bytes 3145736 | tf_op jit(solution)/shard_map/ppermute | solution.py:283
  45.0 42.0 %collective-permute-start.14 = (f32[4,128,512]{2,1,0:T(8,128)S(1)}, f32[4,128,512]{2,1,0:T(8,128)S(1)}, u32[]{:S(2)}, u32[]{:S(2)}) collective-permute-start(f32[4,128,512]{2,1,0:T(8,128)S(1)} %copy-done.2), channel_id=1, source_target_pairs={{0,1},{1,0},{2,3},{3,2},{4,5},{5,4},{6,7},{7,6},{8,9},{9,8},{10,11... | collective-permute-start | bytes 3145736 | tf_op jit(solution)/shard_map/ppermute | solution.py:243
  45.1 44.3 %collective-permute-start.15 = (f32[4,128,512]{2,1,0:T(8,128)}, f32[4,128,512]{2,1,0:T(8,128)S(1)}, u32[]{:S(2)}, u32[]{:S(2)}) collective-permute-start(f32[4,128,512]{2,1,0:T(8,128)} %add_momenta.7.refs_9_.refs_1_), channel_id=1, source_target_pairs={{0,1},{1,0},{2,3},{3,2},{4,5},{5,4},{6,7},{7,6},{8,9},{9,8},{10,11... | collective-permute-start | bytes 3145736 | tf_op jit(solution)/shard_map/ppermute | solution.py:243
  45.6 44.8 %collective-permute-start.6 = (f32[4,128,512]{2,1,0:T(8,128)S(1)}, f32[4,128,512]{2,1,0:T(8,128)}, u32[]{:S(2)}, u32[]{:S(2)}) collective-permute-start(f32[4,128,512]{2,1,0:T(8,128)S(1)} %copy-done.2), channel_id=1, source_target_pairs={{0,4},{4,8},{8,12},{1,5},{5,9},{9,13},{2,6},{6,10},{10,14},{3,7},{... | collective-permute-start | bytes 3145736 | tf_op jit(solution)/shard_map/ppermute | solution.py:241
  57.5 31.8 %copy-start.24 = (f32[4,128,512]{2,1,0:T(8,128)}, f32[4,128,512]{2,1,0:T(8,128)S(1)}, u32[]{:S(2)}) copy-start(f32[4,128,512]{2,1,0:T(8,128)S(1)} %collective-permute-done.1.refs_2_) | copy-start | bytes 3145732
  57.5 36.9 %collective-permute-start.8 = (f32[4,128,512]{2,1,0:T(8,128)S(1)}, f32[4,128,512]{2,1,0:T(8,128)}, u32[]{:S(2)}, u32[]{:S(2)}) collective-permute-start(f32[4,128,512]{2,1,0:T(8,128)S(1)} %copy-done.5), channel_id=1, source_target_pairs={{0,4},{4,8},{8,12},{1,5},{5,9},{9,13},{2,6},{6,10},{10,14},{3,7},{... | collective-permute-start | bytes 3145736 | tf_op jit(solution)/shard_map/ppermute | solution.py:241
  79.6 28.0 %collective-permute-start.16 = (f32[4,128,512]{2,1,0:T(8,128)S(1)}, f32[4,128,512]{2,1,0:T(8,128)}, u32[]{:S(2)}, u32[]{:S(2)}) collective-permute-start(f32[4,128,512]{2,1,0:T(8,128)S(1)} %copy-done.2), channel_id=1, source_target_pairs={{12,8},{8,4},{4,0},{13,9},{9,5},{5,1},{14,10},{10,6},{6,2},{15,11}... | collective-permute-start | bytes 3145736 | tf_op jit(solution)/shard_map/ppermute | solution.py:242
  87.0 91.6 %copy-start.22 = (s32[3]{0:T(128)S(1)}, s32[3]{0:T(128)}, u32[]{:S(2)}) copy-start(s32[3]{0:T(128)} %steps.7) | copy-start | bytes 40
  87.0 91.6 %copy-start.23 = (f32[3]{0:T(128)S(1)}, f32[3]{0:T(128)}, u32[]{:S(2)}) copy-start(f32[3]{0:T(128)} %occupation.7) | copy-start | bytes 40
  88.1 40.9 %collective-permute-start.17 = (f32[4,128,512]{2,1,0:T(8,128)S(1)}, f32[4,128,512]{2,1,0:T(8,128)}, u32[]{:S(2)}, u32[]{:S(2)}) collective-permute-start(f32[4,128,512]{2,1,0:T(8,128)S(1)} %copy-done.5), channel_id=1, source_target_pairs={{12,8},{8,4},{4,0},{13,9},{9,5},{5,1},{14,10},{10,6},{6,2},{15,11}... | collective-permute-start | bytes 3145736 | tf_op jit(solution)/shard_map/ppermute | solution.py:242
  90.4 39.8 %collective-permute-start.27 = (f32[4,128,512]{2,1,0:T(8,128)S(1)}, f32[4,128,512]{2,1,0:T(8,128)S(1)}, u32[]{:S(2)}, u32[]{:S(2)}) collective-permute-start(f32[4,128,512]{2,1,0:T(8,128)S(1)} %collective-permute-done.1.refs_2_), channel_id=1, source_target_pairs={{0,1},{1,0},{2,3},{3,2},{4,5},{5,4},{6,7},{7,6},{8,9},{9,8},{10,11... | collective-permute-start | bytes 3145736 | tf_op jit(solution)/shard_map/ppermute | solution.py:287
  90.4 42.1 %collective-permute-start.28 = (f32[4,128,512]{2,1,0:T(8,128)S(1)}, f32[4,128,512]{2,1,0:T(8,128)S(1)}, u32[]{:S(2)}, u32[]{:S(2)}) collective-permute-start(f32[4,128,512]{2,1,0:T(8,128)S(1)} %collective-permute-done.3.refs_3_), channel_id=1, source_target_pairs={{0,1},{1,0},{2,3},{3,2},{4,5},{5,4},{6,7},{7,6},{8,9},{9,8},{10,11... | collective-permute-start | bytes 3145736 | tf_op jit(solution)/shard_map/ppermute | solution.py:287
  94.4 39.1 %collective-permute-start.7 = (f32[4,128,512]{2,1,0:T(8,128)}, f32[4,128,512]{2,1,0:T(8,128)S(1)}, u32[]{:S(2)}, u32[]{:S(2)}) collective-permute-start(f32[4,128,512]{2,1,0:T(8,128)} %collective-permute-done.6.refs_4_), channel_id=1, source_target_pairs={{4,8},{8,12},{5,9},{9,13},{6,10},{10,14},{7,11},{11,15},{20,24},{2... | collective-permute-start | bytes 3145736 | tf_op jit(solution)/shard_map/ppermute | solution.py:241
  107.6 26.5 %collective-permute-start.9 = (f32[4,128,512]{2,1,0:T(8,128)}, f32[4,128,512]{2,1,0:T(8,128)S(1)}, u32[]{:S(2)}, u32[]{:S(2)}) collective-permute-start(f32[4,128,512]{2,1,0:T(8,128)} %collective-permute-done.8.refs_5_), channel_id=1, source_target_pairs={{4,8},{8,12},{5,9},{9,13},{6,10},{10,14},{7,11},{11,15},{20,24},{2... | collective-permute-start | bytes 3145736 | tf_op jit(solution)/shard_map/ppermute | solution.py:241
  128.9 28.2 %collective-permute-start.20 = (f32[4,128,512]{2,1,0:T(8,128)}, f32[4,128,512]{2,1,0:T(8,128)}, u32[]{:S(2)}, u32[]{:S(2)}) collective-permute-start(f32[4,128,512]{2,1,0:T(8,128)} %collective-permute-done.16.refs_12_), channel_id=1, source_target_pairs={{8,4},{4,0},{9,5},{5,1},{10,6},{6,2},{11,7},{7,3},{24,20},{20,16},... | collective-permute-start | bytes 3145736 | tf_op jit(solution)/shard_map/ppermute | solution.py:242
  131.2 46.4 %collective-permute-start.21 = (f32[4,128,512]{2,1,0:T(8,128)}, f32[4,128,512]{2,1,0:T(8,128)}, u32[]{:S(2)}, u32[]{:S(2)}) collective-permute-start(f32[4,128,512]{2,1,0:T(8,128)} %collective-permute-done.17.refs_13_), channel_id=1, source_target_pairs={{8,4},{4,0},{9,5},{5,1},{10,6},{6,2},{11,7},{7,3},{24,20},{20,16},... | collective-permute-start | bytes 3145736 | tf_op jit(solution)/shard_map/ppermute | solution.py:242
  133.5 44.1 %collective-permute-start.12 = (f32[4,128,512]{2,1,0:T(8,128)}, f32[4,128,512]{2,1,0:T(8,128)}, u32[]{:S(2)}, u32[]{:S(2)}) collective-permute-start(f32[4,128,512]{2,1,0:T(8,128)} %collective-permute-done.6.refs_4_), channel_id=1, source_target_pairs={{0,1},{1,0},{2,3},{3,2},{4,5},{5,4},{6,7},{7,6},{8,9},{9,8},{10,11... | collective-permute-start | bytes 3145736 | tf_op jit(solution)/shard_map/ppermute | solution.py:243
  133.5 44.6 %collective-permute-start.13 = (f32[4,128,512]{2,1,0:T(8,128)}, f32[4,128,512]{2,1,0:T(8,128)}, u32[]{:S(2)}, u32[]{:S(2)}) collective-permute-start(f32[4,128,512]{2,1,0:T(8,128)} %collective-permute-done.8.refs_5_), channel_id=1, source_target_pairs={{0,1},{1,0},{2,3},{3,2},{4,5},{5,4},{6,7},{7,6},{8,9},{9,8},{10,11... | collective-permute-start | bytes 3145736 | tf_op jit(solution)/shard_map/ppermute | solution.py:243
  135.6 42.6 %collective-permute-start.18 = (f32[4,128,512]{2,1,0:T(8,128)}, f32[4,128,512]{2,1,0:T(8,128)}, u32[]{:S(2)}, u32[]{:S(2)}) collective-permute-start(f32[4,128,512]{2,1,0:T(8,128)} %collective-permute-done.16.refs_12_), channel_id=1, source_target_pairs={{0,1},{1,0},{2,3},{3,2},{4,5},{5,4},{6,7},{7,6},{8,9},{9,8},{10,11... | collective-permute-start | bytes 3145736 | tf_op jit(solution)/shard_map/ppermute | solution.py:243
  137.9 72.4 %copy-start = (bf16[3,512,512]{2,1,0:T(8,128)(2,1)}, bf16[3,512,512]{2,1,0:T(8,128)(2,1)S(1)}, u32[]{:S(2)}) copy-start(bf16[3,512,512]{2,1,0:T(8,128)(2,1)S(1)} %copy.6.right_high) | copy-start | bytes 4718596
  140.2 70.1 %copy-start.1 = (bf16[3,512,512]{2,1,0:T(8,128)(2,1)}, bf16[3,512,512]{2,1,0:T(8,128)(2,1)S(1)}, u32[]{:S(2)}) copy-start(bf16[3,512,512]{2,1,0:T(8,128)(2,1)S(1)} %copy.7.right_low) | copy-start | bytes 4718596
  157.2 53.1 %collective-permute-start.19 = (f32[4,128,512]{2,1,0:T(8,128)}, f32[4,128,512]{2,1,0:T(8,128)S(1)}, u32[]{:S(2)}, u32[]{:S(2)}) collective-permute-start(f32[4,128,512]{2,1,0:T(8,128)} %collective-permute-done.17.refs_13_), channel_id=1, source_target_pairs={{0,1},{1,0},{2,3},{3,2},{4,5},{5,4},{6,7},{7,6},{8,9},{9,8},{10,11... | collective-permute-start | bytes 3145736 | tf_op jit(solution)/shard_map/ppermute | solution.py:243
  177.6 34.6 %collective-permute-start.10 = (f32[4,128,512]{2,1,0:T(8,128)}, f32[4,128,512]{2,1,0:T(8,128)S(1)}, u32[]{:S(2)}, u32[]{:S(2)}) collective-permute-start(f32[4,128,512]{2,1,0:T(8,128)} %copy-done.15), channel_id=1, source_target_pairs={{0,1},{1,0},{2,3},{3,2},{4,5},{5,4},{6,7},{7,6},{8,9},{9,8},{10,11... | collective-permute-start | bytes 3145736 | tf_op jit(solution)/shard_map/ppermute | solution.py:243
  177.6 39.7 %collective-permute-start.11 = (f32[4,128,512]{2,1,0:T(8,128)}, f32[4,128,512]{2,1,0:T(8,128)S(1)}, u32[]{:S(2)}, u32[]{:S(2)}) collective-permute-start(f32[4,128,512]{2,1,0:T(8,128)} %copy-done.17), channel_id=1, source_target_pairs={{0,1},{1,0},{2,3},{3,2},{4,5},{5,4},{6,7},{7,6},{8,9},{9,8},{10,11... | collective-permute-start | bytes 3145736 | tf_op jit(solution)/shard_map/ppermute | solution.py:243
  178.2 39.2 %collective-permute-start.22 = (f32[4,128,512]{2,1,0:T(8,128)}, f32[4,128,512]{2,1,0:T(8,128)S(1)}, u32[]{:S(2)}, u32[]{:S(2)}) collective-permute-start(f32[4,128,512]{2,1,0:T(8,128)} %collective-permute-done.20.refs_16_), channel_id=1, source_target_pairs={{0,1},{1,0},{2,3},{3,2},{4,5},{5,4},{6,7},{7,6},{8,9},{9,8},{10,11... | collective-permute-start | bytes 3145736 | tf_op jit(solution)/shard_map/ppermute | solution.py:243
  178.2 40.1 %collective-permute-start.23 = (f32[4,128,512]{2,1,0:T(8,128)}, f32[4,128,512]{2,1,0:T(8,128)}, u32[]{:S(2)}, u32[]{:S(2)}) collective-permute-start(f32[4,128,512]{2,1,0:T(8,128)} %collective-permute-done.21.refs_17_), channel_id=1, source_target_pairs={{0,1},{1,0},{2,3},{3,2},{4,5},{5,4},{6,7},{7,6},{8,9},{9,8},{10,11... | collective-permute-start | bytes 3145736 | tf_op jit(solution)/shard_map/ppermute | solution.py:243
  188.5 29.9 %copy-start.7 = (f32[4,128,512]{2,1,0:T(8,128)S(1)}, f32[4,128,512]{2,1,0:T(8,128)}, u32[]{:S(2)}) copy-start(f32[4,128,512]{2,1,0:T(8,128)} %add_momenta.7.refs_9_.refs_1_) | copy-start | bytes 3145732
  188.5 29.9 %copy-start.10 = (f32[4,128,512]{2,1,0:T(8,128)S(1)}, f32[4,128,512]{2,1,0:T(8,128)}, u32[]{:S(2)}) copy-start(f32[4,128,512]{2,1,0:T(8,128)} %copy-done.8) | copy-start | bytes 3145732
  188.5 29.9 %copy-start.13 = (f32[4,128,512]{2,1,0:T(8,128)S(1)}, f32[4,128,512]{2,1,0:T(8,128)}, u32[]{:S(2)}) copy-start(f32[4,128,512]{2,1,0:T(8,128)} %copy-done.11) | copy-start | bytes 3145732
  188.5 29.9 %copy-start.16 = (f32[4,128,512]{2,1,0:T(8,128)S(1)}, f32[4,128,512]{2,1,0:T(8,128)}, u32[]{:S(2)}) copy-start(f32[4,128,512]{2,1,0:T(8,128)} %copy-done.15) | copy-start | bytes 3145732
  188.5 29.9 %copy-start.18 = (f32[4,128,512]{2,1,0:T(8,128)S(1)}, f32[4,128,512]{2,1,0:T(8,128)}, u32[]{:S(2)}) copy-start(f32[4,128,512]{2,1,0:T(8,128)} %copy-done.17) | copy-start | bytes 3145732
  210.3 36.2 %collective-permute-start.29 = (f32[4,128,512]{2,1,0:T(8,128)S(1)}, f32[4,128,512]{2,1,0:T(8,128)S(1)}, u32[]{:S(2)}, u32[]{:S(2)}) collective-permute-start(f32[4,128,512]{2,1,0:T(8,128)S(1)} %get-tuple-element.37), channel_id=1, source_target_pairs={{0,12},{1,13},{12,0},{13,1},{2,14},{3,15},{14,2},{15,3},{16,28},{1... | collective-permute-start | bytes 3145736 | tf_op jit(solution)/shard_map/ppermute | solution.py:298
  212.2 48.4 %collective-permute-start.36 = (f32[4,128,512]{2,1,0:T(8,128)S(1)}, f32[4,128,512]{2,1,0:T(8,128)S(1)}, u32[]{:S(2)}, u32[]{:S(2)}) collective-permute-start(f32[4,128,512]{2,1,0:T(8,128)S(1)} %get-tuple-element.44), channel_id=1, source_target_pairs={{0,13},{1,12},{12,1},{13,0},{2,15},{3,14},{14,3},{15,2},{16,29},{1... | collective-permute-start | bytes 3145736 | tf_op jit(solution)/shard_map/ppermute | solution.py:298
  225.6 36.5 %collective-permute-start.25 = (f32[1,128,512]{2,1,0:T(8,128)S(1)}, f32[1,128,512]{2,1,0:T(8,128)S(1)}, u32[]{:S(2)}, u32[]{:S(2)}) collective-permute-start(f32[1,128,512]{2,1,0:T(8,128)S(1)} %get-tuple-element.32), channel_id=1, source_target_pairs={{0,2},{1,3},{2,0},{3,1},{4,6},{5,7},{6,4},{7,5},{8,10},{9,11},{10,... | collective-permute-start | bytes 786440 | tf_op jit(solution)/shard_map/ppermute | solution.py:316
  227.1 35.5 %collective-permute-start.31 = (f32[1,128,512]{2,1,0:T(8,128)S(1)}, f32[1,128,512]{2,1,0:T(8,128)S(1)}, u32[]{:S(2)}, u32[]{:S(2)}) collective-permute-start(f32[1,128,512]{2,1,0:T(8,128)S(1)} %get-tuple-element.39), channel_id=1, source_target_pairs={{0,1},{1,0},{2,3},{3,2},{4,5},{5,4},{6,7},{7,6},{8,9},{9,8},{10,11... | collective-permute-start | bytes 786440 | tf_op jit(solution)/shard_map/ppermute | solution.py:316
  237.9 48.3 %collective-permute-start.26 = (f32[2,128,512]{2,1,0:T(8,128)S(1)}, f32[2,128,512]{2,1,0:T(8,128)S(1)}, u32[]{:S(2)}, u32[]{:S(2)}) collective-permute-start(f32[2,128,512]{2,1,0:T(8,128)S(1)} %get-tuple-element.33), channel_id=1, source_target_pairs={{0,2},{1,3},{2,0},{3,1},{4,6},{5,7},{6,4},{7,5},{8,10},{9,11},{10,... | collective-permute-start | bytes 1572872 | tf_op jit(solution)/shard_map/ppermute | solution.py:316
  246.5 40.7 %copy-start.37 = (f32[4,128,512]{2,1,0:T(8,128)}, f32[4,128,512]{2,1,0:T(8,128)S(1)}, u32[]{:S(2)}) copy-start(f32[4,128,512]{2,1,0:T(8,128)S(1)} %collective-permute-done.29.refs_6_) | copy-start | bytes 3145732
  246.5 16.4 %collective-permute-start.34 = (f32[1,128,512]{2,1,0:T(8,128)S(1)}, f32[1,128,512]{2,1,0:T(8,128)S(1)}, u32[]{:S(2)}, u32[]{:S(2)}) collective-permute-start(f32[1,128,512]{2,1,0:T(8,128)S(1)} %get-tuple-element.42), channel_id=1, source_target_pairs={{0,3},{1,2},{2,1},{3,0},{4,7},{5,6},{6,5},{7,4},{8,11},{9,10},{10,... | collective-permute-start | bytes 786440 | tf_op jit(solution)/shard_map/ppermute | solution.py:316
  260.7 9.2 %collective-permute-start.24 = (f32[1,128,512]{2,1,0:T(8,128)S(1)}, f32[1,128,512]{2,1,0:T(8,128)S(1)}, u32[]{:S(2)}, u32[]{:S(2)}) collective-permute-start(f32[1,128,512]{2,1,0:T(8,128)S(1)} %get-tuple-element.31), channel_id=1, source_target_pairs={{0,2},{1,3},{2,0},{3,1},{4,6},{5,7},{6,4},{7,5},{8,10},{9,11},{10,... | collective-permute-start | bytes 786440 | tf_op jit(solution)/shard_map/ppermute | solution.py:316
  262.1 24.1 %collective-permute-start.32 = (f32[2,128,512]{2,1,0:T(8,128)S(1)}, f32[2,128,512]{2,1,0:T(8,128)S(1)}, u32[]{:S(2)}, u32[]{:S(2)}) collective-permute-start(f32[2,128,512]{2,1,0:T(8,128)S(1)} %get-tuple-element.40), channel_id=1, source_target_pairs={{0,1},{1,0},{2,3},{3,2},{4,5},{5,4},{6,7},{7,6},{8,9},{9,8},{10,11... | collective-permute-start | bytes 1572872 | tf_op jit(solution)/shard_map/ppermute | solution.py:316
  262.6 23.7 %collective-permute-start.35 = (f32[2,128,512]{2,1,0:T(8,128)S(1)}, f32[2,128,512]{2,1,0:T(8,128)S(1)}, u32[]{:S(2)}, u32[]{:S(2)}) collective-permute-start(f32[2,128,512]{2,1,0:T(8,128)S(1)} %get-tuple-element.43), channel_id=1, source_target_pairs={{0,3},{1,2},{2,1},{3,0},{4,7},{5,6},{6,5},{7,4},{8,11},{9,10},{10,... | collective-permute-start | bytes 1572872 | tf_op jit(solution)/shard_map/ppermute | solution.py:316
  262.9 7.6 %collective-permute-start.30 = (f32[1,128,512]{2,1,0:T(8,128)S(1)}, f32[1,128,512]{2,1,0:T(8,128)S(1)}, u32[]{:S(2)}, u32[]{:S(2)}) collective-permute-start(f32[1,128,512]{2,1,0:T(8,128)S(1)} %get-tuple-element.38), channel_id=1, source_target_pairs={{0,1},{1,0},{2,3},{3,2},{4,5},{5,4},{6,7},{7,6},{8,9},{9,8},{10,11... | collective-permute-start | bytes 786440 | tf_op jit(solution)/shard_map/ppermute | solution.py:316
  269.9 16.4 %collective-permute-start.33 = (f32[1,128,512]{2,1,0:T(8,128)S(1)}, f32[1,128,512]{2,1,0:T(8,128)S(1)}, u32[]{:S(2)}, u32[]{:S(2)}) collective-permute-start(f32[1,128,512]{2,1,0:T(8,128)S(1)} %get-tuple-element.41), channel_id=1, source_target_pairs={{0,3},{1,2},{2,1},{3,0},{4,7},{5,6},{6,5},{7,4},{8,11},{9,10},{10,... | collective-permute-start | bytes 786440 | tf_op jit(solution)/shard_map/ppermute | solution.py:316
  (38 other events, 269.9 us)

commit v2 on v1

--- a/solution.py
+++ b/solution.py
@@ -149,7 +149,7 @@
         out_shape=[jax.ShapeDtypeStruct((count, out_rows, order), jnp.float32)] * n_out,
         in_specs=[pl.BlockSpec(memory_space=pltpu.SMEM)] * 2
         + [pl.BlockSpec(memory_space=pltpu.VMEM)] * 3
-        + [pl.BlockSpec(memory_space=pl.ANY)] * len(flat),
+        + [pl.BlockSpec(memory_space=pltpu.HBM)] * len(flat),
         out_specs=[pl.BlockSpec(memory_space=pltpu.VMEM)] * n_out,
         scratch_shapes=[
             pltpu.VMEM((2, 2 * MODES, rows, order), jnp.float32),
@@ -173,22 +173,40 @@
 
         @pl.when(core == own)
         def _(own=own):
-            at = 0
-            for half, chunks in enumerate(layout):
-                where = own if half == 0 else 1 - own
-                terms = []
-                for size in chunks:
-                    rows = []
-                    for _ in range(size):
-                        rows.extend((at, k) for k in range(refs[at].shape[0]))
-                        at += 1
-                    terms.append(rows)
-                for j in range(count):
+            for half, energies in enumerate(layout):
+                where = (own if half == 0 else 1 - own) * count
+                for j, terms in enumerate(energies):
                     total = None
-                    for rows in terms:
-                        ref, k = rows[j]
-                        total = refs[ref][k] if total is None else total + refs[ref][k]
-                    out[:, where * count + j, :] = total
+                    for ref, row in terms:
+                        value = refs[ref][:, where + j, :] if row is None else refs[ref][row]
+                        total = value if total is None else total + value
+                    out[:, where + j, :] = total
+
+
+def gathered(layout, count, arrays, before=None):
+    terms = [[[(arrays.index(x), row) for x, row in entry] for entry in energies] for energies in layout]
+    arrays = list(arrays)
+    out_rows, order = arrays[0].shape[1:]
+    step = min(out_rows, 32)
+    whole = pl.BlockSpec((step, 2 * count, order), lambda i: (i, 0, 0))
+    specs = [pl.BlockSpec((x.shape[0], step, order), lambda i: (0, i, 0)) for x in arrays]
+    if before is not None:
+        terms = [[entry + [(len(arrays), None)] for entry in energies] for energies in terms]
+        arrays, specs = arrays + [before], specs + [whole]
+    size = 4 * sum(x.size for x in arrays) + 4 * 2 * count * out_rows * order
+    return pl.pallas_call(
+        functools.partial(gather_up, terms, count),
+        grid=(out_rows // step,),
+        out_shape=jax.ShapeDtypeStruct((out_rows, 2 * count, order), jnp.float32),
+        in_specs=specs,
+        out_specs=whole,
+        cost_estimate=pl.CostEstimate(flops=size // 4, bytes_accessed=size, transcendentals=0),
+    )(*arrays)
+
+
+class Terms(list):
+    def index(self, x):
+        return next(i for i, y in enumerate(self) if y is x)
 
 
 def shards(green, couplings, occupation, offsets, owners):
@@ -208,8 +226,8 @@
         return pl.pallas_call(
             functools.partial(add_momenta, theirs, piece * size),
             out_shape=jax.ShapeDtypeStruct((half, size, order), jnp.float32),
-            in_specs=[pl.BlockSpec(memory_space=pl.ANY)] * (1 + len(more)),
-            out_specs=pl.BlockSpec(memory_space=pl.ANY),
+            in_specs=[pl.BlockSpec(memory_space=pltpu.HBM)] * (1 + len(more)),
+            out_specs=pl.BlockSpec(memory_space=pltpu.HBM),
             scratch_shapes=[
                 pltpu.VMEM((half, momenta_here + len(more), size, order), jnp.float32),
                 pltpu.VMEM((half, size, order), jnp.float32),
@@ -240,7 +258,15 @@
     for d in range(1, REACH + 1):
         streams[-d] = [lax.ppermute(x, "energy", up[d - 1]) for x in streams[1 - d]]
         streams[d] = [lax.ppermute(x, "energy", down[d - 1]) for x in streams[d - 1]]
-    groups = [(streams[d], [lax.ppermute(x, "kz", swap) for x in streams[d]]) for d in range(-REACH, REACH + 1)]
+    groups = []
+    for d in range(-REACH, REACH + 1):
+        axes, pairs = "kz", swap
+        if line and abs(d) == REACH:
+            axes = ("energy", "kz")
+            pairs = [
+                (i * cores + k, i * cores + (k + 1) % cores) for i in range(n) if 0 <= i + d < n for k in range(cores)
+            ]
+        groups.append((streams[d], [lax.ppermute(x, axes, pairs) for x in streams[d]]))
 
     table_rows = couplings.shape[0]
     strip = order // cores
@@ -289,13 +315,8 @@
         sums = sandwich(
             offsets, occupation, right, left_far, [whole], atoms, momenta, 0, grid_total, edev, True, line, out_rows, half
         )
-        for t in range(cores):
-            pairs = [
-                (a * cores + k, b * cores + (k + t) % cores)
-                for a, b in ((0, n - 1), (n - 1, 0))
-                for k in range(cores)
-            ]
-            beyond.append(lax.ppermute(sums[t], ("energy", "kz"), pairs))
+        both = jnp.concatenate([sums[0], lax.ppermute(sums[1], "kz", swap)], 0)
+        beyond.append(lax.ppermute(both, "energy", [(0, n - 1), (n - 1, 0)]))
 
     terms = [[[] for _ in range(atoms)] for _ in range(cores)]
     base = 0
@@ -315,20 +336,24 @@
                     ]
                     block = lax.ppermute(block, ("atom", "kz"), pairs)
                 terms[t][s].append(block)
+    chunks = chunks_of(half)
+    entries = [[[] for _ in range(half)] for _ in range(cores)]
+    late = [[[] for _ in range(half)] for _ in range(cores)]
+    early, last = Terms(beyond), Terms()
     for t in range(cores):
-        if beyond:
-            terms[t].append([beyond[t]])
-    flat = [x for t in range(cores) for term in terms[t] for x in term]
-    layout = [[len(term) for term in terms[t]] for t in range(cores)]
-    step = min(out_rows, 32)
-    return pl.pallas_call(
-        functools.partial(gather_up, layout, half),
-        grid=(out_rows // step,),
-        out_shape=jax.ShapeDtypeStruct((out_rows, edev, order), jnp.float32),
-        in_specs=[pl.BlockSpec((x.shape[0], step, order), lambda i: (0, i, 0)) for x in flat],
-        out_specs=pl.BlockSpec((step, edev, order), lambda i: (i, 0, 0)),
-        name="gather_up",
-    )(*flat)
+        for s in range(atoms):
+            first = 0
+            for chunk, block in enumerate(terms[t][s]):
+                held = (last, late) if s and chunk == len(chunks) - 1 else (early, entries)
+                held[0].append(block)
+                for row in range(chunks[chunk]):
+                    held[1][t][first + row].append((block, row))
+                first += chunks[chunk]
+        for j in range(half):
+            for block in beyond:
+                entries[t][j].append((block, t * half + j))
+    total = gathered(entries, half, early)
+    return gathered(late, half, last, total)
 
 
 def solution(mesh):

time: 294 us -> 255 us (0.87)
  waiting for transfers between devices: 149 us -> 106 us
  local copies, waits for them, and re-layouts: 26.3 us -> 16.4 us
  starting transfers between devices: 39 us -> 48.4 us
  Pallas kernels: 61.1 us -> 64.5 us
    ppermute x4, waiting for transfers between devices: 70.5 us -> 28 us  [shards(): lax.ppermute(x, 'energy', down[d - 1])]
    ppermute x2 -> x12, waiting for transfers between devices: 13.2 us -> 0.03 us  [the longest x10 0.03 us: shards(): lax.ppermute(x, axes, pairs)]
    ppermute x2 -> x12, starting transfers between devices: 7.03 us -> 20.2 us  [the longest x1 12.4 us: shards(): beyond.append(lax.ppermute(both, 'energy', [(0, n - 1), (n - 1, 0)]))]
    ppermute x2, waiting for transfers between devices: 21.3 us -> 32.9 us  [shards(): lax.ppermute(x, 'atom', around[s])]
    unnamed x98 -> x60, local copies, waits for them, and re-layouts: 20.3 us -> 10.5 us
    ppermute x9, waiting for transfers between devices: 22.3 us -> 27.6 us  [shards(): block = lax.ppermute(block, ('atom', 'kz'), pairs)]
    pallas_call x1 -> x2, Pallas kernels: 4.93 us -> 8.84 us  [gathered(): pl.pallas_call(functools.partial(gather_up, terms, count), grid=(out_rows...]
    ppermute x4, waiting for transfers between devices: 3.56 us -> 0.01 us  [shards(): streams[-d] = [lax.ppermute(x, 'energy', up[d - 1]) for x in streams[1 - d]]]
  transfers between devices with their start and end apart: 37 -> 37, of which waited for: 11 -> 5; matrix products, arithmetic and copies ran while one was open for 5% -> 6% of each run, Pallas kernels for 19% -> 24%
where the time goes in v2:
time: 255 us; the launch traced here: 254 us
  waiting for transfers between devices  106 us (42%)
  Pallas kernels  64.5 us (25%)
  starting transfers between devices  48.4 us (19%)
  local copies, waits for them, and re-layouts  16.4 us (6%)
  other arithmetic  10.3 us (4%)
  between operations  8.02 us (3%)
    pallas_call x4, Pallas kernels, sandwich(): pl.pallas_call(functools.partial(split_dot, len(groups), len(groups[0][0]...  45.8 us
    ppermute x2, waiting for transfers between devices, shards(): lax.ppermute(x, 'atom', around[s])  32.9 us
    ppermute x4, waiting for transfers between devices, shards(): lax.ppermute(x, 'energy', down[d - 1])  28 us
    ppermute x9, waiting for transfers between devices, shards(): block = lax.ppermute(block, ('atom', 'kz'), pairs)  27.6 us
    ppermute x1, waiting for transfers between devices, shards(): got = lax.ppermute(mine, 'atom', around[s])  17.9 us
    ppermute x1, starting transfers between devices, shards(): beyond.append(lax.ppermute(both, 'energy', [(0, n - 1), (n - 1, 0)]))  12.4 us
    unnamed x60, local copies, waits for them, and re-layouts  10.5 us
    pallas_call x4, Pallas kernels, summed(): pl.pallas_call(functools.partial(add_momenta, theirs, piece * size), out_...  9.84 us
  transfers between devices with their start and end apart: 37, of which 5 were waited for; matrix products, arithmetic and copies ran while one was open for 6% of the time, Pallas kernels for 24%

profile of v2, /device:TPU:0, one launch (start us, length us, event | category | flops | bytes accessed | tf_op | source)
XLA Modules:
  0.0 254.0 jit_solution(13123254122614757192)
XLA Ops:
  0.0 1.3 constant_dynamic-slice_fusion
  1.3 3.0 %collective-permute-start.4 = (f32[2,256,512]{2,1,0:T(8,128)S(1)}, f32[2,256,512]{2,1,0:T(8,128)S(1)}, u32[]{:S(2)}, u32[]{:S(2)}) collective-permute-start(f32[2,256,512]{2,1,0:T(8,128)S(1)} %constant_dynamic-slice_fusion), channel_id=1, source_target_pairs={{0,2},{2,0},{1,3},{3,1},{4,6},{6,4},{5,7},{7,5},{8,10},{10,8},{9,1... | collective-permute-start | bytes 3145736 | tf_op jit(solution)/shard_map/ppermute | solution.py:276
  4.3 2.3 add_momenta.6
  6.7 2.3 add_momenta.4
  9.6 17.9 %collective-permute-done.4 = f32[2,256,512]{2,1,0:T(8,128)S(1)} collective-permute-done((f32[2,256,512]{2,1,0:T(8,128)S(1)}, f32[2,256,512]{2,1,0:T(8,128)S(1)}, u32[]{:S(2)}, u32[]{:S(2)}) %collective-permute-start.4) | collective-permute-done | bytes 1048608 | tf_op jit(solution)/shard_map/ppermute | solution.py:276
  35.5 1.0 copy-done.21
  36.5 2.6 %add_momenta.7.refs_9_.refs_1_ = f32[4,128,512]{2,1,0:T(8,128)} custom-call(f32[2,8,256,512]{3,2,1,0:T(8,128)} %green.7, f32[4,128,512]{2,1,0:T(8,128)} %copy-done.21), custom_call_target="tpu_custom_call" | custom-call | flops 524288 | bytes 4194304 | tf_op jit(solution)/shard_map/add_momenta/pallas_call | solution.py:226
  39.1 1.3 collective-permute-start.17
  41.0 5.3 %collective-permute-start.8 = (f32[4,128,512]{2,1,0:T(8,128)}, f32[4,128,512]{2,1,0:T(8,128)}, u32[]{:S(2)}, u32[]{:S(2)}) collective-permute-start(f32[4,128,512]{2,1,0:T(8,128)} %add_momenta.7.refs_9_.refs_1_), channel_id=1, source_target_pairs={{0,4},{4,8},{8,12},{1,5},{5,9},{9,13},{2,6},{6,10},{10,14},{3,7},{... | collective-permute-start | bytes 3145736 | tf_op jit(solution)/shard_map/ppermute | solution.py:259
  46.4 1.6 collective-permute-start.3
  48.0 2.6 %add_momenta.5.refs_8_.refs_0_ = f32[4,128,512]{2,1,0:T(8,128)} custom-call(f32[2,8,256,512]{3,2,1,0:T(8,128)} %green.7, f32[4,128,512]{2,1,0:T(8,128)} %collective-permute-done.refs_0_), custom_call_target="tpu_custom_call" | custom-call | flops 524288 | bytes 4194304 | tf_op jit(solution)/shard_map/add_momenta/pallas_call | solution.py:226
  51.1 1.9 dynamic-slice_select_fusion.5
  53.0 0.8 maximum_select_fusion
  54.7 1.5 pad_maximum_fusion.2.left
  56.2 2.2 fusion
  58.4 1.6 pad_maximum_fusion.1.left
  60.0 12.7 %collective-permute-done.3.refs_3_ = f32[4,128,512]{2,1,0:T(8,128)} collective-permute-done((f32[4,128,512]{2,1,0:T(8,128)}, f32[4,128,512]{2,1,0:T(8,128)}, u32[]{:S(2)}, u32[]{:S(2)}) %collective-permute-start.3) | collective-permute-done | bytes 1048608 | tf_op jit(solution)/shard_map/ppermute | solution.py:309
  72.7 1.3 collective-permute-start.16
  74.0 20.1 %collective-permute-done.1.refs_2_ = f32[4,128,512]{2,1,0:T(8,128)} collective-permute-done((f32[4,128,512]{2,1,0:T(8,128)}, f32[4,128,512]{2,1,0:T(8,128)}, u32[]{:S(2)}, u32[]{:S(2)}) %collective-permute-start.1) | collective-permute-done | bytes 1048608 | tf_op jit(solution)/shard_map/ppermute | solution.py:309
  95.1 1.0 copy-done.4
  96.6 1.7 copy.6.right_high
  98.4 2.3 copy.7.right_low
  100.7 2.9 %collective-permute-start.6 = (f32[4,128,512]{2,1,0:T(8,128)}, f32[4,128,512]{2,1,0:T(8,128)S(1)}, u32[]{:S(2)}, u32[]{:S(2)}) collective-permute-start(f32[4,128,512]{2,1,0:T(8,128)} %add_momenta.5.refs_8_.refs_0_), channel_id=1, source_target_pairs={{0,4},{4,8},{8,12},{1,5},{5,9},{9,13},{2,6},{6,10},{10,14},{3,7},{... | collective-permute-start | bytes 3145736 | tf_op jit(solution)/shard_map/ppermute | solution.py:259
  103.6 1.3 collective-permute-start.21
  106.2 1.2 copy-done.2
  107.5 1.2 copy-done.5
  108.7 21.2 %far_sandwich.1 = (f32[4,128,512]{2,1,0:T(8,128)S(1)}, f32[4,128,512]{2,1,0:T(8,128)S(1)}) custom-call(s32[3]{0:T(128)S(1)} %copy-done.10, f32[3]{0:T(128)S(1)} %copy-done.11, bf16[3,512,512]{2,1,0:T(8,128)(2,1)S(1)} %copy.6.right_high, bf16[3,512,512]{2,1,0:T(8,128)(2,1)S(1)} %copy.7.right_low, bf16[3,256,1536]{2,1,0:T(8,128)(2,1)} %pad_maximum_fusion.1.left, ...), custom_call_target="tpu_custom_call" | custom-call | flops 14495514624 | bytes 27262976 | tf_op jit(solution)/shard_map/far_sandwich/pallas_call | solution.py:147
  130.0 1.4 collective-permute-start.20
  132.9 28.0 %collective-permute-done.20.refs_16_ = f32[4,128,512]{2,1,0:T(8,128)S(1)} collective-permute-done((f32[4,128,512]{2,1,0:T(8,128)}, f32[4,128,512]{2,1,0:T(8,128)S(1)}, u32[]{:S(2)}, u32[]{:S(2)}) %collective-permute-start.20) | collective-permute-done | bytes 1048608 | tf_op jit(solution)/shard_map/ppermute | solution.py:260
  160.9 1.9 collective-permute-start.23
  163.5 2.4 collective-permute-start.22
  166.0 0.9 collective-permute-start.10
  166.9 1.5 pad_maximum_fusion.3
  168.4 12.4 %collective-permute-start.29 = (f32[8,128,512]{2,1,0:T(8,128)}, f32[8,128,512]{2,1,0:T(8,128)S(1)}, u32[]{:S(2)}, u32[]{:S(2)}) collective-permute-start(f32[8,128,512]{2,1,0:T(8,128)} %pad_maximum_fusion.3), channel_id=1, source_target_pairs={{0,12},{12,0},{1,13},{13,1},{2,14},{14,2},{3,15},{15,3},{16,28},{2... | collective-permute-start | bytes 6291464 | tf_op jit(solution)/shard_map/ppermute | solution.py:319
  180.9 0.9 copy-done.17
  182.1 7.1 %near_sandwich.5 = (f32[1,128,512]{2,1,0:T(8,128)S(1)}, f32[1,128,512]{2,1,0:T(8,128)S(1)}, f32[1,128,512]{2,1,0:T(8,128)S(1)}, f32[1,128,512]{2,1,0:T(8,128)S(1)}) custom-call(s32[3]{0:T(128)S(1)} %copy-done.10, f32[3]{0:T(128)S(1)} %copy-done.11, bf16[3,512,512]{2,1,0:T(8,128)(2,1)} %copy-done, bf16[3,512,512]{2,1,0:T(8,128)(2,1)} %copy-done.1, ...), custom_call_target="tpu_custom_call" | custom-call | flops 2415919104 | bytes 4194304 | tf_op jit(solution)/shard_map/near_sandwich/pallas_call | solution.py:147
  189.3 1.6 collective-permute-start.31
  191.5 7.3 %near_sandwich.4 = (f32[1,128,512]{2,1,0:T(8,128)S(1)}, f32[1,128,512]{2,1,0:T(8,128)S(1)}, f32[1,128,512]{2,1,0:T(8,128)S(1)}, f32[1,128,512]{2,1,0:T(8,128)S(1)}) custom-call(s32[3]{0:T(128)S(1)} %copy-done.10, f32[3]{0:T(128)S(1)} %copy-done.11, bf16[3,512,512]{2,1,0:T(8,128)(2,1)} %copy-done, bf16[3,512,512]{2,1,0:T(8,128)(2,1)} %copy-done.1, ...), custom_call_target="tpu_custom_call" | custom-call | flops 2415919104 | bytes 4194304 | tf_op jit(solution)/shard_map/near_sandwich/pallas_call | solution.py:147
  199.5 1.5 collective-permute-start.30
  201.0 10.1 %near_sandwich.3 = (f32[2,128,512]{2,1,0:T(8,128)S(1)}, f32[2,128,512]{2,1,0:T(8,128)S(1)}, f32[2,128,512]{2,1,0:T(8,128)S(1)}, f32[2,128,512]{2,1,0:T(8,128)S(1)}) custom-call(s32[3]{0:T(128)S(1)} %copy-done.10, f32[3]{0:T(128)S(1)} %copy-done.11, bf16[3,512,512]{2,1,0:T(8,128)(2,1)} %copy-done, bf16[3,512,512]{2,1,0:T(8,128)(2,1)} %copy-done.1, ...), custom_call_target="tpu_custom_call" | custom-call | flops 4831838208 | bytes 8388608 | tf_op jit(solution)/shard_map/near_sandwich/pallas_call | solution.py:147
  211.1 0.8 copy-done.7
  213.7 0.9 collective-permute-start.25
  214.6 0.9 collective-permute-start.35
  215.4 27.6 %collective-permute-done.35.refs_9_ = f32[1,128,512]{2,1,0:T(8,128)S(1)} collective-permute-done((f32[1,128,512]{2,1,0:T(8,128)S(1)}, f32[1,128,512]{2,1,0:T(8,128)S(1)}, u32[]{:S(2)}, u32[]{:S(2)}) %collective-permute-start.35) | collective-permute-done | bytes 262176 | tf_op jit(solution)/shard_map/ppermute | solution.py:337
  243.0 0.8 copy-done.22
  243.9 1.3 copy-done.20
  245.1 4.5 %shard_map.65.refs_2_ = f32[128,8,512]{2,1,0:T(8,128)} custom-call(f32[8,128,512]{2,1,0:T(8,128)} %copy-done.20, f32[1,128,512]{2,1,0:T(8,128)} %copy-done.9, f32[1,128,512]{2,1,0:T(8,128)} %copy-done.8, f32[2,128,512]{2,1,0:T(8,128)} %copy-done.7, f32[1,128,512]{2,1,0:T(8,128)} %copy-done.26, f32[1,128,512]{2,1,0:T(8,128)} %copy-done.23, ...), custom_call_target="tpu_custom_call" | custom-call | flops 1835008 | bytes 7340032 | tf_op jit(solution)/shard_map/pallas_call | solution.py:197
  249.7 4.3 %shard_map.66 = f32[128,8,512]{2,1,0:T(8,128)} custom-call(f32[2,128,512]{2,1,0:T(8,128)} %collective-permute-done.24.refs_0_, f32[2,128,512]{2,1,0:T(8,128)} %collective-permute-done.25.refs_1_, f32[128,8,512]{2,1,0:T(8,128)} %shard_map.65.refs_2_), custom_call_target="tpu_custom_call" | custom-call | flops 1310720 | bytes 5242880 | tf_op jit(solution)/shard_map/pallas_call | solution.py:197
  (110 shorter events, 11.7 us)
Async XLA Ops:
  1.3 26.2 %collective-permute-start.4 = (f32[2,256,512]{2,1,0:T(8,128)S(1)}, f32[2,256,512]{2,1,0:T(8,128)S(1)}, u32[]{:S(2)}, u32[]{:S(2)}) collective-permute-start(f32[2,256,512]{2,1,0:T(8,128)S(1)} %constant_dynamic-slice_fusion), channel_id=1, source_target_pairs={{0,2},{2,0},{1,3},{3,1},{4,6},{6,4},{5,7},{7,5},{8,10},{10,8},{9,1... | collective-permute-start | bytes 3145736 | tf_op jit(solution)/shard_map/ppermute | solution.py:276
  6.6 20.9 %copy-start.29 = (s32[3]{0:T(128)S(1)}, s32[3]{0:T(128)}, u32[]{:S(2)}) copy-start(s32[3]{0:T(128)} %param.9) | copy-start | bytes 40
  6.6 28.9 %collective-permute-start.2 = (f32[4,128,512]{2,1,0:T(8,128)}, f32[4,128,512]{2,1,0:T(8,128)S(1)}, u32[]{:S(2)}, u32[]{:S(2)}) collective-permute-start(f32[4,128,512]{2,1,0:T(8,128)} %add_momenta.6), channel_id=1, source_target_pairs={{0,1},{1,0},{2,3},{3,2},{4,5},{5,4},{6,7},{7,6},{8,9},{9,8},{10,11... | collective-permute-start | bytes 3145736 | tf_op jit(solution)/shard_map/ppermute | solution.py:248
  9.0 37.3 %collective-permute-start = (f32[4,128,512]{2,1,0:T(8,128)}, f32[4,128,512]{2,1,0:T(8,128)}, u32[]{:S(2)}, u32[]{:S(2)}) collective-permute-start(f32[4,128,512]{2,1,0:T(8,128)} %add_momenta.4), channel_id=1, source_target_pairs={{0,1},{1,0},{2,3},{3,2},{4,5},{5,4},{6,7},{7,6},{8,9},{9,8},{10,11... | collective-permute-start | bytes 3145736 | tf_op jit(solution)/shard_map/ppermute | solution.py:248
  27.5 23.2 %collective-permute-start.5 = (f32[2,256,512]{2,1,0:T(8,128)S(1)}, f32[2,256,512]{2,1,0:T(8,128)}, u32[]{:S(2)}, u32[]{:S(2)}) collective-permute-start(f32[2,256,512]{2,1,0:T(8,128)S(1)} %collective-permute-done.4), channel_id=1, source_target_pairs={{0,1},{1,0},{2,3},{3,2},{4,5},{5,4},{6,7},{7,6},{8,9},{9,8},{10,11... | collective-permute-start | bytes 3145736 | tf_op jit(solution)/shard_map/ppermute | solution.py:277
  39.1 55.0 %collective-permute-start.17 = (f32[4,128,512]{2,1,0:T(8,128)}, f32[4,128,512]{2,1,0:T(8,128)S(1)}, u32[]{:S(2)}, u32[]{:S(2)}) collective-permute-start(f32[4,128,512]{2,1,0:T(8,128)} %add_momenta.7.refs_9_.refs_1_), channel_id=1, source_target_pairs={{12,8},{8,4},{4,0},{13,9},{9,5},{5,1},{14,10},{10,6},{6,2},{15,11}... | collective-permute-start | bytes 3145736 | tf_op jit(solution)/shard_map/ppermute | solution.py:260
  40.4 54.2 %collective-permute-start.15 = (f32[4,128,512]{2,1,0:T(8,128)}, f32[4,128,512]{2,1,0:T(8,128)S(1)}, u32[]{:S(2)}, u32[]{:S(2)}) collective-permute-start(f32[4,128,512]{2,1,0:T(8,128)} %add_momenta.7.refs_9_.refs_1_), channel_id=1, source_target_pairs={{0,1},{1,0},{2,3},{3,2},{4,5},{5,4},{6,7},{7,6},{8,9},{9,8},{10,11... | collective-permute-start | bytes 3145736 | tf_op jit(solution)/shard_map/ppermute | solution.py:269
  41.0 59.7 %collective-permute-start.8 = (f32[4,128,512]{2,1,0:T(8,128)}, f32[4,128,512]{2,1,0:T(8,128)}, u32[]{:S(2)}, u32[]{:S(2)}) collective-permute-start(f32[4,128,512]{2,1,0:T(8,128)} %add_momenta.7.refs_9_.refs_1_), channel_id=1, source_target_pairs={{0,4},{4,8},{8,12},{1,5},{5,9},{9,13},{2,6},{6,10},{10,14},{3,7},{... | collective-permute-start | bytes 3145736 | tf_op jit(solution)/shard_map/ppermute | solution.py:259
  46.4 26.3 %collective-permute-start.3 = (f32[4,128,512]{2,1,0:T(8,128)}, f32[4,128,512]{2,1,0:T(8,128)}, u32[]{:S(2)}, u32[]{:S(2)}) collective-permute-start(f32[4,128,512]{2,1,0:T(8,128)} %add_momenta.7.refs_9_.refs_1_), channel_id=1, source_target_pairs={{0,2},{2,0},{1,3},{3,1},{4,6},{6,4},{5,7},{7,5},{8,10},{10,8},{9,1... | collective-permute-start | bytes 3145736 | tf_op jit(solution)/shard_map/ppermute | solution.py:309
  50.7 43.5 %collective-permute-start.1 = (f32[4,128,512]{2,1,0:T(8,128)}, f32[4,128,512]{2,1,0:T(8,128)}, u32[]{:S(2)}, u32[]{:S(2)}) collective-permute-start(f32[4,128,512]{2,1,0:T(8,128)} %add_momenta.5.refs_8_.refs_0_), channel_id=1, source_target_pairs={{0,2},{2,0},{1,3},{3,1},{4,6},{6,4},{5,7},{7,5},{8,10},{10,8},{9,1... | collective-permute-start | bytes 3145736 | tf_op jit(solution)/shard_map/ppermute | solution.py:309
  72.7 30.9 %collective-permute-start.16 = (f32[4,128,512]{2,1,0:T(8,128)}, f32[4,128,512]{2,1,0:T(8,128)}, u32[]{:S(2)}, u32[]{:S(2)}) collective-permute-start(f32[4,128,512]{2,1,0:T(8,128)} %add_momenta.5.refs_8_.refs_0_), channel_id=1, source_target_pairs={{12,8},{8,4},{4,0},{13,9},{9,5},{5,1},{14,10},{10,6},{6,2},{15,11}... | collective-permute-start | bytes 3145736 | tf_op jit(solution)/shard_map/ppermute | solution.py:260
  94.1 10.8 %collective-permute-start.14 = (f32[4,128,512]{2,1,0:T(8,128)}, f32[4,128,512]{2,1,0:T(8,128)}, u32[]{:S(2)}, u32[]{:S(2)}) collective-permute-start(f32[4,128,512]{2,1,0:T(8,128)} %add_momenta.5.refs_8_.refs_0_), channel_id=1, source_target_pairs={{0,1},{1,0},{2,3},{3,2},{4,5},{5,4},{6,7},{7,6},{8,9},{9,8},{10,11... | collective-permute-start | bytes 3145736 | tf_op jit(solution)/shard_map/ppermute | solution.py:269
  94.1 10.9 %collective-permute-start.26 = (f32[4,128,512]{2,1,0:T(8,128)}, f32[4,128,512]{2,1,0:T(8,128)}, u32[]{:S(2)}, u32[]{:S(2)}) collective-permute-start(f32[4,128,512]{2,1,0:T(8,128)} %collective-permute-done.1.refs_2_), channel_id=1, source_target_pairs={{0,1},{1,0},{2,3},{3,2},{4,5},{5,4},{6,7},{7,6},{8,9},{9,8},{10,11... | collective-permute-start | bytes 3145736 | tf_op jit(solution)/shard_map/ppermute | solution.py:313
  96.1 9.4 %collective-permute-start.27 = (f32[4,128,512]{2,1,0:T(8,128)}, f32[4,128,512]{2,1,0:T(8,128)}, u32[]{:S(2)}, u32[]{:S(2)}) collective-permute-start(f32[4,128,512]{2,1,0:T(8,128)} %collective-permute-done.3.refs_3_), channel_id=1, source_target_pairs={{0,1},{1,0},{2,3},{3,2},{4,5},{5,4},{6,7},{7,6},{8,9},{9,8},{10,11... | collective-permute-start | bytes 3145736 | tf_op jit(solution)/shard_map/ppermute | solution.py:313
  98.3 31.6 %copy-start = (bf16[3,512,512]{2,1,0:T(8,128)(2,1)}, bf16[3,512,512]{2,1,0:T(8,128)(2,1)S(1)}, u32[]{:S(2)}) copy-start(bf16[3,512,512]{2,1,0:T(8,128)(2,1)S(1)} %copy.6.right_high) | copy-start | bytes 4718596
  100.7 29.3 %copy-start.1 = (bf16[3,512,512]{2,1,0:T(8,128)(2,1)}, bf16[3,512,512]{2,1,0:T(8,128)(2,1)S(1)}, u32[]{:S(2)}) copy-start(bf16[3,512,512]{2,1,0:T(8,128)(2,1)S(1)} %copy.7.right_low) | copy-start | bytes 4718596
  100.7 29.3 %collective-permute-start.6 = (f32[4,128,512]{2,1,0:T(8,128)}, f32[4,128,512]{2,1,0:T(8,128)S(1)}, u32[]{:S(2)}, u32[]{:S(2)}) collective-permute-start(f32[4,128,512]{2,1,0:T(8,128)} %add_momenta.5.refs_8_.refs_0_), channel_id=1, source_target_pairs={{0,4},{4,8},{8,12},{1,5},{5,9},{9,13},{2,6},{6,10},{10,14},{3,7},{... | collective-permute-start | bytes 3145736 | tf_op jit(solution)/shard_map/ppermute | solution.py:259
  103.6 27.8 %collective-permute-start.21 = (f32[4,128,512]{2,1,0:T(8,128)}, f32[4,128,512]{2,1,0:T(8,128)S(1)}, u32[]{:S(2)}, u32[]{:S(2)}) collective-permute-start(f32[4,128,512]{2,1,0:T(8,128)} %copy-done.12), channel_id=1, source_target_pairs={{8,4},{4,0},{9,5},{5,1},{10,6},{6,2},{11,7},{7,3},{24,20},{20,16},... | collective-permute-start | bytes 3145736 | tf_op jit(solution)/shard_map/ppermute | solution.py:260
  104.9 26.7 %collective-permute-start.19 = (f32[4,128,512]{2,1,0:T(8,128)}, f32[4,128,512]{2,1,0:T(8,128)S(1)}, u32[]{:S(2)}, u32[]{:S(2)}) collective-permute-start(f32[4,128,512]{2,1,0:T(8,128)} %copy-done.12), channel_id=1, source_target_pairs={{0,1},{1,0},{2,3},{3,2},{4,5},{5,4},{6,7},{7,6},{8,9},{9,8},{10,11... | collective-permute-start | bytes 3145736 | tf_op jit(solution)/shard_map/ppermute | solution.py:269
  105.0 27.3 %collective-permute-start.13 = (f32[4,128,512]{2,1,0:T(8,128)}, f32[4,128,512]{2,1,0:T(8,128)S(1)}, u32[]{:S(2)}, u32[]{:S(2)}) collective-permute-start(f32[4,128,512]{2,1,0:T(8,128)} %collective-permute-done.8.refs_5_), channel_id=1, source_target_pairs={{0,1},{1,0},{2,3},{3,2},{4,5},{5,4},{6,7},{7,6},{8,9},{9,8},{10,11... | collective-permute-start | bytes 3145736 | tf_op jit(solution)/shard_map/ppermute | solution.py:269
  105.5 27.3 %collective-permute-start.9 = (f32[4,128,512]{2,1,0:T(8,128)}, f32[4,128,512]{2,1,0:T(8,128)S(1)}, u32[]{:S(2)}, u32[]{:S(2)}) collective-permute-start(f32[4,128,512]{2,1,0:T(8,128)} %collective-permute-done.8.refs_5_), channel_id=1, source_target_pairs={{4,8},{8,12},{5,9},{9,13},{6,10},{10,14},{7,11},{11,15},{20,24},{2... | collective-permute-start | bytes 3145736 | tf_op jit(solution)/shard_map/ppermute | solution.py:259
  129.9 52.2 %copy-start.3 = (f32[4,128,512]{2,1,0:T(8,128)S(1)}, f32[4,128,512]{2,1,0:T(8,128)}, u32[]{:S(2)}) copy-start(f32[4,128,512]{2,1,0:T(8,128)} %add_momenta.7.refs_9_.refs_1_) | copy-start | bytes 3145732
  129.9 52.1 %copy-start.6 = (f32[4,128,512]{2,1,0:T(8,128)S(1)}, f32[4,128,512]{2,1,0:T(8,128)}, u32[]{:S(2)}) copy-start(f32[4,128,512]{2,1,0:T(8,128)} %copy-done.4) | copy-start | bytes 3145732
  130.0 30.9 %collective-permute-start.20 = (f32[4,128,512]{2,1,0:T(8,128)}, f32[4,128,512]{2,1,0:T(8,128)S(1)}, u32[]{:S(2)}, u32[]{:S(2)}) collective-permute-start(f32[4,128,512]{2,1,0:T(8,128)} %collective-permute-done.16.refs_12_), channel_id=1, source_target_pairs={{8,4},{4,0},{9,5},{5,1},{10,6},{6,2},{11,7},{7,3},{24,20},{20,16},... | collective-permute-start | bytes 3145736 | tf_op jit(solution)/shard_map/ppermute | solution.py:260
  131.4 49.4 %copy-start.13 = (f32[4,128,512]{2,1,0:T(8,128)}, f32[4,128,512]{2,1,0:T(8,128)S(1)}, u32[]{:S(2)}) copy-start(f32[4,128,512]{2,1,0:T(8,128)S(1)} %collective-permute-done.21.refs_17_) | copy-start | bytes 3145732
  131.4 31.4 %collective-permute-start.18 = (f32[4,128,512]{2,1,0:T(8,128)}, f32[4,128,512]{2,1,0:T(8,128)S(1)}, u32[]{:S(2)}, u32[]{:S(2)}) collective-permute-start(f32[4,128,512]{2,1,0:T(8,128)} %collective-permute-done.16.refs_12_), channel_id=1, source_target_pairs={{0,1},{1,0},{2,3},{3,2},{4,5},{5,4},{6,7},{7,6},{8,9},{9,8},{10,11... | collective-permute-start | bytes 3145736 | tf_op jit(solution)/shard_map/ppermute | solution.py:269
  131.6 49.3 %copy-start.14 = (f32[4,128,512]{2,1,0:T(8,128)}, f32[4,128,512]{2,1,0:T(8,128)S(1)}, u32[]{:S(2)}) copy-start(f32[4,128,512]{2,1,0:T(8,128)S(1)} %collective-permute-done.19.refs_15_) | copy-start | bytes 3145732
  131.6 32.0 %collective-permute-start.7 = (f32[4,128,512]{2,1,0:T(8,128)S(1)}, f32[4,128,512]{2,1,0:T(8,128)S(1)}, u32[]{:S(2)}, u32[]{:S(2)}) collective-permute-start(f32[4,128,512]{2,1,0:T(8,128)S(1)} %collective-permute-done.6.refs_4_), channel_id=1, source_target_pairs={{4,8},{8,12},{5,9},{9,13},{6,10},{10,14},{7,11},{11,15},{20,24},{2... | collective-permute-start | bytes 3145736 | tf_op jit(solution)/shard_map/ppermute | solution.py:259
  132.3 33.6 %collective-permute-start.28 = (f32[4,128,512]{2,1,0:T(8,128)S(1)}, f32[4,128,512]{2,1,0:T(8,128)S(1)}, u32[]{:S(2)}, u32[]{:S(2)}) collective-permute-start(f32[4,128,512]{2,1,0:T(8,128)S(1)} %get-tuple-element.34), channel_id=1, source_target_pairs={{0,1},{1,0},{2,3},{3,2},{4,5},{5,4},{6,7},{7,6},{8,9},{9,8},{10,11... | collective-permute-start | bytes 3145736 | tf_op jit(solution)/shard_map/ppermute | solution.py:318
  132.8 35.6 %collective-permute-start.12 = (f32[4,128,512]{2,1,0:T(8,128)S(1)}, f32[4,128,512]{2,1,0:T(8,128)S(1)}, u32[]{:S(2)}, u32[]{:S(2)}) collective-permute-start(f32[4,128,512]{2,1,0:T(8,128)S(1)} %collective-permute-done.6.refs_4_), channel_id=1, source_target_pairs={{0,1},{1,0},{2,3},{3,2},{4,5},{5,4},{6,7},{7,6},{8,9},{9,8},{10,11... | collective-permute-start | bytes 3145736 | tf_op jit(solution)/shard_map/ppermute | solution.py:269
  160.9 19.9 %collective-permute-start.23 = (f32[4,128,512]{2,1,0:T(8,128)S(1)}, f32[4,128,512]{2,1,0:T(8,128)S(1)}, u32[]{:S(2)}, u32[]{:S(2)}) collective-permute-start(f32[4,128,512]{2,1,0:T(8,128)S(1)} %collective-permute-done.21.refs_17_), channel_id=1, source_target_pairs={{0,1},{1,0},{4,5},{5,4},{2,3},{3,2},{6,7},{7,6},{16,17},{17,16},{2... | collective-permute-start | bytes 3145736 | tf_op jit(solution)/shard_map/ppermute | solution.py:269
  162.8 18.0 %collective-permute-start.11 = (f32[4,128,512]{2,1,0:T(8,128)S(1)}, f32[4,128,512]{2,1,0:T(8,128)S(1)}, u32[]{:S(2)}, u32[]{:S(2)}) collective-permute-start(f32[4,128,512]{2,1,0:T(8,128)S(1)} %collective-permute-done.9.refs_1_), channel_id=1, source_target_pairs={{8,9},{9,8},{12,13},{13,12},{10,11},{11,10},{14,15},{15,14},{24,25... | collective-permute-start | bytes 3145736 | tf_op jit(solution)/shard_map/ppermute | solution.py:269
  163.5 17.3 %collective-permute-start.22 = (f32[4,128,512]{2,1,0:T(8,128)S(1)}, f32[4,128,512]{2,1,0:T(8,128)S(1)}, u32[]{:S(2)}, u32[]{:S(2)}) collective-permute-start(f32[4,128,512]{2,1,0:T(8,128)S(1)} %collective-permute-done.20.refs_16_), channel_id=1, source_target_pairs={{0,1},{1,0},{4,5},{5,4},{2,3},{3,2},{6,7},{7,6},{16,17},{17,16},{2... | collective-permute-start | bytes 3145736 | tf_op jit(solution)/shard_map/ppermute | solution.py:269
  166.0 14.9 %collective-permute-start.10 = (f32[4,128,512]{2,1,0:T(8,128)S(1)}, f32[4,128,512]{2,1,0:T(8,128)S(1)}, u32[]{:S(2)}, u32[]{:S(2)}) collective-permute-start(f32[4,128,512]{2,1,0:T(8,128)S(1)} %collective-permute-done.7.refs_0_), channel_id=1, source_target_pairs={{8,9},{9,8},{12,13},{13,12},{10,11},{11,10},{14,15},{15,14},{24,25... | collective-permute-start | bytes 3145736 | tf_op jit(solution)/shard_map/ppermute | solution.py:269
  168.4 74.6 %collective-permute-start.29 = (f32[8,128,512]{2,1,0:T(8,128)}, f32[8,128,512]{2,1,0:T(8,128)S(1)}, u32[]{:S(2)}, u32[]{:S(2)}) collective-permute-start(f32[8,128,512]{2,1,0:T(8,128)} %pad_maximum_fusion.3), channel_id=1, source_target_pairs={{0,12},{12,0},{1,13},{13,1},{2,14},{14,2},{3,15},{15,3},{16,28},{2... | collective-permute-start | bytes 6291464 | tf_op jit(solution)/shard_map/ppermute | solution.py:319
  189.3 22.6 %collective-permute-start.31 = (f32[1,128,512]{2,1,0:T(8,128)S(1)}, f32[1,128,512]{2,1,0:T(8,128)S(1)}, u32[]{:S(2)}, u32[]{:S(2)}) collective-permute-start(f32[1,128,512]{2,1,0:T(8,128)S(1)} %get-tuple-element.39), channel_id=1, source_target_pairs={{0,2},{1,3},{2,0},{3,1},{4,6},{5,7},{6,4},{7,5},{8,10},{9,11},{10,... | collective-permute-start | bytes 786440 | tf_op jit(solution)/shard_map/ppermute | solution.py:337
  190.8 21.1 %collective-permute-start.33 = (f32[1,128,512]{2,1,0:T(8,128)S(1)}, f32[1,128,512]{2,1,0:T(8,128)S(1)}, u32[]{:S(2)}, u32[]{:S(2)}) collective-permute-start(f32[1,128,512]{2,1,0:T(8,128)S(1)} %get-tuple-element.41), channel_id=1, source_target_pairs={{0,1},{1,0},{2,3},{3,2},{4,5},{5,4},{6,7},{7,6},{8,9},{9,8},{10,11... | collective-permute-start | bytes 786440 | tf_op jit(solution)/shard_map/ppermute | solution.py:337
  190.8 22.3 %collective-permute-start.36 = (f32[1,128,512]{2,1,0:T(8,128)S(1)}, f32[1,128,512]{2,1,0:T(8,128)S(1)}, u32[]{:S(2)}, u32[]{:S(2)}) collective-permute-start(f32[1,128,512]{2,1,0:T(8,128)S(1)} %get-tuple-element.44), channel_id=1, source_target_pairs={{0,3},{1,2},{2,1},{3,0},{4,7},{5,6},{6,5},{7,4},{8,11},{9,10},{10,... | collective-permute-start | bytes 786440 | tf_op jit(solution)/shard_map/ppermute | solution.py:337
  199.5 14.2 %collective-permute-start.30 = (f32[1,128,512]{2,1,0:T(8,128)S(1)}, f32[1,128,512]{2,1,0:T(8,128)S(1)}, u32[]{:S(2)}, u32[]{:S(2)}) collective-permute-start(f32[1,128,512]{2,1,0:T(8,128)S(1)} %get-tuple-element.38), channel_id=1, source_target_pairs={{0,2},{1,3},{2,0},{3,1},{4,6},{5,7},{6,4},{7,5},{8,10},{9,11},{10,... | collective-permute-start | bytes 786440 | tf_op jit(solution)/shard_map/ppermute | solution.py:337
  211.9 32.0 %copy-start.23 = (f32[1,128,512]{2,1,0:T(8,128)}, f32[1,128,512]{2,1,0:T(8,128)S(1)}, u32[]{:S(2)}) copy-start(f32[1,128,512]{2,1,0:T(8,128)S(1)} %collective-permute-done.31.refs_5_) | copy-start | bytes 786436
  211.9 2.7 %collective-permute-start.32 = (f32[1,128,512]{2,1,0:T(8,128)S(1)}, f32[1,128,512]{2,1,0:T(8,128)S(1)}, u32[]{:S(2)}, u32[]{:S(2)}) collective-permute-start(f32[1,128,512]{2,1,0:T(8,128)S(1)} %get-tuple-element.40), channel_id=1, source_target_pairs={{0,1},{1,0},{2,3},{3,2},{4,5},{5,4},{6,7},{7,6},{8,9},{9,8},{10,11... | collective-permute-start | bytes 786440 | tf_op jit(solution)/shard_map/ppermute | solution.py:337
  212.7 30.3 %collective-permute-start.34 = (f32[2,128,512]{2,1,0:T(8,128)S(1)}, f32[2,128,512]{2,1,0:T(8,128)S(1)}, u32[]{:S(2)}, u32[]{:S(2)}) collective-permute-start(f32[2,128,512]{2,1,0:T(8,128)S(1)} %get-tuple-element.42), channel_id=1, source_target_pairs={{0,1},{1,0},{2,3},{3,2},{4,5},{5,4},{6,7},{7,6},{8,9},{9,8},{10,11... | collective-permute-start | bytes 1572872 | tf_op jit(solution)/shard_map/ppermute | solution.py:337
  213.1 30.7 %copy-start.25 = (f32[1,128,512]{2,1,0:T(8,128)}, f32[1,128,512]{2,1,0:T(8,128)S(1)}, u32[]{:S(2)}) copy-start(f32[1,128,512]{2,1,0:T(8,128)S(1)} %collective-permute-done.36.refs_10_) | copy-start | bytes 786436
  213.1 36.5 %collective-permute-start.24 = (f32[2,128,512]{2,1,0:T(8,128)S(1)}, f32[2,128,512]{2,1,0:T(8,128)}, u32[]{:S(2)}, u32[]{:S(2)}) collective-permute-start(f32[2,128,512]{2,1,0:T(8,128)S(1)} %get-tuple-element.28), channel_id=1, source_target_pairs={{0,2},{1,3},{2,0},{3,1},{4,6},{5,7},{6,4},{7,5},{8,10},{9,11},{10,... | collective-permute-start | bytes 1572872 | tf_op jit(solution)/shard_map/ppermute | solution.py:337
  213.7 30.1 %copy-start.26 = (f32[1,128,512]{2,1,0:T(8,128)}, f32[1,128,512]{2,1,0:T(8,128)S(1)}, u32[]{:S(2)}) copy-start(f32[1,128,512]{2,1,0:T(8,128)S(1)} %collective-permute-done.30.refs_4_) | copy-start | bytes 786436
  213.7 36.0 %collective-permute-start.25 = (f32[2,128,512]{2,1,0:T(8,128)S(1)}, f32[2,128,512]{2,1,0:T(8,128)}, u32[]{:S(2)}, u32[]{:S(2)}) collective-permute-start(f32[2,128,512]{2,1,0:T(8,128)S(1)} %get-tuple-element.29), channel_id=1, source_target_pairs={{0,3},{1,2},{2,1},{3,0},{4,7},{5,6},{6,5},{7,4},{8,11},{9,10},{10,... | collective-permute-start | bytes 1572872 | tf_op jit(solution)/shard_map/ppermute | solution.py:337
  214.6 29.3 %copy-start.27 = (f32[1,128,512]{2,1,0:T(8,128)}, f32[1,128,512]{2,1,0:T(8,128)S(1)}, u32[]{:S(2)}) copy-start(f32[1,128,512]{2,1,0:T(8,128)S(1)} %collective-permute-done.32.refs_6_) | copy-start | bytes 786436
  214.6 28.4 %collective-permute-start.35 = (f32[1,128,512]{2,1,0:T(8,128)S(1)}, f32[1,128,512]{2,1,0:T(8,128)S(1)}, u32[]{:S(2)}, u32[]{:S(2)}) collective-permute-start(f32[1,128,512]{2,1,0:T(8,128)S(1)} %get-tuple-element.43), channel_id=1, source_target_pairs={{0,3},{1,2},{2,1},{3,0},{4,7},{5,6},{6,5},{7,4},{8,11},{9,10},{10,... | collective-permute-start | bytes 786440 | tf_op jit(solution)/shard_map/ppermute | solution.py:337
  (19 other events, 78.6 us)

commit v3 on v2

--- a/solution.py
+++ b/solution.py
@@ -14,12 +14,49 @@
 
 
 def chunks_of(half):
-    return [1, 1, half - 2] if half > 2 else [1] * half
+    return [1] * half
 
 
 def halves(x):
-    high = lax.reduce_precision(x, exponent_bits=8, mantissa_bits=7)
-    return high.astype(jnp.bfloat16), (x - high).astype(jnp.bfloat16)
+    high = x.astype(jnp.bfloat16)
+    return high, (x - high.astype(jnp.float32)).astype(jnp.bfloat16)
+
+
+def side_by_side(out, x):
+    high, low = halves(x)
+    depth = x.shape[1]
+    out[0, :, pl.ds(0, depth)] = high
+    out[0, :, pl.ds(depth, depth)] = high
+    out[0, :, pl.ds(2 * depth, depth)] = low
+
+
+def prepare_far(coupling, right_high, right_low, left):
+    right_high[0], right_low[0] = halves(coupling[0].T)
+    rows = left.shape[1]
+    first = pl.multiple_of(lax.axis_index("atom") * rows, 8)
+    side_by_side(left, coupling[0, pl.ds(first, rows), :])
+
+
+def prepare_near(coupling, left):
+    depth = left.shape[2] // 3
+    first = pl.multiple_of(lax.axis_index("atom") * depth, 128)
+    side_by_side(left, coupling[0, :, pl.ds(first, depth)])
+
+
+def prepared(kernel, coupling, shapes):
+    order = coupling.shape[-1]
+    return pl.pallas_call(
+        kernel,
+        grid=(MODES,),
+        out_shape=[jax.ShapeDtypeStruct((MODES,) + shape, jnp.bfloat16) for shape in shapes],
+        in_specs=[pl.BlockSpec((1, order, order), lambda m: (m, 0, 0))],
+        out_specs=[pl.BlockSpec((1,) + shape, lambda m: (m, 0, 0)) for shape in shapes],
+        cost_estimate=pl.CostEstimate(
+            flops=8 * coupling.size,
+            bytes_accessed=4 * coupling.size + 2 * MODES * sum(a * b for a, b in shapes),
+            transcendentals=0,
+        ),
+    )(coupling)
 
 
 def add_momenta(theirs, first, green, *refs):
@@ -81,23 +118,25 @@
                 at = lax.rem(plane, half_planes)
                 slot = mode * 2 + side
                 for g in range(n_groups):
-                    for h in range(2):
-
-                        @pl.when((group == g) & (other == h))
-                        def _(g=g, h=h, at=at, slot=slot):
-                            first = 0
-                            for ref in sources[g][h]:
-                                depth = ref.shape[1]
-                                start = first
-                                if far:
-                                    per = rows // n_atoms
-                                    start = pl.multiple_of(
-                                        lax.rem(atom - first // per + n_atoms, n_atoms) * per + first % per, 8
-                                    )
-                                pltpu.make_async_copy(
-                                    ref.at[at], planes.at[buffer, slot, pl.ds(start, depth)], sems.at[buffer, slot]
-                                ).start()
-                                first += depth
+
+                    @pl.when(group == g)
+                    def _(g=g, at=at, slot=slot, other=other):
+                        for h in range(2):
+
+                            @pl.when(other == h)
+                            def _(h=h):
+                                first = 0
+                                for ref in sources[g][h]:
+                                    depth = ref.shape[1]
+                                    start = first
+                                    if far:
+                                        per = rows // n_atoms
+                                        behind = lax.rem(atom - first // per + n_atoms, n_atoms)
+                                        start = pl.multiple_of(behind * per + first % per, 8)
+                                    pltpu.make_async_copy(
+                                        ref.at[at], planes.at[buffer, slot, pl.ds(start, depth)], sems.at[buffer, slot]
+                                    ).start()
+                                    first += depth
 
     fetch(0, 0)
 
@@ -105,9 +144,11 @@
     def _(energy):
         buffer = lax.rem(energy, 2)
 
-        @pl.when(energy + 1 < count)
-        def _():
-            fetch(energy + 1, 1 - buffer)
+        if count > 1:
+
+            @pl.when(energy + 1 < count)
+            def _():
+                fetch(energy + 1, 1 - buffer)
 
         dot = functools.partial(jnp.dot, preferred_element_type=jnp.float32)
         for mode in range(MODES):
@@ -143,6 +184,9 @@
     flat = [part for group in groups for half in group for part in half]
     rows = sum(part.shape[1] for part in groups[0][0])
     n_out = left.shape[1] // out_rows
+    buffers = min(count, 2)
+    held = 4 * (2 * MODES * buffers + 6) * rows * order + 2 * 3 * MODES * rows * order + (6 << 20)
+    held += 4 * left.shape[1] * order * (count + 3) + 4 * MODES * order * order + 2 * left.size
     flops = count * 2 * 3 * MODES * (rows * order * order + left.shape[1] * rows * order)
     return pl.pallas_call(
         functools.partial(split_dot, len(groups), len(groups[0][0]), n_atoms, momenta, base, grid_total, edev, far, line),
@@ -152,11 +196,11 @@
         + [pl.BlockSpec(memory_space=pltpu.HBM)] * len(flat),
         out_specs=[pl.BlockSpec(memory_space=pltpu.VMEM)] * n_out,
         scratch_shapes=[
-            pltpu.VMEM((2, 2 * MODES, rows, order), jnp.float32),
+            pltpu.VMEM((buffers, 2 * MODES, rows, order), jnp.float32),
             pltpu.VMEM((MODES, 3 * rows, order), jnp.bfloat16),
             pltpu.SemaphoreType.DMA((2, 2 * MODES)),
         ],
-        compiler_params=pltpu.CompilerParams(vmem_limit_bytes=40 << 20),
+        compiler_params=pltpu.CompilerParams(vmem_limit_bytes=held),
         cost_estimate=pl.CostEstimate(
             flops=flops,
             bytes_accessed=count * 4 * (2 * MODES * rows * order + left.shape[1] * order),
@@ -166,21 +210,23 @@
     )(steps, occupation, right[0], right[1], left, *flat)
 
 
-def gather_up(layout, count, *refs):
+def gather_up(layout, count, before, *refs):
     out = refs[-1]
     core = lax.axis_index("kz")
     for own in range(2):
 
         @pl.when(core == own)
         def _(own=own):
+            if before:
+                out[...] = refs[-2][...]
             for half, energies in enumerate(layout):
                 where = (own if half == 0 else 1 - own) * count
                 for j, terms in enumerate(energies):
-                    total = None
+                    total = out[:, where + j, :] if before else None
                     for ref, row in terms:
-                        value = refs[ref][:, where + j, :] if row is None else refs[ref][row]
-                        total = value if total is None else total + value
-                    out[:, where + j, :] = total
+                        total = refs[ref][row] if total is None else total + refs[ref][row]
+                    if terms:
+                        out[:, where + j, :] = total
 
 
 def gathered(layout, count, arrays, before=None):
@@ -191,11 +237,10 @@
     whole = pl.BlockSpec((step, 2 * count, order), lambda i: (i, 0, 0))
     specs = [pl.BlockSpec((x.shape[0], step, order), lambda i: (0, i, 0)) for x in arrays]
     if before is not None:
-        terms = [[entry + [(len(arrays), None)] for entry in energies] for energies in terms]
         arrays, specs = arrays + [before], specs + [whole]
     size = 4 * sum(x.size for x in arrays) + 4 * 2 * count * out_rows * order
     return pl.pallas_call(
-        functools.partial(gather_up, terms, count),
+        functools.partial(gather_up, terms, count, before is not None),
         grid=(out_rows // step,),
         out_shape=jax.ShapeDtypeStruct((out_rows, 2 * count, order), jnp.float32),
         in_specs=specs,
@@ -214,7 +259,8 @@
     n, atoms, cores = lax.axis_size("energy"), lax.axis_size("atom"), lax.axis_size("kz")
     momenta = momenta_here * cores
     grid_total = n * edev
-    _, atom, core = (lax.axis_index(a) for a in ("energy", "atom", "kz"))
+    parts = lax.axis_size("grp")
+    atom, core, part = (lax.axis_index(a) for a in ("atom", "kz", "grp"))
     line = n == 2 * REACH
     half = edev // cores
     swap = [(i, (i + 1) % cores) for i in range(cores)]
@@ -269,12 +315,15 @@
         groups.append((streams[d], [lax.ppermute(x, axes, pairs) for x in streams[d]]))
 
     table_rows = couplings.shape[0]
-    strip = order // cores
-    mine = lax.dynamic_slice(couplings, (0, core * strip, 0), (table_rows, strip, order))
+    strip = order // (cores * parts)
+    mine = lax.dynamic_slice(couplings, (0, (part * cores + core) * strip, 0), (table_rows, strip, order))
     others = []
     for s in range(1, atoms):
         got = lax.ppermute(mine, "atom", around[s])
-        others.append((got, lax.ppermute(got, "kz", swap)))
+        ahead = [got] + [
+            lax.ppermute(got, "grp", [(i, (i + d) % parts) for i in range(parts)]) for d in range(1, parts)
+        ]
+        others.append([(x, lax.ppermute(x, "kz", swap)) for x in ahead])
     rows_of = lax.rem(owners, jnp.int32(table_rows))
     behind_of = lax.rem(atom - lax.div(owners, jnp.int32(table_rows)) + atoms, jnp.int32(atoms))
 
@@ -285,29 +334,26 @@
             return lax.dynamic_slice(table, (row, 0, 0), (1,) + table.shape[1:])[0]
 
         value = at(couplings)
-        for s, (got, other) in enumerate(others, 1):
-            first = jnp.where(core == 0, at(got), at(other))
-            second = jnp.where(core == 0, at(other), at(got))
-            value = jnp.where(behind == s, jnp.concatenate([first, second], 0), value)
+        for s, pieces in enumerate(others, 1):
+            strips = []
+            for g in range(parts):
+                for k in range(cores):
+                    chosen = None
+                    for d, (same, other) in enumerate(pieces):
+                        piece = jnp.where(core == k, at(same), at(other))
+                        chosen = piece if d == 0 else jnp.where((g + d) % parts == part, piece, chosen)
+                    strips.append(chosen)
+            value = jnp.where(behind == s, jnp.concatenate(strips, 0), value)
         return value
 
     coupling = jnp.stack([pick(m) for m in range(MODES)], 0)
-    right = halves(coupling.swapaxes(1, 2))
     out_rows = order // (atoms * cores)
-
-    def left_of(x):
-        high, low = halves(x)
-        return jnp.concatenate([high, high, low], 2)
-
-    left_near = left_of(lax.dynamic_slice(coupling, (0, 0, atom * brows), (MODES, order, brows)))
+    *right, left_far = prepared(prepare_far, coupling, [(order, order), (order, order), (cores * out_rows, 3 * order)])
+    (left_near,) = prepared(prepare_near, coupling, [(order, 3 * brows)])
 
     beyond = []
     if line:
-        left_far = left_of(
-            lax.dynamic_slice(coupling, (0, atom * cores * out_rows, 0), (MODES, cores * out_rows, order))
-        )
         got = [lax.ppermute(x, "atom", around[s]) for s in range(1, atoms) for x in own]
-        got, right, left_far, left_near = lax.optimization_barrier((got, right, left_far, left_near))
         whole = (
             list(own) + got,
             groups[REACH][1] + [lax.ppermute(x, "kz", swap) for x in got],

time: 255 us -> 253 us (level)
  waiting for transfers between devices: 106 us -> 90.2 us
  local copies, waits for them, and re-layouts: 16.4 us -> 26.4 us
  Pallas kernels: 64.5 us -> 68.9 us
  other arithmetic: 10.3 us -> 6.62 us
  starting transfers between devices: 48.4 us -> 51.6 us
    unnamed x60 -> x86, local copies, waits for them, and re-layouts: 10.5 us -> 24.7 us
    ppermute x9 -> x12, waiting for transfers between devices: 27.6 us -> 14.6 us  [shards(): block = lax.ppermute(block, ('atom', 'kz'), pairs)]
    pallas_call x2 -> x4, Pallas kernels: 8.84 us -> 18.2 us  [the longest x2 9.59 us: prepared(): pl.pallas_call(kernel, grid=(MODES,), out_shape=[jax.ShapeDtypeStruct((MO...]
    ppermute x1, waiting for transfers between devices: 17.9 us -> 12.2 us  [shards(): got = lax.ppermute(mine, 'atom', around[s])]
    ppermute x1 -> x3, waiting for transfers between devices: 0.01 us -> 5.2 us  [the longest x1 3.08 us: shards(): lax.ppermute(got, 'grp', [(i, (i + d) % parts) for i in range(parts)])]
    pallas_call x4 -> x5, Pallas kernels: 45.8 us -> 40.8 us  [sandwich(): pl.pallas_call(functools.partial(split_dot, len(groups), len(groups[0][0]...]
    optimization_barrier x2 -> x0, local copies, waits for them, and re-layouts: 4.01 us -> none  [shards(): lax.optimization_barrier((got, right, left_far, left_near))]
    ppermute x2, waiting for transfers between devices: 32.9 us -> 29.2 us  [shards(): lax.ppermute(x, 'atom', around[s])]
  transfers between devices with their start and end apart: 37 -> 42, of which waited for: 5 -> 12; matrix products, arithmetic and copies ran while one was open for 6% -> 3% of each run, Pallas kernels for 24% -> 25%
where the time goes in v3:
time: 253 us; the launch traced here: 251 us
  waiting for transfers between devices  90.2 us (36%)
  Pallas kernels  68.9 us (27%)
  starting transfers between devices  51.6 us (20%)
  local copies, waits for them, and re-layouts  26.4 us (10%)
  between operations  7.67 us (3%)
  other arithmetic  6.62 us (3%)
    pallas_call x5, Pallas kernels, sandwich(): pl.pallas_call(functools.partial(split_dot, len(groups), len(groups[0][0]...  40.8 us
    ppermute x2, waiting for transfers between devices, shards(): lax.ppermute(x, 'atom', around[s])  29.2 us
    ppermute x4, waiting for transfers between devices, shards(): lax.ppermute(x, 'energy', down[d - 1])  28.9 us
    unnamed x86, local copies, waits for them, and re-layouts  24.7 us
    ppermute x12, waiting for transfers between devices, shards(): block = lax.ppermute(block, ('atom', 'kz'), pairs)  14.6 us
    ppermute x1, waiting for transfers between devices, shards(): got = lax.ppermute(mine, 'atom', around[s])  12.2 us
    ppermute x4, starting transfers between devices, shards(): streams[-d] = [lax.ppermute(x, 'energy', up[d - 1]) for x in streams[1 - d]]  11.5 us
    pallas_call x4, Pallas kernels, summed(): pl.pallas_call(functools.partial(add_momenta, theirs, piece * size), out_...  9.85 us
  transfers between devices with their start and end apart: 42, of which 12 were waited for; matrix products, arithmetic and copies ran while one was open for 3% of the time, Pallas kernels for 25%

profile of v3, /device:TPU:0, one launch (start us, length us, event | category | flops | bytes accessed | tf_op | source)
XLA Modules:
  0.0 251.3 jit_solution(6281517293529195049)
XLA Ops:
  0.0 2.3 add_momenta.6
  2.9 2.3 add_momenta.4
  6.3 3.0 %collective-permute-start = (f32[2,128,512]{2,1,0:T(8,128)S(1)}, f32[2,128,512]{2,1,0:T(8,128)}, u32[]{:S(2)}, u32[]{:S(2)}) collective-permute-start(f32[2,128,512]{2,1,0:T(8,128)S(1)} %constant_dynamic-slice_fusion), channel_id=1, source_target_pairs={{0,2},{2,0},{1,3},{3,1},{4,6},{6,4},{5,7},{7,5},{8,10},{10,8},{9,1... | collective-permute-start | bytes 1572872 | tf_op jit(solution)/shard_map/ppermute | solution.py:322
  9.4 12.2 %collective-permute-done = f32[2,128,512]{2,1,0:T(8,128)} collective-permute-done((f32[2,128,512]{2,1,0:T(8,128)S(1)}, f32[2,128,512]{2,1,0:T(8,128)}, u32[]{:S(2)}, u32[]{:S(2)}) %collective-permute-start) | collective-permute-done | bytes 524320 | tf_op jit(solution)/shard_map/ppermute | solution.py:322
  21.6 1.8 collective-permute-start.1
  24.3 2.6 %add_momenta.7.refs_9_.refs_1_ = f32[4,128,512]{2,1,0:T(8,128)} custom-call(f32[2,8,256,512]{3,2,1,0:T(8,128)} %green.7, f32[4,128,512]{2,1,0:T(8,128)} %copy-done.29), custom_call_target="tpu_custom_call" | custom-call | flops 524288 | bytes 4194304 | tf_op jit(solution)/shard_map/add_momenta/pallas_call | solution.py:272
  27.0 1.6 collective-permute-start.27
  29.9 2.6 %add_momenta.5.refs_8_.refs_0_ = f32[4,128,512]{2,1,0:T(8,128)} custom-call(f32[2,8,256,512]{3,2,1,0:T(8,128)} %green.7, f32[4,128,512]{2,1,0:T(8,128)} %collective-permute-done.4.refs_0_), custom_call_target="tpu_custom_call" | custom-call | flops 524288 | bytes 4194304 | tf_op jit(solution)/shard_map/add_momenta/pallas_call | solution.py:272
  33.2 3.1 %collective-permute-done.1 = f32[2,128,512]{2,1,0:T(8,128)} collective-permute-done((f32[2,128,512]{2,1,0:T(8,128)}, f32[2,128,512]{2,1,0:T(8,128)}, u32[]{:S(2)}, u32[]{:S(2)}) %collective-permute-start.1) | collective-permute-done | bytes 524320 | tf_op jit(solution)/shard_map/ppermute | solution.py:324
  36.3 2.1 collective-permute-done.2
  38.4 4.7 %collective-permute-start.8 = (f32[4,128,512]{2,1,0:T(8,128)S(1)}, f32[4,128,512]{2,1,0:T(8,128)}, u32[]{:S(2)}, u32[]{:S(2)}) collective-permute-start(f32[4,128,512]{2,1,0:T(8,128)S(1)} %copy-done.1), channel_id=1, source_target_pairs={{0,4},{4,8},{8,12},{1,5},{5,9},{9,13},{2,6},{6,10},{10,14},{3,7},{... | collective-permute-start | bytes 3145736 | tf_op jit(solution)/shard_map/ppermute | solution.py:305
  43.1 10.3 %collective-permute-done.27.refs_3_ = f32[4,128,512]{2,1,0:T(8,128)} collective-permute-done((f32[4,128,512]{2,1,0:T(8,128)}, f32[4,128,512]{2,1,0:T(8,128)}, u32[]{:S(2)}, u32[]{:S(2)}) %collective-permute-start.27) | collective-permute-done | bytes 1048608 | tf_op jit(solution)/shard_map/ppermute | solution.py:356
  56.2 18.9 %collective-permute-done.26.refs_2_ = f32[4,128,512]{2,1,0:T(8,128)} collective-permute-done((f32[4,128,512]{2,1,0:T(8,128)}, f32[4,128,512]{2,1,0:T(8,128)}, u32[]{:S(2)}, u32[]{:S(2)}) %collective-permute-start.26) | collective-permute-done | bytes 1048608 | tf_op jit(solution)/shard_map/ppermute | solution.py:356
  83.0 2.4 broadcast_select_fusion.11
  86.2 1.9 pad_maximum_fusion.coupling
  88.2 5.4 %shard_map.65 = (bf16[3,512,512]{2,1,0:T(8,128)(2,1)}, bf16[3,512,512]{2,1,0:T(8,128)(2,1)}, bf16[3,256,1536]{2,1,0:T(8,128)(2,1)}) custom-call(f32[3,512,512]{2,1,0:T(8,128)} %pad_maximum_fusion.coupling), custom_call_target="tpu_custom_call" | custom-call | flops 6291456 | bytes 8650752 | tf_op jit(solution)/shard_map/pallas_call | solution.py:48
  93.6 3.5 %collective-permute-start.5 = (f32[4,128,512]{2,1,0:T(8,128)S(1)}, f32[4,128,512]{2,1,0:T(8,128)S(1)}, u32[]{:S(2)}, u32[]{:S(2)}) collective-permute-start(f32[4,128,512]{2,1,0:T(8,128)S(1)} %copy-done.2), channel_id=1, source_target_pairs={{0,4},{4,8},{8,12},{1,5},{5,9},{9,13},{2,6},{6,10},{10,14},{3,7},{... | collective-permute-start | bytes 3145736 | tf_op jit(solution)/shard_map/ppermute | solution.py:305
  99.1 1.6 collective-permute-start.9
  100.7 1.4 copy-done.3
  102.1 1.4 copy-done.5
  104.7 1.7 copy-done.26
  106.4 19.9 %far_sandwich.1 = (f32[4,128,512]{2,1,0:T(8,128)S(1)}, f32[4,128,512]{2,1,0:T(8,128)S(1)}) custom-call(s32[3]{0:T(128)S(1)} %copy-done.24, f32[3]{0:T(128)S(1)} %copy-done.25, bf16[3,512,512]{2,1,0:T(8,128)(2,1)S(1)} %copy-done.3, bf16[3,512,512]{2,1,0:T(8,128)(2,1)S(1)} %copy-done.5, bf16[3,256,1536]{2,1,0:T(8,128)(2,1)S(1)} %copy-done.26, ...), custom_call_target="tpu_custom_call" | custom-call | flops 14495514624 | bytes 27262976 | tf_op jit(solution)/shard_map/far_sandwich/pallas_call | solution.py:191
  128.0 1.6 collective-permute-start.6
  130.1 27.9 %collective-permute-done.20.refs_16_ = f32[4,128,512]{2,1,0:T(8,128)} collective-permute-done((f32[4,128,512]{2,1,0:T(8,128)}, f32[4,128,512]{2,1,0:T(8,128)}, u32[]{:S(2)}, u32[]{:S(2)}) %collective-permute-start.20) | collective-permute-done | bytes 1048608 | tf_op jit(solution)/shard_map/ppermute | solution.py:306
  158.0 1.9 collective-permute-start.23
  160.0 1.7 collective-permute-start.11
  161.6 2.4 collective-permute-start.22
  164.1 1.7 collective-permute-start.10
  165.8 1.5 pad_maximum_fusion.1
  168.3 9.4 %collective-permute-start.31 = (f32[8,128,512]{2,1,0:T(8,128)}, f32[8,128,512]{2,1,0:T(8,128)}, u32[]{:S(2)}, u32[]{:S(2)}) collective-permute-start(f32[8,128,512]{2,1,0:T(8,128)} %pad_maximum_fusion.1), channel_id=1, source_target_pairs={{0,12},{12,0},{1,13},{13,1},{2,14},{14,2},{3,15},{15,3},{16,28},{2... | collective-permute-start | bytes 6291464 | tf_op jit(solution)/shard_map/ppermute | solution.py:365
  177.7 4.2 %shard_map.66.left = bf16[3,512,768]{2,1,0:T(8,128)(2,1)} custom-call(f32[3,512,512]{2,1,0:T(8,128)} %pad_maximum_fusion.coupling), custom_call_target="tpu_custom_call" | custom-call | flops 6291456 | bytes 5505024 | tf_op jit(solution)/shard_map/pallas_call | solution.py:48
  181.9 1.7 copy-done
  183.6 1.4 copy-done.4
  185.0 1.4 copy-done.6
  193.7 5.1 %near_sandwich.7 = (f32[1,128,512]{2,1,0:T(8,128)S(1)}, f32[1,128,512]{2,1,0:T(8,128)S(1)}, f32[1,128,512]{2,1,0:T(8,128)S(1)}, f32[1,128,512]{2,1,0:T(8,128)S(1)}) custom-call(s32[3]{0:T(128)S(1)} %copy-done.24, f32[3]{0:T(128)S(1)} %copy-done.25, bf16[3,512,512]{2,1,0:T(8,128)(2,1)S(1)} %copy-done.4, bf16[3,512,512]{2,1,0:T(8,128)(2,1)S(1)} %copy-done.6, ...), custom_call_target="tpu_custom_call" | custom-call | flops 2415919104 | bytes 4194304 | tf_op jit(solution)/shard_map/near_sandwich/pallas_call | solution.py:191
  199.6 1.5 collective-permute-start.34
  201.7 5.1 %near_sandwich.6 = (f32[1,128,512]{2,1,0:T(8,128)S(1)}, f32[1,128,512]{2,1,0:T(8,128)S(1)}, f32[1,128,512]{2,1,0:T(8,128)S(1)}, f32[1,128,512]{2,1,0:T(8,128)S(1)}) custom-call(s32[3]{0:T(128)S(1)} %copy-done.24, f32[3]{0:T(128)S(1)} %copy-done.25, bf16[3,512,512]{2,1,0:T(8,128)(2,1)S(1)} %copy-done.4, bf16[3,512,512]{2,1,0:T(8,128)(2,1)S(1)} %copy-done.6, ...), custom_call_target="tpu_custom_call" | custom-call | flops 2415919104 | bytes 4194304 | tf_op jit(solution)/shard_map/near_sandwich/pallas_call | solution.py:191
  207.6 1.5 collective-permute-start.33
  210.4 5.1 %near_sandwich.5 = (f32[1,128,512]{2,1,0:T(8,128)S(1)}, f32[1,128,512]{2,1,0:T(8,128)S(1)}, f32[1,128,512]{2,1,0:T(8,128)S(1)}, f32[1,128,512]{2,1,0:T(8,128)S(1)}) custom-call(s32[3]{0:T(128)S(1)} %copy-done.24, f32[3]{0:T(128)S(1)} %copy-done.25, bf16[3,512,512]{2,1,0:T(8,128)(2,1)S(1)} %copy-done.4, bf16[3,512,512]{2,1,0:T(8,128)(2,1)S(1)} %copy-done.6, ...), custom_call_target="tpu_custom_call" | custom-call | flops 2415919104 | bytes 4194304 | tf_op jit(solution)/shard_map/near_sandwich/pallas_call | solution.py:191
  217.1 2.9 %collective-permute-done.33.refs_6_ = f32[1,128,512]{2,1,0:T(8,128)S(1)} collective-permute-done((f32[1,128,512]{2,1,0:T(8,128)S(1)}, f32[1,128,512]{2,1,0:T(8,128)S(1)}, u32[]{:S(2)}, u32[]{:S(2)}) %collective-permute-start.33) | collective-permute-done | bytes 262176 | tf_op jit(solution)/shard_map/ppermute | solution.py:383
  220.0 5.5 %near_sandwich.4 = (f32[1,128,512]{2,1,0:T(8,128)S(1)}, f32[1,128,512]{2,1,0:T(8,128)S(1)}, f32[1,128,512]{2,1,0:T(8,128)}, f32[1,128,512]{2,1,0:T(8,128)S(1)}) custom-call(s32[3]{0:T(128)S(1)} %copy-done.24, f32[3]{0:T(128)S(1)} %copy-done.25, bf16[3,512,512]{2,1,0:T(8,128)(2,1)S(1)} %copy-done.4, bf16[3,512,512]{2,1,0:T(8,128)(2,1)S(1)} %copy-done.6, ...), custom_call_target="tpu_custom_call" | custom-call | flops 2415919104 | bytes 4194304 | tf_op jit(solution)/shard_map/near_sandwich/pallas_call | solution.py:191
  226.2 1.6 collective-permute-start.39
  227.9 3.4 %collective-permute-done.32.refs_5_ = f32[1,128,512]{2,1,0:T(8,128)S(1)} collective-permute-done((f32[1,128,512]{2,1,0:T(8,128)S(1)}, f32[1,128,512]{2,1,0:T(8,128)S(1)}, u32[]{:S(2)}, u32[]{:S(2)}) %collective-permute-start.32) | collective-permute-done | bytes 262176 | tf_op jit(solution)/shard_map/ppermute | solution.py:383
  231.2 1.5 collective-permute-start.24
  232.7 3.1 %collective-permute-done.39.refs_12_ = f32[1,128,512]{2,1,0:T(8,128)S(1)} collective-permute-done((f32[1,128,512]{2,1,0:T(8,128)S(1)}, f32[1,128,512]{2,1,0:T(8,128)S(1)}, u32[]{:S(2)}, u32[]{:S(2)}) %collective-permute-start.39) | collective-permute-done | bytes 262176 | tf_op jit(solution)/shard_map/ppermute | solution.py:383
  236.7 4.6 %shard_map.67.refs_2_ = f32[128,8,512]{2,1,0:T(8,128)} custom-call(f32[8,128,512]{2,1,0:T(8,128)} %collective-permute-done.31.refs_0_, f32[1,128,512]{2,1,0:T(8,128)} %copy-done.22, f32[1,128,512]{2,1,0:T(8,128)} %copy-done.21, f32[1,128,512]{2,1,0:T(8,128)} %copy-done.20, f32[1,128,512]{2,1,0:T(8,128)} %copy-done.23, f32[1,128,512]{2,1,0:T(8,128)} %copy-done.36, ...), custom_call_target="tpu_custom_call" | custom-call | flops 1966080 | bytes 7864320 | tf_op jit(solution)/shard_map/pallas_call | solution.py:242
  242.5 4.1 %collective-permute-done.25.refs_1_ = f32[1,128,512]{2,1,0:T(8,128)S(1)} collective-permute-done((f32[1,128,512]{2,1,0:T(8,128)S(1)}, f32[1,128,512]{2,1,0:T(8,128)S(1)}, u32[]{:S(2)}, u32[]{:S(2)}) %collective-permute-start.25) | collective-permute-done | bytes 262176 | tf_op jit(solution)/shard_map/ppermute | solution.py:383
  247.3 4.1 %shard_map.68 = f32[128,8,512]{2,1,0:T(8,128)} custom-call(f32[1,128,512]{2,1,0:T(8,128)} %copy-done.39, f32[1,128,512]{2,1,0:T(8,128)} %copy-done.41, f32[128,8,512]{2,1,0:T(8,128)} %shard_map.67.refs_2_), custom_call_target="tpu_custom_call" | custom-call | flops 1179648 | bytes 4718592 | tf_op jit(solution)/shard_map/pallas_call | solution.py:242
  (142 shorter events, 31.0 us)
Async XLA Ops:
  2.3 21.1 %collective-permute-start.7 = (f32[4,128,512]{2,1,0:T(8,128)}, f32[4,128,512]{2,1,0:T(8,128)S(1)}, u32[]{:S(2)}, u32[]{:S(2)}) collective-permute-start(f32[4,128,512]{2,1,0:T(8,128)} %add_momenta.6), channel_id=1, source_target_pairs={{0,1},{1,0},{2,3},{3,2},{4,5},{5,4},{6,7},{7,6},{8,9},{9,8},{10,11... | collective-permute-start | bytes 3145736 | tf_op jit(solution)/shard_map/ppermute | solution.py:294
  5.2 24.7 %collective-permute-start.4 = (f32[4,128,512]{2,1,0:T(8,128)}, f32[4,128,512]{2,1,0:T(8,128)}, u32[]{:S(2)}, u32[]{:S(2)}) collective-permute-start(f32[4,128,512]{2,1,0:T(8,128)} %add_momenta.4), channel_id=1, source_target_pairs={{0,1},{1,0},{2,3},{3,2},{4,5},{5,4},{6,7},{7,6},{8,9},{9,8},{10,11... | collective-permute-start | bytes 3145736 | tf_op jit(solution)/shard_map/ppermute | solution.py:294
  6.3 15.2 %collective-permute-start = (f32[2,128,512]{2,1,0:T(8,128)S(1)}, f32[2,128,512]{2,1,0:T(8,128)}, u32[]{:S(2)}, u32[]{:S(2)}) collective-permute-start(f32[2,128,512]{2,1,0:T(8,128)S(1)} %constant_dynamic-slice_fusion), channel_id=1, source_target_pairs={{0,2},{2,0},{1,3},{3,1},{4,6},{6,4},{5,7},{7,5},{8,10},{10,8},{9,1... | collective-permute-start | bytes 1572872 | tf_op jit(solution)/shard_map/ppermute | solution.py:322
  21.6 11.0 %collective-permute-start.3 = (f32[2,128,512]{2,1,0:T(8,128)}, f32[2,128,512]{2,1,0:T(8,128)}, u32[]{:S(2)}, u32[]{:S(2)}) collective-permute-start(f32[2,128,512]{2,1,0:T(8,128)} %collective-permute-done), channel_id=1, source_target_pairs={{0,1},{1,0},{2,3},{3,2},{4,5},{5,4},{6,7},{7,6},{8,9},{9,8},{10,11... | collective-permute-start | bytes 1572872 | tf_op jit(solution)/shard_map/ppermute | solution.py:326
  21.6 14.7 %collective-permute-start.1 = (f32[2,128,512]{2,1,0:T(8,128)}, f32[2,128,512]{2,1,0:T(8,128)}, u32[]{:S(2)}, u32[]{:S(2)}) collective-permute-start(f32[2,128,512]{2,1,0:T(8,128)} %collective-permute-done), channel_id=1, source_target_pairs={{0,16},{16,0},{1,17},{17,1},{2,18},{18,2},{3,19},{19,3},{4,20},{20... | collective-permute-start | bytes 1572872 | tf_op jit(solution)/shard_map/ppermute | solution.py:324
  27.0 48.2 %copy-start.42 = (s32[3]{0:T(128)S(1)}, s32[3]{0:T(128)}, u32[]{:S(2)}) copy-start(s32[3]{0:T(128)} %param.9) | copy-start | bytes 40
  27.0 26.4 %collective-permute-start.27 = (f32[4,128,512]{2,1,0:T(8,128)}, f32[4,128,512]{2,1,0:T(8,128)}, u32[]{:S(2)}, u32[]{:S(2)}) collective-permute-start(f32[4,128,512]{2,1,0:T(8,128)} %add_momenta.7.refs_9_.refs_1_), channel_id=1, source_target_pairs={{0,2},{2,0},{1,3},{3,1},{4,6},{6,4},{5,7},{7,5},{8,10},{10,8},{9,1... | collective-permute-start | bytes 3145736 | tf_op jit(solution)/shard_map/ppermute | solution.py:356
  28.6 27.1 %collective-permute-start.17 = (f32[4,128,512]{2,1,0:T(8,128)}, f32[4,128,512]{2,1,0:T(8,128)S(1)}, u32[]{:S(2)}, u32[]{:S(2)}) collective-permute-start(f32[4,128,512]{2,1,0:T(8,128)} %add_momenta.7.refs_9_.refs_1_), channel_id=1, source_target_pairs={{12,8},{8,4},{4,0},{13,9},{9,5},{5,1},{14,10},{10,6},{6,2},{15,11}... | collective-permute-start | bytes 3145736 | tf_op jit(solution)/shard_map/ppermute | solution.py:306
  29.9 25.8 %collective-permute-start.15 = (f32[4,128,512]{2,1,0:T(8,128)}, f32[4,128,512]{2,1,0:T(8,128)S(1)}, u32[]{:S(2)}, u32[]{:S(2)}) collective-permute-start(f32[4,128,512]{2,1,0:T(8,128)} %add_momenta.7.refs_9_.refs_1_), channel_id=1, source_target_pairs={{0,1},{1,0},{2,3},{3,2},{4,5},{5,4},{6,7},{7,6},{8,9},{9,8},{10,11... | collective-permute-start | bytes 3145736 | tf_op jit(solution)/shard_map/ppermute | solution.py:315
  32.6 42.6 %collective-permute-start.26 = (f32[4,128,512]{2,1,0:T(8,128)}, f32[4,128,512]{2,1,0:T(8,128)}, u32[]{:S(2)}, u32[]{:S(2)}) collective-permute-start(f32[4,128,512]{2,1,0:T(8,128)} %add_momenta.5.refs_8_.refs_0_), channel_id=1, source_target_pairs={{0,2},{2,0},{1,3},{3,1},{4,6},{6,4},{5,7},{7,5},{8,10},{10,8},{9,1... | collective-permute-start | bytes 3145736 | tf_op jit(solution)/shard_map/ppermute | solution.py:356
  36.3 2.1 collective-permute-start.2
  38.4 17.3 %copy-start.28 = (f32[2,128,512]{2,1,0:T(8,128)}, f32[2,128,512]{2,1,0:T(8,128)S(1)}, u32[]{:S(2)}) copy-start(f32[2,128,512]{2,1,0:T(8,128)S(1)} %collective-permute-done.2) | copy-start | bytes 1572868
  38.4 55.2 %collective-permute-start.8 = (f32[4,128,512]{2,1,0:T(8,128)S(1)}, f32[4,128,512]{2,1,0:T(8,128)}, u32[]{:S(2)}, u32[]{:S(2)}) collective-permute-start(f32[4,128,512]{2,1,0:T(8,128)S(1)} %copy-done.1), channel_id=1, source_target_pairs={{0,4},{4,8},{8,12},{1,5},{5,9},{9,13},{2,6},{6,10},{10,14},{3,7},{... | collective-permute-start | bytes 3145736 | tf_op jit(solution)/shard_map/ppermute | solution.py:305
  53.4 43.7 %collective-permute-start.16 = (f32[4,128,512]{2,1,0:T(8,128)}, f32[4,128,512]{2,1,0:T(8,128)}, u32[]{:S(2)}, u32[]{:S(2)}) collective-permute-start(f32[4,128,512]{2,1,0:T(8,128)} %add_momenta.5.refs_8_.refs_0_), channel_id=1, source_target_pairs={{12,8},{8,4},{4,0},{13,9},{9,5},{5,1},{14,10},{10,6},{6,2},{15,11}... | collective-permute-start | bytes 3145736 | tf_op jit(solution)/shard_map/ppermute | solution.py:306
  55.7 42.8 %collective-permute-start.14 = (f32[4,128,512]{2,1,0:T(8,128)}, f32[4,128,512]{2,1,0:T(8,128)}, u32[]{:S(2)}, u32[]{:S(2)}) collective-permute-start(f32[4,128,512]{2,1,0:T(8,128)} %add_momenta.5.refs_8_.refs_0_), channel_id=1, source_target_pairs={{0,1},{1,0},{2,3},{3,2},{4,5},{5,4},{6,7},{7,6},{8,9},{9,8},{10,11... | collective-permute-start | bytes 3145736 | tf_op jit(solution)/shard_map/ppermute | solution.py:315
  55.7 29.7 %copy-start.7 = (f32[4,128,512]{2,1,0:T(8,128)}, f32[4,128,512]{2,1,0:T(8,128)S(1)}, u32[]{:S(2)}) copy-start(f32[4,128,512]{2,1,0:T(8,128)S(1)} %collective-permute-done.15.refs_11_.refs_5_) | copy-start | bytes 3145732
  55.7 43.1 %collective-permute-start.29 = (f32[4,128,512]{2,1,0:T(8,128)}, f32[4,128,512]{2,1,0:T(8,128)}, u32[]{:S(2)}, u32[]{:S(2)}) collective-permute-start(f32[4,128,512]{2,1,0:T(8,128)} %collective-permute-done.27.refs_3_), channel_id=1, source_target_pairs={{0,1},{1,0},{2,3},{3,2},{4,5},{5,4},{6,7},{7,6},{8,9},{9,8},{10,11... | collective-permute-start | bytes 3145736 | tf_op jit(solution)/shard_map/ppermute | solution.py:359
  75.1 23.9 %collective-permute-start.28 = (f32[4,128,512]{2,1,0:T(8,128)}, f32[4,128,512]{2,1,0:T(8,128)}, u32[]{:S(2)}, u32[]{:S(2)}) collective-permute-start(f32[4,128,512]{2,1,0:T(8,128)} %collective-permute-done.26.refs_2_), channel_id=1, source_target_pairs={{0,1},{1,0},{2,3},{3,2},{4,5},{5,4},{6,7},{7,6},{8,9},{9,8},{10,11... | collective-permute-start | bytes 3145736 | tf_op jit(solution)/shard_map/ppermute | solution.py:359
  93.6 32.8 %collective-permute-start.5 = (f32[4,128,512]{2,1,0:T(8,128)S(1)}, f32[4,128,512]{2,1,0:T(8,128)S(1)}, u32[]{:S(2)}, u32[]{:S(2)}) collective-permute-start(f32[4,128,512]{2,1,0:T(8,128)S(1)} %copy-done.2), channel_id=1, source_target_pairs={{0,4},{4,8},{8,12},{1,5},{5,9},{9,13},{2,6},{6,10},{10,14},{3,7},{... | collective-permute-start | bytes 3145736 | tf_op jit(solution)/shard_map/ppermute | solution.py:305
  97.2 30.5 %collective-permute-start.21 = (f32[4,128,512]{2,1,0:T(8,128)S(1)}, f32[4,128,512]{2,1,0:T(8,128)}, u32[]{:S(2)}, u32[]{:S(2)}) collective-permute-start(f32[4,128,512]{2,1,0:T(8,128)S(1)} %collective-permute-done.17.refs_13_), channel_id=1, source_target_pairs={{8,4},{4,0},{9,5},{5,1},{10,6},{6,2},{11,7},{7,3},{24,20},{20,16},... | collective-permute-start | bytes 3145736 | tf_op jit(solution)/shard_map/ppermute | solution.py:306
  98.5 29.5 %collective-permute-start.19 = (f32[4,128,512]{2,1,0:T(8,128)S(1)}, f32[4,128,512]{2,1,0:T(8,128)S(1)}, u32[]{:S(2)}, u32[]{:S(2)}) collective-permute-start(f32[4,128,512]{2,1,0:T(8,128)S(1)} %collective-permute-done.17.refs_13_), channel_id=1, source_target_pairs={{0,1},{1,0},{2,3},{3,2},{4,5},{5,4},{6,7},{7,6},{8,9},{9,8},{10,11... | collective-permute-start | bytes 3145736 | tf_op jit(solution)/shard_map/ppermute | solution.py:315
  98.8 30.9 %collective-permute-start.13 = (f32[4,128,512]{2,1,0:T(8,128)}, f32[4,128,512]{2,1,0:T(8,128)S(1)}, u32[]{:S(2)}, u32[]{:S(2)}) collective-permute-start(f32[4,128,512]{2,1,0:T(8,128)} %collective-permute-done.8.refs_5_), channel_id=1, source_target_pairs={{0,1},{1,0},{2,3},{3,2},{4,5},{5,4},{6,7},{7,6},{8,9},{9,8},{10,11... | collective-permute-start | bytes 3145736 | tf_op jit(solution)/shard_map/ppermute | solution.py:315
  99.1 30.8 %collective-permute-start.9 = (f32[4,128,512]{2,1,0:T(8,128)}, f32[4,128,512]{2,1,0:T(8,128)}, u32[]{:S(2)}, u32[]{:S(2)}) collective-permute-start(f32[4,128,512]{2,1,0:T(8,128)} %collective-permute-done.8.refs_5_), channel_id=1, source_target_pairs={{4,8},{8,12},{5,9},{9,13},{6,10},{10,14},{7,11},{11,15},{20,24},{2... | collective-permute-start | bytes 3145736 | tf_op jit(solution)/shard_map/ppermute | solution.py:305
  126.4 40.9 %copy-start.10 = (f32[4,128,512]{2,1,0:T(8,128)}, f32[4,128,512]{2,1,0:T(8,128)S(1)}, u32[]{:S(2)}) copy-start(f32[4,128,512]{2,1,0:T(8,128)S(1)} %collective-permute-done.5.refs_4_) | copy-start | bytes 3145732
  126.4 31.7 %collective-permute-start.20 = (f32[4,128,512]{2,1,0:T(8,128)}, f32[4,128,512]{2,1,0:T(8,128)}, u32[]{:S(2)}, u32[]{:S(2)}) collective-permute-start(f32[4,128,512]{2,1,0:T(8,128)} %collective-permute-done.16.refs_12_), channel_id=1, source_target_pairs={{8,4},{4,0},{9,5},{5,1},{10,6},{6,2},{11,7},{7,3},{24,20},{20,16},... | collective-permute-start | bytes 3145736 | tf_op jit(solution)/shard_map/ppermute | solution.py:306
  127.7 32.3 %collective-permute-start.18 = (f32[4,128,512]{2,1,0:T(8,128)}, f32[4,128,512]{2,1,0:T(8,128)S(1)}, u32[]{:S(2)}, u32[]{:S(2)}) collective-permute-start(f32[4,128,512]{2,1,0:T(8,128)} %collective-permute-done.16.refs_12_), channel_id=1, source_target_pairs={{0,1},{1,0},{2,3},{3,2},{4,5},{5,4},{6,7},{7,6},{8,9},{9,8},{10,11... | collective-permute-start | bytes 3145736 | tf_op jit(solution)/shard_map/ppermute | solution.py:315
  128.0 39.3 %copy-start.12 = (f32[4,128,512]{2,1,0:T(8,128)}, f32[4,128,512]{2,1,0:T(8,128)S(1)}, u32[]{:S(2)}) copy-start(f32[4,128,512]{2,1,0:T(8,128)S(1)} %collective-permute-done.19.refs_15_) | copy-start | bytes 3145732
  128.0 33.6 %collective-permute-start.6 = (f32[4,128,512]{2,1,0:T(8,128)S(1)}, f32[4,128,512]{2,1,0:T(8,128)}, u32[]{:S(2)}, u32[]{:S(2)}) collective-permute-start(f32[4,128,512]{2,1,0:T(8,128)S(1)} %collective-permute-done.5.refs_4_), channel_id=1, source_target_pairs={{4,8},{8,12},{5,9},{9,13},{6,10},{10,14},{7,11},{11,15},{20,24},{2... | collective-permute-start | bytes 3145736 | tf_op jit(solution)/shard_map/ppermute | solution.py:305
  129.6 37.6 %copy-start.14 = (f32[4,128,512]{2,1,0:T(8,128)}, f32[4,128,512]{2,1,0:T(8,128)S(1)}, u32[]{:S(2)}) copy-start(f32[4,128,512]{2,1,0:T(8,128)S(1)} %collective-permute-done.13.refs_7_) | copy-start | bytes 3145732
  129.6 34.4 %collective-permute-start.30 = (f32[4,128,512]{2,1,0:T(8,128)S(1)}, f32[4,128,512]{2,1,0:T(8,128)S(1)}, u32[]{:S(2)}, u32[]{:S(2)}) collective-permute-start(f32[4,128,512]{2,1,0:T(8,128)S(1)} %get-tuple-element.32), channel_id=1, source_target_pairs={{0,1},{1,0},{2,3},{3,2},{4,5},{5,4},{6,7},{7,6},{8,9},{9,8},{10,11... | collective-permute-start | bytes 3145736 | tf_op jit(solution)/shard_map/ppermute | solution.py:364
  129.9 37.3 %collective-permute-start.12 = (f32[4,128,512]{2,1,0:T(8,128)S(1)}, f32[4,128,512]{2,1,0:T(8,128)S(1)}, u32[]{:S(2)}, u32[]{:S(2)}) collective-permute-start(f32[4,128,512]{2,1,0:T(8,128)S(1)} %collective-permute-done.5.refs_4_), channel_id=1, source_target_pairs={{0,1},{1,0},{2,3},{3,2},{4,5},{5,4},{6,7},{7,6},{8,9},{9,8},{10,11... | collective-permute-start | bytes 3145736 | tf_op jit(solution)/shard_map/ppermute | solution.py:315
  158.0 23.8 %collective-permute-start.23 = (f32[4,128,512]{2,1,0:T(8,128)}, f32[4,128,512]{2,1,0:T(8,128)}, u32[]{:S(2)}, u32[]{:S(2)}) collective-permute-start(f32[4,128,512]{2,1,0:T(8,128)} %collective-permute-done.21.refs_17_), channel_id=1, source_target_pairs={{0,1},{1,0},{4,5},{5,4},{2,3},{3,2},{6,7},{7,6},{16,17},{17,16},{2... | collective-permute-start | bytes 3145736 | tf_op jit(solution)/shard_map/ppermute | solution.py:315
  160.0 21.9 %collective-permute-start.11 = (f32[4,128,512]{2,1,0:T(8,128)}, f32[4,128,512]{2,1,0:T(8,128)}, u32[]{:S(2)}, u32[]{:S(2)}) collective-permute-start(f32[4,128,512]{2,1,0:T(8,128)} %collective-permute-done.9.refs_1_), channel_id=1, source_target_pairs={{8,9},{9,8},{12,13},{13,12},{10,11},{11,10},{14,15},{15,14},{24,25... | collective-permute-start | bytes 3145736 | tf_op jit(solution)/shard_map/ppermute | solution.py:315
  161.6 20.2 %collective-permute-start.22 = (f32[4,128,512]{2,1,0:T(8,128)}, f32[4,128,512]{2,1,0:T(8,128)}, u32[]{:S(2)}, u32[]{:S(2)}) collective-permute-start(f32[4,128,512]{2,1,0:T(8,128)} %collective-permute-done.20.refs_16_), channel_id=1, source_target_pairs={{0,1},{1,0},{4,5},{5,4},{2,3},{3,2},{6,7},{7,6},{16,17},{17,16},{2... | collective-permute-start | bytes 3145736 | tf_op jit(solution)/shard_map/ppermute | solution.py:315
  164.1 17.8 %collective-permute-start.10 = (f32[4,128,512]{2,1,0:T(8,128)}, f32[4,128,512]{2,1,0:T(8,128)}, u32[]{:S(2)}, u32[]{:S(2)}) collective-permute-start(f32[4,128,512]{2,1,0:T(8,128)} %collective-permute-done.6.refs_0_), channel_id=1, source_target_pairs={{8,9},{9,8},{12,13},{13,12},{10,11},{11,10},{14,15},{15,14},{24,25... | collective-permute-start | bytes 3145736 | tf_op jit(solution)/shard_map/ppermute | solution.py:315
  168.3 67.6 %collective-permute-start.31 = (f32[8,128,512]{2,1,0:T(8,128)}, f32[8,128,512]{2,1,0:T(8,128)}, u32[]{:S(2)}, u32[]{:S(2)}) collective-permute-start(f32[8,128,512]{2,1,0:T(8,128)} %pad_maximum_fusion.1), channel_id=1, source_target_pairs={{0,12},{12,0},{1,13},{13,1},{2,14},{14,2},{3,15},{15,3},{16,28},{2... | collective-permute-start | bytes 6291464 | tf_op jit(solution)/shard_map/ppermute | solution.py:365
  199.6 9.5 %collective-permute-start.34 = (f32[1,128,512]{2,1,0:T(8,128)S(1)}, f32[1,128,512]{2,1,0:T(8,128)S(1)}, u32[]{:S(2)}, u32[]{:S(2)}) collective-permute-start(f32[1,128,512]{2,1,0:T(8,128)S(1)} %get-tuple-element.39), channel_id=1, source_target_pairs={{0,2},{1,3},{2,0},{3,1},{4,6},{5,7},{6,4},{7,5},{8,10},{9,11},{10,... | collective-permute-start | bytes 786440 | tf_op jit(solution)/shard_map/ppermute | solution.py:383
  201.1 8.0 %collective-permute-start.37 = (f32[1,128,512]{2,1,0:T(8,128)S(1)}, f32[1,128,512]{2,1,0:T(8,128)S(1)}, u32[]{:S(2)}, u32[]{:S(2)}) collective-permute-start(f32[1,128,512]{2,1,0:T(8,128)S(1)} %get-tuple-element.42), channel_id=1, source_target_pairs={{0,1},{1,0},{2,3},{3,2},{4,5},{5,4},{6,7},{7,6},{8,9},{9,8},{10,11... | collective-permute-start | bytes 786440 | tf_op jit(solution)/shard_map/ppermute | solution.py:383
  201.1 15.2 %collective-permute-start.41 = (f32[1,128,512]{2,1,0:T(8,128)S(1)}, f32[1,128,512]{2,1,0:T(8,128)S(1)}, u32[]{:S(2)}, u32[]{:S(2)}) collective-permute-start(f32[1,128,512]{2,1,0:T(8,128)S(1)} %get-tuple-element.46), channel_id=1, source_target_pairs={{0,3},{1,2},{2,1},{3,0},{4,7},{5,6},{6,5},{7,4},{8,11},{9,10},{10,... | collective-permute-start | bytes 786440 | tf_op jit(solution)/shard_map/ppermute | solution.py:383
  207.6 12.4 %collective-permute-start.33 = (f32[1,128,512]{2,1,0:T(8,128)S(1)}, f32[1,128,512]{2,1,0:T(8,128)S(1)}, u32[]{:S(2)}, u32[]{:S(2)}) collective-permute-start(f32[1,128,512]{2,1,0:T(8,128)S(1)} %get-tuple-element.38), channel_id=1, source_target_pairs={{0,2},{1,3},{2,0},{3,1},{4,6},{5,7},{6,4},{7,5},{8,10},{9,11},{10,... | collective-permute-start | bytes 786440 | tf_op jit(solution)/shard_map/ppermute | solution.py:383
  209.1 17.2 %collective-permute-start.36 = (f32[1,128,512]{2,1,0:T(8,128)S(1)}, f32[1,128,512]{2,1,0:T(8,128)S(1)}, u32[]{:S(2)}, u32[]{:S(2)}) collective-permute-start(f32[1,128,512]{2,1,0:T(8,128)S(1)} %get-tuple-element.41), channel_id=1, source_target_pairs={{0,1},{1,0},{2,3},{3,2},{4,5},{5,4},{6,7},{7,6},{8,9},{9,8},{10,11... | collective-permute-start | bytes 786440 | tf_op jit(solution)/shard_map/ppermute | solution.py:383
  209.8 18.1 %collective-permute-start.40 = (f32[1,128,512]{2,1,0:T(8,128)S(1)}, f32[1,128,512]{2,1,0:T(8,128)S(1)}, u32[]{:S(2)}, u32[]{:S(2)}) collective-permute-start(f32[1,128,512]{2,1,0:T(8,128)S(1)} %get-tuple-element.45), channel_id=1, source_target_pairs={{0,3},{1,2},{2,1},{3,0},{4,7},{5,6},{6,5},{7,4},{8,11},{9,10},{10,... | collective-permute-start | bytes 786440 | tf_op jit(solution)/shard_map/ppermute | solution.py:383
  216.3 14.9 %collective-permute-start.32 = (f32[1,128,512]{2,1,0:T(8,128)S(1)}, f32[1,128,512]{2,1,0:T(8,128)S(1)}, u32[]{:S(2)}, u32[]{:S(2)}) collective-permute-start(f32[1,128,512]{2,1,0:T(8,128)S(1)} %get-tuple-element.37), channel_id=1, source_target_pairs={{0,2},{1,3},{2,0},{3,1},{4,6},{5,7},{6,4},{7,5},{8,10},{9,11},{10,... | collective-permute-start | bytes 786440 | tf_op jit(solution)/shard_map/ppermute | solution.py:383
  220.0 12.7 %collective-permute-start.35 = (f32[1,128,512]{2,1,0:T(8,128)S(1)}, f32[1,128,512]{2,1,0:T(8,128)S(1)}, u32[]{:S(2)}, u32[]{:S(2)}) collective-permute-start(f32[1,128,512]{2,1,0:T(8,128)S(1)} %get-tuple-element.40), channel_id=1, source_target_pairs={{0,1},{1,0},{2,3},{3,2},{4,5},{5,4},{6,7},{7,6},{8,9},{9,8},{10,11... | collective-permute-start | bytes 786440 | tf_op jit(solution)/shard_map/ppermute | solution.py:383
  226.2 9.6 %collective-permute-start.39 = (f32[1,128,512]{2,1,0:T(8,128)S(1)}, f32[1,128,512]{2,1,0:T(8,128)S(1)}, u32[]{:S(2)}, u32[]{:S(2)}) collective-permute-start(f32[1,128,512]{2,1,0:T(8,128)S(1)} %get-tuple-element.44), channel_id=1, source_target_pairs={{0,3},{1,2},{2,1},{3,0},{4,7},{5,6},{6,5},{7,4},{8,11},{9,10},{10,... | collective-permute-start | bytes 786440 | tf_op jit(solution)/shard_map/ppermute | solution.py:383
  227.9 8.0 %collective-permute-start.38 = (f32[1,128,512]{2,1,0:T(8,128)S(1)}, f32[1,128,512]{2,1,0:T(8,128)S(1)}, u32[]{:S(2)}, u32[]{:S(2)}) collective-permute-start(f32[1,128,512]{2,1,0:T(8,128)S(1)} %get-tuple-element.43), channel_id=1, source_target_pairs={{0,1},{1,0},{2,3},{3,2},{4,5},{5,4},{6,7},{7,6},{8,9},{9,8},{10,11... | collective-permute-start | bytes 786440 | tf_op jit(solution)/shard_map/ppermute | solution.py:383
  231.2 11.2 %collective-permute-start.24 = (f32[1,128,512]{2,1,0:T(8,128)}, f32[1,128,512]{2,1,0:T(8,128)S(1)}, u32[]{:S(2)}, u32[]{:S(2)}) collective-permute-start(f32[1,128,512]{2,1,0:T(8,128)} %get-tuple-element.28), channel_id=1, source_target_pairs={{0,2},{1,3},{2,0},{3,1},{4,6},{5,7},{6,4},{7,5},{8,10},{9,11},{10,... | collective-permute-start | bytes 786440 | tf_op jit(solution)/shard_map/ppermute | solution.py:383
  232.7 13.8 %collective-permute-start.25 = (f32[1,128,512]{2,1,0:T(8,128)S(1)}, f32[1,128,512]{2,1,0:T(8,128)S(1)}, u32[]{:S(2)}, u32[]{:S(2)}) collective-permute-start(f32[1,128,512]{2,1,0:T(8,128)S(1)} %get-tuple-element.29), channel_id=1, source_target_pairs={{0,3},{1,2},{2,1},{3,0},{4,7},{5,6},{6,5},{7,4},{8,11},{9,10},{10,... | collective-permute-start | bytes 786440 | tf_op jit(solution)/shard_map/ppermute | solution.py:383
  (37 other events, 127.9 us)

commit v4 on v3

--- a/solution.py
+++ b/solution.py
@@ -60,8 +60,8 @@
 
 
 def add_momenta(theirs, first, green, *refs):
-    out, held, total, arrived, left = refs[-5:]
-    given = refs[:-5]
+    out, held, total, arrived, left = refs[-6:-1]
+    given = refs[:-6]
     momenta, count, size = green.shape[0], held.shape[0], held.shape[2]
     core = lax.axis_index("kz")
     base = (1 - core if theirs else core) * count
@@ -210,41 +210,71 @@
     )(steps, occupation, right[0], right[1], left, *flat)
 
 
-def gather_up(layout, count, before, *refs):
+def gather_early(layout, count, *refs):
     out = refs[-1]
     core = lax.axis_index("kz")
     for own in range(2):
 
         @pl.when(core == own)
         def _(own=own):
-            if before:
-                out[...] = refs[-2][...]
             for half, energies in enumerate(layout):
                 where = (own if half == 0 else 1 - own) * count
                 for j, terms in enumerate(energies):
-                    total = out[:, where + j, :] if before else None
+                    total = None
                     for ref, row in terms:
                         total = refs[ref][row] if total is None else total + refs[ref][row]
-                    if terms:
-                        out[:, where + j, :] = total
-
-
-def gathered(layout, count, arrays, before=None):
+                    out[:, where + j, :] = total
+
+
+def gather_late(layout, count, whole, *refs):
+    out, total, sems = refs[-3:]
+    full = refs[-3 - whole : -3]
+    core = lax.axis_index("kz")
+    step = total.shape[0] // sems.shape[0]
+    for part in range(sems.shape[0]):
+        rows = pl.ds(part * step, step)
+        value = full[0][rows]
+        for ref in full[1:]:
+            value = value + ref[rows]
+        total[rows] = value
+        for own in range(2):
+
+            @pl.when(core == own)
+            def _(own=own, rows=rows):
+                for half, energies in enumerate(layout):
+                    where = (own if half == 0 else 1 - own) * count
+                    for j, terms in enumerate(energies):
+                        if terms:
+                            value = total[rows, where + j, :]
+                            for ref, row in terms:
+                                value = value + refs[ref][row, rows]
+                            total[rows, where + j, :] = value
+
+        pltpu.make_async_copy(total.at[rows], out.at[rows], sems.at[part]).start()
+    for part in range(sems.shape[0]):
+        rows = pl.ds(part * step, step)
+        pltpu.make_async_copy(total.at[rows], out.at[rows], sems.at[part]).wait()
+
+
+def gathered(layout, count, arrays, before=()):
     terms = [[[(arrays.index(x), row) for x, row in entry] for entry in energies] for energies in layout]
-    arrays = list(arrays)
     out_rows, order = arrays[0].shape[1:]
-    step = min(out_rows, 32)
-    whole = pl.BlockSpec((step, 2 * count, order), lambda i: (i, 0, 0))
-    specs = [pl.BlockSpec((x.shape[0], step, order), lambda i: (0, i, 0)) for x in arrays]
-    if before is not None:
-        arrays, specs = arrays + [before], specs + [whole]
+    arrays = list(arrays) + list(before)
+    shape = (out_rows, 2 * count, order)
     size = 4 * sum(x.size for x in arrays) + 4 * 2 * count * out_rows * order
+    vmem = pl.BlockSpec(memory_space=pltpu.VMEM)
+    if before:
+        parts = 4 if out_rows % 32 == 0 else 1
+        kernel = functools.partial(gather_late, terms, count, len(before))
+        scratch = [pltpu.VMEM(shape, jnp.float32), pltpu.SemaphoreType.DMA((parts,))]
+    else:
+        kernel, scratch = functools.partial(gather_early, terms, count), []
     return pl.pallas_call(
-        functools.partial(gather_up, terms, count, before is not None),
-        grid=(out_rows // step,),
-        out_shape=jax.ShapeDtypeStruct((out_rows, 2 * count, order), jnp.float32),
-        in_specs=specs,
-        out_specs=whole,
+        kernel,
+        out_shape=jax.ShapeDtypeStruct(shape, jnp.float32),
+        in_specs=[vmem] * len(arrays),
+        out_specs=pl.BlockSpec(memory_space=pltpu.HBM) if before else vmem,
+        scratch_shapes=scratch,
         cost_estimate=pl.CostEstimate(flops=size // 4, bytes_accessed=size, transcendentals=0),
     )(*arrays)
 
@@ -279,7 +309,9 @@
                 pltpu.VMEM((half, size, order), jnp.float32),
                 pltpu.SemaphoreType.DMA((half,)),
                 pltpu.SemaphoreType.DMA((half,)),
+                pltpu.VMEM((48 << 10, 256), jnp.float32),
             ],
+            compiler_params=pltpu.CompilerParams(vmem_limit_bytes=60 << 20),
             cost_estimate=pl.CostEstimate(
                 flops=momenta_here * half * size * order,
                 bytes_accessed=4 * (momenta_here + 1 + len(more)) * half * size * order,
@@ -361,7 +393,10 @@
         sums = sandwich(
             offsets, occupation, right, left_far, [whole], atoms, momenta, 0, grid_total, edev, True, line, out_rows, half
         )
-        both = jnp.concatenate([sums[0], lax.ppermute(sums[1], "kz", swap)], 0)
+        swapped = lax.ppermute(sums[1], "kz", swap)
+        both = jnp.concatenate(
+            [jnp.where(core == 0, sums[0], swapped), jnp.where(core == 0, swapped, sums[0])], 0
+        ).swapaxes(0, 1)
         beyond.append(lax.ppermute(both, "energy", [(0, n - 1), (n - 1, 0)]))
 
     terms = [[[] for _ in range(atoms)] for _ in range(cores)]
@@ -385,7 +420,7 @@
     chunks = chunks_of(half)
     entries = [[[] for _ in range(half)] for _ in range(cores)]
     late = [[[] for _ in range(half)] for _ in range(cores)]
-    early, last = Terms(beyond), Terms()
+    early, last = Terms(), Terms()
     for t in range(cores):
         for s in range(atoms):
             first = 0
@@ -395,11 +430,8 @@
                 for row in range(chunks[chunk]):
                     held[1][t][first + row].append((block, row))
                 first += chunks[chunk]
-        for j in range(half):
-            for block in beyond:
-                entries[t][j].append((block, t * half + j))
     total = gathered(entries, half, early)
-    return gathered(late, half, last, total)
+    return gathered(late, half, last, [total] + beyond)
 
 
 def solution(mesh):

time: 253 us -> 253 us (level)
  starting transfers between devices: 51.6 us -> 43.8 us
  waiting for transfers between devices: 90.2 us -> 94.4 us
  local copies, waits for them, and re-layouts: 26.4 us -> 29 us
    ppermute x1, waiting for transfers between devices: 3.08 us -> 11.4 us  [shards(): lax.ppermute(got, 'grp', [(i, (i + d) % parts) for i in range(parts)])]
    ppermute x1, starting transfers between devices: 9.41 us -> 1.91 us  [shards(): beyond.append(lax.ppermute(both, 'energy', [(0, n - 1), (n - 1, 0)]))]
    ppermute x2, waiting for transfers between devices: 29.2 us -> 35.5 us  [shards(): lax.ppermute(x, 'atom', around[s])]
    ppermute x1, waiting for transfers between devices: 12.2 us -> 6.66 us  [shards(): got = lax.ppermute(mine, 'atom', around[s])]
    ppermute x4, waiting for transfers between devices: 28.9 us -> 24.7 us  [shards(): lax.ppermute(x, 'energy', down[d - 1])]
    unnamed x86 -> x88, local copies, waits for them, and re-layouts: 24.7 us -> 26.5 us
  transfers between devices with their start and end apart: 42 -> 42, of which waited for: 12 -> 11; matrix products, arithmetic and copies ran while one was open for 3% -> 4% of each run, Pallas kernels for 25% -> 25%
where the time goes in v4:
time: 253 us; the launch traced here: 251 us
  waiting for transfers between devices  94.4 us (37%)
  Pallas kernels  67.9 us (27%)
  starting transfers between devices  43.8 us (17%)
  local copies, waits for them, and re-layouts  29 us (11%)
  between operations  8.53 us (3%)
  other arithmetic  7.8 us (3%)
    pallas_call x5, Pallas kernels, sandwich(): pl.pallas_call(functools.partial(split_dot, len(groups), len(groups[0][0]...  40.6 us
    ppermute x2, waiting for transfers between devices, shards(): lax.ppermute(x, 'atom', around[s])  35.5 us
    unnamed x88, local copies, waits for them, and re-layouts  26.5 us
    ppermute x4, waiting for transfers between devices, shards(): lax.ppermute(x, 'energy', down[d - 1])  24.7 us
    ppermute x12, waiting for transfers between devices, shards(): block = lax.ppermute(block, ('atom', 'kz'), pairs)  16 us
    ppermute x1, waiting for transfers between devices, shards(): lax.ppermute(got, 'grp', [(i, (i + d) % parts) for i in range(parts)])  11.4 us
    ppermute x4, starting transfers between devices, shards(): streams[-d] = [lax.ppermute(x, 'energy', up[d - 1]) for x in streams[1 - d]]  11.3 us
    pallas_call x4, Pallas kernels, summed(): pl.pallas_call(functools.partial(add_momenta, theirs, piece * size), out_...  9.89 us
  transfers between devices with their start and end apart: 42, of which 11 were waited for; matrix products, arithmetic and copies ran while one was open for 4% of the time, Pallas kernels for 25%

profile of v4, /device:TPU:0, one launch (start us, length us, event | category | flops | bytes accessed | tf_op | source)
XLA Modules:
  0.0 251.3 jit_solution(2283196978234138433)
XLA Ops:
  1.1 3.0 %collective-permute-start = (f32[2,128,512]{2,1,0:T(8,128)S(1)}, f32[2,128,512]{2,1,0:T(8,128)S(1)}, u32[]{:S(2)}, u32[]{:S(2)}) collective-permute-start(f32[2,128,512]{2,1,0:T(8,128)S(1)} %constant_dynamic-slice_fusion), channel_id=1, source_target_pairs={{0,2},{2,0},{1,3},{3,1},{4,6},{6,4},{5,7},{7,5},{8,10},{10,8},{9,1... | collective-permute-start | bytes 1572872 | tf_op jit(solution)/shard_map/ppermute | solution.py:354
  4.1 2.3 add_momenta.4
  6.5 2.3 add_momenta.6
  9.4 6.7 %collective-permute-done = f32[2,128,512]{2,1,0:T(8,128)S(1)} collective-permute-done((f32[2,128,512]{2,1,0:T(8,128)S(1)}, f32[2,128,512]{2,1,0:T(8,128)S(1)}, u32[]{:S(2)}, u32[]{:S(2)}) %collective-permute-start) | collective-permute-done | bytes 524320 | tf_op jit(solution)/shard_map/ppermute | solution.py:354
  16.0 1.8 collective-permute-start.1
  17.8 11.4 %collective-permute-done.1 = f32[2,128,512]{2,1,0:T(8,128)} collective-permute-done((f32[2,128,512]{2,1,0:T(8,128)S(1)}, f32[2,128,512]{2,1,0:T(8,128)}, u32[]{:S(2)}, u32[]{:S(2)}) %collective-permute-start.1) | collective-permute-done | bytes 524320 | tf_op jit(solution)/shard_map/ppermute | solution.py:356
  30.2 2.6 %add_momenta.5.refs_8_.refs_0_ = f32[4,128,512]{2,1,0:T(8,128)} custom-call(f32[2,8,256,512]{3,2,1,0:T(8,128)} %green.7, f32[4,128,512]{2,1,0:T(8,128)} %copy-done.30), custom_call_target="tpu_custom_call" | custom-call | flops 524288 | bytes 4194304 | tf_op jit(solution)/shard_map/add_momenta/pallas_call | solution.py:302
  34.4 2.6 %add_momenta.7.refs_9_.refs_1_ = f32[4,128,512]{2,1,0:T(8,128)} custom-call(f32[2,8,256,512]{3,2,1,0:T(8,128)} %green.7, f32[4,128,512]{2,1,0:T(8,128)} %copy-done.29), custom_call_target="tpu_custom_call" | custom-call | flops 524288 | bytes 4194304 | tf_op jit(solution)/shard_map/add_momenta/pallas_call | solution.py:302
  37.2 1.5 collective-permute-start.36
  39.3 3.5 %collective-permute-start.5 = (f32[4,128,512]{2,1,0:T(8,128)S(1)}, f32[4,128,512]{2,1,0:T(8,128)S(1)}, u32[]{:S(2)}, u32[]{:S(2)}) collective-permute-start(f32[4,128,512]{2,1,0:T(8,128)S(1)} %copy-done.1), channel_id=1, source_target_pairs={{0,4},{4,8},{8,12},{1,5},{5,9},{9,13},{2,6},{6,10},{10,14},{3,7},{... | collective-permute-start | bytes 3145736 | tf_op jit(solution)/shard_map/ppermute | solution.py:337
  42.8 4.5 %collective-permute-start.8 = (f32[4,128,512]{2,1,0:T(8,128)}, f32[4,128,512]{2,1,0:T(8,128)}, u32[]{:S(2)}, u32[]{:S(2)}) collective-permute-start(f32[4,128,512]{2,1,0:T(8,128)} %add_momenta.7.refs_9_.refs_1_), channel_id=1, source_target_pairs={{0,4},{4,8},{8,12},{1,5},{5,9},{9,13},{2,6},{6,10},{10,14},{3,7},{... | collective-permute-start | bytes 3145736 | tf_op jit(solution)/shard_map/ppermute | solution.py:337
  48.5 14.8 %collective-permute-done.36.refs_2_ = f32[4,128,512]{2,1,0:T(8,128)} collective-permute-done((f32[4,128,512]{2,1,0:T(8,128)S(1)}, f32[4,128,512]{2,1,0:T(8,128)}, u32[]{:S(2)}, u32[]{:S(2)}) %collective-permute-start.36) | collective-permute-done | bytes 1048608 | tf_op jit(solution)/shard_map/ppermute | solution.py:388
  64.7 20.6 %collective-permute-done.37.refs_3_ = f32[4,128,512]{2,1,0:T(8,128)} collective-permute-done((f32[4,128,512]{2,1,0:T(8,128)}, f32[4,128,512]{2,1,0:T(8,128)}, u32[]{:S(2)}, u32[]{:S(2)}) %collective-permute-start.37) | collective-permute-done | bytes 1048608 | tf_op jit(solution)/shard_map/ppermute | solution.py:388
  95.3 2.4 broadcast_select_fusion.11
  98.6 1.9 pad_maximum_fusion.coupling
  100.6 5.4 %shard_map.65 = (bf16[3,512,512]{2,1,0:T(8,128)(2,1)}, bf16[3,512,512]{2,1,0:T(8,128)(2,1)}, bf16[3,256,1536]{2,1,0:T(8,128)(2,1)}) custom-call(f32[3,512,512]{2,1,0:T(8,128)} %pad_maximum_fusion.coupling), custom_call_target="tpu_custom_call" | custom-call | flops 6291456 | bytes 8650752 | tf_op jit(solution)/shard_map/pallas_call | solution.py:48
  106.0 1.7 collective-permute-start.6
  107.7 1.7 collective-permute-start.9
  113.4 1.4 copy-done.5
  116.0 1.7 copy-done.26
  117.7 20.1 %far_sandwich.1 = (f32[4,128,512]{2,1,0:T(8,128)S(1)}, f32[4,128,512]{2,1,0:T(8,128)S(1)}) custom-call(s32[3]{0:T(128)S(1)} %copy-done.24, f32[3]{0:T(128)S(1)} %copy-done.25, bf16[3,512,512]{2,1,0:T(8,128)(2,1)S(1)} %copy-done.3, bf16[3,512,512]{2,1,0:T(8,128)(2,1)S(1)} %copy-done.5, bf16[3,256,1536]{2,1,0:T(8,128)(2,1)S(1)} %copy-done.26, ...), custom_call_target="tpu_custom_call" | custom-call | flops 14495514624 | bytes 27262976 | tf_op jit(solution)/shard_map/far_sandwich/pallas_call | solution.py:191
  139.1 2.7 %collective-permute-done.20.refs_16_ = f32[4,128,512]{2,1,0:T(8,128)} collective-permute-done((f32[4,128,512]{2,1,0:T(8,128)}, f32[4,128,512]{2,1,0:T(8,128)}, u32[]{:S(2)}, u32[]{:S(2)}) %collective-permute-start.20) | collective-permute-done | bytes 1048608 | tf_op jit(solution)/shard_map/ppermute | solution.py:338
  141.8 22.0 %collective-permute-done.21.refs_17_ = f32[4,128,512]{2,1,0:T(8,128)} collective-permute-done((f32[4,128,512]{2,1,0:T(8,128)}, f32[4,128,512]{2,1,0:T(8,128)}, u32[]{:S(2)}, u32[]{:S(2)}) %collective-permute-start.21) | collective-permute-done | bytes 1048608 | tf_op jit(solution)/shard_map/ppermute | solution.py:338
  163.8 1.7 collective-permute-start.10
  165.5 1.6 collective-permute-start.11
  167.1 2.4 collective-permute-start.22
  169.5 2.1 collective-permute-start.23
  172.6 1.8 maximum_bitcast_fusion
  175.4 1.9 collective-permute-start.41
  177.3 4.2 %shard_map.66.left = bf16[3,512,768]{2,1,0:T(8,128)(2,1)} custom-call(f32[3,512,512]{2,1,0:T(8,128)} %pad_maximum_fusion.coupling), custom_call_target="tpu_custom_call" | custom-call | flops 6291456 | bytes 5505024 | tf_op jit(solution)/shard_map/pallas_call | solution.py:48
  181.5 1.7 copy-done
  183.2 1.4 copy-done.4
  184.6 1.4 copy-done.6
  193.3 5.0 %near_sandwich.7 = (f32[1,128,512]{2,1,0:T(8,128)S(1)}, f32[1,128,512]{2,1,0:T(8,128)S(1)}, f32[1,128,512]{2,1,0:T(8,128)S(1)}, f32[1,128,512]{2,1,0:T(8,128)S(1)}) custom-call(s32[3]{0:T(128)S(1)} %copy-done.24, f32[3]{0:T(128)S(1)} %copy-done.25, bf16[3,512,512]{2,1,0:T(8,128)(2,1)S(1)} %copy-done.4, bf16[3,512,512]{2,1,0:T(8,128)(2,1)S(1)} %copy-done.6, ...), custom_call_target="tpu_custom_call" | custom-call | flops 2415919104 | bytes 4194304 | tf_op jit(solution)/shard_map/near_sandwich/pallas_call | solution.py:191
  199.0 1.5 collective-permute-start.28
  201.2 5.1 %near_sandwich.6 = (f32[1,128,512]{2,1,0:T(8,128)S(1)}, f32[1,128,512]{2,1,0:T(8,128)S(1)}, f32[1,128,512]{2,1,0:T(8,128)S(1)}, f32[1,128,512]{2,1,0:T(8,128)S(1)}) custom-call(s32[3]{0:T(128)S(1)} %copy-done.24, f32[3]{0:T(128)S(1)} %copy-done.25, bf16[3,512,512]{2,1,0:T(8,128)(2,1)S(1)} %copy-done.4, bf16[3,512,512]{2,1,0:T(8,128)(2,1)S(1)} %copy-done.6, ...), custom_call_target="tpu_custom_call" | custom-call | flops 2415919104 | bytes 4194304 | tf_op jit(solution)/shard_map/near_sandwich/pallas_call | solution.py:191
  207.0 1.5 collective-permute-start.27
  209.9 5.0 %near_sandwich.5 = (f32[1,128,512]{2,1,0:T(8,128)S(1)}, f32[1,128,512]{2,1,0:T(8,128)S(1)}, f32[1,128,512]{2,1,0:T(8,128)S(1)}, f32[1,128,512]{2,1,0:T(8,128)S(1)}) custom-call(s32[3]{0:T(128)S(1)} %copy-done.24, f32[3]{0:T(128)S(1)} %copy-done.25, bf16[3,512,512]{2,1,0:T(8,128)(2,1)S(1)} %copy-done.4, bf16[3,512,512]{2,1,0:T(8,128)(2,1)S(1)} %copy-done.6, ...), custom_call_target="tpu_custom_call" | custom-call | flops 2415919104 | bytes 4194304 | tf_op jit(solution)/shard_map/near_sandwich/pallas_call | solution.py:191
  216.5 2.9 %collective-permute-done.27.refs_5_ = f32[1,128,512]{2,1,0:T(8,128)S(1)} collective-permute-done((f32[1,128,512]{2,1,0:T(8,128)S(1)}, f32[1,128,512]{2,1,0:T(8,128)S(1)}, u32[]{:S(2)}, u32[]{:S(2)}) %collective-permute-start.27) | collective-permute-done | bytes 262176 | tf_op jit(solution)/shard_map/ppermute | solution.py:418
  219.5 5.4 %near_sandwich.4 = (f32[1,128,512]{2,1,0:T(8,128)S(1)}, f32[1,128,512]{2,1,0:T(8,128)S(1)}, f32[1,128,512]{2,1,0:T(8,128)}, f32[1,128,512]{2,1,0:T(8,128)S(1)}) custom-call(s32[3]{0:T(128)S(1)} %copy-done.24, f32[3]{0:T(128)S(1)} %copy-done.25, bf16[3,512,512]{2,1,0:T(8,128)(2,1)S(1)} %copy-done.4, bf16[3,512,512]{2,1,0:T(8,128)(2,1)S(1)} %copy-done.6, ...), custom_call_target="tpu_custom_call" | custom-call | flops 2415919104 | bytes 4194304 | tf_op jit(solution)/shard_map/near_sandwich/pallas_call | solution.py:191
  225.6 1.6 collective-permute-start.33
  227.2 3.5 %collective-permute-done.26.refs_4_ = f32[1,128,512]{2,1,0:T(8,128)S(1)} collective-permute-done((f32[1,128,512]{2,1,0:T(8,128)S(1)}, f32[1,128,512]{2,1,0:T(8,128)S(1)}, u32[]{:S(2)}, u32[]{:S(2)}) %collective-permute-start.26) | collective-permute-done | bytes 262176 | tf_op jit(solution)/shard_map/ppermute | solution.py:418
  230.7 1.5 collective-permute-start.24
  232.2 3.2 %collective-permute-done.33.refs_11_ = f32[1,128,512]{2,1,0:T(8,128)S(1)} collective-permute-done((f32[1,128,512]{2,1,0:T(8,128)S(1)}, f32[1,128,512]{2,1,0:T(8,128)S(1)}, u32[]{:S(2)}, u32[]{:S(2)}) %collective-permute-start.33) | collective-permute-done | bytes 262176 | tf_op jit(solution)/shard_map/ppermute | solution.py:418
  236.2 3.9 %shard_map.67.refs_2_ = f32[128,8,512]{2,1,0:T(8,128)} custom-call(f32[1,128,512]{2,1,0:T(8,128)} %copy-done.22, f32[1,128,512]{2,1,0:T(8,128)} %copy-done.21, f32[1,128,512]{2,1,0:T(8,128)} %copy-done.20, f32[1,128,512]{2,1,0:T(8,128)} %copy-done.23, f32[1,128,512]{2,1,0:T(8,128)} %copy-done.37, f32[1,128,512]{2,1,0:T(8,128)} %copy-done.34, ...), custom_call_target="tpu_custom_call" | custom-call | flops 1441792 | bytes 5767168 | tf_op jit(solution)/shard_map/pallas_call | solution.py:272
  240.1 1.8 collective-permute-done.24.refs_0_
  241.9 4.7 %collective-permute-done.25.refs_1_ = f32[1,128,512]{2,1,0:T(8,128)S(1)} collective-permute-done((f32[1,128,512]{2,1,0:T(8,128)S(1)}, f32[1,128,512]{2,1,0:T(8,128)S(1)}, u32[]{:S(2)}, u32[]{:S(2)}) %collective-permute-start.25) | collective-permute-done | bytes 262176 | tf_op jit(solution)/shard_map/ppermute | solution.py:418
  247.3 3.9 %shard_map.68 = f32[128,8,512]{2,1,0:T(8,128)} custom-call(f32[1,128,512]{2,1,0:T(8,128)} %copy-done.41, f32[1,128,512]{2,1,0:T(8,128)} %copy-done.42, f32[128,8,512]{2,1,0:T(8,128)} %shard_map.67.refs_2_, f32[128,8,512]{2,1,0:T(8,128)} %collective-permute-done.41.refs_3_), custom_call_target="tpu_custom_call" | custom-call | flops 1703936 | bytes 6815744 | tf_op jit(solution)/shard_map/pallas_call | solution.py:272
  (146 shorter events, 33.5 us)
Async XLA Ops:
  1.1 15.0 %collective-permute-start = (f32[2,128,512]{2,1,0:T(8,128)S(1)}, f32[2,128,512]{2,1,0:T(8,128)S(1)}, u32[]{:S(2)}, u32[]{:S(2)}) collective-permute-start(f32[2,128,512]{2,1,0:T(8,128)S(1)} %constant_dynamic-slice_fusion), channel_id=1, source_target_pairs={{0,2},{2,0},{1,3},{3,1},{4,6},{6,4},{5,7},{7,5},{8,10},{10,8},{9,1... | collective-permute-start | bytes 1572872 | tf_op jit(solution)/shard_map/ppermute | solution.py:354
  6.4 22.8 %collective-permute-start.4 = (f32[4,128,512]{2,1,0:T(8,128)}, f32[4,128,512]{2,1,0:T(8,128)S(1)}, u32[]{:S(2)}, u32[]{:S(2)}) collective-permute-start(f32[4,128,512]{2,1,0:T(8,128)} %add_momenta.4), channel_id=1, source_target_pairs={{0,1},{1,0},{2,3},{3,2},{4,5},{5,4},{6,7},{7,6},{8,9},{9,8},{10,11... | collective-permute-start | bytes 3145736 | tf_op jit(solution)/shard_map/ppermute | solution.py:326
  8.8 24.6 %collective-permute-start.7 = (f32[4,128,512]{2,1,0:T(8,128)}, f32[4,128,512]{2,1,0:T(8,128)S(1)}, u32[]{:S(2)}, u32[]{:S(2)}) collective-permute-start(f32[4,128,512]{2,1,0:T(8,128)} %add_momenta.6), channel_id=1, source_target_pairs={{0,1},{1,0},{2,3},{3,2},{4,5},{5,4},{6,7},{7,6},{8,9},{9,8},{10,11... | collective-permute-start | bytes 3145736 | tf_op jit(solution)/shard_map/ppermute | solution.py:326
  16.0 16.8 %copy-start.28 = (f32[2,128,512]{2,1,0:T(8,128)}, f32[2,128,512]{2,1,0:T(8,128)S(1)}, u32[]{:S(2)}) copy-start(f32[2,128,512]{2,1,0:T(8,128)S(1)} %collective-permute-done) | copy-start | bytes 1572868
  16.0 13.2 %collective-permute-start.1 = (f32[2,128,512]{2,1,0:T(8,128)S(1)}, f32[2,128,512]{2,1,0:T(8,128)}, u32[]{:S(2)}, u32[]{:S(2)}) collective-permute-start(f32[2,128,512]{2,1,0:T(8,128)S(1)} %collective-permute-done), channel_id=1, source_target_pairs={{0,16},{16,0},{1,17},{17,1},{2,18},{18,2},{3,19},{19,3},{4,20},{20... | collective-permute-start | bytes 1572872 | tf_op jit(solution)/shard_map/ppermute | solution.py:356
  17.8 20.9 %collective-permute-start.3 = (f32[2,128,512]{2,1,0:T(8,128)S(1)}, f32[2,128,512]{2,1,0:T(8,128)}, u32[]{:S(2)}, u32[]{:S(2)}) collective-permute-start(f32[2,128,512]{2,1,0:T(8,128)S(1)} %collective-permute-done), channel_id=1, source_target_pairs={{0,1},{1,0},{2,3},{3,2},{4,5},{5,4},{6,7},{7,6},{8,9},{9,8},{10,11... | collective-permute-start | bytes 1572872 | tf_op jit(solution)/shard_map/ppermute | solution.py:358
  29.2 10.0 %collective-permute-start.2 = (f32[2,128,512]{2,1,0:T(8,128)}, f32[2,128,512]{2,1,0:T(8,128)}, u32[]{:S(2)}, u32[]{:S(2)}) collective-permute-start(f32[2,128,512]{2,1,0:T(8,128)} %collective-permute-done.1), channel_id=1, source_target_pairs={{0,1},{1,0},{2,3},{3,2},{4,5},{5,4},{6,7},{7,6},{8,9},{9,8},{10,11... | collective-permute-start | bytes 1572872 | tf_op jit(solution)/shard_map/ppermute | solution.py:358
  32.9 53.9 %copy-start.43 = (s32[3]{0:T(128)S(1)}, s32[3]{0:T(128)}, u32[]{:S(2)}) copy-start(s32[3]{0:T(128)} %param.9) | copy-start | bytes 40
  32.9 9.9 %collective-permute-start.14 = (f32[4,128,512]{2,1,0:T(8,128)}, f32[4,128,512]{2,1,0:T(8,128)S(1)}, u32[]{:S(2)}, u32[]{:S(2)}) collective-permute-start(f32[4,128,512]{2,1,0:T(8,128)} %add_momenta.5.refs_8_.refs_0_), channel_id=1, source_target_pairs={{0,1},{1,0},{2,3},{3,2},{4,5},{5,4},{6,7},{7,6},{8,9},{9,8},{10,11... | collective-permute-start | bytes 3145736 | tf_op jit(solution)/shard_map/ppermute | solution.py:347
  37.1 10.2 %collective-permute-start.15 = (f32[4,128,512]{2,1,0:T(8,128)}, f32[4,128,512]{2,1,0:T(8,128)S(1)}, u32[]{:S(2)}, u32[]{:S(2)}) collective-permute-start(f32[4,128,512]{2,1,0:T(8,128)} %add_momenta.7.refs_9_.refs_1_), channel_id=1, source_target_pairs={{0,1},{1,0},{2,3},{3,2},{4,5},{5,4},{6,7},{7,6},{8,9},{9,8},{10,11... | collective-permute-start | bytes 3145736 | tf_op jit(solution)/shard_map/ppermute | solution.py:347
  37.2 26.2 %collective-permute-start.36 = (f32[4,128,512]{2,1,0:T(8,128)S(1)}, f32[4,128,512]{2,1,0:T(8,128)}, u32[]{:S(2)}, u32[]{:S(2)}) collective-permute-start(f32[4,128,512]{2,1,0:T(8,128)S(1)} %copy-done.1), channel_id=1, source_target_pairs={{0,2},{2,0},{1,3},{3,1},{4,6},{6,4},{5,7},{7,5},{8,10},{10,8},{9,1... | collective-permute-start | bytes 3145736 | tf_op jit(solution)/shard_map/ppermute | solution.py:388
  38.7 46.6 %collective-permute-start.37 = (f32[4,128,512]{2,1,0:T(8,128)}, f32[4,128,512]{2,1,0:T(8,128)}, u32[]{:S(2)}, u32[]{:S(2)}) collective-permute-start(f32[4,128,512]{2,1,0:T(8,128)} %add_momenta.7.refs_9_.refs_1_), channel_id=1, source_target_pairs={{0,2},{2,0},{1,3},{3,1},{4,6},{6,4},{5,7},{7,5},{8,10},{10,8},{9,1... | collective-permute-start | bytes 3145736 | tf_op jit(solution)/shard_map/ppermute | solution.py:388
  39.3 46.0 %collective-permute-start.5 = (f32[4,128,512]{2,1,0:T(8,128)S(1)}, f32[4,128,512]{2,1,0:T(8,128)S(1)}, u32[]{:S(2)}, u32[]{:S(2)}) collective-permute-start(f32[4,128,512]{2,1,0:T(8,128)S(1)} %copy-done.1), channel_id=1, source_target_pairs={{0,4},{4,8},{8,12},{1,5},{5,9},{9,13},{2,6},{6,10},{10,14},{3,7},{... | collective-permute-start | bytes 3145736 | tf_op jit(solution)/shard_map/ppermute | solution.py:337
  42.8 63.2 %collective-permute-start.8 = (f32[4,128,512]{2,1,0:T(8,128)}, f32[4,128,512]{2,1,0:T(8,128)}, u32[]{:S(2)}, u32[]{:S(2)}) collective-permute-start(f32[4,128,512]{2,1,0:T(8,128)} %add_momenta.7.refs_9_.refs_1_), channel_id=1, source_target_pairs={{0,4},{4,8},{8,12},{1,5},{5,9},{9,13},{2,6},{6,10},{10,14},{3,7},{... | collective-permute-start | bytes 3145736 | tf_op jit(solution)/shard_map/ppermute | solution.py:337
  47.3 50.5 %copy-start.7 = (f32[4,128,512]{2,1,0:T(8,128)}, f32[4,128,512]{2,1,0:T(8,128)S(1)}, u32[]{:S(2)}) copy-start(f32[4,128,512]{2,1,0:T(8,128)S(1)} %collective-permute-done.15.refs_11_.refs_5_) | copy-start | bytes 3145732
  47.3 60.4 %collective-permute-start.16 = (f32[4,128,512]{2,1,0:T(8,128)S(1)}, f32[4,128,512]{2,1,0:T(8,128)}, u32[]{:S(2)}, u32[]{:S(2)}) collective-permute-start(f32[4,128,512]{2,1,0:T(8,128)S(1)} %copy-done.1), channel_id=1, source_target_pairs={{12,8},{8,4},{4,0},{13,9},{9,5},{5,1},{14,10},{10,6},{6,2},{15,11}... | collective-permute-start | bytes 3145736 | tf_op jit(solution)/shard_map/ppermute | solution.py:338
  63.4 44.3 %collective-permute-start.17 = (f32[4,128,512]{2,1,0:T(8,128)}, f32[4,128,512]{2,1,0:T(8,128)}, u32[]{:S(2)}, u32[]{:S(2)}) collective-permute-start(f32[4,128,512]{2,1,0:T(8,128)} %add_momenta.7.refs_9_.refs_1_), channel_id=1, source_target_pairs={{12,8},{8,4},{4,0},{13,9},{9,5},{5,1},{14,10},{10,6},{6,2},{15,11}... | collective-permute-start | bytes 3145736 | tf_op jit(solution)/shard_map/ppermute | solution.py:338
  85.3 24.0 %collective-permute-start.38 = (f32[4,128,512]{2,1,0:T(8,128)}, f32[4,128,512]{2,1,0:T(8,128)}, u32[]{:S(2)}, u32[]{:S(2)}) collective-permute-start(f32[4,128,512]{2,1,0:T(8,128)} %collective-permute-done.36.refs_2_), channel_id=1, source_target_pairs={{0,1},{1,0},{2,3},{3,2},{4,5},{5,4},{6,7},{7,6},{8,9},{9,8},{10,11... | collective-permute-start | bytes 3145736 | tf_op jit(solution)/shard_map/ppermute | solution.py:391
  86.3 24.3 %collective-permute-start.39 = (f32[4,128,512]{2,1,0:T(8,128)}, f32[4,128,512]{2,1,0:T(8,128)}, u32[]{:S(2)}, u32[]{:S(2)}) collective-permute-start(f32[4,128,512]{2,1,0:T(8,128)} %collective-permute-done.37.refs_3_), channel_id=1, source_target_pairs={{0,1},{1,0},{2,3},{3,2},{4,5},{5,4},{6,7},{7,6},{8,9},{9,8},{10,11... | collective-permute-start | bytes 3145736 | tf_op jit(solution)/shard_map/ppermute | solution.py:391
  100.6 11.4 %copy-start.2 = (f32[4,128,512]{2,1,0:T(8,128)S(1)}, f32[4,128,512]{2,1,0:T(8,128)}, u32[]{:S(2)}) copy-start(f32[4,128,512]{2,1,0:T(8,128)} %add_momenta.7.refs_9_.refs_1_) | copy-start | bytes 3145732
  100.6 11.4 %copy-start.24 = (s32[3]{0:T(128)S(1)}, s32[3]{0:T(128)}, u32[]{:S(2)}) copy-start(s32[3]{0:T(128)} %steps.9) | copy-start | bytes 40
  100.6 11.4 %copy-start.25 = (f32[3]{0:T(128)S(1)}, f32[3]{0:T(128)}, u32[]{:S(2)}) copy-start(f32[3]{0:T(128)} %occupation.9) | copy-start | bytes 40
  106.0 32.5 %collective-permute-start.6 = (f32[4,128,512]{2,1,0:T(8,128)}, f32[4,128,512]{2,1,0:T(8,128)}, u32[]{:S(2)}, u32[]{:S(2)}) collective-permute-start(f32[4,128,512]{2,1,0:T(8,128)} %copy-done.10), channel_id=1, source_target_pairs={{4,8},{8,12},{5,9},{9,13},{6,10},{10,14},{7,11},{11,15},{20,24},{2... | collective-permute-start | bytes 3145736 | tf_op jit(solution)/shard_map/ppermute | solution.py:337
  107.7 56.2 %collective-permute-start.12 = (f32[4,128,512]{2,1,0:T(8,128)}, f32[4,128,512]{2,1,0:T(8,128)S(1)}, u32[]{:S(2)}, u32[]{:S(2)}) collective-permute-start(f32[4,128,512]{2,1,0:T(8,128)} %copy-done.10), channel_id=1, source_target_pairs={{0,1},{1,0},{2,3},{3,2},{4,5},{5,4},{6,7},{7,6},{8,9},{9,8},{10,11... | collective-permute-start | bytes 3145736 | tf_op jit(solution)/shard_map/ppermute | solution.py:347
  107.7 31.4 %collective-permute-start.9 = (f32[4,128,512]{2,1,0:T(8,128)}, f32[4,128,512]{2,1,0:T(8,128)}, u32[]{:S(2)}, u32[]{:S(2)}) collective-permute-start(f32[4,128,512]{2,1,0:T(8,128)} %collective-permute-done.8.refs_5_), channel_id=1, source_target_pairs={{4,8},{8,12},{5,9},{9,13},{6,10},{10,14},{7,11},{11,15},{20,24},{2... | collective-permute-start | bytes 3145736 | tf_op jit(solution)/shard_map/ppermute | solution.py:337
  109.3 32.5 %collective-permute-start.20 = (f32[4,128,512]{2,1,0:T(8,128)}, f32[4,128,512]{2,1,0:T(8,128)}, u32[]{:S(2)}, u32[]{:S(2)}) collective-permute-start(f32[4,128,512]{2,1,0:T(8,128)} %collective-permute-done.16.refs_12_), channel_id=1, source_target_pairs={{8,4},{4,0},{9,5},{5,1},{10,6},{6,2},{11,7},{7,3},{24,20},{20,16},... | collective-permute-start | bytes 3145736 | tf_op jit(solution)/shard_map/ppermute | solution.py:338
  110.6 53.2 %collective-permute-start.21 = (f32[4,128,512]{2,1,0:T(8,128)}, f32[4,128,512]{2,1,0:T(8,128)}, u32[]{:S(2)}, u32[]{:S(2)}) collective-permute-start(f32[4,128,512]{2,1,0:T(8,128)} %collective-permute-done.17.refs_13_), channel_id=1, source_target_pairs={{8,4},{4,0},{9,5},{5,1},{10,6},{6,2},{11,7},{7,3},{24,20},{20,16},... | collective-permute-start | bytes 3145736 | tf_op jit(solution)/shard_map/ppermute | solution.py:338
  138.5 27.0 %collective-permute-start.13 = (f32[4,128,512]{2,1,0:T(8,128)}, f32[4,128,512]{2,1,0:T(8,128)S(1)}, u32[]{:S(2)}, u32[]{:S(2)}) collective-permute-start(f32[4,128,512]{2,1,0:T(8,128)} %collective-permute-done.8.refs_5_), channel_id=1, source_target_pairs={{0,1},{1,0},{2,3},{3,2},{4,5},{5,4},{6,7},{7,6},{8,9},{9,8},{10,11... | collective-permute-start | bytes 3145736 | tf_op jit(solution)/shard_map/ppermute | solution.py:347
  139.0 28.1 %collective-permute-start.18 = (f32[4,128,512]{2,1,0:T(8,128)}, f32[4,128,512]{2,1,0:T(8,128)S(1)}, u32[]{:S(2)}, u32[]{:S(2)}) collective-permute-start(f32[4,128,512]{2,1,0:T(8,128)} %collective-permute-done.16.refs_12_), channel_id=1, source_target_pairs={{0,1},{1,0},{2,3},{3,2},{4,5},{5,4},{6,7},{7,6},{8,9},{9,8},{10,11... | collective-permute-start | bytes 3145736 | tf_op jit(solution)/shard_map/ppermute | solution.py:347
  141.8 27.7 %collective-permute-start.40 = (f32[4,128,512]{2,0,1:T(4,128)S(1)}, f32[4,128,512]{2,0,1:T(4,128)S(1)}, u32[]{:S(2)}, u32[]{:S(2)}) collective-permute-start(f32[4,128,512]{2,0,1:T(4,128)S(1)} %copy.6), channel_id=1, source_target_pairs={{0,1},{1,0},{2,3},{3,2},{4,5},{5,4},{6,7},{7,6},{8,9},{9,8},{10,11... | collective-permute-start | bytes 3145736 | tf_op jit(solution)/shard_map/ppermute | solution.py:396
  163.8 10.5 %collective-permute-start.19 = (f32[4,128,512]{2,1,0:T(8,128)}, f32[4,128,512]{2,1,0:T(8,128)S(1)}, u32[]{:S(2)}, u32[]{:S(2)}) collective-permute-start(f32[4,128,512]{2,1,0:T(8,128)} %collective-permute-done.17.refs_13_), channel_id=1, source_target_pairs={{0,1},{1,0},{2,3},{3,2},{4,5},{5,4},{6,7},{7,6},{8,9},{9,8},{10,11... | collective-permute-start | bytes 3145736 | tf_op jit(solution)/shard_map/ppermute | solution.py:347
  163.8 17.7 %collective-permute-start.10 = (f32[4,128,512]{2,1,0:T(8,128)}, f32[4,128,512]{2,1,0:T(8,128)}, u32[]{:S(2)}, u32[]{:S(2)}) collective-permute-start(f32[4,128,512]{2,1,0:T(8,128)} %collective-permute-done.6.refs_0_), channel_id=1, source_target_pairs={{8,9},{9,8},{12,13},{13,12},{10,11},{11,10},{14,15},{15,14},{24,25... | collective-permute-start | bytes 3145736 | tf_op jit(solution)/shard_map/ppermute | solution.py:347
  165.5 16.0 %collective-permute-start.11 = (f32[4,128,512]{2,1,0:T(8,128)}, f32[4,128,512]{2,1,0:T(8,128)}, u32[]{:S(2)}, u32[]{:S(2)}) collective-permute-start(f32[4,128,512]{2,1,0:T(8,128)} %collective-permute-done.9.refs_1_), channel_id=1, source_target_pairs={{8,9},{9,8},{12,13},{13,12},{10,11},{11,10},{14,15},{15,14},{24,25... | collective-permute-start | bytes 3145736 | tf_op jit(solution)/shard_map/ppermute | solution.py:347
  167.1 14.4 %collective-permute-start.22 = (f32[4,128,512]{2,1,0:T(8,128)}, f32[4,128,512]{2,1,0:T(8,128)}, u32[]{:S(2)}, u32[]{:S(2)}) collective-permute-start(f32[4,128,512]{2,1,0:T(8,128)} %collective-permute-done.20.refs_16_), channel_id=1, source_target_pairs={{0,1},{1,0},{4,5},{5,4},{2,3},{3,2},{6,7},{7,6},{16,17},{17,16},{2... | collective-permute-start | bytes 3145736 | tf_op jit(solution)/shard_map/ppermute | solution.py:347
  169.5 12.0 %collective-permute-start.23 = (f32[4,128,512]{2,1,0:T(8,128)}, f32[4,128,512]{2,1,0:T(8,128)}, u32[]{:S(2)}, u32[]{:S(2)}) collective-permute-start(f32[4,128,512]{2,1,0:T(8,128)} %collective-permute-done.21.refs_17_), channel_id=1, source_target_pairs={{0,1},{1,0},{4,5},{5,4},{2,3},{3,2},{6,7},{7,6},{16,17},{17,16},{2... | collective-permute-start | bytes 3145736 | tf_op jit(solution)/shard_map/ppermute | solution.py:347
  175.4 71.2 %collective-permute-start.41 = (f32[128,8,512]{2,1,0:T(8,128)}, f32[128,8,512]{2,1,0:T(8,128)}, u32[]{:S(2)}, u32[]{:S(2)}) collective-permute-start(f32[128,8,512]{2,1,0:T(8,128)} %maximum_bitcast_fusion), channel_id=1, source_target_pairs={{0,12},{12,0},{1,13},{13,1},{2,14},{14,2},{3,15},{15,3},{16,28},{2... | collective-permute-start | bytes 6291464 | tf_op jit(solution)/shard_map/ppermute | solution.py:400
  199.0 9.5 %collective-permute-start.28 = (f32[1,128,512]{2,1,0:T(8,128)S(1)}, f32[1,128,512]{2,1,0:T(8,128)S(1)}, u32[]{:S(2)}, u32[]{:S(2)}) collective-permute-start(f32[1,128,512]{2,1,0:T(8,128)S(1)} %get-tuple-element.36), channel_id=1, source_target_pairs={{0,2},{1,3},{2,0},{3,1},{4,6},{5,7},{6,4},{7,5},{8,10},{9,11},{10,... | collective-permute-start | bytes 786440 | tf_op jit(solution)/shard_map/ppermute | solution.py:418
  200.5 8.0 %collective-permute-start.31 = (f32[1,128,512]{2,1,0:T(8,128)S(1)}, f32[1,128,512]{2,1,0:T(8,128)S(1)}, u32[]{:S(2)}, u32[]{:S(2)}) collective-permute-start(f32[1,128,512]{2,1,0:T(8,128)S(1)} %get-tuple-element.39), channel_id=1, source_target_pairs={{0,1},{1,0},{2,3},{3,2},{4,5},{5,4},{6,7},{7,6},{8,9},{9,8},{10,11... | collective-permute-start | bytes 786440 | tf_op jit(solution)/shard_map/ppermute | solution.py:418
  200.8 14.9 %collective-permute-start.35 = (f32[1,128,512]{2,1,0:T(8,128)S(1)}, f32[1,128,512]{2,1,0:T(8,128)S(1)}, u32[]{:S(2)}, u32[]{:S(2)}) collective-permute-start(f32[1,128,512]{2,1,0:T(8,128)S(1)} %get-tuple-element.43), channel_id=1, source_target_pairs={{0,3},{1,2},{2,1},{3,0},{4,7},{5,6},{6,5},{7,4},{8,11},{9,10},{10,... | collective-permute-start | bytes 786440 | tf_op jit(solution)/shard_map/ppermute | solution.py:418
  207.0 12.5 %collective-permute-start.27 = (f32[1,128,512]{2,1,0:T(8,128)S(1)}, f32[1,128,512]{2,1,0:T(8,128)S(1)}, u32[]{:S(2)}, u32[]{:S(2)}) collective-permute-start(f32[1,128,512]{2,1,0:T(8,128)S(1)} %get-tuple-element.35), channel_id=1, source_target_pairs={{0,2},{1,3},{2,0},{3,1},{4,6},{5,7},{6,4},{7,5},{8,10},{9,11},{10,... | collective-permute-start | bytes 786440 | tf_op jit(solution)/shard_map/ppermute | solution.py:418
  208.5 17.1 %collective-permute-start.30 = (f32[1,128,512]{2,1,0:T(8,128)S(1)}, f32[1,128,512]{2,1,0:T(8,128)S(1)}, u32[]{:S(2)}, u32[]{:S(2)}) collective-permute-start(f32[1,128,512]{2,1,0:T(8,128)S(1)} %get-tuple-element.38), channel_id=1, source_target_pairs={{0,1},{1,0},{2,3},{3,2},{4,5},{5,4},{6,7},{7,6},{8,9},{9,8},{10,11... | collective-permute-start | bytes 786440 | tf_op jit(solution)/shard_map/ppermute | solution.py:418
  209.2 18.0 %collective-permute-start.34 = (f32[1,128,512]{2,1,0:T(8,128)S(1)}, f32[1,128,512]{2,1,0:T(8,128)S(1)}, u32[]{:S(2)}, u32[]{:S(2)}) collective-permute-start(f32[1,128,512]{2,1,0:T(8,128)S(1)} %get-tuple-element.42), channel_id=1, source_target_pairs={{0,3},{1,2},{2,1},{3,0},{4,7},{5,6},{6,5},{7,4},{8,11},{9,10},{10,... | collective-permute-start | bytes 786440 | tf_op jit(solution)/shard_map/ppermute | solution.py:418
  215.7 15.0 %collective-permute-start.26 = (f32[1,128,512]{2,1,0:T(8,128)S(1)}, f32[1,128,512]{2,1,0:T(8,128)S(1)}, u32[]{:S(2)}, u32[]{:S(2)}) collective-permute-start(f32[1,128,512]{2,1,0:T(8,128)S(1)} %get-tuple-element.34), channel_id=1, source_target_pairs={{0,2},{1,3},{2,0},{3,1},{4,6},{5,7},{6,4},{7,5},{8,10},{9,11},{10,... | collective-permute-start | bytes 786440 | tf_op jit(solution)/shard_map/ppermute | solution.py:418
  219.5 12.7 %collective-permute-start.29 = (f32[1,128,512]{2,1,0:T(8,128)S(1)}, f32[1,128,512]{2,1,0:T(8,128)S(1)}, u32[]{:S(2)}, u32[]{:S(2)}) collective-permute-start(f32[1,128,512]{2,1,0:T(8,128)S(1)} %get-tuple-element.37), channel_id=1, source_target_pairs={{0,1},{1,0},{2,3},{3,2},{4,5},{5,4},{6,7},{7,6},{8,9},{9,8},{10,11... | collective-permute-start | bytes 786440 | tf_op jit(solution)/shard_map/ppermute | solution.py:418
  225.6 9.8 %collective-permute-start.33 = (f32[1,128,512]{2,1,0:T(8,128)S(1)}, f32[1,128,512]{2,1,0:T(8,128)S(1)}, u32[]{:S(2)}, u32[]{:S(2)}) collective-permute-start(f32[1,128,512]{2,1,0:T(8,128)S(1)} %get-tuple-element.41), channel_id=1, source_target_pairs={{0,3},{1,2},{2,1},{3,0},{4,7},{5,6},{6,5},{7,4},{8,11},{9,10},{10,... | collective-permute-start | bytes 786440 | tf_op jit(solution)/shard_map/ppermute | solution.py:418
  227.2 8.2 %collective-permute-start.32 = (f32[1,128,512]{2,1,0:T(8,128)S(1)}, f32[1,128,512]{2,1,0:T(8,128)S(1)}, u32[]{:S(2)}, u32[]{:S(2)}) collective-permute-start(f32[1,128,512]{2,1,0:T(8,128)S(1)} %get-tuple-element.40), channel_id=1, source_target_pairs={{0,1},{1,0},{2,3},{3,2},{4,5},{5,4},{6,7},{7,6},{8,9},{9,8},{10,11... | collective-permute-start | bytes 786440 | tf_op jit(solution)/shard_map/ppermute | solution.py:418
  230.7 11.2 %collective-permute-start.24 = (f32[1,128,512]{2,1,0:T(8,128)}, f32[1,128,512]{2,1,0:T(8,128)S(1)}, u32[]{:S(2)}, u32[]{:S(2)}) collective-permute-start(f32[1,128,512]{2,1,0:T(8,128)} %get-tuple-element.28), channel_id=1, source_target_pairs={{0,2},{1,3},{2,0},{3,1},{4,6},{5,7},{6,4},{7,5},{8,10},{9,11},{10,... | collective-permute-start | bytes 786440 | tf_op jit(solution)/shard_map/ppermute | solution.py:418
  232.2 14.4 %collective-permute-start.25 = (f32[1,128,512]{2,1,0:T(8,128)S(1)}, f32[1,128,512]{2,1,0:T(8,128)S(1)}, u32[]{:S(2)}, u32[]{:S(2)}) collective-permute-start(f32[1,128,512]{2,1,0:T(8,128)S(1)} %get-tuple-element.29), channel_id=1, source_target_pairs={{0,3},{1,2},{2,1},{3,0},{4,7},{5,6},{6,5},{7,4},{8,11},{9,10},{10,... | collective-permute-start | bytes 786440 | tf_op jit(solution)/shard_map/ppermute | solution.py:418
  (38 other events, 107.0 us)

commit v5 on v4

--- a/solution.py
+++ b/solution.py
@@ -22,46 +22,56 @@
     return high, (x - high.astype(jnp.float32)).astype(jnp.bfloat16)
 
 
-def side_by_side(out, x):
+def side_by_side(out, mode, x):
     high, low = halves(x)
     depth = x.shape[1]
-    out[0, :, pl.ds(0, depth)] = high
-    out[0, :, pl.ds(depth, depth)] = high
-    out[0, :, pl.ds(2 * depth, depth)] = low
-
-
-def prepare_far(coupling, right_high, right_low, left):
-    right_high[0], right_low[0] = halves(coupling[0].T)
-    rows = left.shape[1]
-    first = pl.multiple_of(lax.axis_index("atom") * rows, 8)
-    side_by_side(left, coupling[0, pl.ds(first, rows), :])
-
-
-def prepare_near(coupling, left):
-    depth = left.shape[2] // 3
-    first = pl.multiple_of(lax.axis_index("atom") * depth, 128)
-    side_by_side(left, coupling[0, :, pl.ds(first, depth)])
-
-
-def prepared(kernel, coupling, shapes):
-    order = coupling.shape[-1]
-    return pl.pallas_call(
-        kernel,
-        grid=(MODES,),
-        out_shape=[jax.ShapeDtypeStruct((MODES,) + shape, jnp.bfloat16) for shape in shapes],
-        in_specs=[pl.BlockSpec((1, order, order), lambda m: (m, 0, 0))],
-        out_specs=[pl.BlockSpec((1,) + shape, lambda m: (m, 0, 0)) for shape in shapes],
-        cost_estimate=pl.CostEstimate(
-            flops=8 * coupling.size,
-            bytes_accessed=4 * coupling.size + 2 * MODES * sum(a * b for a, b in shapes),
-            transcendentals=0,
-        ),
-    )(coupling)
+    out[mode, :, pl.ds(0, depth)] = high
+    out[mode, :, pl.ds(depth, depth)] = high
+    out[mode, :, pl.ds(2 * depth, depth)] = low
+
+
+def prepare(atoms, parts, cores, owners, couplings, *refs):
+    right_high, right_low, far, near, held, sems = refs[-6:]
+    pieces = refs[:-6]
+    atom, core, part = (lax.axis_index(a) for a in ("atom", "kz", "grp"))
+    table_rows = couplings.shape[0]
+    for mode in range(MODES):
+        row = lax.rem(owners[mode], table_rows)
+        behind = lax.rem(atom - lax.div(owners[mode], table_rows) + atoms, atoms)
+
+        @pl.when(behind == 0)
+        def _(mode=mode, row=row):
+            pltpu.make_async_copy(couplings.at[row], held.at[mode], sems.at[mode]).start()
+
+        for s in range(1, atoms):
+
+            @pl.when(behind == s)
+            def _(mode=mode, row=row, s=s):
+                for d in range(parts):
+                    for o in range(cores):
+                        piece = pieces[((s - 1) * parts + d) * cores + o]
+                        strip = piece.shape[1]
+                        at = lax.rem(part - d + parts, parts) * cores + lax.rem(core - o + cores, cores)
+                        rows = pl.ds(pl.multiple_of(at * strip, 8), strip)
+                        pltpu.make_async_copy(piece.at[row], held.at[mode, rows], sems.at[mode]).start()
+
+    @pl.loop(0, MODES)
+    def _(mode):
+        pltpu.make_async_copy(held.at[mode], held.at[mode], sems.at[mode]).wait()
+        right_high[mode], right_low[mode] = halves(held[mode].T)
+        rows, depth = far.shape[1], near.shape[2] // 3
+        side_by_side(far, mode, held[mode, pl.ds(pl.multiple_of(atom * rows, 8), rows), :])
+        side_by_side(near, mode, held[mode, :, pl.ds(pl.multiple_of(atom * depth, 128), depth)])
+
+
+def guard(steps, out):
+    for mode in range(MODES):
+        out[mode] = steps[mode]
 
 
 def add_momenta(theirs, first, green, *refs):
-    out, held, total, arrived, left = refs[-6:-1]
-    given = refs[:-6]
+    out, held, total, arrived, left = refs[-5:]
+    given = refs[:-5]
     momenta, count, size = green.shape[0], held.shape[0], held.shape[2]
     core = lax.axis_index("kz")
     base = (1 - core if theirs else core) * count
@@ -70,13 +80,16 @@
             pltpu.make_async_copy(green.at[k, base + e, pl.ds(first, size)], held.at[e, k], arrived.at[e]).start()
         for ref in given:
             pltpu.make_async_copy(ref.at[e], held.at[e, momenta], arrived.at[e]).start()
-    for e in range(count):
+
+    @pl.loop(0, count)
+    def _(e):
         pltpu.make_async_copy(held.at[e], held.at[e], arrived.at[e]).wait()
         value = held[e, 0]
         for k in range(1, held.shape[1]):
             value = value + held[e, k]
         total[e] = value
         pltpu.make_async_copy(total.at[e], out.at[e], left.at[e]).start()
+
     for e in range(count):
         pltpu.make_async_copy(total.at[e], out.at[e], left.at[e]).wait()
 
@@ -151,32 +164,37 @@
                 fetch(energy + 1, 1 - buffer)
 
         dot = functools.partial(jnp.dot, preferred_element_type=jnp.float32)
-        for mode in range(MODES):
+
+        @pl.loop(0, MODES)
+        def _(mode):
             scales = []
             for side in range(2):
-                slot = mode * 2 + side
-                held = planes.at[buffer, slot]
-                pltpu.make_async_copy(held, held, sems.at[buffer, slot]).wait()
-                scales.append(jnp.where(source_of(energy, mode, side)[0], (occupation[mode] + (1.0 - side)) * (1.0 / momenta), 0.0))
+                held = planes.at[buffer, mode * 2 + side]
+                pltpu.make_async_copy(held, held, sems.at[buffer, mode * 2 + side]).wait()
+                scale = (occupation[mode] + (1.0 - side)) * (1.0 / momenta)
+                scales.append(jnp.where(source_of(energy, mode, side)[0], scale, 0.0))
             combined = scales[0] * planes[buffer, 2 * mode] + scales[1] * planes[buffer, 2 * mode + 1]
-            high = combined.astype(jnp.bfloat16)
-            low = (combined - high.astype(jnp.float32)).astype(jnp.bfloat16)
+            high, low = halves(combined)
             product = dot(high, right_high[mode]) + dot(low, right_high[mode]) + dot(high, right_low[mode])
-            high = product.astype(jnp.bfloat16)
-            low = (product - high.astype(jnp.float32)).astype(jnp.bfloat16)
-            inner[mode, pl.ds(0, rows)] = high
-            inner[mode, pl.ds(rows, rows)] = low
-            inner[mode, pl.ds(2 * rows, rows)] = high
-        for index, out in enumerate(outs):
-            s, t = index // 2, index % 2
-            block = lax.rem(core + t, 2)
-            if not far:
-                block = block + 2 * lax.rem(atom + s, n_atoms)
-            where = pl.ds(pl.multiple_of(block * size, 8), size)
-            total = dot(left[0, where], inner[0])
-            for mode in range(1, MODES):
-                total = total + dot(left[mode, where], inner[mode])
-            out[energy] = total
+            high, low = halves(product)
+            inner[pl.ds(0, rows)] = high
+            inner[pl.ds(rows, rows)] = low
+            inner[pl.ds(2 * rows, rows)] = high
+            for index, out in enumerate(outs):
+                s, t = index // 2, index % 2
+                block = lax.rem(core + t, 2)
+                if not far:
+                    block = block + 2 * lax.rem(atom + s, n_atoms)
+                where = pl.ds(pl.multiple_of(block * size, 8), size)
+                total = dot(left[mode, where], inner[...])
+
+                @pl.when(mode == 0)
+                def _(out=out, total=total):
+                    out[energy] = total
+
+                @pl.when(mode > 0)
+                def _(out=out, total=total):
+                    out[energy] += total
 
 
 def sandwich(steps, occupation, right, left, groups, n_atoms, momenta, base, grid_total, edev, far, line, out_rows, count):
@@ -197,7 +215,7 @@
         out_specs=[pl.BlockSpec(memory_space=pltpu.VMEM)] * n_out,
         scratch_shapes=[
             pltpu.VMEM((buffers, 2 * MODES, rows, order), jnp.float32),
-            pltpu.VMEM((MODES, 3 * rows, order), jnp.bfloat16),
+            pltpu.VMEM((3 * rows, order), jnp.bfloat16),
             pltpu.SemaphoreType.DMA((2, 2 * MODES)),
         ],
         compiler_params=pltpu.CompilerParams(vmem_limit_bytes=held),
@@ -213,26 +231,32 @@
 def gather_early(layout, count, *refs):
     out = refs[-1]
     core = lax.axis_index("kz")
+    group = 16
     for own in range(2):
 
         @pl.when(core == own)
         def _(own=own):
-            for half, energies in enumerate(layout):
-                where = (own if half == 0 else 1 - own) * count
-                for j, terms in enumerate(energies):
-                    total = None
-                    for ref, row in terms:
-                        total = refs[ref][row] if total is None else total + refs[ref][row]
-                    out[:, where + j, :] = total
+            @pl.loop(0, out.shape[0] // group)
+            def _(at):
+                rows = pl.ds(pl.multiple_of(at * group, group), group)
+                for half, energies in enumerate(layout):
+                    where = (own if half == 0 else 1 - own) * count
+                    for j, terms in enumerate(energies):
+                        total = None
+                        for ref, row in terms:
+                            total = refs[ref][row, rows] if total is None else total + refs[ref][row, rows]
+                        out[rows, where + j, :] = total
 
 
 def gather_late(layout, count, whole, *refs):
-    out, total, sems = refs[-3:]
+    out, total, sem = refs[-3:]
     full = refs[-3 - whole : -3]
     core = lax.axis_index("kz")
-    step = total.shape[0] // sems.shape[0]
-    for part in range(sems.shape[0]):
-        rows = pl.ds(part * step, step)
+    group = 16
+
+    @pl.loop(0, total.shape[0] // group)
+    def _(at):
+        rows = pl.ds(pl.multiple_of(at * group, group), group)
         value = full[0][rows]
         for ref in full[1:]:
             value = value + ref[rows]
@@ -240,7 +264,7 @@
         for own in range(2):
 
             @pl.when(core == own)
-            def _(own=own, rows=rows):
+            def _(own=own):
                 for half, energies in enumerate(layout):
                     where = (own if half == 0 else 1 - own) * count
                     for j, terms in enumerate(energies):
@@ -250,10 +274,9 @@
                                 value = value + refs[ref][row, rows]
                             total[rows, where + j, :] = value
 
-        pltpu.make_async_copy(total.at[rows], out.at[rows], sems.at[part]).start()
-    for part in range(sems.shape[0]):
-        rows = pl.ds(part * step, step)
-        pltpu.make_async_copy(total.at[rows], out.at[rows], sems.at[part]).wait()
+        pltpu.make_async_copy(total.at[rows], out.at[rows], sem).start()
+
+    pltpu.make_async_copy(total, out, sem).wait()
 
 
 def gathered(layout, count, arrays, before=()):
@@ -264,9 +287,8 @@
     size = 4 * sum(x.size for x in arrays) + 4 * 2 * count * out_rows * order
     vmem = pl.BlockSpec(memory_space=pltpu.VMEM)
     if before:
-        parts = 4 if out_rows % 32 == 0 else 1
         kernel = functools.partial(gather_late, terms, count, len(before))
-        scratch = [pltpu.VMEM(shape, jnp.float32), pltpu.SemaphoreType.DMA((parts,))]
+        scratch = [pltpu.VMEM(shape, jnp.float32), pltpu.SemaphoreType.DMA]
     else:
         kernel, scratch = functools.partial(gather_early, terms, count), []
     return pl.pallas_call(
@@ -290,7 +312,7 @@
     momenta = momenta_here * cores
     grid_total = n * edev
     parts = lax.axis_size("grp")
-    atom, core, part = (lax.axis_index(a) for a in ("atom", "kz", "grp"))
+    _, core, part = (lax.axis_index(a) for a in ("atom", "kz", "grp"))
     line = n == 2 * REACH
     half = edev // cores
     swap = [(i, (i + 1) % cores) for i in range(cores)]
@@ -309,9 +331,8 @@
                 pltpu.VMEM((half, size, order), jnp.float32),
                 pltpu.SemaphoreType.DMA((half,)),
                 pltpu.SemaphoreType.DMA((half,)),
-                pltpu.VMEM((48 << 10, 256), jnp.float32),
             ],
-            compiler_params=pltpu.CompilerParams(vmem_limit_bytes=60 << 20),
+            compiler_params=pltpu.CompilerParams(vmem_limit_bytes=67_000_000),
             cost_estimate=pl.CostEstimate(
                 flops=momenta_here * half * size * order,
                 bytes_accessed=4 * (momenta_here + 1 + len(more)) * half * size * order,
@@ -356,32 +377,22 @@
             lax.ppermute(got, "grp", [(i, (i + d) % parts) for i in range(parts)]) for d in range(1, parts)
         ]
         others.append([(x, lax.ppermute(x, "kz", swap)) for x in ahead])
-    rows_of = lax.rem(owners, jnp.int32(table_rows))
-    behind_of = lax.rem(atom - lax.div(owners, jnp.int32(table_rows)) + atoms, jnp.int32(atoms))
-
-    def pick(m):
-        row, behind = rows_of[m], behind_of[m]
-
-        def at(table):
-            return lax.dynamic_slice(table, (row, 0, 0), (1,) + table.shape[1:])[0]
-
-        value = at(couplings)
-        for s, pieces in enumerate(others, 1):
-            strips = []
-            for g in range(parts):
-                for k in range(cores):
-                    chosen = None
-                    for d, (same, other) in enumerate(pieces):
-                        piece = jnp.where(core == k, at(same), at(other))
-                        chosen = piece if d == 0 else jnp.where((g + d) % parts == part, piece, chosen)
-                    strips.append(chosen)
-            value = jnp.where(behind == s, jnp.concatenate(strips, 0), value)
-        return value
-
-    coupling = jnp.stack([pick(m) for m in range(MODES)], 0)
     out_rows = order // (atoms * cores)
-    *right, left_far = prepared(prepare_far, coupling, [(order, order), (order, order), (cores * out_rows, 3 * order)])
-    (left_near,) = prepared(prepare_near, coupling, [(order, 3 * brows)])
+    flat = [x for pieces in others for both in pieces for x in both]
+    hbm, vmem = pl.BlockSpec(memory_space=pltpu.HBM), pl.BlockSpec(memory_space=pltpu.VMEM)
+    shapes = [(order, order), (order, order), (cores * out_rows, 3 * order), (order, 3 * brows)]
+    *right, left_far, left_near = pl.pallas_call(
+        functools.partial(prepare, atoms, parts, cores),
+        out_shape=[jax.ShapeDtypeStruct((MODES,) + shape, jnp.bfloat16) for shape in shapes],
+        in_specs=[pl.BlockSpec(memory_space=pltpu.SMEM)] + [hbm] * (1 + len(flat)),
+        out_specs=[vmem] * len(shapes),
+        scratch_shapes=[pltpu.VMEM((MODES, order, order), jnp.float32), pltpu.SemaphoreType.DMA((MODES,))],
+        compiler_params=pltpu.CompilerParams(vmem_limit_bytes=32 << 20),
+        cost_estimate=pl.CostEstimate(
+            flops=8 * MODES * order * order, bytes_accessed=10 * MODES * order * order, transcendentals=0
+        ),
+        name="prepare",
+    )(owners, couplings, *flat)
 
     beyond = []
     if line:
@@ -390,8 +401,16 @@
             list(own) + got,
             groups[REACH][1] + [lax.ppermute(x, "kz", swap) for x in got],
         )
+        smem = pl.BlockSpec(memory_space=pltpu.SMEM)
+        held = pl.pallas_call(
+            guard,
+            out_shape=jax.ShapeDtypeStruct(offsets.shape, offsets.dtype),
+            in_specs=[smem],
+            out_specs=smem,
+            name="guard",
+        )(offsets)
         sums = sandwich(
-            offsets, occupation, right, left_far, [whole], atoms, momenta, 0, grid_total, edev, True, line, out_rows, half
+            held, occupation, right, left_far, [whole], atoms, momenta, 0, grid_total, edev, True, line, out_rows, half
         )
         swapped = lax.ppermute(sums[1], "kz", swap)
         both = jnp.concatenate(

time: 253 us -> 226 us (0.89)
  local copies, waits for them, and re-layouts: 29 us -> 12.1 us
  Pallas kernels: 67.9 us -> 76.5 us
  between operations: 8.53 us -> 0.76 us
  waiting for transfers between devices: 94.4 us -> 89.9 us
  other arithmetic: 7.8 us -> 4.26 us
    unnamed x88 -> x64, local copies, waits for them, and re-layouts: 26.5 us -> 8.58 us
    pallas_call x5, Pallas kernels: 40.6 us -> 54.4 us  [sandwich(): pl.pallas_call(functools.partial(split_dot, len(groups), len(groups[0][0]...]
    pallas_call x2, Pallas kernels: 9.6 us -> 4.45 us  [the longest x1 3.27 us: shards(): pl.pallas_call(functools.partial(prepare, atoms, parts, cores), out_shape...]
    ppermute x12, waiting for transfers between devices: 16 us -> 12.4 us  [shards(): block = lax.ppermute(block, ('atom', 'kz'), pairs)]
    select_n x2 -> x0, other arithmetic: 3.19 us -> none  [the longest x1 2.44 us: pick(): jnp.where((g + d) % parts == part, piece, chosen)]
  transfers between devices with their start and end apart: 42 -> 42, of which waited for: 11 -> 9; matrix products, arithmetic and copies ran while one was open for 4% -> 3% of each run, Pallas kernels for 25% -> 32%
where the time goes in v5:
time: 226 us; the launch traced here: 225 us
  waiting for transfers between devices  89.9 us (40%)
  Pallas kernels  76.5 us (34%)
  starting transfers between devices  42 us (19%)
  local copies, waits for them, and re-layouts  12.1 us (5%)
  other arithmetic  4.26 us (2%)
    pallas_call x5, Pallas kernels, sandwich(): pl.pallas_call(functools.partial(split_dot, len(groups), len(groups[0][0]...  54.4 us
    ppermute x2, waiting for transfers between devices, shards(): lax.ppermute(x, 'atom', around[s])  34.7 us
    ppermute x4, waiting for transfers between devices, shards(): lax.ppermute(x, 'energy', down[d - 1])  24.2 us
    ppermute x12, waiting for transfers between devices, shards(): block = lax.ppermute(block, ('atom', 'kz'), pairs)  12.4 us
    ppermute x1, waiting for transfers between devices, shards(): lax.ppermute(got, 'grp', [(i, (i + d) % parts) for i in range(parts)])  11.6 us
    ppermute x4, starting transfers between devices, shards(): streams[-d] = [lax.ppermute(x, 'energy', up[d - 1]) for x in streams[1 - d]]  11.6 us
    pallas_call x4, Pallas kernels, summed(): pl.pallas_call(functools.partial(add_momenta, theirs, piece * size), out_...  9.9 us
    unnamed x64, local copies, waits for them, and re-layouts  8.58 us
  transfers between devices with their start and end apart: 42, of which 9 were waited for; matrix products, arithmetic and copies ran while one was open for 3% of the time, Pallas kernels for 32%

profile of v5, /device:TPU:0, one launch (start us, length us, event | category | flops | bytes accessed | tf_op | source)
XLA Modules:
  0.0 225.5 jit_solution(13625280643471349850)
XLA Ops:
  0.0 1.9 constant_dynamic-slice_fusion
  1.9 3.0 %collective-permute-start = (f32[2,128,512]{2,1,0:T(8,128)}, f32[2,128,512]{2,1,0:T(8,128)}, u32[]{:S(2)}, u32[]{:S(2)}) collective-permute-start(f32[2,128,512]{2,1,0:T(8,128)} %constant_dynamic-slice_fusion), channel_id=1, source_target_pairs={{0,2},{2,0},{1,3},{3,1},{4,6},{6,4},{5,7},{7,5},{8,10},{10,8},{9,1... | collective-permute-start | bytes 1572872 | tf_op jit(solution)/shard_map/ppermute | solution.py:375
  4.9 2.3 %add_momenta.4 = f32[4,128,512]{2,1,0:T(8,128)} custom-call(f32[2,8,256,512]{3,2,1,0:T(8,128)} %green.7), custom_call_target="tpu_custom_call" | custom-call | flops 524288 | bytes 3145728 | tf_op jit(solution)/shard_map/add_momenta/pallas_call | solution.py:324
  7.2 2.3 %add_momenta.6 = f32[4,128,512]{2,1,0:T(8,128)} custom-call(f32[2,8,256,512]{3,2,1,0:T(8,128)} %green.7), custom_call_target="tpu_custom_call" | custom-call | flops 524288 | bytes 3145728 | tf_op jit(solution)/shard_map/add_momenta/pallas_call | solution.py:324
  10.1 6.9 %collective-permute-done.refs_0_ = f32[2,128,512]{2,1,0:T(8,128)} collective-permute-done((f32[2,128,512]{2,1,0:T(8,128)}, f32[2,128,512]{2,1,0:T(8,128)}, u32[]{:S(2)}, u32[]{:S(2)}) %collective-permute-start) | collective-permute-done | bytes 524320 | tf_op jit(solution)/shard_map/ppermute | solution.py:375
  17.1 1.8 collective-permute-start.2
  18.9 11.6 %collective-permute-done.2.refs_2_ = f32[2,128,512]{2,1,0:T(8,128)} collective-permute-done((f32[2,128,512]{2,1,0:T(8,128)}, f32[2,128,512]{2,1,0:T(8,128)}, u32[]{:S(2)}, u32[]{:S(2)}) %collective-permute-start.2) | collective-permute-done | bytes 524320 | tf_op jit(solution)/shard_map/ppermute | solution.py:377
  30.5 2.6 %add_momenta.5.refs_8_.refs_0_ = f32[4,128,512]{2,1,0:T(8,128)} custom-call(f32[2,8,256,512]{3,2,1,0:T(8,128)} %green.7, f32[4,128,512]{2,1,0:T(8,128)} %collective-permute-done.4.refs_0_), custom_call_target="tpu_custom_call" | custom-call | flops 524288 | bytes 4194304 | tf_op jit(solution)/shard_map/add_momenta/pallas_call | solution.py:324
  33.7 2.6 %add_momenta.7.refs_9_.refs_1_ = f32[4,128,512]{2,1,0:T(8,128)} custom-call(f32[2,8,256,512]{3,2,1,0:T(8,128)} %green.7, f32[4,128,512]{2,1,0:T(8,128)} %collective-permute-done.7.refs_0_), custom_call_target="tpu_custom_call" | custom-call | flops 524288 | bytes 4194304 | tf_op jit(solution)/shard_map/add_momenta/pallas_call | solution.py:324
  36.5 1.5 collective-permute-start.36
  38.5 4.5 %collective-permute-start.5 = (f32[4,128,512]{2,1,0:T(8,128)}, f32[4,128,512]{2,1,0:T(8,128)}, u32[]{:S(2)}, u32[]{:S(2)}) collective-permute-start(f32[4,128,512]{2,1,0:T(8,128)} %add_momenta.5.refs_8_.refs_0_), channel_id=1, source_target_pairs={{0,4},{4,8},{8,12},{1,5},{5,9},{9,13},{2,6},{6,10},{10,14},{3,7},{... | collective-permute-start | bytes 3145736 | tf_op jit(solution)/shard_map/ppermute | solution.py:358
  43.0 3.5 %collective-permute-start.8 = (f32[4,128,512]{2,1,0:T(8,128)}, f32[4,128,512]{2,1,0:T(8,128)}, u32[]{:S(2)}, u32[]{:S(2)}) collective-permute-start(f32[4,128,512]{2,1,0:T(8,128)} %add_momenta.7.refs_9_.refs_1_), channel_id=1, source_target_pairs={{0,4},{4,8},{8,12},{1,5},{5,9},{9,13},{2,6},{6,10},{10,14},{3,7},{... | collective-permute-start | bytes 3145736 | tf_op jit(solution)/shard_map/ppermute | solution.py:358
  46.6 1.0 copy-done.7
  47.5 1.3 collective-permute-start.16
  48.8 14.0 %collective-permute-done.36.refs_2_ = f32[4,128,512]{2,1,0:T(8,128)} collective-permute-done((f32[4,128,512]{2,1,0:T(8,128)}, f32[4,128,512]{2,1,0:T(8,128)}, u32[]{:S(2)}, u32[]{:S(2)}) %collective-permute-start.36) | collective-permute-done | bytes 1048608 | tf_op jit(solution)/shard_map/ppermute | solution.py:399
  62.9 1.3 collective-permute-start.17
  64.1 20.6 %collective-permute-done.37.refs_3_ = f32[4,128,512]{2,1,0:T(8,128)} collective-permute-done((f32[4,128,512]{2,1,0:T(8,128)}, f32[4,128,512]{2,1,0:T(8,128)}, u32[]{:S(2)}, u32[]{:S(2)}) %collective-permute-start.37) | collective-permute-done | bytes 1048608 | tf_op jit(solution)/shard_map/ppermute | solution.py:399
  85.3 1.2 guard.1.steps
  86.5 1.6 copy-done.10
  88.1 3.3 %prepare.1 = (bf16[3,512,512]{2,1,0:T(8,128)(2,1)S(1)}, bf16[3,512,512]{2,1,0:T(8,128)(2,1)S(1)}, bf16[3,256,1536]{2,1,0:T(8,128)(2,1)S(1)}, bf16[3,512,768]{2,1,0:T(8,128)(2,1)S(1)}) custom-call(s32[3]{0:T(128)S(1)} %copy-done.18, f32[2,512,512]{2,1,0:T(8,128)S(1)} %copy-done.10, f32[2,128,512]{2,1,0:T(8,128)} %collective-permute-done.refs_0_, ...), custom_call_target="tpu_custom_call" | custom-call | flops 6291456 | bytes 7864320 | tf_op jit(solution)/shard_map/prepare/pallas_call | solution.py:384
  91.4 2.0 collective-permute-start.6
  93.4 3.2 %collective-permute-done.17.refs_13_ = f32[4,128,512]{2,1,0:T(8,128)} collective-permute-done((f32[4,128,512]{2,1,0:T(8,128)}, f32[4,128,512]{2,1,0:T(8,128)}, u32[]{:S(2)}, u32[]{:S(2)}) %collective-permute-start.17) | collective-permute-done | bytes 1048608 | tf_op jit(solution)/shard_map/ppermute | solution.py:359
  96.6 1.6 collective-permute-start.9
  98.2 1.3 collective-permute-start.20
  99.5 1.3 collective-permute-start.21
  100.8 24.1 %far_sandwich.1 = (f32[4,128,512]{2,1,0:T(8,128)S(1)}, f32[4,128,512]{2,1,0:T(8,128)S(1)}) custom-call(s32[3]{0:T(128)S(1)} %copy-done.19, f32[3]{0:T(128)S(1)} %copy-done.17, bf16[3,512,512]{2,1,0:T(8,128)(2,1)S(1)} %get-tuple-element.27.right_high, bf16[3,512,512]{2,1,0:T(8,128)(2,1)S(1)} %get-tuple-element.28.right_low, ...), custom_call_target="tpu_custom_call" | custom-call | flops 14495514624 | bytes 27262976 | tf_op jit(solution)/shard_map/far_sandwich/pallas_call | solution.py:209
  125.0 1.0 copy-done.11
  126.0 1.6 copy.6
  128.2 21.0 %collective-permute-done.21.refs_17_ = f32[4,128,512]{2,1,0:T(8,128)} collective-permute-done((f32[4,128,512]{2,1,0:T(8,128)}, f32[4,128,512]{2,1,0:T(8,128)}, u32[]{:S(2)}, u32[]{:S(2)}) %collective-permute-start.21) | collective-permute-done | bytes 1048608 | tf_op jit(solution)/shard_map/ppermute | solution.py:359
  150.0 0.7 collective-permute-start.11
  150.7 2.4 %collective-permute-start.22 = (f32[4,128,512]{2,1,0:T(8,128)}, f32[4,128,512]{2,1,0:T(8,128)S(1)}, u32[]{:S(2)}, u32[]{:S(2)}) collective-permute-start(f32[4,128,512]{2,1,0:T(8,128)} %collective-permute-done.20.refs_16_), channel_id=1, source_target_pairs={{0,1},{1,0},{4,5},{5,4},{2,3},{3,2},{6,7},{7,6},{16,17},{17,16},{2... | collective-permute-start | bytes 3145736 | tf_op jit(solution)/shard_map/ppermute | solution.py:368
  153.1 1.9 collective-permute-start.23
  155.1 2.5 %copy_select_fusion.1 = (f32[4,128,512]{2,0,1:T(4,128)S(1)}, f32[4,128,512]{2,0,1:T(4,128)S(1)}) fusion(f32[4,128,512]{2,0,1:T(4,128)} %collective-permute-done.40, f32[4,128,512]{2,1,0:T(8,128)} %copy-done.11, pred[]{:T(512)S(6)} %eq.4), kind=kLoop, calls=%fused_computation.2 | loop fusion | flops 524288 | bytes 4194305 | tf_op jit(solution)/shard_map/jit(_where)/select_n | solution.py:417
  157.6 1.8 maximum_bitcast_fusion
  159.4 2.0 collective-permute-start.41
  161.5 7.4 %near_sandwich.7 = (f32[1,128,512]{2,1,0:T(8,128)S(1)}, f32[1,128,512]{2,1,0:T(8,128)S(1)}, f32[1,128,512]{2,1,0:T(8,128)S(1)}, f32[1,128,512]{2,1,0:T(8,128)S(1)}) custom-call(s32[3]{0:T(128)S(1)} %copy-done.16, f32[3]{0:T(128)S(1)} %copy-done.17, bf16[3,512,512]{2,1,0:T(8,128)(2,1)S(1)} %copy-done.4, bf16[3,512,512]{2,1,0:T(8,128)(2,1)S(1)} %copy-done.6, ...), custom_call_target="tpu_custom_call" | custom-call | flops 2415919104 | bytes 4194304 | tf_op jit(solution)/shard_map/near_sandwich/pallas_call | solution.py:209
  169.6 2.0 collective-permute-start.28
  171.9 7.3 %near_sandwich.6 = (f32[1,128,512]{2,1,0:T(8,128)S(1)}, f32[1,128,512]{2,1,0:T(8,128)S(1)}, f32[1,128,512]{2,1,0:T(8,128)S(1)}, f32[1,128,512]{2,1,0:T(8,128)S(1)}) custom-call(s32[3]{0:T(128)S(1)} %copy-done.16, f32[3]{0:T(128)S(1)} %copy-done.17, bf16[3,512,512]{2,1,0:T(8,128)(2,1)S(1)} %copy-done.4, bf16[3,512,512]{2,1,0:T(8,128)(2,1)S(1)} %copy-done.6, ...), custom_call_target="tpu_custom_call" | custom-call | flops 2415919104 | bytes 4194304 | tf_op jit(solution)/shard_map/near_sandwich/pallas_call | solution.py:209
  179.9 1.9 collective-permute-start.27
  182.5 7.3 %near_sandwich.5 = (f32[1,128,512]{2,1,0:T(8,128)S(1)}, f32[1,128,512]{2,1,0:T(8,128)S(1)}, f32[1,128,512]{2,1,0:T(8,128)S(1)}, f32[1,128,512]{2,1,0:T(8,128)S(1)}) custom-call(s32[3]{0:T(128)S(1)} %copy-done.16, f32[3]{0:T(128)S(1)} %copy-done.17, bf16[3,512,512]{2,1,0:T(8,128)(2,1)S(1)} %copy-done.4, bf16[3,512,512]{2,1,0:T(8,128)(2,1)S(1)} %copy-done.6, ...), custom_call_target="tpu_custom_call" | custom-call | flops 2415919104 | bytes 4194304 | tf_op jit(solution)/shard_map/near_sandwich/pallas_call | solution.py:209
  190.5 1.6 collective-permute-start.26
  192.4 8.3 %near_sandwich.4 = (f32[1,128,512]{2,1,0:T(8,128)S(1)}, f32[1,128,512]{2,1,0:T(8,128)S(1)}, f32[1,128,512]{2,1,0:T(8,128)}, f32[1,128,512]{2,1,0:T(8,128)}) custom-call(s32[3]{0:T(128)S(1)} %copy-done.16, f32[3]{0:T(128)S(1)} %copy-done.17, bf16[3,512,512]{2,1,0:T(8,128)(2,1)S(1)} %copy-done.4, bf16[3,512,512]{2,1,0:T(8,128)(2,1)S(1)} %copy-done.6, ...), custom_call_target="tpu_custom_call" | custom-call | flops 2415919104 | bytes 4194304 | tf_op jit(solution)/shard_map/near_sandwich/pallas_call | solution.py:209
  202.0 1.7 collective-permute-start.24
  203.7 5.9 %collective-permute-done.33.refs_11_ = f32[1,128,512]{2,1,0:T(8,128)S(1)} collective-permute-done((f32[1,128,512]{2,1,0:T(8,128)S(1)}, f32[1,128,512]{2,1,0:T(8,128)S(1)}, u32[]{:S(2)}, u32[]{:S(2)}) %collective-permute-start.33) | collective-permute-done | bytes 262176 | tf_op jit(solution)/shard_map/ppermute | solution.py:437
  210.4 4.0 %shard_map.55.refs_2_ = f32[128,8,512]{2,1,0:T(8,128)} custom-call(f32[1,128,512]{2,1,0:T(8,128)} %copy-done.14, f32[1,128,512]{2,1,0:T(8,128)} %copy-done.13, f32[1,128,512]{2,1,0:T(8,128)} %copy-done.12, f32[1,128,512]{2,1,0:T(8,128)} %copy-done.15, f32[1,128,512]{2,1,0:T(8,128)} %copy-done.26, f32[1,128,512]{2,1,0:T(8,128)} %copy-done.23, ...), custom_call_target="tpu_custom_call" | custom-call | flops 1441792 | bytes 5767168 | tf_op jit(solution)/shard_map/pallas_call | solution.py:294
  214.4 1.8 collective-permute-done.24.refs_0_
  216.2 4.7 %collective-permute-done.25.refs_1_ = f32[1,128,512]{2,1,0:T(8,128)S(1)} collective-permute-done((f32[1,128,512]{2,1,0:T(8,128)}, f32[1,128,512]{2,1,0:T(8,128)S(1)}, u32[]{:S(2)}, u32[]{:S(2)}) %collective-permute-start.25) | collective-permute-done | bytes 262176 | tf_op jit(solution)/shard_map/ppermute | solution.py:437
  221.6 3.8 %shard_map.56 = f32[128,8,512]{2,1,0:T(8,128)} custom-call(f32[1,128,512]{2,1,0:T(8,128)} %copy-done.30, f32[1,128,512]{2,1,0:T(8,128)} %copy-done.31, f32[128,8,512]{2,1,0:T(8,128)} %shard_map.55.refs_2_, f32[128,8,512]{2,1,0:T(8,128)} %collective-permute-done.41.refs_3_), custom_call_target="tpu_custom_call" | custom-call | flops 1703936 | bytes 6815744 | tf_op jit(solution)/shard_map/pallas_call | solution.py:294
  (117 shorter events, 9.9 us)
Async XLA Ops:
  1.9 15.2 %collective-permute-start = (f32[2,128,512]{2,1,0:T(8,128)}, f32[2,128,512]{2,1,0:T(8,128)}, u32[]{:S(2)}, u32[]{:S(2)}) collective-permute-start(f32[2,128,512]{2,1,0:T(8,128)} %constant_dynamic-slice_fusion), channel_id=1, source_target_pairs={{0,2},{2,0},{1,3},{3,1},{4,6},{6,4},{5,7},{7,5},{8,10},{10,8},{9,1... | collective-permute-start | bytes 1572872 | tf_op jit(solution)/shard_map/ppermute | solution.py:375
  7.2 23.3 %collective-permute-start.4 = (f32[4,128,512]{2,1,0:T(8,128)}, f32[4,128,512]{2,1,0:T(8,128)}, u32[]{:S(2)}, u32[]{:S(2)}) collective-permute-start(f32[4,128,512]{2,1,0:T(8,128)} %add_momenta.4), channel_id=1, source_target_pairs={{0,1},{1,0},{2,3},{3,2},{4,5},{5,4},{6,7},{7,6},{8,9},{9,8},{10,11... | collective-permute-start | bytes 3145736 | tf_op jit(solution)/shard_map/ppermute | solution.py:347
  9.6 24.1 %collective-permute-start.7 = (f32[4,128,512]{2,1,0:T(8,128)}, f32[4,128,512]{2,1,0:T(8,128)}, u32[]{:S(2)}, u32[]{:S(2)}) collective-permute-start(f32[4,128,512]{2,1,0:T(8,128)} %add_momenta.6), channel_id=1, source_target_pairs={{0,1},{1,0},{2,3},{3,2},{4,5},{5,4},{6,7},{7,6},{8,9},{9,8},{10,11... | collective-permute-start | bytes 3145736 | tf_op jit(solution)/shard_map/ppermute | solution.py:347
  17.1 13.4 %collective-permute-start.2 = (f32[2,128,512]{2,1,0:T(8,128)}, f32[2,128,512]{2,1,0:T(8,128)}, u32[]{:S(2)}, u32[]{:S(2)}) collective-permute-start(f32[2,128,512]{2,1,0:T(8,128)} %collective-permute-done.refs_0_), channel_id=1, source_target_pairs={{0,16},{16,0},{1,17},{17,1},{2,18},{18,2},{3,19},{19,3},{4,20},{20... | collective-permute-start | bytes 1572872 | tf_op jit(solution)/shard_map/ppermute | solution.py:377
  18.9 19.1 %collective-permute-start.1 = (f32[2,128,512]{2,1,0:T(8,128)}, f32[2,128,512]{2,1,0:T(8,128)}, u32[]{:S(2)}, u32[]{:S(2)}) collective-permute-start(f32[2,128,512]{2,1,0:T(8,128)} %collective-permute-done.refs_0_), channel_id=1, source_target_pairs={{0,1},{1,0},{2,3},{3,2},{4,5},{5,4},{6,7},{7,6},{8,9},{9,8},{10,11... | collective-permute-start | bytes 1572872 | tf_op jit(solution)/shard_map/ppermute | solution.py:379
  30.5 8.0 %collective-permute-start.3 = (f32[2,128,512]{2,1,0:T(8,128)}, f32[2,128,512]{2,1,0:T(8,128)}, u32[]{:S(2)}, u32[]{:S(2)}) collective-permute-start(f32[2,128,512]{2,1,0:T(8,128)} %collective-permute-done.2.refs_2_), channel_id=1, source_target_pairs={{0,1},{1,0},{2,3},{3,2},{4,5},{5,4},{6,7},{7,6},{8,9},{9,8},{10,11... | collective-permute-start | bytes 1572872 | tf_op jit(solution)/shard_map/ppermute | solution.py:379
  33.1 53.4 %copy-start.18 = (s32[3]{0:T(128)S(1)}, s32[3]{0:T(128)}, u32[]{:S(2)}) copy-start(s32[3]{0:T(128)} %owners.1) | copy-start | bytes 40
  33.1 9.9 %collective-permute-start.14 = (f32[4,128,512]{2,1,0:T(8,128)}, f32[4,128,512]{2,1,0:T(8,128)}, u32[]{:S(2)}, u32[]{:S(2)}) collective-permute-start(f32[4,128,512]{2,1,0:T(8,128)} %add_momenta.5.refs_8_.refs_0_), channel_id=1, source_target_pairs={{0,1},{1,0},{2,3},{3,2},{4,5},{5,4},{6,7},{7,6},{8,9},{9,8},{10,11... | collective-permute-start | bytes 3145736 | tf_op jit(solution)/shard_map/ppermute | solution.py:368
  36.4 10.2 %collective-permute-start.15 = (f32[4,128,512]{2,1,0:T(8,128)}, f32[4,128,512]{2,1,0:T(8,128)S(1)}, u32[]{:S(2)}, u32[]{:S(2)}) collective-permute-start(f32[4,128,512]{2,1,0:T(8,128)} %add_momenta.7.refs_9_.refs_1_), channel_id=1, source_target_pairs={{0,1},{1,0},{2,3},{3,2},{4,5},{5,4},{6,7},{7,6},{8,9},{9,8},{10,11... | collective-permute-start | bytes 3145736 | tf_op jit(solution)/shard_map/ppermute | solution.py:368
  36.5 26.4 %collective-permute-start.36 = (f32[4,128,512]{2,1,0:T(8,128)}, f32[4,128,512]{2,1,0:T(8,128)}, u32[]{:S(2)}, u32[]{:S(2)}) collective-permute-start(f32[4,128,512]{2,1,0:T(8,128)} %add_momenta.5.refs_8_.refs_0_), channel_id=1, source_target_pairs={{0,2},{2,0},{1,3},{3,1},{4,6},{6,4},{5,7},{7,5},{8,10},{10,8},{9,1... | collective-permute-start | bytes 3145736 | tf_op jit(solution)/shard_map/ppermute | solution.py:399
  38.0 46.8 %collective-permute-start.37 = (f32[4,128,512]{2,1,0:T(8,128)}, f32[4,128,512]{2,1,0:T(8,128)}, u32[]{:S(2)}, u32[]{:S(2)}) collective-permute-start(f32[4,128,512]{2,1,0:T(8,128)} %add_momenta.7.refs_9_.refs_1_), channel_id=1, source_target_pairs={{0,2},{2,0},{1,3},{3,1},{4,6},{6,4},{5,7},{7,5},{8,10},{10,8},{9,1... | collective-permute-start | bytes 3145736 | tf_op jit(solution)/shard_map/ppermute | solution.py:399
  38.5 46.3 %collective-permute-start.5 = (f32[4,128,512]{2,1,0:T(8,128)}, f32[4,128,512]{2,1,0:T(8,128)}, u32[]{:S(2)}, u32[]{:S(2)}) collective-permute-start(f32[4,128,512]{2,1,0:T(8,128)} %add_momenta.5.refs_8_.refs_0_), channel_id=1, source_target_pairs={{0,4},{4,8},{8,12},{1,5},{5,9},{9,13},{2,6},{6,10},{10,14},{3,7},{... | collective-permute-start | bytes 3145736 | tf_op jit(solution)/shard_map/ppermute | solution.py:358
  43.0 48.4 %collective-permute-start.8 = (f32[4,128,512]{2,1,0:T(8,128)}, f32[4,128,512]{2,1,0:T(8,128)}, u32[]{:S(2)}, u32[]{:S(2)}) collective-permute-start(f32[4,128,512]{2,1,0:T(8,128)} %add_momenta.7.refs_9_.refs_1_), channel_id=1, source_target_pairs={{0,4},{4,8},{8,12},{1,5},{5,9},{9,13},{2,6},{6,10},{10,14},{3,7},{... | collective-permute-start | bytes 3145736 | tf_op jit(solution)/shard_map/ppermute | solution.py:358
  47.5 45.9 %collective-permute-start.16 = (f32[4,128,512]{2,1,0:T(8,128)}, f32[4,128,512]{2,1,0:T(8,128)}, u32[]{:S(2)}, u32[]{:S(2)}) collective-permute-start(f32[4,128,512]{2,1,0:T(8,128)} %add_momenta.5.refs_8_.refs_0_), channel_id=1, source_target_pairs={{12,8},{8,4},{4,0},{13,9},{9,5},{5,1},{14,10},{10,6},{6,2},{15,11}... | collective-permute-start | bytes 3145736 | tf_op jit(solution)/shard_map/ppermute | solution.py:359
  62.9 33.7 %collective-permute-start.17 = (f32[4,128,512]{2,1,0:T(8,128)}, f32[4,128,512]{2,1,0:T(8,128)}, u32[]{:S(2)}, u32[]{:S(2)}) collective-permute-start(f32[4,128,512]{2,1,0:T(8,128)} %add_momenta.7.refs_9_.refs_1_), channel_id=1, source_target_pairs={{12,8},{8,4},{4,0},{13,9},{9,5},{5,1},{14,10},{10,6},{6,2},{15,11}... | collective-permute-start | bytes 3145736 | tf_op jit(solution)/shard_map/ppermute | solution.py:359
  84.8 13.4 %collective-permute-start.38 = (f32[4,128,512]{2,1,0:T(8,128)}, f32[4,128,512]{2,1,0:T(8,128)}, u32[]{:S(2)}, u32[]{:S(2)}) collective-permute-start(f32[4,128,512]{2,1,0:T(8,128)} %collective-permute-done.36.refs_2_), channel_id=1, source_target_pairs={{0,1},{1,0},{2,3},{3,2},{4,5},{5,4},{6,7},{7,6},{8,9},{9,8},{10,11... | collective-permute-start | bytes 3145736 | tf_op jit(solution)/shard_map/ppermute | solution.py:402
  84.8 14.7 %collective-permute-start.39 = (f32[4,128,512]{2,1,0:T(8,128)}, f32[4,128,512]{2,1,0:T(8,128)}, u32[]{:S(2)}, u32[]{:S(2)}) collective-permute-start(f32[4,128,512]{2,1,0:T(8,128)} %collective-permute-done.37.refs_3_), channel_id=1, source_target_pairs={{0,1},{1,0},{2,3},{3,2},{4,5},{5,4},{6,7},{7,6},{8,9},{9,8},{10,11... | collective-permute-start | bytes 3145736 | tf_op jit(solution)/shard_map/ppermute | solution.py:402
  88.1 12.7 %copy-start.8 = (f32[4,128,512]{2,1,0:T(8,128)S(1)}, f32[4,128,512]{2,1,0:T(8,128)}, u32[]{:S(2)}) copy-start(f32[4,128,512]{2,1,0:T(8,128)} %copy-done.7) | copy-start | bytes 3145732
  88.1 12.7 %copy-start.17 = (f32[3]{0:T(128)S(1)}, f32[3]{0:T(128)}, u32[]{:S(2)}) copy-start(f32[3]{0:T(128)} %occupation.9) | copy-start | bytes 40
  88.1 12.7 %copy-start.19 = (s32[3]{0:T(128)S(1)}, s32[3]{0:T(128)}, u32[]{:S(2)}) copy-start(s32[3]{0:T(128)} %guard.1.steps) | copy-start | bytes 40
  91.4 33.6 %copy-start.3 = (bf16[3,512,512]{2,1,0:T(8,128)(2,1)}, bf16[3,512,512]{2,1,0:T(8,128)(2,1)S(1)}, u32[]{:S(2)}) copy-start(bf16[3,512,512]{2,1,0:T(8,128)(2,1)S(1)} %get-tuple-element.27.right_high) | copy-start | bytes 4718596
  91.4 33.6 %copy-start.5 = (bf16[3,512,512]{2,1,0:T(8,128)(2,1)}, bf16[3,512,512]{2,1,0:T(8,128)(2,1)S(1)}, u32[]{:S(2)}) copy-start(bf16[3,512,512]{2,1,0:T(8,128)(2,1)S(1)} %get-tuple-element.28.right_low) | copy-start | bytes 4718596
  91.4 36.2 %collective-permute-start.6 = (f32[4,128,512]{2,1,0:T(8,128)}, f32[4,128,512]{2,1,0:T(8,128)}, u32[]{:S(2)}, u32[]{:S(2)}) collective-permute-start(f32[4,128,512]{2,1,0:T(8,128)} %collective-permute-done.5.refs_4_), channel_id=1, source_target_pairs={{4,8},{8,12},{5,9},{9,13},{6,10},{10,14},{7,11},{11,15},{20,24},{2... | collective-permute-start | bytes 3145736 | tf_op jit(solution)/shard_map/ppermute | solution.py:358
  93.4 55.8 %collective-permute-start.12 = (f32[4,128,512]{2,1,0:T(8,128)}, f32[4,128,512]{2,1,0:T(8,128)}, u32[]{:S(2)}, u32[]{:S(2)}) collective-permute-start(f32[4,128,512]{2,1,0:T(8,128)} %collective-permute-done.5.refs_4_), channel_id=1, source_target_pairs={{0,1},{1,0},{2,3},{3,2},{4,5},{5,4},{6,7},{7,6},{8,9},{9,8},{10,11... | collective-permute-start | bytes 3145736 | tf_op jit(solution)/shard_map/ppermute | solution.py:368
  96.6 31.1 %collective-permute-start.9 = (f32[4,128,512]{2,1,0:T(8,128)}, f32[4,128,512]{2,1,0:T(8,128)}, u32[]{:S(2)}, u32[]{:S(2)}) collective-permute-start(f32[4,128,512]{2,1,0:T(8,128)} %collective-permute-done.8.refs_5_), channel_id=1, source_target_pairs={{4,8},{8,12},{5,9},{9,13},{6,10},{10,14},{7,11},{11,15},{20,24},{2... | collective-permute-start | bytes 3145736 | tf_op jit(solution)/shard_map/ppermute | solution.py:358
  98.2 30.0 %collective-permute-start.20 = (f32[4,128,512]{2,1,0:T(8,128)}, f32[4,128,512]{2,1,0:T(8,128)}, u32[]{:S(2)}, u32[]{:S(2)}) collective-permute-start(f32[4,128,512]{2,1,0:T(8,128)} %collective-permute-done.16.refs_12_), channel_id=1, source_target_pairs={{8,4},{4,0},{9,5},{5,1},{10,6},{6,2},{11,7},{7,3},{24,20},{20,16},... | collective-permute-start | bytes 3145736 | tf_op jit(solution)/shard_map/ppermute | solution.py:359
  99.5 49.7 %collective-permute-start.21 = (f32[4,128,512]{2,1,0:T(8,128)}, f32[4,128,512]{2,1,0:T(8,128)}, u32[]{:S(2)}, u32[]{:S(2)}) collective-permute-start(f32[4,128,512]{2,1,0:T(8,128)} %collective-permute-done.17.refs_13_), channel_id=1, source_target_pairs={{8,4},{4,0},{9,5},{5,1},{10,6},{6,2},{11,7},{7,3},{24,20},{20,16},... | collective-permute-start | bytes 3145736 | tf_op jit(solution)/shard_map/ppermute | solution.py:359
  127.6 22.3 %collective-permute-start.13 = (f32[4,128,512]{2,1,0:T(8,128)}, f32[4,128,512]{2,1,0:T(8,128)}, u32[]{:S(2)}, u32[]{:S(2)}) collective-permute-start(f32[4,128,512]{2,1,0:T(8,128)} %collective-permute-done.8.refs_5_), channel_id=1, source_target_pairs={{0,1},{1,0},{2,3},{3,2},{4,5},{5,4},{6,7},{7,6},{8,9},{9,8},{10,11... | collective-permute-start | bytes 3145736 | tf_op jit(solution)/shard_map/ppermute | solution.py:368
  127.6 23.1 %collective-permute-start.18 = (f32[4,128,512]{2,1,0:T(8,128)}, f32[4,128,512]{2,1,0:T(8,128)}, u32[]{:S(2)}, u32[]{:S(2)}) collective-permute-start(f32[4,128,512]{2,1,0:T(8,128)} %collective-permute-done.16.refs_12_), channel_id=1, source_target_pairs={{0,1},{1,0},{2,3},{3,2},{4,5},{5,4},{6,7},{7,6},{8,9},{9,8},{10,11... | collective-permute-start | bytes 3145736 | tf_op jit(solution)/shard_map/ppermute | solution.py:368
  128.2 25.0 %collective-permute-start.40 = (f32[4,128,512]{2,0,1:T(4,128)}, f32[4,128,512]{2,0,1:T(4,128)}, u32[]{:S(2)}, u32[]{:S(2)}) collective-permute-start(f32[4,128,512]{2,0,1:T(4,128)} %copy.6), channel_id=1, source_target_pairs={{0,1},{1,0},{2,3},{3,2},{4,5},{5,4},{6,7},{7,6},{8,9},{9,8},{10,11... | collective-permute-start | bytes 3145736 | tf_op jit(solution)/shard_map/ppermute | solution.py:415
  149.2 10.2 %collective-permute-start.19 = (f32[4,128,512]{2,1,0:T(8,128)}, f32[4,128,512]{2,1,0:T(8,128)}, u32[]{:S(2)}, u32[]{:S(2)}) collective-permute-start(f32[4,128,512]{2,1,0:T(8,128)} %collective-permute-done.17.refs_13_), channel_id=1, source_target_pairs={{0,1},{1,0},{2,3},{3,2},{4,5},{5,4},{6,7},{7,6},{8,9},{9,8},{10,11... | collective-permute-start | bytes 3145736 | tf_op jit(solution)/shard_map/ppermute | solution.py:368
  149.2 12.2 %collective-permute-start.10 = (f32[4,128,512]{2,1,0:T(8,128)}, f32[4,128,512]{2,1,0:T(8,128)S(1)}, u32[]{:S(2)}, u32[]{:S(2)}) collective-permute-start(f32[4,128,512]{2,1,0:T(8,128)} %collective-permute-done.6.refs_0_), channel_id=1, source_target_pairs={{8,9},{9,8},{12,13},{13,12},{10,11},{11,10},{14,15},{15,14},{24,25... | collective-permute-start | bytes 3145736 | tf_op jit(solution)/shard_map/ppermute | solution.py:368
  150.0 11.5 %collective-permute-start.11 = (f32[4,128,512]{2,1,0:T(8,128)}, f32[4,128,512]{2,1,0:T(8,128)S(1)}, u32[]{:S(2)}, u32[]{:S(2)}) collective-permute-start(f32[4,128,512]{2,1,0:T(8,128)} %collective-permute-done.9.refs_1_), channel_id=1, source_target_pairs={{8,9},{9,8},{12,13},{13,12},{10,11},{11,10},{14,15},{15,14},{24,25... | collective-permute-start | bytes 3145736 | tf_op jit(solution)/shard_map/ppermute | solution.py:368
  150.7 10.8 %collective-permute-start.22 = (f32[4,128,512]{2,1,0:T(8,128)}, f32[4,128,512]{2,1,0:T(8,128)S(1)}, u32[]{:S(2)}, u32[]{:S(2)}) collective-permute-start(f32[4,128,512]{2,1,0:T(8,128)} %collective-permute-done.20.refs_16_), channel_id=1, source_target_pairs={{0,1},{1,0},{4,5},{5,4},{2,3},{3,2},{6,7},{7,6},{16,17},{17,16},{2... | collective-permute-start | bytes 3145736 | tf_op jit(solution)/shard_map/ppermute | solution.py:368
  153.1 8.3 %collective-permute-start.23 = (f32[4,128,512]{2,1,0:T(8,128)}, f32[4,128,512]{2,1,0:T(8,128)S(1)}, u32[]{:S(2)}, u32[]{:S(2)}) collective-permute-start(f32[4,128,512]{2,1,0:T(8,128)} %collective-permute-done.21.refs_17_), channel_id=1, source_target_pairs={{0,1},{1,0},{4,5},{5,4},{2,3},{3,2},{6,7},{7,6},{16,17},{17,16},{2... | collective-permute-start | bytes 3145736 | tf_op jit(solution)/shard_map/ppermute | solution.py:368
  159.4 61.5 %collective-permute-start.41 = (f32[128,8,512]{2,1,0:T(8,128)}, f32[128,8,512]{2,1,0:T(8,128)}, u32[]{:S(2)}, u32[]{:S(2)}) collective-permute-start(f32[128,8,512]{2,1,0:T(8,128)} %maximum_bitcast_fusion), channel_id=1, source_target_pairs={{0,12},{12,0},{1,13},{13,1},{2,14},{14,2},{3,15},{15,3},{16,28},{2... | collective-permute-start | bytes 6291464 | tf_op jit(solution)/shard_map/ppermute | solution.py:419
  169.6 12.2 %collective-permute-start.28 = (f32[1,128,512]{2,1,0:T(8,128)S(1)}, f32[1,128,512]{2,1,0:T(8,128)S(1)}, u32[]{:S(2)}, u32[]{:S(2)}) collective-permute-start(f32[1,128,512]{2,1,0:T(8,128)S(1)} %get-tuple-element.38), channel_id=1, source_target_pairs={{0,2},{1,3},{2,0},{3,1},{4,6},{5,7},{6,4},{7,5},{8,10},{9,11},{10,... | collective-permute-start | bytes 786440 | tf_op jit(solution)/shard_map/ppermute | solution.py:437
  171.6 10.2 %collective-permute-start.31 = (f32[1,128,512]{2,1,0:T(8,128)S(1)}, f32[1,128,512]{2,1,0:T(8,128)S(1)}, u32[]{:S(2)}, u32[]{:S(2)}) collective-permute-start(f32[1,128,512]{2,1,0:T(8,128)S(1)} %get-tuple-element.41), channel_id=1, source_target_pairs={{0,1},{1,0},{2,3},{3,2},{4,5},{5,4},{6,7},{7,6},{8,9},{9,8},{10,11... | collective-permute-start | bytes 786440 | tf_op jit(solution)/shard_map/ppermute | solution.py:437
  171.9 18.7 %collective-permute-start.35 = (f32[1,128,512]{2,1,0:T(8,128)S(1)}, f32[1,128,512]{2,1,0:T(8,128)S(1)}, u32[]{:S(2)}, u32[]{:S(2)}) collective-permute-start(f32[1,128,512]{2,1,0:T(8,128)S(1)} %get-tuple-element.45), channel_id=1, source_target_pairs={{0,3},{1,2},{2,1},{3,0},{4,7},{5,6},{6,5},{7,4},{8,11},{9,10},{10,... | collective-permute-start | bytes 786440 | tf_op jit(solution)/shard_map/ppermute | solution.py:437
  179.9 12.3 %collective-permute-start.27 = (f32[1,128,512]{2,1,0:T(8,128)S(1)}, f32[1,128,512]{2,1,0:T(8,128)S(1)}, u32[]{:S(2)}, u32[]{:S(2)}) collective-permute-start(f32[1,128,512]{2,1,0:T(8,128)S(1)} %get-tuple-element.37), channel_id=1, source_target_pairs={{0,2},{1,3},{2,0},{3,1},{4,6},{5,7},{6,4},{7,5},{8,10},{9,11},{10,... | collective-permute-start | bytes 786440 | tf_op jit(solution)/shard_map/ppermute | solution.py:437
  181.8 19.7 %collective-permute-start.30 = (f32[1,128,512]{2,1,0:T(8,128)S(1)}, f32[1,128,512]{2,1,0:T(8,128)S(1)}, u32[]{:S(2)}, u32[]{:S(2)}) collective-permute-start(f32[1,128,512]{2,1,0:T(8,128)S(1)} %get-tuple-element.40), channel_id=1, source_target_pairs={{0,1},{1,0},{2,3},{3,2},{4,5},{5,4},{6,7},{7,6},{8,9},{9,8},{10,11... | collective-permute-start | bytes 786440 | tf_op jit(solution)/shard_map/ppermute | solution.py:437
  182.5 19.3 %collective-permute-start.34 = (f32[1,128,512]{2,1,0:T(8,128)S(1)}, f32[1,128,512]{2,1,0:T(8,128)S(1)}, u32[]{:S(2)}, u32[]{:S(2)}) collective-permute-start(f32[1,128,512]{2,1,0:T(8,128)S(1)} %get-tuple-element.44), channel_id=1, source_target_pairs={{0,3},{1,2},{2,1},{3,0},{4,7},{5,6},{6,5},{7,4},{8,11},{9,10},{10,... | collective-permute-start | bytes 786440 | tf_op jit(solution)/shard_map/ppermute | solution.py:437
  190.5 11.4 %collective-permute-start.26 = (f32[1,128,512]{2,1,0:T(8,128)S(1)}, f32[1,128,512]{2,1,0:T(8,128)S(1)}, u32[]{:S(2)}, u32[]{:S(2)}) collective-permute-start(f32[1,128,512]{2,1,0:T(8,128)S(1)} %get-tuple-element.36), channel_id=1, source_target_pairs={{0,2},{1,3},{2,0},{3,1},{4,6},{5,7},{6,4},{7,5},{8,10},{9,11},{10,... | collective-permute-start | bytes 786440 | tf_op jit(solution)/shard_map/ppermute | solution.py:437
  192.1 11.5 %collective-permute-start.29 = (f32[1,128,512]{2,1,0:T(8,128)S(1)}, f32[1,128,512]{2,1,0:T(8,128)S(1)}, u32[]{:S(2)}, u32[]{:S(2)}) collective-permute-start(f32[1,128,512]{2,1,0:T(8,128)S(1)} %get-tuple-element.39), channel_id=1, source_target_pairs={{0,1},{1,0},{2,3},{3,2},{4,5},{5,4},{6,7},{7,6},{8,9},{9,8},{10,11... | collective-permute-start | bytes 786440 | tf_op jit(solution)/shard_map/ppermute | solution.py:437
  201.5 8.1 %collective-permute-start.33 = (f32[1,128,512]{2,1,0:T(8,128)S(1)}, f32[1,128,512]{2,1,0:T(8,128)S(1)}, u32[]{:S(2)}, u32[]{:S(2)}) collective-permute-start(f32[1,128,512]{2,1,0:T(8,128)S(1)} %get-tuple-element.43), channel_id=1, source_target_pairs={{0,3},{1,2},{2,1},{3,0},{4,7},{5,6},{6,5},{7,4},{8,11},{9,10},{10,... | collective-permute-start | bytes 786440 | tf_op jit(solution)/shard_map/ppermute | solution.py:437
  201.8 7.8 %collective-permute-start.32 = (f32[1,128,512]{2,1,0:T(8,128)S(1)}, f32[1,128,512]{2,1,0:T(8,128)S(1)}, u32[]{:S(2)}, u32[]{:S(2)}) collective-permute-start(f32[1,128,512]{2,1,0:T(8,128)S(1)} %get-tuple-element.42), channel_id=1, source_target_pairs={{0,1},{1,0},{2,3},{3,2},{4,5},{5,4},{6,7},{7,6},{8,9},{9,8},{10,11... | collective-permute-start | bytes 786440 | tf_op jit(solution)/shard_map/ppermute | solution.py:437
  202.0 14.2 %collective-permute-start.24 = (f32[1,128,512]{2,1,0:T(8,128)}, f32[1,128,512]{2,1,0:T(8,128)S(1)}, u32[]{:S(2)}, u32[]{:S(2)}) collective-permute-start(f32[1,128,512]{2,1,0:T(8,128)} %get-tuple-element.30), channel_id=1, source_target_pairs={{0,2},{1,3},{2,0},{3,1},{4,6},{5,7},{6,4},{7,5},{8,10},{9,11},{10,... | collective-permute-start | bytes 786440 | tf_op jit(solution)/shard_map/ppermute | solution.py:437
  203.6 17.2 %collective-permute-start.25 = (f32[1,128,512]{2,1,0:T(8,128)}, f32[1,128,512]{2,1,0:T(8,128)S(1)}, u32[]{:S(2)}, u32[]{:S(2)}) collective-permute-start(f32[1,128,512]{2,1,0:T(8,128)} %get-tuple-element.31), channel_id=1, source_target_pairs={{0,3},{1,2},{2,1},{3,0},{4,7},{5,6},{6,5},{7,4},{8,11},{9,10},{10,... | collective-permute-start | bytes 786440 | tf_op jit(solution)/shard_map/ppermute | solution.py:437
  (26 other events, 117.9 us)

commit v6 on v5

--- a/solution.py
+++ b/solution.py
@@ -164,37 +164,32 @@
                 fetch(energy + 1, 1 - buffer)
 
         dot = functools.partial(jnp.dot, preferred_element_type=jnp.float32)
-
-        @pl.loop(0, MODES)
-        def _(mode):
+        for mode in range(MODES):
             scales = []
             for side in range(2):
-                held = planes.at[buffer, mode * 2 + side]
-                pltpu.make_async_copy(held, held, sems.at[buffer, mode * 2 + side]).wait()
-                scale = (occupation[mode] + (1.0 - side)) * (1.0 / momenta)
-                scales.append(jnp.where(source_of(energy, mode, side)[0], scale, 0.0))
+                slot = mode * 2 + side
+                held = planes.at[buffer, slot]
+                pltpu.make_async_copy(held, held, sems.at[buffer, slot]).wait()
+                scales.append(jnp.where(source_of(energy, mode, side)[0], (occupation[mode] + (1.0 - side)) * (1.0 / momenta), 0.0))
             combined = scales[0] * planes[buffer, 2 * mode] + scales[1] * planes[buffer, 2 * mode + 1]
-            high, low = halves(combined)
+            high = combined.astype(jnp.bfloat16)
+            low = (combined - high.astype(jnp.float32)).astype(jnp.bfloat16)
             product = dot(high, right_high[mode]) + dot(low, right_high[mode]) + dot(high, right_low[mode])
-            high, low = halves(product)
-            inner[pl.ds(0, rows)] = high
-            inner[pl.ds(rows, rows)] = low
-            inner[pl.ds(2 * rows, rows)] = high
-            for index, out in enumerate(outs):
-                s, t = index // 2, index % 2
-                block = lax.rem(core + t, 2)
-                if not far:
-                    block = block + 2 * lax.rem(atom + s, n_atoms)
-                where = pl.ds(pl.multiple_of(block * size, 8), size)
-                total = dot(left[mode, where], inner[...])
-
-                @pl.when(mode == 0)
-                def _(out=out, total=total):
-                    out[energy] = total
-
-                @pl.when(mode > 0)
-                def _(out=out, total=total):
-                    out[energy] += total
+            high = product.astype(jnp.bfloat16)
+            low = (product - high.astype(jnp.float32)).astype(jnp.bfloat16)
+            inner[mode, pl.ds(0, rows)] = high
+            inner[mode, pl.ds(rows, rows)] = low
+            inner[mode, pl.ds(2 * rows, rows)] = high
+        for index, out in enumerate(outs):
+            s, t = index // 2, index % 2
+            block = lax.rem(core + t, 2)
+            if not far:
+                block = block + 2 * lax.rem(atom + s, n_atoms)
+            where = pl.ds(pl.multiple_of(block * size, 8), size)
+            total = dot(left[0, where], inner[0])
+            for mode in range(1, MODES):
+                total = total + dot(left[mode, where], inner[mode])
+            out[energy] = total
 
 
 def sandwich(steps, occupation, right, left, groups, n_atoms, momenta, base, grid_total, edev, far, line, out_rows, count):
@@ -215,7 +210,7 @@
         out_specs=[pl.BlockSpec(memory_space=pltpu.VMEM)] * n_out,
         scratch_shapes=[
             pltpu.VMEM((buffers, 2 * MODES, rows, order), jnp.float32),
-            pltpu.VMEM((3 * rows, order), jnp.bfloat16),
+            pltpu.VMEM((MODES, 3 * rows, order), jnp.bfloat16),
             pltpu.SemaphoreType.DMA((2, 2 * MODES)),
         ],
         compiler_params=pltpu.CompilerParams(vmem_limit_bytes=held),
@@ -297,6 +292,7 @@
         in_specs=[vmem] * len(arrays),
         out_specs=pl.BlockSpec(memory_space=pltpu.HBM) if before else vmem,
         scratch_shapes=scratch,
+        compiler_params=pltpu.CompilerParams(vmem_limit_bytes=8 << 20),
         cost_estimate=pl.CostEstimate(flops=size // 4, bytes_accessed=size, transcendentals=0),
     )(*arrays)
 
@@ -407,6 +403,7 @@
             out_shape=jax.ShapeDtypeStruct(offsets.shape, offsets.dtype),
             in_specs=[smem],
             out_specs=smem,
+            compiler_params=pltpu.CompilerParams(vmem_limit_bytes=1 << 20),
             name="guard",
         )(offsets)
         sums = sandwich(
@@ -416,7 +413,8 @@
         both = jnp.concatenate(
             [jnp.where(core == 0, sums[0], swapped), jnp.where(core == 0, swapped, sums[0])], 0
         ).swapaxes(0, 1)
-        beyond.append(lax.ppermute(both, "energy", [(0, n - 1), (n - 1, 0)]))
+        beyond.append(lax.ppermute(both, "energy", [(0, n - 1)]))
+        beyond.append(lax.ppermute(both, "energy", [(n - 1, 0)]))
 
     terms = [[[] for _ in range(atoms)] for _ in range(cores)]
     base = 0

time: 226 us -> 287 us (1.27)
  waiting for transfers between devices: 89.9 us -> 169 us
  Pallas kernels: 76.5 us -> 57.1 us
  starting transfers between devices: 42 us -> 45.6 us
    ppermute x4, waiting for transfers between devices: 24.2 us -> 76.4 us  [shards(): lax.ppermute(x, 'energy', down[d - 1])]
    ppermute x4, waiting for transfers between devices: 0.01 us -> 37.5 us  [shards(): streams[-d] = [lax.ppermute(x, 'energy', up[d - 1]) for x in streams[1 - d]]]
    ppermute x2, waiting for transfers between devices: 34.7 us -> 5.99 us  [shards(): lax.ppermute(x, 'atom', around[s])]
    ppermute x12, waiting for transfers between devices: 12.4 us -> 30.4 us  [shards(): block = lax.ppermute(block, ('atom', 'kz'), pairs)]
    pallas_call x5, Pallas kernels: 54.4 us -> 41.1 us  [sandwich(): pl.pallas_call(functools.partial(split_dot, len(groups), len(groups[0][0]...]
    pallas_call x2, Pallas kernels: 7.73 us -> 2.01 us  [gathered(): pl.pallas_call(kernel, out_shape=jax.ShapeDtypeStruct(shape, jnp.float32)...]
    unnamed x64 -> x52, local copies, waits for them, and re-layouts: 8.58 us -> 8.32 us
  transfers between devices with their start and end apart: 42 -> 43, of which waited for: 9 -> 16; matrix products, arithmetic and copies ran while one was open for 3% -> 1% of each run, Pallas kernels for 32% -> 19%
where the time goes in v6:
time: 287 us; the launch traced here: 286 us
  waiting for transfers between devices  169 us (59%)
  Pallas kernels  57.1 us (20%)
  starting transfers between devices  45.6 us (16%)
  local copies, waits for them, and re-layouts  10.9 us (4%)
  other arithmetic  3.01 us (1%)
    ppermute x4, waiting for transfers between devices, shards(): lax.ppermute(x, 'energy', down[d - 1])  76.4 us
    pallas_call x5, Pallas kernels, sandwich(): pl.pallas_call(functools.partial(split_dot, len(groups), len(groups[0][0]...  41.1 us
    ppermute x4, waiting for transfers between devices, shards(): streams[-d] = [lax.ppermute(x, 'energy', up[d - 1]) for x in streams[1 - d]]  37.5 us
    ppermute x12, waiting for transfers between devices, shards(): block = lax.ppermute(block, ('atom', 'kz'), pairs)  30.4 us
    ppermute x1, waiting for transfers between devices, shards(): lax.ppermute(got, 'grp', [(i, (i + d) % parts) for i in range(parts)])  11.6 us
    ppermute x4, starting transfers between devices, shards(): streams[-d] = [lax.ppermute(x, 'energy', up[d - 1]) for x in streams[1 - d]]  10.8 us
    ppermute x12, starting transfers between devices, shards(): block = lax.ppermute(block, ('atom', 'kz'), pairs)  10.4 us
    pallas_call x4, Pallas kernels, summed(): pl.pallas_call(functools.partial(add_momenta, theirs, piece * size), out_...  9.89 us
  transfers between devices with their start and end apart: 43, of which 16 were waited for; matrix products, arithmetic and copies ran while one was open for 1% of the time, Pallas kernels for 19%

profile of v6, /device:TPU:0, one launch (start us, length us, event | category | flops | bytes accessed | tf_op | source)
XLA Modules:
  0.0 286.3 jit_solution(2244329458673341571)
XLA Ops:
  0.0 1.9 constant_dynamic-slice_fusion
  1.9 3.0 %collective-permute-start = (f32[2,128,512]{2,1,0:T(8,128)}, f32[2,128,512]{2,1,0:T(8,128)}, u32[]{:S(2)}, u32[]{:S(2)}) collective-permute-start(f32[2,128,512]{2,1,0:T(8,128)} %constant_dynamic-slice_fusion), channel_id=1, source_target_pairs={{0,2},{2,0},{1,3},{3,1},{4,6},{6,4},{5,7},{7,5},{8,10},{10,8},{9,1... | collective-permute-start | bytes 1572872 | tf_op jit(solution)/shard_map/ppermute | solution.py:371
  4.9 2.3 add_momenta.4
  7.2 2.3 add_momenta.6
  10.1 7.0 %collective-permute-done.refs_0_ = f32[2,128,512]{2,1,0:T(8,128)} collective-permute-done((f32[2,128,512]{2,1,0:T(8,128)}, f32[2,128,512]{2,1,0:T(8,128)}, u32[]{:S(2)}, u32[]{:S(2)}) %collective-permute-start) | collective-permute-done | bytes 524320 | tf_op jit(solution)/shard_map/ppermute | solution.py:371
  17.1 1.8 collective-permute-start.2
  18.9 11.6 %collective-permute-done.2.refs_2_ = f32[2,128,512]{2,1,0:T(8,128)} collective-permute-done((f32[2,128,512]{2,1,0:T(8,128)}, f32[2,128,512]{2,1,0:T(8,128)}, u32[]{:S(2)}, u32[]{:S(2)}) %collective-permute-start.2) | collective-permute-done | bytes 524320 | tf_op jit(solution)/shard_map/ppermute | solution.py:373
  30.5 2.6 add_momenta.5.refs_8_.refs_0_
  33.2 4.5 %collective-permute-start.5 = (f32[4,128,512]{2,1,0:T(8,128)}, f32[4,128,512]{2,1,0:T(8,128)}, u32[]{:S(2)}, u32[]{:S(2)}) collective-permute-start(f32[4,128,512]{2,1,0:T(8,128)} %add_momenta.5.refs_8_.refs_0_), channel_id=1, source_target_pairs={{0,4},{4,8},{8,12},{1,5},{5,9},{9,13},{2,6},{6,10},{10,14},{3,7},{... | collective-permute-start | bytes 3145736 | tf_op jit(solution)/shard_map/ppermute | solution.py:354
  37.6 2.6 add_momenta.7.refs_9_.refs_1_
  40.3 2.6 collective-permute-start.8
  43.0 1.6 collective-permute-start.36
  45.0 15.4 %collective-permute-done.5.refs_4_ = f32[4,128,512]{2,1,0:T(8,128)} collective-permute-done((f32[4,128,512]{2,1,0:T(8,128)}, f32[4,128,512]{2,1,0:T(8,128)}, u32[]{:S(2)}, u32[]{:S(2)}) %collective-permute-start.5) | collective-permute-done | bytes 1048608 | tf_op jit(solution)/shard_map/ppermute | solution.py:354
  60.5 22.0 %collective-permute-done.8.refs_5_ = f32[4,128,512]{2,1,0:T(8,128)S(1)} collective-permute-done((f32[4,128,512]{2,1,0:T(8,128)}, f32[4,128,512]{2,1,0:T(8,128)S(1)}, u32[]{:S(2)}, u32[]{:S(2)}) %collective-permute-start.8) | collective-permute-done | bytes 1048608 | tf_op jit(solution)/shard_map/ppermute | solution.py:354
  83.8 1.3 collective-permute-start.17
  85.2 6.0 %collective-permute-done.37.refs_3_ = f32[4,128,512]{2,1,0:T(8,128)S(1)} collective-permute-done((f32[4,128,512]{2,1,0:T(8,128)}, f32[4,128,512]{2,1,0:T(8,128)S(1)}, u32[]{:S(2)}, u32[]{:S(2)}) %collective-permute-start.37) | collective-permute-done | bytes 1048608 | tf_op jit(solution)/shard_map/ppermute | solution.py:395
  92.4 1.6 copy-done.21
  94.0 3.0 %prepare.1 = (bf16[3,512,512]{2,1,0:T(8,128)(2,1)S(1)}, bf16[3,512,512]{2,1,0:T(8,128)(2,1)S(1)}, bf16[3,256,1536]{2,1,0:T(8,128)(2,1)S(1)}, bf16[3,512,768]{2,1,0:T(8,128)(2,1)S(1)}) custom-call(s32[3]{0:T(128)S(1)} %copy-done.25, f32[2,512,512]{2,1,0:T(8,128)S(1)} %copy-done.21, f32[2,128,512]{2,1,0:T(8,128)} %collective-permute-done.refs_0_, ...), custom_call_target="tpu_custom_call" | custom-call | flops 6291456 | bytes 7864320 | tf_op jit(solution)/shard_map/prepare/pallas_call | solution.py:380
  97.0 2.1 collective-permute-start.6
  99.1 11.9 %collective-permute-done.16.refs_12_ = f32[4,128,512]{2,1,0:T(8,128)S(1)} collective-permute-done((f32[4,128,512]{2,1,0:T(8,128)}, f32[4,128,512]{2,1,0:T(8,128)S(1)}, u32[]{:S(2)}, u32[]{:S(2)}) %collective-permute-start.16) | collective-permute-done | bytes 1048608 | tf_op jit(solution)/shard_map/ppermute | solution.py:355
  111.0 21.5 %collective-permute-done.17.refs_13_ = f32[4,128,512]{2,1,0:T(8,128)} collective-permute-done((f32[4,128,512]{2,1,0:T(8,128)}, f32[4,128,512]{2,1,0:T(8,128)}, u32[]{:S(2)}, u32[]{:S(2)}) %collective-permute-start.17) | collective-permute-done | bytes 1048608 | tf_op jit(solution)/shard_map/ppermute | solution.py:355
  132.5 1.6 collective-permute-start.9
  134.7 20.5 %far_sandwich.1 = (f32[4,128,512]{2,1,0:T(8,128)S(1)}, f32[4,128,512]{2,1,0:T(8,128)S(1)}) custom-call(s32[3]{0:T(128)S(1)} %guard.1.steps, f32[3]{0:T(128)S(1)} %copy-done.24, bf16[3,512,512]{2,1,0:T(8,128)(2,1)S(1)} %get-tuple-element.27.right_high, bf16[3,512,512]{2,1,0:T(8,128)(2,1)S(1)} %get-tuple-element.28.right_low, ...), custom_call_target="tpu_custom_call" | custom-call | flops 14495514624 | bytes 27262976 | tf_op jit(solution)/shard_map/far_sandwich/pallas_call | solution.py:204
  156.0 1.3 collective-permute-start.20
  162.1 1.6 collective-permute-start.10
  163.8 22.8 %collective-permute-done.20.refs_16_ = f32[4,128,512]{2,1,0:T(8,128)} collective-permute-done((f32[4,128,512]{2,1,0:T(8,128)S(1)}, f32[4,128,512]{2,1,0:T(8,128)}, u32[]{:S(2)}, u32[]{:S(2)}) %collective-permute-start.20) | collective-permute-done | bytes 1048608 | tf_op jit(solution)/shard_map/ppermute | solution.py:355
  186.6 1.6 collective-permute-start.11
  188.2 20.2 %collective-permute-done.21.refs_17_ = f32[4,128,512]{2,1,0:T(8,128)} collective-permute-done((f32[4,128,512]{2,1,0:T(8,128)}, f32[4,128,512]{2,1,0:T(8,128)}, u32[]{:S(2)}, u32[]{:S(2)}) %collective-permute-start.21) | collective-permute-done | bytes 1048608 | tf_op jit(solution)/shard_map/ppermute | solution.py:355
  208.4 1.9 collective-permute-start.22
  210.4 2.4 collective-permute-start.23
  212.8 2.6 copy_select_fusion.1
  215.9 1.6 collective-permute-start.41
  217.4 1.5 collective-permute-start.42
  222.7 5.1 %near_sandwich.5 = (f32[1,128,512]{2,1,0:T(8,128)S(1)}, f32[1,128,512]{2,1,0:T(8,128)S(1)}, f32[1,128,512]{2,1,0:T(8,128)S(1)}, f32[1,128,512]{2,1,0:T(8,128)S(1)}) custom-call(s32[3]{0:T(128)S(1)} %copy-done.23, f32[3]{0:T(128)S(1)} %copy-done.24, bf16[3,512,512]{2,1,0:T(8,128)(2,1)S(1)} %copy-done.4, bf16[3,512,512]{2,1,0:T(8,128)(2,1)S(1)} %copy-done.6, ...), custom_call_target="tpu_custom_call" | custom-call | flops 2415919104 | bytes 4194304 | tf_op jit(solution)/shard_map/near_sandwich/pallas_call | solution.py:204
  227.8 1.6 collective-permute-start.26
  229.4 5.1 %near_sandwich.6 = (f32[1,128,512]{2,1,0:T(8,128)S(1)}, f32[1,128,512]{2,1,0:T(8,128)S(1)}, f32[1,128,512]{2,1,0:T(8,128)S(1)}, f32[1,128,512]{2,1,0:T(8,128)S(1)}) custom-call(s32[3]{0:T(128)S(1)} %copy-done.23, f32[3]{0:T(128)S(1)} %copy-done.24, bf16[3,512,512]{2,1,0:T(8,128)(2,1)S(1)} %copy-done.4, bf16[3,512,512]{2,1,0:T(8,128)(2,1)S(1)} %copy-done.6, ...), custom_call_target="tpu_custom_call" | custom-call | flops 2415919104 | bytes 4194304 | tf_op jit(solution)/shard_map/near_sandwich/pallas_call | solution.py:204
  235.1 5.2 %near_sandwich.7 = (f32[1,128,512]{2,1,0:T(8,128)S(1)}, f32[1,128,512]{2,1,0:T(8,128)S(1)}, f32[1,128,512]{2,1,0:T(8,128)S(1)}, f32[1,128,512]{2,1,0:T(8,128)S(1)}) custom-call(s32[3]{0:T(128)S(1)} %copy-done.23, f32[3]{0:T(128)S(1)} %copy-done.24, bf16[3,512,512]{2,1,0:T(8,128)(2,1)S(1)} %copy-done.4, bf16[3,512,512]{2,1,0:T(8,128)(2,1)S(1)} %copy-done.6, ...), custom_call_target="tpu_custom_call" | custom-call | flops 2415919104 | bytes 4194304 | tf_op jit(solution)/shard_map/near_sandwich/pallas_call | solution.py:204
  240.3 1.6 collective-permute-start.28
  242.6 5.6 %collective-permute-done.28.refs_6_ = f32[1,128,512]{2,1,0:T(8,128)S(1)} collective-permute-done((f32[1,128,512]{2,1,0:T(8,128)S(1)}, f32[1,128,512]{2,1,0:T(8,128)S(1)}, u32[]{:S(2)}, u32[]{:S(2)}) %collective-permute-start.28) | collective-permute-done | bytes 262176 | tf_op jit(solution)/shard_map/ppermute | solution.py:435
  248.2 5.1 %near_sandwich.4 = (f32[1,128,512]{2,1,0:T(8,128)S(1)}, f32[1,128,512]{2,1,0:T(8,128)S(1)}, f32[1,128,512]{2,1,0:T(8,128)S(1)}, f32[1,128,512]{2,1,0:T(8,128)S(1)}) custom-call(s32[3]{0:T(128)S(1)} %copy-done.23, f32[3]{0:T(128)S(1)} %copy-done.24, bf16[3,512,512]{2,1,0:T(8,128)(2,1)S(1)} %copy-done.4, bf16[3,512,512]{2,1,0:T(8,128)(2,1)S(1)} %copy-done.6, ...), custom_call_target="tpu_custom_call" | custom-call | flops 2415919104 | bytes 4194304 | tf_op jit(solution)/shard_map/near_sandwich/pallas_call | solution.py:204
  256.9 5.4 %collective-permute-done.33.refs_11_ = f32[1,128,512]{2,1,0:T(8,128)S(1)} collective-permute-done((f32[1,128,512]{2,1,0:T(8,128)S(1)}, f32[1,128,512]{2,1,0:T(8,128)S(1)}, u32[]{:S(2)}, u32[]{:S(2)}) %collective-permute-start.33) | collective-permute-done | bytes 262176 | tf_op jit(solution)/shard_map/ppermute | solution.py:435
  262.3 1.5 collective-permute-start.24
  263.8 4.1 %collective-permute-done.34.refs_12_ = f32[1,128,512]{2,1,0:T(8,128)S(1)} collective-permute-done((f32[1,128,512]{2,1,0:T(8,128)S(1)}, f32[1,128,512]{2,1,0:T(8,128)S(1)}, u32[]{:S(2)}, u32[]{:S(2)}) %collective-permute-start.34) | collective-permute-done | bytes 262176 | tf_op jit(solution)/shard_map/ppermute | solution.py:435
  267.9 1.7 collective-permute-start.25
  269.6 3.9 %collective-permute-done.35.refs_13_ = f32[1,128,512]{2,1,0:T(8,128)S(1)} collective-permute-done((f32[1,128,512]{2,1,0:T(8,128)S(1)}, f32[1,128,512]{2,1,0:T(8,128)S(1)}, u32[]{:S(2)}, u32[]{:S(2)}) %collective-permute-start.35) | collective-permute-done | bytes 262176 | tf_op jit(solution)/shard_map/ppermute | solution.py:435
  274.1 5.5 %collective-permute-done.24.refs_0_ = f32[1,128,512]{2,1,0:T(8,128)S(1)} collective-permute-done((f32[1,128,512]{2,1,0:T(8,128)S(1)}, f32[1,128,512]{2,1,0:T(8,128)S(1)}, u32[]{:S(2)}, u32[]{:S(2)}) %collective-permute-start.24) | collective-permute-done | bytes 262176 | tf_op jit(solution)/shard_map/ppermute | solution.py:435
  279.7 5.1 %collective-permute-done.25.refs_1_ = f32[1,128,512]{2,1,0:T(8,128)S(1)} collective-permute-done((f32[1,128,512]{2,1,0:T(8,128)S(1)}, f32[1,128,512]{2,1,0:T(8,128)S(1)}, u32[]{:S(2)}, u32[]{:S(2)}) %collective-permute-start.25) | collective-permute-done | bytes 262176 | tf_op jit(solution)/shard_map/ppermute | solution.py:435
  284.7 1.4 shard_map.56
  (107 shorter events, 19.4 us)
Async XLA Ops:
  1.9 15.2 %collective-permute-start = (f32[2,128,512]{2,1,0:T(8,128)}, f32[2,128,512]{2,1,0:T(8,128)}, u32[]{:S(2)}, u32[]{:S(2)}) collective-permute-start(f32[2,128,512]{2,1,0:T(8,128)} %constant_dynamic-slice_fusion), channel_id=1, source_target_pairs={{0,2},{2,0},{1,3},{3,1},{4,6},{6,4},{5,7},{7,5},{8,10},{10,8},{9,1... | collective-permute-start | bytes 1572872 | tf_op jit(solution)/shard_map/ppermute | solution.py:371
  7.2 23.3 %collective-permute-start.4 = (f32[4,128,512]{2,1,0:T(8,128)}, f32[4,128,512]{2,1,0:T(8,128)}, u32[]{:S(2)}, u32[]{:S(2)}) collective-permute-start(f32[4,128,512]{2,1,0:T(8,128)} %add_momenta.4), channel_id=1, source_target_pairs={{0,1},{1,0},{2,3},{3,2},{4,5},{5,4},{6,7},{7,6},{8,9},{9,8},{10,11... | collective-permute-start | bytes 3145736 | tf_op jit(solution)/shard_map/ppermute | solution.py:343
  9.6 28.1 %collective-permute-start.7 = (f32[4,128,512]{2,1,0:T(8,128)}, f32[4,128,512]{2,1,0:T(8,128)}, u32[]{:S(2)}, u32[]{:S(2)}) collective-permute-start(f32[4,128,512]{2,1,0:T(8,128)} %add_momenta.6), channel_id=1, source_target_pairs={{0,1},{1,0},{2,3},{3,2},{4,5},{5,4},{6,7},{7,6},{8,9},{9,8},{10,11... | collective-permute-start | bytes 3145736 | tf_op jit(solution)/shard_map/ppermute | solution.py:343
  17.1 13.4 %collective-permute-start.2 = (f32[2,128,512]{2,1,0:T(8,128)}, f32[2,128,512]{2,1,0:T(8,128)}, u32[]{:S(2)}, u32[]{:S(2)}) collective-permute-start(f32[2,128,512]{2,1,0:T(8,128)} %collective-permute-done.refs_0_), channel_id=1, source_target_pairs={{0,16},{16,0},{1,17},{17,1},{2,18},{18,2},{3,19},{19,3},{4,20},{20... | collective-permute-start | bytes 1572872 | tf_op jit(solution)/shard_map/ppermute | solution.py:373
  18.9 24.1 %collective-permute-start.1 = (f32[2,128,512]{2,1,0:T(8,128)}, f32[2,128,512]{2,1,0:T(8,128)}, u32[]{:S(2)}, u32[]{:S(2)}) collective-permute-start(f32[2,128,512]{2,1,0:T(8,128)} %collective-permute-done.refs_0_), channel_id=1, source_target_pairs={{0,1},{1,0},{2,3},{3,2},{4,5},{5,4},{6,7},{7,6},{8,9},{9,8},{10,11... | collective-permute-start | bytes 1572872 | tf_op jit(solution)/shard_map/ppermute | solution.py:375
  30.5 14.0 %collective-permute-start.3 = (f32[2,128,512]{2,1,0:T(8,128)}, f32[2,128,512]{2,1,0:T(8,128)}, u32[]{:S(2)}, u32[]{:S(2)}) collective-permute-start(f32[2,128,512]{2,1,0:T(8,128)} %collective-permute-done.2.refs_2_), channel_id=1, source_target_pairs={{0,1},{1,0},{2,3},{3,2},{4,5},{5,4},{6,7},{7,6},{8,9},{9,8},{10,11... | collective-permute-start | bytes 1572872 | tf_op jit(solution)/shard_map/ppermute | solution.py:375
  33.2 58.0 %copy-start.23 = (s32[3]{0:T(128)S(1)}, s32[3]{0:T(128)}, u32[]{:S(2)}) copy-start(s32[3]{0:T(128)} %steps.9) | copy-start | bytes 40
  33.2 59.2 %copy-start.25 = (s32[3]{0:T(128)S(1)}, s32[3]{0:T(128)}, u32[]{:S(2)}) copy-start(s32[3]{0:T(128)} %owners.1) | copy-start | bytes 40
  33.2 27.3 %collective-permute-start.5 = (f32[4,128,512]{2,1,0:T(8,128)}, f32[4,128,512]{2,1,0:T(8,128)}, u32[]{:S(2)}, u32[]{:S(2)}) collective-permute-start(f32[4,128,512]{2,1,0:T(8,128)} %add_momenta.5.refs_8_.refs_0_), channel_id=1, source_target_pairs={{0,4},{4,8},{8,12},{1,5},{5,9},{9,13},{2,6},{6,10},{10,14},{3,7},{... | collective-permute-start | bytes 3145736 | tf_op jit(solution)/shard_map/ppermute | solution.py:354
  40.3 42.2 %collective-permute-start.8 = (f32[4,128,512]{2,1,0:T(8,128)}, f32[4,128,512]{2,1,0:T(8,128)S(1)}, u32[]{:S(2)}, u32[]{:S(2)}) collective-permute-start(f32[4,128,512]{2,1,0:T(8,128)} %add_momenta.7.refs_9_.refs_1_), channel_id=1, source_target_pairs={{0,4},{4,8},{8,12},{1,5},{5,9},{9,13},{2,6},{6,10},{10,14},{3,7},{... | collective-permute-start | bytes 3145736 | tf_op jit(solution)/shard_map/ppermute | solution.py:354
  42.9 40.9 %collective-permute-start.14 = (f32[4,128,512]{2,1,0:T(8,128)}, f32[4,128,512]{2,1,0:T(8,128)S(1)}, u32[]{:S(2)}, u32[]{:S(2)}) collective-permute-start(f32[4,128,512]{2,1,0:T(8,128)} %add_momenta.5.refs_8_.refs_0_), channel_id=1, source_target_pairs={{0,1},{1,0},{2,3},{3,2},{4,5},{5,4},{6,7},{7,6},{8,9},{9,8},{10,11... | collective-permute-start | bytes 3145736 | tf_op jit(solution)/shard_map/ppermute | solution.py:364
  43.0 42.2 %collective-permute-start.36 = (f32[4,128,512]{2,1,0:T(8,128)}, f32[4,128,512]{2,1,0:T(8,128)S(1)}, u32[]{:S(2)}, u32[]{:S(2)}) collective-permute-start(f32[4,128,512]{2,1,0:T(8,128)} %add_momenta.5.refs_8_.refs_0_), channel_id=1, source_target_pairs={{0,2},{2,0},{1,3},{3,1},{4,6},{6,4},{5,7},{7,5},{8,10},{10,8},{9,1... | collective-permute-start | bytes 3145736 | tf_op jit(solution)/shard_map/ppermute | solution.py:395
  44.5 46.7 %collective-permute-start.37 = (f32[4,128,512]{2,1,0:T(8,128)}, f32[4,128,512]{2,1,0:T(8,128)S(1)}, u32[]{:S(2)}, u32[]{:S(2)}) collective-permute-start(f32[4,128,512]{2,1,0:T(8,128)} %add_momenta.7.refs_9_.refs_1_), channel_id=1, source_target_pairs={{0,2},{2,0},{1,3},{3,1},{4,6},{6,4},{5,7},{7,5},{8,10},{10,8},{9,1... | collective-permute-start | bytes 3145736 | tf_op jit(solution)/shard_map/ppermute | solution.py:395
  60.5 36.5 %collective-permute-start.15 = (f32[4,128,512]{2,1,0:T(8,128)}, f32[4,128,512]{2,1,0:T(8,128)S(1)}, u32[]{:S(2)}, u32[]{:S(2)}) collective-permute-start(f32[4,128,512]{2,1,0:T(8,128)} %add_momenta.7.refs_9_.refs_1_), channel_id=1, source_target_pairs={{0,1},{1,0},{2,3},{3,2},{4,5},{5,4},{6,7},{7,6},{8,9},{9,8},{10,11... | collective-permute-start | bytes 3145736 | tf_op jit(solution)/shard_map/ppermute | solution.py:364
  82.5 28.5 %collective-permute-start.16 = (f32[4,128,512]{2,1,0:T(8,128)}, f32[4,128,512]{2,1,0:T(8,128)S(1)}, u32[]{:S(2)}, u32[]{:S(2)}) collective-permute-start(f32[4,128,512]{2,1,0:T(8,128)} %add_momenta.5.refs_8_.refs_0_), channel_id=1, source_target_pairs={{12,8},{8,4},{4,0},{13,9},{9,5},{5,1},{14,10},{10,6},{6,2},{15,11}... | collective-permute-start | bytes 3145736 | tf_op jit(solution)/shard_map/ppermute | solution.py:355
  83.8 48.7 %collective-permute-start.17 = (f32[4,128,512]{2,1,0:T(8,128)}, f32[4,128,512]{2,1,0:T(8,128)}, u32[]{:S(2)}, u32[]{:S(2)}) collective-permute-start(f32[4,128,512]{2,1,0:T(8,128)} %add_momenta.7.refs_9_.refs_1_), channel_id=1, source_target_pairs={{12,8},{8,4},{4,0},{13,9},{9,5},{5,1},{14,10},{10,6},{6,2},{15,11}... | collective-permute-start | bytes 3145736 | tf_op jit(solution)/shard_map/ppermute | solution.py:355
  85.1 49.0 %collective-permute-start.38 = (f32[4,128,512]{2,1,0:T(8,128)S(1)}, f32[4,128,512]{2,1,0:T(8,128)S(1)}, u32[]{:S(2)}, u32[]{:S(2)}) collective-permute-start(f32[4,128,512]{2,1,0:T(8,128)S(1)} %collective-permute-done.36.refs_2_), channel_id=1, source_target_pairs={{0,1},{1,0},{2,3},{3,2},{4,5},{5,4},{6,7},{7,6},{8,9},{9,8},{10,11... | collective-permute-start | bytes 3145736 | tf_op jit(solution)/shard_map/ppermute | solution.py:398
  91.2 43.0 %collective-permute-start.39 = (f32[4,128,512]{2,1,0:T(8,128)S(1)}, f32[4,128,512]{2,1,0:T(8,128)S(1)}, u32[]{:S(2)}, u32[]{:S(2)}) collective-permute-start(f32[4,128,512]{2,1,0:T(8,128)S(1)} %collective-permute-done.37.refs_3_), channel_id=1, source_target_pairs={{0,1},{1,0},{2,3},{3,2},{4,5},{5,4},{6,7},{7,6},{8,9},{9,8},{10,11... | collective-permute-start | bytes 3145736 | tf_op jit(solution)/shard_map/ppermute | solution.py:398
  97.0 58.3 %copy-start.3 = (bf16[3,512,512]{2,1,0:T(8,128)(2,1)}, bf16[3,512,512]{2,1,0:T(8,128)(2,1)S(1)}, u32[]{:S(2)}) copy-start(bf16[3,512,512]{2,1,0:T(8,128)(2,1)S(1)} %get-tuple-element.27.right_high) | copy-start | bytes 4718596
  97.0 58.3 %copy-start.5 = (bf16[3,512,512]{2,1,0:T(8,128)(2,1)}, bf16[3,512,512]{2,1,0:T(8,128)(2,1)S(1)}, u32[]{:S(2)}) copy-start(bf16[3,512,512]{2,1,0:T(8,128)(2,1)S(1)} %get-tuple-element.28.right_low) | copy-start | bytes 4718596
  97.0 58.3 %copy-start.11 = (f32[4,128,512]{2,1,0:T(8,128)}, f32[4,128,512]{2,1,0:T(8,128)S(1)}, u32[]{:S(2)}) copy-start(f32[4,128,512]{2,1,0:T(8,128)S(1)} %collective-permute-done.15.refs_11_.refs_5_) | copy-start | bytes 3145732
  97.0 59.0 %collective-permute-start.6 = (f32[4,128,512]{2,1,0:T(8,128)}, f32[4,128,512]{2,1,0:T(8,128)}, u32[]{:S(2)}, u32[]{:S(2)}) collective-permute-start(f32[4,128,512]{2,1,0:T(8,128)} %collective-permute-done.5.refs_4_), channel_id=1, source_target_pairs={{4,8},{8,12},{5,9},{9,13},{6,10},{10,14},{7,11},{11,15},{20,24},{2... | collective-permute-start | bytes 3145736 | tf_op jit(solution)/shard_map/ppermute | solution.py:354
  111.0 47.6 %collective-permute-start.12 = (f32[4,128,512]{2,1,0:T(8,128)}, f32[4,128,512]{2,1,0:T(8,128)S(1)}, u32[]{:S(2)}, u32[]{:S(2)}) collective-permute-start(f32[4,128,512]{2,1,0:T(8,128)} %collective-permute-done.5.refs_4_), channel_id=1, source_target_pairs={{0,1},{1,0},{2,3},{3,2},{4,5},{5,4},{6,7},{7,6},{8,9},{9,8},{10,11... | collective-permute-start | bytes 3145736 | tf_op jit(solution)/shard_map/ppermute | solution.py:364
  132.5 24.8 %collective-permute-start.9 = (f32[4,128,512]{2,1,0:T(8,128)S(1)}, f32[4,128,512]{2,1,0:T(8,128)}, u32[]{:S(2)}, u32[]{:S(2)}) collective-permute-start(f32[4,128,512]{2,1,0:T(8,128)S(1)} %collective-permute-done.8.refs_5_), channel_id=1, source_target_pairs={{4,8},{8,12},{5,9},{9,13},{6,10},{10,14},{7,11},{11,15},{20,24},{2... | collective-permute-start | bytes 3145736 | tf_op jit(solution)/shard_map/ppermute | solution.py:354
  134.2 25.5 %collective-permute-start.13 = (f32[4,128,512]{2,1,0:T(8,128)S(1)}, f32[4,128,512]{2,1,0:T(8,128)S(1)}, u32[]{:S(2)}, u32[]{:S(2)}) collective-permute-start(f32[4,128,512]{2,1,0:T(8,128)S(1)} %collective-permute-done.8.refs_5_), channel_id=1, source_target_pairs={{0,1},{1,0},{2,3},{3,2},{4,5},{5,4},{6,7},{7,6},{8,9},{9,8},{10,11... | collective-permute-start | bytes 3145736 | tf_op jit(solution)/shard_map/ppermute | solution.py:364
  134.2 26.9 %collective-permute-start.18 = (f32[4,128,512]{2,1,0:T(8,128)S(1)}, f32[4,128,512]{2,1,0:T(8,128)S(1)}, u32[]{:S(2)}, u32[]{:S(2)}) collective-permute-start(f32[4,128,512]{2,1,0:T(8,128)S(1)} %collective-permute-done.16.refs_12_), channel_id=1, source_target_pairs={{0,1},{1,0},{2,3},{3,2},{4,5},{5,4},{6,7},{7,6},{8,9},{9,8},{10,11... | collective-permute-start | bytes 3145736 | tf_op jit(solution)/shard_map/ppermute | solution.py:364
  156.0 30.6 %collective-permute-start.20 = (f32[4,128,512]{2,1,0:T(8,128)S(1)}, f32[4,128,512]{2,1,0:T(8,128)}, u32[]{:S(2)}, u32[]{:S(2)}) collective-permute-start(f32[4,128,512]{2,1,0:T(8,128)S(1)} %collective-permute-done.16.refs_12_), channel_id=1, source_target_pairs={{8,4},{4,0},{9,5},{5,1},{10,6},{6,2},{11,7},{7,3},{24,20},{20,16},... | collective-permute-start | bytes 3145736 | tf_op jit(solution)/shard_map/ppermute | solution.py:355
  157.3 51.1 %collective-permute-start.21 = (f32[4,128,512]{2,1,0:T(8,128)}, f32[4,128,512]{2,1,0:T(8,128)}, u32[]{:S(2)}, u32[]{:S(2)}) collective-permute-start(f32[4,128,512]{2,1,0:T(8,128)} %collective-permute-done.17.refs_13_), channel_id=1, source_target_pairs={{8,4},{4,0},{9,5},{5,1},{10,6},{6,2},{11,7},{7,3},{24,20},{20,16},... | collective-permute-start | bytes 3145736 | tf_op jit(solution)/shard_map/ppermute | solution.py:355
  159.6 50.7 %collective-permute-start.40 = (f32[4,128,512]{2,0,1:T(4,128)S(1)}, f32[4,128,512]{2,0,1:T(4,128)}, u32[]{:S(2)}, u32[]{:S(2)}) collective-permute-start(f32[4,128,512]{2,0,1:T(4,128)S(1)} %copy.6), channel_id=1, source_target_pairs={{0,1},{1,0},{2,3},{3,2},{4,5},{5,4},{6,7},{7,6},{8,9},{9,8},{10,11... | collective-permute-start | bytes 3145736 | tf_op jit(solution)/shard_map/ppermute | solution.py:412
  160.7 55.2 %collective-permute-start.19 = (f32[4,128,512]{2,1,0:T(8,128)}, f32[4,128,512]{2,1,0:T(8,128)}, u32[]{:S(2)}, u32[]{:S(2)}) collective-permute-start(f32[4,128,512]{2,1,0:T(8,128)} %collective-permute-done.17.refs_13_), channel_id=1, source_target_pairs={{0,1},{1,0},{2,3},{3,2},{4,5},{5,4},{6,7},{7,6},{8,9},{9,8},{10,11... | collective-permute-start | bytes 3145736 | tf_op jit(solution)/shard_map/ppermute | solution.py:364
  162.1 55.3 %collective-permute-start.10 = (f32[4,128,512]{2,1,0:T(8,128)}, f32[4,128,512]{2,1,0:T(8,128)}, u32[]{:S(2)}, u32[]{:S(2)}) collective-permute-start(f32[4,128,512]{2,1,0:T(8,128)} %collective-permute-done.6.refs_0_), channel_id=1, source_target_pairs={{8,9},{9,8},{12,13},{13,12},{10,11},{11,10},{14,15},{15,14},{24,25... | collective-permute-start | bytes 3145736 | tf_op jit(solution)/shard_map/ppermute | solution.py:364
  186.6 32.4 %collective-permute-start.11 = (f32[4,128,512]{2,1,0:T(8,128)}, f32[4,128,512]{2,1,0:T(8,128)}, u32[]{:S(2)}, u32[]{:S(2)}) collective-permute-start(f32[4,128,512]{2,1,0:T(8,128)} %collective-permute-done.9.refs_1_), channel_id=1, source_target_pairs={{8,9},{9,8},{12,13},{13,12},{10,11},{11,10},{14,15},{15,14},{24,25... | collective-permute-start | bytes 3145736 | tf_op jit(solution)/shard_map/ppermute | solution.py:364
  208.4 10.5 %collective-permute-start.22 = (f32[4,128,512]{2,1,0:T(8,128)}, f32[4,128,512]{2,1,0:T(8,128)}, u32[]{:S(2)}, u32[]{:S(2)}) collective-permute-start(f32[4,128,512]{2,1,0:T(8,128)} %collective-permute-done.20.refs_16_), channel_id=1, source_target_pairs={{0,1},{1,0},{4,5},{5,4},{2,3},{3,2},{6,7},{7,6},{16,17},{17,16},{2... | collective-permute-start | bytes 3145736 | tf_op jit(solution)/shard_map/ppermute | solution.py:364
  210.4 8.6 %collective-permute-start.23 = (f32[4,128,512]{2,1,0:T(8,128)}, f32[4,128,512]{2,1,0:T(8,128)}, u32[]{:S(2)}, u32[]{:S(2)}) collective-permute-start(f32[4,128,512]{2,1,0:T(8,128)} %collective-permute-done.21.refs_17_), channel_id=1, source_target_pairs={{0,1},{1,0},{4,5},{5,4},{2,3},{3,2},{6,7},{7,6},{16,17},{17,16},{2... | collective-permute-start | bytes 3145736 | tf_op jit(solution)/shard_map/ppermute | solution.py:364
  215.9 68.9 %collective-permute-start.41 = (f32[128,8,512]{2,1,0:T(8,128)S(1)}, f32[128,8,512]{2,1,0:T(8,128)S(1)}, u32[]{:S(2)}, u32[]{:S(2)}) collective-permute-start(f32[128,8,512]{2,1,0:T(8,128)S(1)} %maximum_bitcast_fusion), channel_id=1, source_target_pairs={{0,12},{1,13},{2,14},{3,15},{16,28},{17,29},{18,30},{19,31}} | collective-permute-start | bytes 6291464 | tf_op jit(solution)/shard_map/ppermute | solution.py:416
  217.4 67.3 %collective-permute-start.42 = (f32[128,8,512]{2,1,0:T(8,128)S(1)}, f32[128,8,512]{2,1,0:T(8,128)S(1)}, u32[]{:S(2)}, u32[]{:S(2)}) collective-permute-start(f32[128,8,512]{2,1,0:T(8,128)S(1)} %maximum_bitcast_fusion), channel_id=1, source_target_pairs={{12,0},{13,1},{14,2},{15,3},{28,16},{29,17},{30,18},{31,19}} | collective-permute-start | bytes 6291464 | tf_op jit(solution)/shard_map/ppermute | solution.py:417
  227.8 14.0 %collective-permute-start.26 = (f32[1,128,512]{2,1,0:T(8,128)S(1)}, f32[1,128,512]{2,1,0:T(8,128)S(1)}, u32[]{:S(2)}, u32[]{:S(2)}) collective-permute-start(f32[1,128,512]{2,1,0:T(8,128)S(1)} %get-tuple-element.36), channel_id=1, source_target_pairs={{0,2},{1,3},{2,0},{3,1},{4,6},{5,7},{6,4},{7,5},{8,10},{9,11},{10,... | collective-permute-start | bytes 786440 | tf_op jit(solution)/shard_map/ppermute | solution.py:435
  234.5 8.1 %collective-permute-start.27 = (f32[1,128,512]{2,1,0:T(8,128)S(1)}, f32[1,128,512]{2,1,0:T(8,128)S(1)}, u32[]{:S(2)}, u32[]{:S(2)}) collective-permute-start(f32[1,128,512]{2,1,0:T(8,128)S(1)} %get-tuple-element.37), channel_id=1, source_target_pairs={{0,2},{1,3},{2,0},{3,1},{4,6},{5,7},{6,4},{7,5},{8,10},{9,11},{10,... | collective-permute-start | bytes 786440 | tf_op jit(solution)/shard_map/ppermute | solution.py:435
  240.3 7.9 %collective-permute-start.28 = (f32[1,128,512]{2,1,0:T(8,128)S(1)}, f32[1,128,512]{2,1,0:T(8,128)S(1)}, u32[]{:S(2)}, u32[]{:S(2)}) collective-permute-start(f32[1,128,512]{2,1,0:T(8,128)S(1)} %get-tuple-element.38), channel_id=1, source_target_pairs={{0,2},{1,3},{2,0},{3,1},{4,6},{5,7},{6,4},{7,5},{8,10},{9,11},{10,... | collective-permute-start | bytes 786440 | tf_op jit(solution)/shard_map/ppermute | solution.py:435
  241.9 11.5 %collective-permute-start.29 = (f32[1,128,512]{2,1,0:T(8,128)S(1)}, f32[1,128,512]{2,1,0:T(8,128)S(1)}, u32[]{:S(2)}, u32[]{:S(2)}) collective-permute-start(f32[1,128,512]{2,1,0:T(8,128)S(1)} %get-tuple-element.39), channel_id=1, source_target_pairs={{0,1},{1,0},{2,3},{3,2},{4,5},{5,4},{6,7},{7,6},{8,9},{9,8},{10,11... | collective-permute-start | bytes 786440 | tf_op jit(solution)/shard_map/ppermute | solution.py:435
  242.6 11.3 %collective-permute-start.30 = (f32[1,128,512]{2,1,0:T(8,128)S(1)}, f32[1,128,512]{2,1,0:T(8,128)S(1)}, u32[]{:S(2)}, u32[]{:S(2)}) collective-permute-start(f32[1,128,512]{2,1,0:T(8,128)S(1)} %get-tuple-element.40), channel_id=1, source_target_pairs={{0,1},{1,0},{2,3},{3,2},{4,5},{5,4},{6,7},{7,6},{8,9},{9,8},{10,11... | collective-permute-start | bytes 786440 | tf_op jit(solution)/shard_map/ppermute | solution.py:435
  248.2 6.9 %collective-permute-start.31 = (f32[1,128,512]{2,1,0:T(8,128)S(1)}, f32[1,128,512]{2,1,0:T(8,128)S(1)}, u32[]{:S(2)}, u32[]{:S(2)}) collective-permute-start(f32[1,128,512]{2,1,0:T(8,128)S(1)} %get-tuple-element.41), channel_id=1, source_target_pairs={{0,1},{1,0},{2,3},{3,2},{4,5},{5,4},{6,7},{7,6},{8,9},{9,8},{10,11... | collective-permute-start | bytes 786440 | tf_op jit(solution)/shard_map/ppermute | solution.py:435
  253.4 2.3 collective-permute-start.32
  253.9 8.3 %collective-permute-start.33 = (f32[1,128,512]{2,1,0:T(8,128)S(1)}, f32[1,128,512]{2,1,0:T(8,128)S(1)}, u32[]{:S(2)}, u32[]{:S(2)}) collective-permute-start(f32[1,128,512]{2,1,0:T(8,128)S(1)} %get-tuple-element.43), channel_id=1, source_target_pairs={{0,3},{1,2},{2,1},{3,0},{4,7},{5,6},{6,5},{7,4},{8,11},{9,10},{10,... | collective-permute-start | bytes 786440 | tf_op jit(solution)/shard_map/ppermute | solution.py:435
  255.1 12.8 %collective-permute-start.34 = (f32[1,128,512]{2,1,0:T(8,128)S(1)}, f32[1,128,512]{2,1,0:T(8,128)S(1)}, u32[]{:S(2)}, u32[]{:S(2)}) collective-permute-start(f32[1,128,512]{2,1,0:T(8,128)S(1)} %get-tuple-element.44), channel_id=1, source_target_pairs={{0,3},{1,2},{2,1},{3,0},{4,7},{5,6},{6,5},{7,4},{8,11},{9,10},{10,... | collective-permute-start | bytes 786440 | tf_op jit(solution)/shard_map/ppermute | solution.py:435
  255.7 17.8 %collective-permute-start.35 = (f32[1,128,512]{2,1,0:T(8,128)S(1)}, f32[1,128,512]{2,1,0:T(8,128)S(1)}, u32[]{:S(2)}, u32[]{:S(2)}) collective-permute-start(f32[1,128,512]{2,1,0:T(8,128)S(1)} %get-tuple-element.45), channel_id=1, source_target_pairs={{0,3},{1,2},{2,1},{3,0},{4,7},{5,6},{6,5},{7,4},{8,11},{9,10},{10,... | collective-permute-start | bytes 786440 | tf_op jit(solution)/shard_map/ppermute | solution.py:435
  262.3 17.4 %collective-permute-start.24 = (f32[1,128,512]{2,1,0:T(8,128)S(1)}, f32[1,128,512]{2,1,0:T(8,128)S(1)}, u32[]{:S(2)}, u32[]{:S(2)}) collective-permute-start(f32[1,128,512]{2,1,0:T(8,128)S(1)} %get-tuple-element.30), channel_id=1, source_target_pairs={{0,2},{1,3},{2,0},{3,1},{4,6},{5,7},{6,4},{7,5},{8,10},{9,11},{10,... | collective-permute-start | bytes 786440 | tf_op jit(solution)/shard_map/ppermute | solution.py:435
  267.9 16.9 %collective-permute-start.25 = (f32[1,128,512]{2,1,0:T(8,128)S(1)}, f32[1,128,512]{2,1,0:T(8,128)S(1)}, u32[]{:S(2)}, u32[]{:S(2)}) collective-permute-start(f32[1,128,512]{2,1,0:T(8,128)S(1)} %get-tuple-element.31), channel_id=1, source_target_pairs={{0,3},{1,2},{2,1},{3,0},{4,7},{5,6},{6,5},{7,4},{8,11},{9,10},{10,... | collective-permute-start | bytes 786440 | tf_op jit(solution)/shard_map/ppermute | solution.py:435
  (21 other events, 344.9 us)

commit v7 on v6

--- a/solution.py
+++ b/solution.py
@@ -72,6 +72,8 @@
 def add_momenta(theirs, first, green, *refs):
     out, held, total, arrived, left = refs[-5:]
     given = refs[:-5]
+    if theirs:
+        total = out
     momenta, count, size = green.shape[0], held.shape[0], held.shape[2]
     core = lax.axis_index("kz")
     base = (1 - core if theirs else core) * count
@@ -88,9 +90,10 @@
         for k in range(1, held.shape[1]):
             value = value + held[e, k]
         total[e] = value
-        pltpu.make_async_copy(total.at[e], out.at[e], left.at[e]).start()
-
-    for e in range(count):
+        if not theirs:
+            pltpu.make_async_copy(total.at[e], out.at[e], left.at[e]).start()
+
+    for e in range(0 if theirs else count):
         pltpu.make_async_copy(total.at[e], out.at[e], left.at[e]).wait()
 
 
@@ -99,8 +102,8 @@
         [refs[(g * 2 + h) * n_parts : (g * 2 + h + 1) * n_parts] for h in range(2)]
         for g in range(n_groups)
     ]
-    outs = refs[n_groups * 2 * n_parts : -3]
-    planes, inner, sems = refs[-3:]
+    outs = refs[n_groups * 2 * n_parts : -4]
+    planes, inner, total, sems = refs[-4:]
     count, size = outs[0].shape[:2]
     rows = planes.shape[2]
     half_planes = edev // 2
@@ -172,6 +175,15 @@
                 pltpu.make_async_copy(held, held, sems.at[buffer, slot]).wait()
                 scales.append(jnp.where(source_of(energy, mode, side)[0], (occupation[mode] + (1.0 - side)) * (1.0 / momenta), 0.0))
             combined = scales[0] * planes[buffer, 2 * mode] + scales[1] * planes[buffer, 2 * mode + 1]
+            if far:
+                high, low = halves(combined)
+                inner[mode, pl.ds(0, rows)] = high
+                inner[mode, pl.ds(rows, rows)] = low
+                inner[mode, pl.ds(2 * rows, rows)] = high
+                high, low = halves(dot(left[mode], inner[mode]))
+                term = dot(high, right_high[mode]) + dot(low, right_high[mode]) + dot(high, right_low[mode])
+                total[...] = term if mode == 0 else total[...] + term
+                continue
             high = combined.astype(jnp.bfloat16)
             low = (combined - high.astype(jnp.float32)).astype(jnp.bfloat16)
             product = dot(high, right_high[mode]) + dot(low, right_high[mode]) + dot(high, right_low[mode])
@@ -183,13 +195,15 @@
         for index, out in enumerate(outs):
             s, t = index // 2, index % 2
             block = lax.rem(core + t, 2)
-            if not far:
-                block = block + 2 * lax.rem(atom + s, n_atoms)
+            if far:
+                out[energy] = total[pl.ds(pl.multiple_of(block * size, 8), size)]
+                continue
+            block = block + 2 * lax.rem(atom + s, n_atoms)
             where = pl.ds(pl.multiple_of(block * size, 8), size)
-            total = dot(left[0, where], inner[0])
+            result = dot(left[0, where], inner[0])
             for mode in range(1, MODES):
-                total = total + dot(left[mode, where], inner[mode])
-            out[energy] = total
+                result = result + dot(left[mode, where], inner[mode])
+            out[energy] = result
 
 
 def sandwich(steps, occupation, right, left, groups, n_atoms, momenta, base, grid_total, edev, far, line, out_rows, count):
@@ -211,6 +225,7 @@
         scratch_shapes=[
             pltpu.VMEM((buffers, 2 * MODES, rows, order), jnp.float32),
             pltpu.VMEM((MODES, 3 * rows, order), jnp.bfloat16),
+            pltpu.VMEM((left.shape[1] if far else 8, order), jnp.float32),
             pltpu.SemaphoreType.DMA((2, 2 * MODES)),
         ],
         compiler_params=pltpu.CompilerParams(vmem_limit_bytes=held),
@@ -321,14 +336,14 @@
             functools.partial(add_momenta, theirs, piece * size),
             out_shape=jax.ShapeDtypeStruct((half, size, order), jnp.float32),
             in_specs=[pl.BlockSpec(memory_space=pltpu.HBM)] * (1 + len(more)),
-            out_specs=pl.BlockSpec(memory_space=pltpu.HBM),
+            out_specs=pl.BlockSpec(memory_space=pltpu.VMEM if theirs else pltpu.HBM),
             scratch_shapes=[
                 pltpu.VMEM((half, momenta_here + len(more), size, order), jnp.float32),
-                pltpu.VMEM((half, size, order), jnp.float32),
+                pltpu.VMEM((8, order) if theirs else (half, size, order), jnp.float32),
                 pltpu.SemaphoreType.DMA((half,)),
                 pltpu.SemaphoreType.DMA((half,)),
             ],
-            compiler_params=pltpu.CompilerParams(vmem_limit_bytes=67_000_000),
+            compiler_params=pltpu.CompilerParams(vmem_limit_bytes=8 << 20 if theirs else 67_000_000),
             cost_estimate=pl.CostEstimate(
                 flops=momenta_here * half * size * order,
                 bytes_accessed=4 * (momenta_here + 1 + len(more)) * half * size * order,

time: 287 us -> 281 us (0.979)
  Pallas kernels: 57.1 us -> 49.3 us
    pallas_call x5, Pallas kernels: 41.1 us -> 36.1 us  [sandwich(): pl.pallas_call(functools.partial(split_dot, len(groups), len(groups[0][0]...]
    unnamed x52 -> x54, local copies, waits for them, and re-layouts: 8.32 us -> 11.7 us
    pallas_call x4, Pallas kernels: 9.89 us -> 6.94 us  [summed(): pl.pallas_call(functools.partial(add_momenta, theirs, piece * size), out_...]
  transfers between devices with their start and end apart: 43 -> 43, of which waited for: 16 -> 16; matrix products, arithmetic and copies ran while one was open for 1% -> 1% of each run, Pallas kernels for 19% -> 17%
where the time goes in v7:
time: 281 us
  waiting for transfers between devices  169 us (60%)
  Pallas kernels  49.3 us (18%)
  starting transfers between devices  44.9 us (16%)
  local copies, waits for them, and re-layouts  13.4 us (5%)
  other arithmetic  3 us (1%)
    ppermute x4, waiting for transfers between devices, shards(): lax.ppermute(x, 'energy', down[d - 1])  76.5 us
    ppermute x4, waiting for transfers between devices, shards(): streams[-d] = [lax.ppermute(x, 'energy', up[d - 1]) for x in streams[1 - d]]  37.4 us
    pallas_call x5, Pallas kernels, sandwich(): pl.pallas_call(functools.partial(split_dot, len(groups), len(groups[0][0]...  36.1 us
    ppermute x12, waiting for transfers between devices, shards(): block = lax.ppermute(block, ('atom', 'kz'), pairs)  31.2 us
    unnamed x54, local copies, waits for them, and re-layouts  11.7 us
    ppermute x1, waiting for transfers between devices, shards(): lax.ppermute(got, 'grp', [(i, (i + d) % parts) for i in range(parts)])  11.6 us
    ppermute x4, starting transfers between devices, shards(): streams[-d] = [lax.ppermute(x, 'energy', up[d - 1]) for x in streams[1 - d]]  10.8 us
    ppermute x12, starting transfers between devices, shards(): block = lax.ppermute(block, ('atom', 'kz'), pairs)  9.93 us
  transfers between devices with their start and end apart: 43, of which 16 were waited for; matrix products, arithmetic and copies ran while one was open for 1% of the time, Pallas kernels for 17%

profile of v7, /device:TPU:0, one launch (start us, length us, event | category | flops | bytes accessed | tf_op | source)
XLA Modules:
  0.0 280.5 jit_solution(2167082266805603613)
XLA Ops:
  1.1 3.0 %collective-permute-start = (f32[2,128,512]{2,1,0:T(8,128)S(1)}, f32[2,128,512]{2,1,0:T(8,128)}, u32[]{:S(2)}, u32[]{:S(2)}) collective-permute-start(f32[2,128,512]{2,1,0:T(8,128)S(1)} %constant_dynamic-slice_fusion), channel_id=1, source_target_pairs={{0,2},{2,0},{1,3},{3,1},{4,6},{6,4},{5,7},{7,5},{8,10},{10,8},{9,1... | collective-permute-start | bytes 1572872 | tf_op jit(solution)/shard_map/ppermute | solution.py:386
  4.1 3.4 %copy-done = f32[2,8,256,512]{3,2,1,0:T(8,128)S(1)} copy-done((f32[2,8,256,512]{3,2,1,0:T(8,128)S(1)}, f32[2,8,256,512]{3,2,1,0:T(8,128)}, u32[]{:S(2)}) %copy-start) | copy-done | bytes 8388632
  7.9 1.3 add_momenta.6
  9.8 6.3 %collective-permute-done.refs_0_ = f32[2,128,512]{2,1,0:T(8,128)} collective-permute-done((f32[2,128,512]{2,1,0:T(8,128)S(1)}, f32[2,128,512]{2,1,0:T(8,128)}, u32[]{:S(2)}, u32[]{:S(2)}) %collective-permute-start) | collective-permute-done | bytes 524320 | tf_op jit(solution)/shard_map/ppermute | solution.py:386
  16.1 1.8 collective-permute-start.2
  17.9 11.6 %collective-permute-done.2.refs_2_ = f32[2,128,512]{2,1,0:T(8,128)} collective-permute-done((f32[2,128,512]{2,1,0:T(8,128)}, f32[2,128,512]{2,1,0:T(8,128)}, u32[]{:S(2)}, u32[]{:S(2)}) %collective-permute-start.2) | collective-permute-done | bytes 524320 | tf_op jit(solution)/shard_map/ppermute | solution.py:388
  29.6 2.6 add_momenta.5.refs_8_.refs_0_
  32.2 4.4 %collective-permute-start.5 = (f32[4,128,512]{2,1,0:T(8,128)}, f32[4,128,512]{2,1,0:T(8,128)}, u32[]{:S(2)}, u32[]{:S(2)}) collective-permute-start(f32[4,128,512]{2,1,0:T(8,128)} %add_momenta.5.refs_8_.refs_0_), channel_id=1, source_target_pairs={{0,4},{4,8},{8,12},{1,5},{5,9},{9,13},{2,6},{6,10},{10,14},{3,7},{... | collective-permute-start | bytes 3145736 | tf_op jit(solution)/shard_map/ppermute | solution.py:369
  36.7 2.6 add_momenta.7.refs_9_.refs_1_
  39.3 2.6 collective-permute-start.8
  42.0 1.6 collective-permute-start.36
  44.1 15.4 %collective-permute-done.5.refs_4_ = f32[4,128,512]{2,1,0:T(8,128)} collective-permute-done((f32[4,128,512]{2,1,0:T(8,128)}, f32[4,128,512]{2,1,0:T(8,128)}, u32[]{:S(2)}, u32[]{:S(2)}) %collective-permute-start.5) | collective-permute-done | bytes 1048608 | tf_op jit(solution)/shard_map/ppermute | solution.py:369
  59.5 22.0 %collective-permute-done.8.refs_5_ = f32[4,128,512]{2,1,0:T(8,128)S(1)} collective-permute-done((f32[4,128,512]{2,1,0:T(8,128)}, f32[4,128,512]{2,1,0:T(8,128)S(1)}, u32[]{:S(2)}, u32[]{:S(2)}) %collective-permute-start.8) | collective-permute-done | bytes 1048608 | tf_op jit(solution)/shard_map/ppermute | solution.py:369
  82.8 1.3 collective-permute-start.17
  84.2 6.0 %collective-permute-done.37.refs_3_ = f32[4,128,512]{2,1,0:T(8,128)S(1)} collective-permute-done((f32[4,128,512]{2,1,0:T(8,128)}, f32[4,128,512]{2,1,0:T(8,128)S(1)}, u32[]{:S(2)}, u32[]{:S(2)}) %collective-permute-start.37) | collective-permute-done | bytes 1048608 | tf_op jit(solution)/shard_map/ppermute | solution.py:410
  91.4 1.6 copy-done.22
  93.0 3.0 %prepare.1 = (bf16[3,512,512]{2,1,0:T(8,128)(2,1)S(1)}, bf16[3,512,512]{2,1,0:T(8,128)(2,1)S(1)}, bf16[3,256,1536]{2,1,0:T(8,128)(2,1)S(1)}, bf16[3,512,768]{2,1,0:T(8,128)(2,1)S(1)}) custom-call(s32[3]{0:T(128)S(1)} %copy-done.26, f32[2,512,512]{2,1,0:T(8,128)S(1)} %copy-done.22, f32[2,128,512]{2,1,0:T(8,128)} %collective-permute-done.refs_0_, ...), custom_call_target="tpu_custom_call" | custom-call | flops 6291456 | bytes 7864320 | tf_op jit(solution)/shard_map/prepare/pallas_call | solution.py:395
  96.0 2.1 collective-permute-start.6
  98.1 11.9 %collective-permute-done.16.refs_12_ = f32[4,128,512]{2,1,0:T(8,128)S(1)} collective-permute-done((f32[4,128,512]{2,1,0:T(8,128)}, f32[4,128,512]{2,1,0:T(8,128)S(1)}, u32[]{:S(2)}, u32[]{:S(2)}) %collective-permute-start.16) | collective-permute-done | bytes 1048608 | tf_op jit(solution)/shard_map/ppermute | solution.py:370
  110.0 21.5 %collective-permute-done.17.refs_13_ = f32[4,128,512]{2,1,0:T(8,128)} collective-permute-done((f32[4,128,512]{2,1,0:T(8,128)}, f32[4,128,512]{2,1,0:T(8,128)}, u32[]{:S(2)}, u32[]{:S(2)}) %collective-permute-start.17) | collective-permute-done | bytes 1048608 | tf_op jit(solution)/shard_map/ppermute | solution.py:370
  131.6 1.6 collective-permute-start.9
  133.7 16.0 %far_sandwich.1 = (f32[4,128,512]{2,1,0:T(8,128)S(1)}, f32[4,128,512]{2,1,0:T(8,128)S(1)}) custom-call(s32[3]{0:T(128)S(1)} %guard.1.steps, f32[3]{0:T(128)S(1)} %copy-done.25, bf16[3,512,512]{2,1,0:T(8,128)(2,1)S(1)} %get-tuple-element.27.right_high, bf16[3,512,512]{2,1,0:T(8,128)(2,1)S(1)} %get-tuple-element.28.right_low, ...), custom_call_target="tpu_custom_call" | custom-call | flops 14495514624 | bytes 27262976 | tf_op jit(solution)/shard_map/far_sandwich/pallas_call | solution.py:218
  150.5 1.3 collective-permute-start.20
  151.8 1.3 collective-permute-start.21
  156.6 1.6 collective-permute-start.10
  158.2 22.8 %collective-permute-done.20.refs_16_ = f32[4,128,512]{2,1,0:T(8,128)} collective-permute-done((f32[4,128,512]{2,1,0:T(8,128)S(1)}, f32[4,128,512]{2,1,0:T(8,128)}, u32[]{:S(2)}, u32[]{:S(2)}) %collective-permute-start.20) | collective-permute-done | bytes 1048608 | tf_op jit(solution)/shard_map/ppermute | solution.py:370
  181.1 1.6 collective-permute-start.11
  182.7 20.2 %collective-permute-done.21.refs_17_ = f32[4,128,512]{2,1,0:T(8,128)} collective-permute-done((f32[4,128,512]{2,1,0:T(8,128)}, f32[4,128,512]{2,1,0:T(8,128)}, u32[]{:S(2)}, u32[]{:S(2)}) %collective-permute-start.21) | collective-permute-done | bytes 1048608 | tf_op jit(solution)/shard_map/ppermute | solution.py:370
  202.9 1.9 collective-permute-start.22
  204.9 2.4 collective-permute-start.23
  207.3 2.6 copy_select_fusion.1
  210.4 1.6 collective-permute-start.41
  212.0 1.3 collective-permute-start.42
  217.0 5.2 %near_sandwich.5 = (f32[1,128,512]{2,1,0:T(8,128)S(1)}, f32[1,128,512]{2,1,0:T(8,128)S(1)}, f32[1,128,512]{2,1,0:T(8,128)S(1)}, f32[1,128,512]{2,1,0:T(8,128)S(1)}) custom-call(s32[3]{0:T(128)S(1)} %copy-done.24, f32[3]{0:T(128)S(1)} %copy-done.25, bf16[3,512,512]{2,1,0:T(8,128)(2,1)S(1)} %copy-done.5, bf16[3,512,512]{2,1,0:T(8,128)(2,1)S(1)} %copy-done.7, ...), custom_call_target="tpu_custom_call" | custom-call | flops 2415919104 | bytes 4194304 | tf_op jit(solution)/shard_map/near_sandwich/pallas_call | solution.py:218
  222.2 1.6 collective-permute-start.26
  223.8 5.0 %near_sandwich.6 = (f32[1,128,512]{2,1,0:T(8,128)S(1)}, f32[1,128,512]{2,1,0:T(8,128)S(1)}, f32[1,128,512]{2,1,0:T(8,128)S(1)}, f32[1,128,512]{2,1,0:T(8,128)S(1)}) custom-call(s32[3]{0:T(128)S(1)} %copy-done.24, f32[3]{0:T(128)S(1)} %copy-done.25, bf16[3,512,512]{2,1,0:T(8,128)(2,1)S(1)} %copy-done.5, bf16[3,512,512]{2,1,0:T(8,128)(2,1)S(1)} %copy-done.7, ...), custom_call_target="tpu_custom_call" | custom-call | flops 2415919104 | bytes 4194304 | tf_op jit(solution)/shard_map/near_sandwich/pallas_call | solution.py:218
  229.4 5.0 %near_sandwich.7 = (f32[1,128,512]{2,1,0:T(8,128)S(1)}, f32[1,128,512]{2,1,0:T(8,128)S(1)}, f32[1,128,512]{2,1,0:T(8,128)S(1)}, f32[1,128,512]{2,1,0:T(8,128)S(1)}) custom-call(s32[3]{0:T(128)S(1)} %copy-done.24, f32[3]{0:T(128)S(1)} %copy-done.25, bf16[3,512,512]{2,1,0:T(8,128)(2,1)S(1)} %copy-done.5, bf16[3,512,512]{2,1,0:T(8,128)(2,1)S(1)} %copy-done.7, ...), custom_call_target="tpu_custom_call" | custom-call | flops 2415919104 | bytes 4194304 | tf_op jit(solution)/shard_map/near_sandwich/pallas_call | solution.py:218
  234.4 1.5 collective-permute-start.28
  237.1 5.4 %collective-permute-done.28.refs_6_ = f32[1,128,512]{2,1,0:T(8,128)S(1)} collective-permute-done((f32[1,128,512]{2,1,0:T(8,128)S(1)}, f32[1,128,512]{2,1,0:T(8,128)S(1)}, u32[]{:S(2)}, u32[]{:S(2)}) %collective-permute-start.28) | collective-permute-done | bytes 262176 | tf_op jit(solution)/shard_map/ppermute | solution.py:450
  242.5 5.0 %near_sandwich.4 = (f32[1,128,512]{2,1,0:T(8,128)S(1)}, f32[1,128,512]{2,1,0:T(8,128)S(1)}, f32[1,128,512]{2,1,0:T(8,128)S(1)}, f32[1,128,512]{2,1,0:T(8,128)S(1)}) custom-call(s32[3]{0:T(128)S(1)} %copy-done.24, f32[3]{0:T(128)S(1)} %copy-done.25, bf16[3,512,512]{2,1,0:T(8,128)(2,1)S(1)} %copy-done.5, bf16[3,512,512]{2,1,0:T(8,128)(2,1)S(1)} %copy-done.7, ...), custom_call_target="tpu_custom_call" | custom-call | flops 2415919104 | bytes 4194304 | tf_op jit(solution)/shard_map/near_sandwich/pallas_call | solution.py:218
  250.9 5.6 %collective-permute-done.33.refs_11_ = f32[1,128,512]{2,1,0:T(8,128)S(1)} collective-permute-done((f32[1,128,512]{2,1,0:T(8,128)S(1)}, f32[1,128,512]{2,1,0:T(8,128)S(1)}, u32[]{:S(2)}, u32[]{:S(2)}) %collective-permute-start.33) | collective-permute-done | bytes 262176 | tf_op jit(solution)/shard_map/ppermute | solution.py:450
  256.5 1.3 collective-permute-start.24
  257.8 4.3 %collective-permute-done.34.refs_12_ = f32[1,128,512]{2,1,0:T(8,128)S(1)} collective-permute-done((f32[1,128,512]{2,1,0:T(8,128)S(1)}, f32[1,128,512]{2,1,0:T(8,128)S(1)}, u32[]{:S(2)}, u32[]{:S(2)}) %collective-permute-start.34) | collective-permute-done | bytes 262176 | tf_op jit(solution)/shard_map/ppermute | solution.py:450
  262.1 1.5 collective-permute-start.25
  263.6 4.1 %collective-permute-done.35.refs_13_ = f32[1,128,512]{2,1,0:T(8,128)S(1)} collective-permute-done((f32[1,128,512]{2,1,0:T(8,128)S(1)}, f32[1,128,512]{2,1,0:T(8,128)S(1)}, u32[]{:S(2)}, u32[]{:S(2)}) %collective-permute-start.35) | collective-permute-done | bytes 262176 | tf_op jit(solution)/shard_map/ppermute | solution.py:450
  268.4 5.5 %collective-permute-done.24.refs_0_ = f32[1,128,512]{2,1,0:T(8,128)S(1)} collective-permute-done((f32[1,128,512]{2,1,0:T(8,128)S(1)}, f32[1,128,512]{2,1,0:T(8,128)S(1)}, u32[]{:S(2)}, u32[]{:S(2)}) %collective-permute-start.24) | collective-permute-done | bytes 262176 | tf_op jit(solution)/shard_map/ppermute | solution.py:450
  273.9 5.1 %collective-permute-done.25.refs_1_ = f32[1,128,512]{2,1,0:T(8,128)S(1)} collective-permute-done((f32[1,128,512]{2,1,0:T(8,128)S(1)}, f32[1,128,512]{2,1,0:T(8,128)S(1)}, u32[]{:S(2)}, u32[]{:S(2)}) %collective-permute-start.25) | collective-permute-done | bytes 262176 | tf_op jit(solution)/shard_map/ppermute | solution.py:450
  279.0 1.4 shard_map.56
  (109 shorter events, 19.8 us)
Async XLA Ops:
  1.1 15.1 %collective-permute-start = (f32[2,128,512]{2,1,0:T(8,128)S(1)}, f32[2,128,512]{2,1,0:T(8,128)}, u32[]{:S(2)}, u32[]{:S(2)}) collective-permute-start(f32[2,128,512]{2,1,0:T(8,128)S(1)} %constant_dynamic-slice_fusion), channel_id=1, source_target_pairs={{0,2},{2,0},{1,3},{3,1},{4,6},{6,4},{5,7},{7,5},{8,10},{10,8},{9,1... | collective-permute-start | bytes 1572872 | tf_op jit(solution)/shard_map/ppermute | solution.py:386
  7.8 21.7 %collective-permute-start.4 = (f32[4,128,512]{2,1,0:T(8,128)S(1)}, f32[4,128,512]{2,1,0:T(8,128)}, u32[]{:S(2)}, u32[]{:S(2)}) collective-permute-start(f32[4,128,512]{2,1,0:T(8,128)S(1)} %add_momenta.4), channel_id=1, source_target_pairs={{0,1},{1,0},{2,3},{3,2},{4,5},{5,4},{6,7},{7,6},{8,9},{9,8},{10,11... | collective-permute-start | bytes 3145736 | tf_op jit(solution)/shard_map/ppermute | solution.py:358
  9.2 27.4 %collective-permute-start.7 = (f32[4,128,512]{2,1,0:T(8,128)}, f32[4,128,512]{2,1,0:T(8,128)}, u32[]{:S(2)}, u32[]{:S(2)}) collective-permute-start(f32[4,128,512]{2,1,0:T(8,128)} %add_momenta.6), channel_id=1, source_target_pairs={{0,1},{1,0},{2,3},{3,2},{4,5},{5,4},{6,7},{7,6},{8,9},{9,8},{10,11... | collective-permute-start | bytes 3145736 | tf_op jit(solution)/shard_map/ppermute | solution.py:358
  16.1 13.4 %collective-permute-start.2 = (f32[2,128,512]{2,1,0:T(8,128)}, f32[2,128,512]{2,1,0:T(8,128)}, u32[]{:S(2)}, u32[]{:S(2)}) collective-permute-start(f32[2,128,512]{2,1,0:T(8,128)} %collective-permute-done.refs_0_), channel_id=1, source_target_pairs={{0,16},{16,0},{1,17},{17,1},{2,18},{18,2},{3,19},{19,3},{4,20},{20... | collective-permute-start | bytes 1572872 | tf_op jit(solution)/shard_map/ppermute | solution.py:388
  17.9 24.1 %collective-permute-start.1 = (f32[2,128,512]{2,1,0:T(8,128)}, f32[2,128,512]{2,1,0:T(8,128)}, u32[]{:S(2)}, u32[]{:S(2)}) collective-permute-start(f32[2,128,512]{2,1,0:T(8,128)} %collective-permute-done.refs_0_), channel_id=1, source_target_pairs={{0,1},{1,0},{2,3},{3,2},{4,5},{5,4},{6,7},{7,6},{8,9},{9,8},{10,11... | collective-permute-start | bytes 1572872 | tf_op jit(solution)/shard_map/ppermute | solution.py:390
  29.5 14.0 %collective-permute-start.3 = (f32[2,128,512]{2,1,0:T(8,128)}, f32[2,128,512]{2,1,0:T(8,128)}, u32[]{:S(2)}, u32[]{:S(2)}) collective-permute-start(f32[2,128,512]{2,1,0:T(8,128)} %collective-permute-done.2.refs_2_), channel_id=1, source_target_pairs={{0,1},{1,0},{2,3},{3,2},{4,5},{5,4},{6,7},{7,6},{8,9},{9,8},{10,11... | collective-permute-start | bytes 1572872 | tf_op jit(solution)/shard_map/ppermute | solution.py:390
  32.2 58.0 %copy-start.24 = (s32[3]{0:T(128)S(1)}, s32[3]{0:T(128)}, u32[]{:S(2)}) copy-start(s32[3]{0:T(128)} %steps.9) | copy-start | bytes 40
  32.2 59.2 %copy-start.26 = (s32[3]{0:T(128)S(1)}, s32[3]{0:T(128)}, u32[]{:S(2)}) copy-start(s32[3]{0:T(128)} %owners.1) | copy-start | bytes 40
  32.2 27.3 %collective-permute-start.5 = (f32[4,128,512]{2,1,0:T(8,128)}, f32[4,128,512]{2,1,0:T(8,128)}, u32[]{:S(2)}, u32[]{:S(2)}) collective-permute-start(f32[4,128,512]{2,1,0:T(8,128)} %add_momenta.5.refs_8_.refs_0_), channel_id=1, source_target_pairs={{0,4},{4,8},{8,12},{1,5},{5,9},{9,13},{2,6},{6,10},{10,14},{3,7},{... | collective-permute-start | bytes 3145736 | tf_op jit(solution)/shard_map/ppermute | solution.py:369
  39.3 42.2 %collective-permute-start.8 = (f32[4,128,512]{2,1,0:T(8,128)}, f32[4,128,512]{2,1,0:T(8,128)S(1)}, u32[]{:S(2)}, u32[]{:S(2)}) collective-permute-start(f32[4,128,512]{2,1,0:T(8,128)} %add_momenta.7.refs_9_.refs_1_), channel_id=1, source_target_pairs={{0,4},{4,8},{8,12},{1,5},{5,9},{9,13},{2,6},{6,10},{10,14},{3,7},{... | collective-permute-start | bytes 3145736 | tf_op jit(solution)/shard_map/ppermute | solution.py:369
  41.9 40.9 %collective-permute-start.14 = (f32[4,128,512]{2,1,0:T(8,128)}, f32[4,128,512]{2,1,0:T(8,128)S(1)}, u32[]{:S(2)}, u32[]{:S(2)}) collective-permute-start(f32[4,128,512]{2,1,0:T(8,128)} %add_momenta.5.refs_8_.refs_0_), channel_id=1, source_target_pairs={{0,1},{1,0},{2,3},{3,2},{4,5},{5,4},{6,7},{7,6},{8,9},{9,8},{10,11... | collective-permute-start | bytes 3145736 | tf_op jit(solution)/shard_map/ppermute | solution.py:379
  42.0 42.1 %collective-permute-start.36 = (f32[4,128,512]{2,1,0:T(8,128)}, f32[4,128,512]{2,1,0:T(8,128)S(1)}, u32[]{:S(2)}, u32[]{:S(2)}) collective-permute-start(f32[4,128,512]{2,1,0:T(8,128)} %add_momenta.5.refs_8_.refs_0_), channel_id=1, source_target_pairs={{0,2},{2,0},{1,3},{3,1},{4,6},{6,4},{5,7},{7,5},{8,10},{10,8},{9,1... | collective-permute-start | bytes 3145736 | tf_op jit(solution)/shard_map/ppermute | solution.py:410
  43.6 46.7 %collective-permute-start.37 = (f32[4,128,512]{2,1,0:T(8,128)}, f32[4,128,512]{2,1,0:T(8,128)S(1)}, u32[]{:S(2)}, u32[]{:S(2)}) collective-permute-start(f32[4,128,512]{2,1,0:T(8,128)} %add_momenta.7.refs_9_.refs_1_), channel_id=1, source_target_pairs={{0,2},{2,0},{1,3},{3,1},{4,6},{6,4},{5,7},{7,5},{8,10},{10,8},{9,1... | collective-permute-start | bytes 3145736 | tf_op jit(solution)/shard_map/ppermute | solution.py:410
  59.5 36.5 %collective-permute-start.15 = (f32[4,128,512]{2,1,0:T(8,128)}, f32[4,128,512]{2,1,0:T(8,128)S(1)}, u32[]{:S(2)}, u32[]{:S(2)}) collective-permute-start(f32[4,128,512]{2,1,0:T(8,128)} %add_momenta.7.refs_9_.refs_1_), channel_id=1, source_target_pairs={{0,1},{1,0},{2,3},{3,2},{4,5},{5,4},{6,7},{7,6},{8,9},{9,8},{10,11... | collective-permute-start | bytes 3145736 | tf_op jit(solution)/shard_map/ppermute | solution.py:379
  81.5 28.5 %collective-permute-start.16 = (f32[4,128,512]{2,1,0:T(8,128)}, f32[4,128,512]{2,1,0:T(8,128)S(1)}, u32[]{:S(2)}, u32[]{:S(2)}) collective-permute-start(f32[4,128,512]{2,1,0:T(8,128)} %add_momenta.5.refs_8_.refs_0_), channel_id=1, source_target_pairs={{12,8},{8,4},{4,0},{13,9},{9,5},{5,1},{14,10},{10,6},{6,2},{15,11}... | collective-permute-start | bytes 3145736 | tf_op jit(solution)/shard_map/ppermute | solution.py:370
  82.8 48.7 %collective-permute-start.17 = (f32[4,128,512]{2,1,0:T(8,128)}, f32[4,128,512]{2,1,0:T(8,128)}, u32[]{:S(2)}, u32[]{:S(2)}) collective-permute-start(f32[4,128,512]{2,1,0:T(8,128)} %add_momenta.7.refs_9_.refs_1_), channel_id=1, source_target_pairs={{12,8},{8,4},{4,0},{13,9},{9,5},{5,1},{14,10},{10,6},{6,2},{15,11}... | collective-permute-start | bytes 3145736 | tf_op jit(solution)/shard_map/ppermute | solution.py:370
  84.2 49.0 %collective-permute-start.38 = (f32[4,128,512]{2,1,0:T(8,128)S(1)}, f32[4,128,512]{2,1,0:T(8,128)S(1)}, u32[]{:S(2)}, u32[]{:S(2)}) collective-permute-start(f32[4,128,512]{2,1,0:T(8,128)S(1)} %collective-permute-done.36.refs_2_), channel_id=1, source_target_pairs={{0,1},{1,0},{2,3},{3,2},{4,5},{5,4},{6,7},{7,6},{8,9},{9,8},{10,11... | collective-permute-start | bytes 3145736 | tf_op jit(solution)/shard_map/ppermute | solution.py:413
  90.2 43.0 %collective-permute-start.39 = (f32[4,128,512]{2,1,0:T(8,128)S(1)}, f32[4,128,512]{2,1,0:T(8,128)S(1)}, u32[]{:S(2)}, u32[]{:S(2)}) collective-permute-start(f32[4,128,512]{2,1,0:T(8,128)S(1)} %collective-permute-done.37.refs_3_), channel_id=1, source_target_pairs={{0,1},{1,0},{2,3},{3,2},{4,5},{5,4},{6,7},{7,6},{8,9},{9,8},{10,11... | collective-permute-start | bytes 3145736 | tf_op jit(solution)/shard_map/ppermute | solution.py:413
  96.0 53.8 %copy-start.4 = (bf16[3,512,512]{2,1,0:T(8,128)(2,1)}, bf16[3,512,512]{2,1,0:T(8,128)(2,1)S(1)}, u32[]{:S(2)}) copy-start(bf16[3,512,512]{2,1,0:T(8,128)(2,1)S(1)} %get-tuple-element.27.right_high) | copy-start | bytes 4718596
  96.0 53.8 %copy-start.6 = (bf16[3,512,512]{2,1,0:T(8,128)(2,1)}, bf16[3,512,512]{2,1,0:T(8,128)(2,1)S(1)}, u32[]{:S(2)}) copy-start(bf16[3,512,512]{2,1,0:T(8,128)(2,1)S(1)} %get-tuple-element.28.right_low) | copy-start | bytes 4718596
  96.0 53.8 %copy-start.12 = (f32[4,128,512]{2,1,0:T(8,128)}, f32[4,128,512]{2,1,0:T(8,128)S(1)}, u32[]{:S(2)}) copy-start(f32[4,128,512]{2,1,0:T(8,128)S(1)} %collective-permute-done.15.refs_11_.refs_5_) | copy-start | bytes 3145732
  96.0 54.4 %collective-permute-start.6 = (f32[4,128,512]{2,1,0:T(8,128)}, f32[4,128,512]{2,1,0:T(8,128)}, u32[]{:S(2)}, u32[]{:S(2)}) collective-permute-start(f32[4,128,512]{2,1,0:T(8,128)} %collective-permute-done.5.refs_4_), channel_id=1, source_target_pairs={{4,8},{8,12},{5,9},{9,13},{6,10},{10,14},{7,11},{11,15},{20,24},{2... | collective-permute-start | bytes 3145736 | tf_op jit(solution)/shard_map/ppermute | solution.py:369
  110.0 43.1 %collective-permute-start.12 = (f32[4,128,512]{2,1,0:T(8,128)}, f32[4,128,512]{2,1,0:T(8,128)S(1)}, u32[]{:S(2)}, u32[]{:S(2)}) collective-permute-start(f32[4,128,512]{2,1,0:T(8,128)} %collective-permute-done.5.refs_4_), channel_id=1, source_target_pairs={{0,1},{1,0},{2,3},{3,2},{4,5},{5,4},{6,7},{7,6},{8,9},{9,8},{10,11... | collective-permute-start | bytes 3145736 | tf_op jit(solution)/shard_map/ppermute | solution.py:379
  131.6 20.2 %collective-permute-start.9 = (f32[4,128,512]{2,1,0:T(8,128)S(1)}, f32[4,128,512]{2,1,0:T(8,128)}, u32[]{:S(2)}, u32[]{:S(2)}) collective-permute-start(f32[4,128,512]{2,1,0:T(8,128)S(1)} %collective-permute-done.8.refs_5_), channel_id=1, source_target_pairs={{4,8},{8,12},{5,9},{9,13},{6,10},{10,14},{7,11},{11,15},{20,24},{2... | collective-permute-start | bytes 3145736 | tf_op jit(solution)/shard_map/ppermute | solution.py:369
  133.2 21.0 %collective-permute-start.13 = (f32[4,128,512]{2,1,0:T(8,128)S(1)}, f32[4,128,512]{2,1,0:T(8,128)S(1)}, u32[]{:S(2)}, u32[]{:S(2)}) collective-permute-start(f32[4,128,512]{2,1,0:T(8,128)S(1)} %collective-permute-done.8.refs_5_), channel_id=1, source_target_pairs={{0,1},{1,0},{2,3},{3,2},{4,5},{5,4},{6,7},{7,6},{8,9},{9,8},{10,11... | collective-permute-start | bytes 3145736 | tf_op jit(solution)/shard_map/ppermute | solution.py:379
  133.2 22.4 %collective-permute-start.18 = (f32[4,128,512]{2,1,0:T(8,128)S(1)}, f32[4,128,512]{2,1,0:T(8,128)S(1)}, u32[]{:S(2)}, u32[]{:S(2)}) collective-permute-start(f32[4,128,512]{2,1,0:T(8,128)S(1)} %collective-permute-done.16.refs_12_), channel_id=1, source_target_pairs={{0,1},{1,0},{2,3},{3,2},{4,5},{5,4},{6,7},{7,6},{8,9},{9,8},{10,11... | collective-permute-start | bytes 3145736 | tf_op jit(solution)/shard_map/ppermute | solution.py:379
  150.5 30.6 %collective-permute-start.20 = (f32[4,128,512]{2,1,0:T(8,128)S(1)}, f32[4,128,512]{2,1,0:T(8,128)}, u32[]{:S(2)}, u32[]{:S(2)}) collective-permute-start(f32[4,128,512]{2,1,0:T(8,128)S(1)} %collective-permute-done.16.refs_12_), channel_id=1, source_target_pairs={{8,4},{4,0},{9,5},{5,1},{10,6},{6,2},{11,7},{7,3},{24,20},{20,16},... | collective-permute-start | bytes 3145736 | tf_op jit(solution)/shard_map/ppermute | solution.py:370
  151.8 51.1 %collective-permute-start.21 = (f32[4,128,512]{2,1,0:T(8,128)}, f32[4,128,512]{2,1,0:T(8,128)}, u32[]{:S(2)}, u32[]{:S(2)}) collective-permute-start(f32[4,128,512]{2,1,0:T(8,128)} %collective-permute-done.17.refs_13_), channel_id=1, source_target_pairs={{8,4},{4,0},{9,5},{5,1},{10,6},{6,2},{11,7},{7,3},{24,20},{20,16},... | collective-permute-start | bytes 3145736 | tf_op jit(solution)/shard_map/ppermute | solution.py:370
  154.1 50.8 %collective-permute-start.40 = (f32[4,128,512]{2,0,1:T(4,128)S(1)}, f32[4,128,512]{2,0,1:T(4,128)}, u32[]{:S(2)}, u32[]{:S(2)}) collective-permute-start(f32[4,128,512]{2,0,1:T(4,128)S(1)} %copy.6), channel_id=1, source_target_pairs={{0,1},{1,0},{2,3},{3,2},{4,5},{5,4},{6,7},{7,6},{8,9},{9,8},{10,11... | collective-permute-start | bytes 3145736 | tf_op jit(solution)/shard_map/ppermute | solution.py:427
  155.2 55.2 %collective-permute-start.19 = (f32[4,128,512]{2,1,0:T(8,128)}, f32[4,128,512]{2,1,0:T(8,128)}, u32[]{:S(2)}, u32[]{:S(2)}) collective-permute-start(f32[4,128,512]{2,1,0:T(8,128)} %collective-permute-done.17.refs_13_), channel_id=1, source_target_pairs={{0,1},{1,0},{2,3},{3,2},{4,5},{5,4},{6,7},{7,6},{8,9},{9,8},{10,11... | collective-permute-start | bytes 3145736 | tf_op jit(solution)/shard_map/ppermute | solution.py:379
  156.6 55.3 %collective-permute-start.10 = (f32[4,128,512]{2,1,0:T(8,128)}, f32[4,128,512]{2,1,0:T(8,128)}, u32[]{:S(2)}, u32[]{:S(2)}) collective-permute-start(f32[4,128,512]{2,1,0:T(8,128)} %collective-permute-done.6.refs_0_), channel_id=1, source_target_pairs={{8,9},{9,8},{12,13},{13,12},{10,11},{11,10},{14,15},{15,14},{24,25... | collective-permute-start | bytes 3145736 | tf_op jit(solution)/shard_map/ppermute | solution.py:379
  181.1 32.2 %collective-permute-start.11 = (f32[4,128,512]{2,1,0:T(8,128)}, f32[4,128,512]{2,1,0:T(8,128)}, u32[]{:S(2)}, u32[]{:S(2)}) collective-permute-start(f32[4,128,512]{2,1,0:T(8,128)} %collective-permute-done.9.refs_1_), channel_id=1, source_target_pairs={{8,9},{9,8},{12,13},{13,12},{10,11},{11,10},{14,15},{15,14},{24,25... | collective-permute-start | bytes 3145736 | tf_op jit(solution)/shard_map/ppermute | solution.py:379
  202.9 10.3 %collective-permute-start.22 = (f32[4,128,512]{2,1,0:T(8,128)}, f32[4,128,512]{2,1,0:T(8,128)}, u32[]{:S(2)}, u32[]{:S(2)}) collective-permute-start(f32[4,128,512]{2,1,0:T(8,128)} %collective-permute-done.20.refs_16_), channel_id=1, source_target_pairs={{0,1},{1,0},{4,5},{5,4},{2,3},{3,2},{6,7},{7,6},{16,17},{17,16},{2... | collective-permute-start | bytes 3145736 | tf_op jit(solution)/shard_map/ppermute | solution.py:379
  204.9 8.4 %collective-permute-start.23 = (f32[4,128,512]{2,1,0:T(8,128)}, f32[4,128,512]{2,1,0:T(8,128)}, u32[]{:S(2)}, u32[]{:S(2)}) collective-permute-start(f32[4,128,512]{2,1,0:T(8,128)} %collective-permute-done.21.refs_17_), channel_id=1, source_target_pairs={{0,1},{1,0},{4,5},{5,4},{2,3},{3,2},{6,7},{7,6},{16,17},{17,16},{2... | collective-permute-start | bytes 3145736 | tf_op jit(solution)/shard_map/ppermute | solution.py:379
  210.4 68.6 %collective-permute-start.41 = (f32[128,8,512]{2,1,0:T(8,128)S(1)}, f32[128,8,512]{2,1,0:T(8,128)S(1)}, u32[]{:S(2)}, u32[]{:S(2)}) collective-permute-start(f32[128,8,512]{2,1,0:T(8,128)S(1)} %maximum_bitcast_fusion), channel_id=1, source_target_pairs={{0,12},{1,13},{2,14},{3,15},{16,28},{17,29},{18,30},{19,31}} | collective-permute-start | bytes 6291464 | tf_op jit(solution)/shard_map/ppermute | solution.py:431
  212.0 67.0 %collective-permute-start.42 = (f32[128,8,512]{2,1,0:T(8,128)S(1)}, f32[128,8,512]{2,1,0:T(8,128)S(1)}, u32[]{:S(2)}, u32[]{:S(2)}) collective-permute-start(f32[128,8,512]{2,1,0:T(8,128)S(1)} %maximum_bitcast_fusion), channel_id=1, source_target_pairs={{12,0},{13,1},{14,2},{15,3},{28,16},{29,17},{30,18},{31,19}} | collective-permute-start | bytes 6291464 | tf_op jit(solution)/shard_map/ppermute | solution.py:432
  222.2 13.7 %collective-permute-start.26 = (f32[1,128,512]{2,1,0:T(8,128)S(1)}, f32[1,128,512]{2,1,0:T(8,128)S(1)}, u32[]{:S(2)}, u32[]{:S(2)}) collective-permute-start(f32[1,128,512]{2,1,0:T(8,128)S(1)} %get-tuple-element.36), channel_id=1, source_target_pairs={{0,2},{1,3},{2,0},{3,1},{4,6},{5,7},{6,4},{7,5},{8,10},{9,11},{10,... | collective-permute-start | bytes 786440 | tf_op jit(solution)/shard_map/ppermute | solution.py:450
  228.8 8.3 %collective-permute-start.27 = (f32[1,128,512]{2,1,0:T(8,128)S(1)}, f32[1,128,512]{2,1,0:T(8,128)S(1)}, u32[]{:S(2)}, u32[]{:S(2)}) collective-permute-start(f32[1,128,512]{2,1,0:T(8,128)S(1)} %get-tuple-element.37), channel_id=1, source_target_pairs={{0,2},{1,3},{2,0},{3,1},{4,6},{5,7},{6,4},{7,5},{8,10},{9,11},{10,... | collective-permute-start | bytes 786440 | tf_op jit(solution)/shard_map/ppermute | solution.py:450
  234.4 8.1 %collective-permute-start.28 = (f32[1,128,512]{2,1,0:T(8,128)S(1)}, f32[1,128,512]{2,1,0:T(8,128)S(1)}, u32[]{:S(2)}, u32[]{:S(2)}) collective-permute-start(f32[1,128,512]{2,1,0:T(8,128)S(1)} %get-tuple-element.38), channel_id=1, source_target_pairs={{0,2},{1,3},{2,0},{3,1},{4,6},{5,7},{6,4},{7,5},{8,10},{9,11},{10,... | collective-permute-start | bytes 786440 | tf_op jit(solution)/shard_map/ppermute | solution.py:450
  236.0 11.5 %collective-permute-start.29 = (f32[1,128,512]{2,1,0:T(8,128)S(1)}, f32[1,128,512]{2,1,0:T(8,128)S(1)}, u32[]{:S(2)}, u32[]{:S(2)}) collective-permute-start(f32[1,128,512]{2,1,0:T(8,128)S(1)} %get-tuple-element.39), channel_id=1, source_target_pairs={{0,1},{1,0},{2,3},{3,2},{4,5},{5,4},{6,7},{7,6},{8,9},{9,8},{10,11... | collective-permute-start | bytes 786440 | tf_op jit(solution)/shard_map/ppermute | solution.py:450
  237.1 11.1 %collective-permute-start.30 = (f32[1,128,512]{2,1,0:T(8,128)S(1)}, f32[1,128,512]{2,1,0:T(8,128)S(1)}, u32[]{:S(2)}, u32[]{:S(2)}) collective-permute-start(f32[1,128,512]{2,1,0:T(8,128)S(1)} %get-tuple-element.40), channel_id=1, source_target_pairs={{0,1},{1,0},{2,3},{3,2},{4,5},{5,4},{6,7},{7,6},{8,9},{9,8},{10,11... | collective-permute-start | bytes 786440 | tf_op jit(solution)/shard_map/ppermute | solution.py:450
  242.5 6.6 %collective-permute-start.31 = (f32[1,128,512]{2,1,0:T(8,128)S(1)}, f32[1,128,512]{2,1,0:T(8,128)S(1)}, u32[]{:S(2)}, u32[]{:S(2)}) collective-permute-start(f32[1,128,512]{2,1,0:T(8,128)S(1)} %get-tuple-element.41), channel_id=1, source_target_pairs={{0,1},{1,0},{2,3},{3,2},{4,5},{5,4},{6,7},{7,6},{8,9},{9,8},{10,11... | collective-permute-start | bytes 786440 | tf_op jit(solution)/shard_map/ppermute | solution.py:450
  247.5 2.4 collective-permute-start.32
  248.2 8.3 %collective-permute-start.33 = (f32[1,128,512]{2,1,0:T(8,128)S(1)}, f32[1,128,512]{2,1,0:T(8,128)S(1)}, u32[]{:S(2)}, u32[]{:S(2)}) collective-permute-start(f32[1,128,512]{2,1,0:T(8,128)S(1)} %get-tuple-element.43), channel_id=1, source_target_pairs={{0,3},{1,2},{2,1},{3,0},{4,7},{5,6},{6,5},{7,4},{8,11},{9,10},{10,... | collective-permute-start | bytes 786440 | tf_op jit(solution)/shard_map/ppermute | solution.py:450
  249.1 13.0 %collective-permute-start.34 = (f32[1,128,512]{2,1,0:T(8,128)S(1)}, f32[1,128,512]{2,1,0:T(8,128)S(1)}, u32[]{:S(2)}, u32[]{:S(2)}) collective-permute-start(f32[1,128,512]{2,1,0:T(8,128)S(1)} %get-tuple-element.44), channel_id=1, source_target_pairs={{0,3},{1,2},{2,1},{3,0},{4,7},{5,6},{6,5},{7,4},{8,11},{9,10},{10,... | collective-permute-start | bytes 786440 | tf_op jit(solution)/shard_map/ppermute | solution.py:450
  249.9 17.8 %collective-permute-start.35 = (f32[1,128,512]{2,1,0:T(8,128)S(1)}, f32[1,128,512]{2,1,0:T(8,128)S(1)}, u32[]{:S(2)}, u32[]{:S(2)}) collective-permute-start(f32[1,128,512]{2,1,0:T(8,128)S(1)} %get-tuple-element.45), channel_id=1, source_target_pairs={{0,3},{1,2},{2,1},{3,0},{4,7},{5,6},{6,5},{7,4},{8,11},{9,10},{10,... | collective-permute-start | bytes 786440 | tf_op jit(solution)/shard_map/ppermute | solution.py:450
  256.5 17.4 %collective-permute-start.24 = (f32[1,128,512]{2,1,0:T(8,128)S(1)}, f32[1,128,512]{2,1,0:T(8,128)S(1)}, u32[]{:S(2)}, u32[]{:S(2)}) collective-permute-start(f32[1,128,512]{2,1,0:T(8,128)S(1)} %get-tuple-element.30), channel_id=1, source_target_pairs={{0,2},{1,3},{2,0},{3,1},{4,6},{5,7},{6,4},{7,5},{8,10},{9,11},{10,... | collective-permute-start | bytes 786440 | tf_op jit(solution)/shard_map/ppermute | solution.py:450
  262.1 16.9 %collective-permute-start.25 = (f32[1,128,512]{2,1,0:T(8,128)S(1)}, f32[1,128,512]{2,1,0:T(8,128)S(1)}, u32[]{:S(2)}, u32[]{:S(2)}) collective-permute-start(f32[1,128,512]{2,1,0:T(8,128)S(1)} %get-tuple-element.31), channel_id=1, source_target_pairs={{0,3},{1,2},{2,1},{3,0},{4,7},{5,6},{6,5},{7,4},{8,11},{9,10},{10,... | collective-permute-start | bytes 786440 | tf_op jit(solution)/shard_map/ppermute | solution.py:450
  (22 other events, 342.4 us)

commit v8 on v7

--- a/solution.py
+++ b/solution.py
@@ -72,8 +72,6 @@
 def add_momenta(theirs, first, green, *refs):
     out, held, total, arrived, left = refs[-5:]
     given = refs[:-5]
-    if theirs:
-        total = out
     momenta, count, size = green.shape[0], held.shape[0], held.shape[2]
     core = lax.axis_index("kz")
     base = (1 - core if theirs else core) * count
@@ -90,10 +88,9 @@
         for k in range(1, held.shape[1]):
             value = value + held[e, k]
         total[e] = value
-        if not theirs:
-            pltpu.make_async_copy(total.at[e], out.at[e], left.at[e]).start()
-
-    for e in range(0 if theirs else count):
+        pltpu.make_async_copy(total.at[e], out.at[e], left.at[e]).start()
+
+    for e in range(count):
         pltpu.make_async_copy(total.at[e], out.at[e], left.at[e]).wait()
 
 
@@ -336,14 +333,14 @@
             functools.partial(add_momenta, theirs, piece * size),
             out_shape=jax.ShapeDtypeStruct((half, size, order), jnp.float32),
             in_specs=[pl.BlockSpec(memory_space=pltpu.HBM)] * (1 + len(more)),
-            out_specs=pl.BlockSpec(memory_space=pltpu.VMEM if theirs else pltpu.HBM),
+            out_specs=pl.BlockSpec(memory_space=pltpu.HBM),
             scratch_shapes=[
                 pltpu.VMEM((half, momenta_here + len(more), size, order), jnp.float32),
-                pltpu.VMEM((8, order) if theirs else (half, size, order), jnp.float32),
+                pltpu.VMEM((half, size, order), jnp.float32),
                 pltpu.SemaphoreType.DMA((half,)),
                 pltpu.SemaphoreType.DMA((half,)),
             ],
-            compiler_params=pltpu.CompilerParams(vmem_limit_bytes=8 << 20 if theirs else 67_000_000),
+            compiler_params=pltpu.CompilerParams(vmem_limit_bytes=67_000_000),
             cost_estimate=pl.CostEstimate(
                 flops=momenta_here * half * size * order,
                 bytes_accessed=4 * (momenta_here + 1 + len(more)) * half * size * order,

time: 281 us -> 283 us (level)
  Pallas kernels: 49.3 us -> 52.8 us
    unnamed x54 -> x52, local copies, waits for them, and re-layouts: 11.7 us -> 8.32 us
    pallas_call x4, Pallas kernels: 6.94 us -> 9.89 us  [summed(): pl.pallas_call(functools.partial(add_momenta, theirs, piece * size), out_...]
  transfers between devices with their start and end apart: 43 -> 43, of which waited for: 16 -> 16; matrix products, arithmetic and copies ran while one was open for 1% -> 1% of each run, Pallas kernels for 17% -> 18%
where the time goes in v8:
time: 283 us; the launch traced here: 282 us
  waiting for transfers between devices  169 us (60%)
  Pallas kernels  52.8 us (19%)
  starting transfers between devices  45.5 us (16%)
  local copies, waits for them, and re-layouts  10.9 us (4%)
  other arithmetic  3.01 us (1%)
    ppermute x4, waiting for transfers between devices, shards(): lax.ppermute(x, 'energy', down[d - 1])  76.4 us
    ppermute x4, waiting for transfers between devices, shards(): streams[-d] = [lax.ppermute(x, 'energy', up[d - 1]) for x in streams[1 - d]]  37.5 us
    pallas_call x5, Pallas kernels, sandwich(): pl.pallas_call(functools.partial(split_dot, len(groups), len(groups[0][0]...  36.8 us
    ppermute x12, waiting for transfers between devices, shards(): block = lax.ppermute(block, ('atom', 'kz'), pairs)  30.4 us
    ppermute x1, waiting for transfers between devices, shards(): lax.ppermute(got, 'grp', [(i, (i + d) % parts) for i in range(parts)])  11.6 us
    ppermute x4, starting transfers between devices, shards(): streams[-d] = [lax.ppermute(x, 'energy', up[d - 1]) for x in streams[1 - d]]  10.8 us
    ppermute x12, starting transfers between devices, shards(): block = lax.ppermute(block, ('atom', 'kz'), pairs)  10.5 us
    pallas_call x4, Pallas kernels, summed(): pl.pallas_call(functools.partial(add_momenta, theirs, piece * size), out_...  9.89 us
  transfers between devices with their start and end apart: 43, of which 16 were waited for; matrix products, arithmetic and copies ran while one was open for 1% of the time, Pallas kernels for 18%

profile of v8, /device:TPU:0, one launch (start us, length us, event | category | flops | bytes accessed | tf_op | source)
XLA Modules:
  0.0 281.9 jit_solution(7533713321845808345)
XLA Ops:
  0.0 1.9 constant_dynamic-slice_fusion
  1.9 3.0 %collective-permute-start = (f32[2,128,512]{2,1,0:T(8,128)}, f32[2,128,512]{2,1,0:T(8,128)}, u32[]{:S(2)}, u32[]{:S(2)}) collective-permute-start(f32[2,128,512]{2,1,0:T(8,128)} %constant_dynamic-slice_fusion), channel_id=1, source_target_pairs={{0,2},{2,0},{1,3},{3,1},{4,6},{6,4},{5,7},{7,5},{8,10},{10,8},{9,1... | collective-permute-start | bytes 1572872 | tf_op jit(solution)/shard_map/ppermute | solution.py:383
  4.9 2.3 add_momenta.4
  7.2 2.3 add_momenta.6
  10.1 7.0 %collective-permute-done.refs_0_ = f32[2,128,512]{2,1,0:T(8,128)} collective-permute-done((f32[2,128,512]{2,1,0:T(8,128)}, f32[2,128,512]{2,1,0:T(8,128)}, u32[]{:S(2)}, u32[]{:S(2)}) %collective-permute-start) | collective-permute-done | bytes 524320 | tf_op jit(solution)/shard_map/ppermute | solution.py:383
  17.1 1.8 collective-permute-start.2
  18.9 11.6 %collective-permute-done.2.refs_2_ = f32[2,128,512]{2,1,0:T(8,128)} collective-permute-done((f32[2,128,512]{2,1,0:T(8,128)}, f32[2,128,512]{2,1,0:T(8,128)}, u32[]{:S(2)}, u32[]{:S(2)}) %collective-permute-start.2) | collective-permute-done | bytes 524320 | tf_op jit(solution)/shard_map/ppermute | solution.py:385
  30.5 2.6 add_momenta.5.refs_8_.refs_0_
  33.2 4.5 %collective-permute-start.5 = (f32[4,128,512]{2,1,0:T(8,128)}, f32[4,128,512]{2,1,0:T(8,128)}, u32[]{:S(2)}, u32[]{:S(2)}) collective-permute-start(f32[4,128,512]{2,1,0:T(8,128)} %add_momenta.5.refs_8_.refs_0_), channel_id=1, source_target_pairs={{0,4},{4,8},{8,12},{1,5},{5,9},{9,13},{2,6},{6,10},{10,14},{3,7},{... | collective-permute-start | bytes 3145736 | tf_op jit(solution)/shard_map/ppermute | solution.py:366
  37.6 2.6 add_momenta.7.refs_9_.refs_1_
  40.3 2.6 collective-permute-start.8
  43.0 1.6 collective-permute-start.36
  45.0 15.4 %collective-permute-done.5.refs_4_ = f32[4,128,512]{2,1,0:T(8,128)} collective-permute-done((f32[4,128,512]{2,1,0:T(8,128)}, f32[4,128,512]{2,1,0:T(8,128)}, u32[]{:S(2)}, u32[]{:S(2)}) %collective-permute-start.5) | collective-permute-done | bytes 1048608 | tf_op jit(solution)/shard_map/ppermute | solution.py:366
  60.5 22.0 %collective-permute-done.8.refs_5_ = f32[4,128,512]{2,1,0:T(8,128)S(1)} collective-permute-done((f32[4,128,512]{2,1,0:T(8,128)}, f32[4,128,512]{2,1,0:T(8,128)S(1)}, u32[]{:S(2)}, u32[]{:S(2)}) %collective-permute-start.8) | collective-permute-done | bytes 1048608 | tf_op jit(solution)/shard_map/ppermute | solution.py:366
  83.8 1.3 collective-permute-start.17
  85.2 6.0 %collective-permute-done.37.refs_3_ = f32[4,128,512]{2,1,0:T(8,128)S(1)} collective-permute-done((f32[4,128,512]{2,1,0:T(8,128)}, f32[4,128,512]{2,1,0:T(8,128)S(1)}, u32[]{:S(2)}, u32[]{:S(2)}) %collective-permute-start.37) | collective-permute-done | bytes 1048608 | tf_op jit(solution)/shard_map/ppermute | solution.py:407
  92.4 1.6 copy-done.21
  94.0 3.0 %prepare.1 = (bf16[3,512,512]{2,1,0:T(8,128)(2,1)S(1)}, bf16[3,512,512]{2,1,0:T(8,128)(2,1)S(1)}, bf16[3,256,1536]{2,1,0:T(8,128)(2,1)S(1)}, bf16[3,512,768]{2,1,0:T(8,128)(2,1)S(1)}) custom-call(s32[3]{0:T(128)S(1)} %copy-done.25, f32[2,512,512]{2,1,0:T(8,128)S(1)} %copy-done.21, f32[2,128,512]{2,1,0:T(8,128)} %collective-permute-done.refs_0_, ...), custom_call_target="tpu_custom_call" | custom-call | flops 6291456 | bytes 7864320 | tf_op jit(solution)/shard_map/prepare/pallas_call | solution.py:392
  97.0 2.1 collective-permute-start.6
  99.1 11.9 %collective-permute-done.16.refs_12_ = f32[4,128,512]{2,1,0:T(8,128)S(1)} collective-permute-done((f32[4,128,512]{2,1,0:T(8,128)}, f32[4,128,512]{2,1,0:T(8,128)S(1)}, u32[]{:S(2)}, u32[]{:S(2)}) %collective-permute-start.16) | collective-permute-done | bytes 1048608 | tf_op jit(solution)/shard_map/ppermute | solution.py:367
  111.0 21.5 %collective-permute-done.17.refs_13_ = f32[4,128,512]{2,1,0:T(8,128)} collective-permute-done((f32[4,128,512]{2,1,0:T(8,128)}, f32[4,128,512]{2,1,0:T(8,128)}, u32[]{:S(2)}, u32[]{:S(2)}) %collective-permute-start.17) | collective-permute-done | bytes 1048608 | tf_op jit(solution)/shard_map/ppermute | solution.py:367
  132.5 1.6 collective-permute-start.9
  134.7 16.3 %far_sandwich.1 = (f32[4,128,512]{2,1,0:T(8,128)S(1)}, f32[4,128,512]{2,1,0:T(8,128)S(1)}) custom-call(s32[3]{0:T(128)S(1)} %guard.1.steps, f32[3]{0:T(128)S(1)} %copy-done.24, bf16[3,512,512]{2,1,0:T(8,128)(2,1)S(1)} %get-tuple-element.27.right_high, bf16[3,512,512]{2,1,0:T(8,128)(2,1)S(1)} %get-tuple-element.28.right_low, ...), custom_call_target="tpu_custom_call" | custom-call | flops 14495514624 | bytes 27262976 | tf_op jit(solution)/shard_map/far_sandwich/pallas_call | solution.py:215
  151.8 1.3 collective-permute-start.20
  157.9 1.6 collective-permute-start.10
  159.6 22.8 %collective-permute-done.20.refs_16_ = f32[4,128,512]{2,1,0:T(8,128)} collective-permute-done((f32[4,128,512]{2,1,0:T(8,128)S(1)}, f32[4,128,512]{2,1,0:T(8,128)}, u32[]{:S(2)}, u32[]{:S(2)}) %collective-permute-start.20) | collective-permute-done | bytes 1048608 | tf_op jit(solution)/shard_map/ppermute | solution.py:367
  182.4 1.6 collective-permute-start.11
  184.0 20.2 %collective-permute-done.21.refs_17_ = f32[4,128,512]{2,1,0:T(8,128)} collective-permute-done((f32[4,128,512]{2,1,0:T(8,128)}, f32[4,128,512]{2,1,0:T(8,128)}, u32[]{:S(2)}, u32[]{:S(2)}) %collective-permute-start.21) | collective-permute-done | bytes 1048608 | tf_op jit(solution)/shard_map/ppermute | solution.py:367
  204.2 1.9 collective-permute-start.22
  206.2 2.4 collective-permute-start.23
  208.6 2.6 copy_select_fusion.1
  211.7 1.6 collective-permute-start.41
  213.3 1.3 collective-permute-start.42
  218.3 5.0 %near_sandwich.5 = (f32[1,128,512]{2,1,0:T(8,128)S(1)}, f32[1,128,512]{2,1,0:T(8,128)S(1)}, f32[1,128,512]{2,1,0:T(8,128)S(1)}, f32[1,128,512]{2,1,0:T(8,128)S(1)}) custom-call(s32[3]{0:T(128)S(1)} %copy-done.23, f32[3]{0:T(128)S(1)} %copy-done.24, bf16[3,512,512]{2,1,0:T(8,128)(2,1)S(1)} %copy-done.4, bf16[3,512,512]{2,1,0:T(8,128)(2,1)S(1)} %copy-done.6, ...), custom_call_target="tpu_custom_call" | custom-call | flops 2415919104 | bytes 4194304 | tf_op jit(solution)/shard_map/near_sandwich/pallas_call | solution.py:215
  223.4 1.6 collective-permute-start.26
  224.9 5.1 %near_sandwich.6 = (f32[1,128,512]{2,1,0:T(8,128)S(1)}, f32[1,128,512]{2,1,0:T(8,128)S(1)}, f32[1,128,512]{2,1,0:T(8,128)S(1)}, f32[1,128,512]{2,1,0:T(8,128)S(1)}) custom-call(s32[3]{0:T(128)S(1)} %copy-done.23, f32[3]{0:T(128)S(1)} %copy-done.24, bf16[3,512,512]{2,1,0:T(8,128)(2,1)S(1)} %copy-done.4, bf16[3,512,512]{2,1,0:T(8,128)(2,1)S(1)} %copy-done.6, ...), custom_call_target="tpu_custom_call" | custom-call | flops 2415919104 | bytes 4194304 | tf_op jit(solution)/shard_map/near_sandwich/pallas_call | solution.py:215
  230.6 5.2 %near_sandwich.7 = (f32[1,128,512]{2,1,0:T(8,128)S(1)}, f32[1,128,512]{2,1,0:T(8,128)S(1)}, f32[1,128,512]{2,1,0:T(8,128)S(1)}, f32[1,128,512]{2,1,0:T(8,128)S(1)}) custom-call(s32[3]{0:T(128)S(1)} %copy-done.23, f32[3]{0:T(128)S(1)} %copy-done.24, bf16[3,512,512]{2,1,0:T(8,128)(2,1)S(1)} %copy-done.4, bf16[3,512,512]{2,1,0:T(8,128)(2,1)S(1)} %copy-done.6, ...), custom_call_target="tpu_custom_call" | custom-call | flops 2415919104 | bytes 4194304 | tf_op jit(solution)/shard_map/near_sandwich/pallas_call | solution.py:215
  235.9 1.6 collective-permute-start.28
  238.2 5.6 %collective-permute-done.28.refs_6_ = f32[1,128,512]{2,1,0:T(8,128)S(1)} collective-permute-done((f32[1,128,512]{2,1,0:T(8,128)S(1)}, f32[1,128,512]{2,1,0:T(8,128)S(1)}, u32[]{:S(2)}, u32[]{:S(2)}) %collective-permute-start.28) | collective-permute-done | bytes 262176 | tf_op jit(solution)/shard_map/ppermute | solution.py:447
  243.8 5.1 %near_sandwich.4 = (f32[1,128,512]{2,1,0:T(8,128)S(1)}, f32[1,128,512]{2,1,0:T(8,128)S(1)}, f32[1,128,512]{2,1,0:T(8,128)S(1)}, f32[1,128,512]{2,1,0:T(8,128)S(1)}) custom-call(s32[3]{0:T(128)S(1)} %copy-done.23, f32[3]{0:T(128)S(1)} %copy-done.24, bf16[3,512,512]{2,1,0:T(8,128)(2,1)S(1)} %copy-done.4, bf16[3,512,512]{2,1,0:T(8,128)(2,1)S(1)} %copy-done.6, ...), custom_call_target="tpu_custom_call" | custom-call | flops 2415919104 | bytes 4194304 | tf_op jit(solution)/shard_map/near_sandwich/pallas_call | solution.py:215
  252.4 5.4 %collective-permute-done.33.refs_11_ = f32[1,128,512]{2,1,0:T(8,128)S(1)} collective-permute-done((f32[1,128,512]{2,1,0:T(8,128)S(1)}, f32[1,128,512]{2,1,0:T(8,128)S(1)}, u32[]{:S(2)}, u32[]{:S(2)}) %collective-permute-start.33) | collective-permute-done | bytes 262176 | tf_op jit(solution)/shard_map/ppermute | solution.py:447
  257.8 1.5 collective-permute-start.24
  259.3 4.1 %collective-permute-done.34.refs_12_ = f32[1,128,512]{2,1,0:T(8,128)S(1)} collective-permute-done((f32[1,128,512]{2,1,0:T(8,128)S(1)}, f32[1,128,512]{2,1,0:T(8,128)S(1)}, u32[]{:S(2)}, u32[]{:S(2)}) %collective-permute-start.34) | collective-permute-done | bytes 262176 | tf_op jit(solution)/shard_map/ppermute | solution.py:447
  263.5 1.7 collective-permute-start.25
  265.2 3.9 %collective-permute-done.35.refs_13_ = f32[1,128,512]{2,1,0:T(8,128)S(1)} collective-permute-done((f32[1,128,512]{2,1,0:T(8,128)S(1)}, f32[1,128,512]{2,1,0:T(8,128)S(1)}, u32[]{:S(2)}, u32[]{:S(2)}) %collective-permute-start.35) | collective-permute-done | bytes 262176 | tf_op jit(solution)/shard_map/ppermute | solution.py:447
  269.7 5.5 %collective-permute-done.24.refs_0_ = f32[1,128,512]{2,1,0:T(8,128)S(1)} collective-permute-done((f32[1,128,512]{2,1,0:T(8,128)S(1)}, f32[1,128,512]{2,1,0:T(8,128)S(1)}, u32[]{:S(2)}, u32[]{:S(2)}) %collective-permute-start.24) | collective-permute-done | bytes 262176 | tf_op jit(solution)/shard_map/ppermute | solution.py:447
  275.2 5.1 %collective-permute-done.25.refs_1_ = f32[1,128,512]{2,1,0:T(8,128)S(1)} collective-permute-done((f32[1,128,512]{2,1,0:T(8,128)S(1)}, f32[1,128,512]{2,1,0:T(8,128)S(1)}, u32[]{:S(2)}, u32[]{:S(2)}) %collective-permute-start.25) | collective-permute-done | bytes 262176 | tf_op jit(solution)/shard_map/ppermute | solution.py:447
  280.3 1.4 shard_map.56
  (107 shorter events, 19.5 us)
Async XLA Ops:
  1.9 15.2 %collective-permute-start = (f32[2,128,512]{2,1,0:T(8,128)}, f32[2,128,512]{2,1,0:T(8,128)}, u32[]{:S(2)}, u32[]{:S(2)}) collective-permute-start(f32[2,128,512]{2,1,0:T(8,128)} %constant_dynamic-slice_fusion), channel_id=1, source_target_pairs={{0,2},{2,0},{1,3},{3,1},{4,6},{6,4},{5,7},{7,5},{8,10},{10,8},{9,1... | collective-permute-start | bytes 1572872 | tf_op jit(solution)/shard_map/ppermute | solution.py:383
  7.2 23.3 %collective-permute-start.4 = (f32[4,128,512]{2,1,0:T(8,128)}, f32[4,128,512]{2,1,0:T(8,128)}, u32[]{:S(2)}, u32[]{:S(2)}) collective-permute-start(f32[4,128,512]{2,1,0:T(8,128)} %add_momenta.4), channel_id=1, source_target_pairs={{0,1},{1,0},{2,3},{3,2},{4,5},{5,4},{6,7},{7,6},{8,9},{9,8},{10,11... | collective-permute-start | bytes 3145736 | tf_op jit(solution)/shard_map/ppermute | solution.py:355
  9.6 28.1 %collective-permute-start.7 = (f32[4,128,512]{2,1,0:T(8,128)}, f32[4,128,512]{2,1,0:T(8,128)}, u32[]{:S(2)}, u32[]{:S(2)}) collective-permute-start(f32[4,128,512]{2,1,0:T(8,128)} %add_momenta.6), channel_id=1, source_target_pairs={{0,1},{1,0},{2,3},{3,2},{4,5},{5,4},{6,7},{7,6},{8,9},{9,8},{10,11... | collective-permute-start | bytes 3145736 | tf_op jit(solution)/shard_map/ppermute | solution.py:355
  17.1 13.4 %collective-permute-start.2 = (f32[2,128,512]{2,1,0:T(8,128)}, f32[2,128,512]{2,1,0:T(8,128)}, u32[]{:S(2)}, u32[]{:S(2)}) collective-permute-start(f32[2,128,512]{2,1,0:T(8,128)} %collective-permute-done.refs_0_), channel_id=1, source_target_pairs={{0,16},{16,0},{1,17},{17,1},{2,18},{18,2},{3,19},{19,3},{4,20},{20... | collective-permute-start | bytes 1572872 | tf_op jit(solution)/shard_map/ppermute | solution.py:385
  18.9 24.1 %collective-permute-start.1 = (f32[2,128,512]{2,1,0:T(8,128)}, f32[2,128,512]{2,1,0:T(8,128)}, u32[]{:S(2)}, u32[]{:S(2)}) collective-permute-start(f32[2,128,512]{2,1,0:T(8,128)} %collective-permute-done.refs_0_), channel_id=1, source_target_pairs={{0,1},{1,0},{2,3},{3,2},{4,5},{5,4},{6,7},{7,6},{8,9},{9,8},{10,11... | collective-permute-start | bytes 1572872 | tf_op jit(solution)/shard_map/ppermute | solution.py:387
  30.5 14.0 %collective-permute-start.3 = (f32[2,128,512]{2,1,0:T(8,128)}, f32[2,128,512]{2,1,0:T(8,128)}, u32[]{:S(2)}, u32[]{:S(2)}) collective-permute-start(f32[2,128,512]{2,1,0:T(8,128)} %collective-permute-done.2.refs_2_), channel_id=1, source_target_pairs={{0,1},{1,0},{2,3},{3,2},{4,5},{5,4},{6,7},{7,6},{8,9},{9,8},{10,11... | collective-permute-start | bytes 1572872 | tf_op jit(solution)/shard_map/ppermute | solution.py:387
  33.2 58.0 %copy-start.23 = (s32[3]{0:T(128)S(1)}, s32[3]{0:T(128)}, u32[]{:S(2)}) copy-start(s32[3]{0:T(128)} %steps.9) | copy-start | bytes 40
  33.2 59.2 %copy-start.25 = (s32[3]{0:T(128)S(1)}, s32[3]{0:T(128)}, u32[]{:S(2)}) copy-start(s32[3]{0:T(128)} %owners.1) | copy-start | bytes 40
  33.2 27.3 %collective-permute-start.5 = (f32[4,128,512]{2,1,0:T(8,128)}, f32[4,128,512]{2,1,0:T(8,128)}, u32[]{:S(2)}, u32[]{:S(2)}) collective-permute-start(f32[4,128,512]{2,1,0:T(8,128)} %add_momenta.5.refs_8_.refs_0_), channel_id=1, source_target_pairs={{0,4},{4,8},{8,12},{1,5},{5,9},{9,13},{2,6},{6,10},{10,14},{3,7},{... | collective-permute-start | bytes 3145736 | tf_op jit(solution)/shard_map/ppermute | solution.py:366
  40.3 42.2 %collective-permute-start.8 = (f32[4,128,512]{2,1,0:T(8,128)}, f32[4,128,512]{2,1,0:T(8,128)S(1)}, u32[]{:S(2)}, u32[]{:S(2)}) collective-permute-start(f32[4,128,512]{2,1,0:T(8,128)} %add_momenta.7.refs_9_.refs_1_), channel_id=1, source_target_pairs={{0,4},{4,8},{8,12},{1,5},{5,9},{9,13},{2,6},{6,10},{10,14},{3,7},{... | collective-permute-start | bytes 3145736 | tf_op jit(solution)/shard_map/ppermute | solution.py:366
  42.9 40.9 %collective-permute-start.14 = (f32[4,128,512]{2,1,0:T(8,128)}, f32[4,128,512]{2,1,0:T(8,128)S(1)}, u32[]{:S(2)}, u32[]{:S(2)}) collective-permute-start(f32[4,128,512]{2,1,0:T(8,128)} %add_momenta.5.refs_8_.refs_0_), channel_id=1, source_target_pairs={{0,1},{1,0},{2,3},{3,2},{4,5},{5,4},{6,7},{7,6},{8,9},{9,8},{10,11... | collective-permute-start | bytes 3145736 | tf_op jit(solution)/shard_map/ppermute | solution.py:376
  43.0 42.2 %collective-permute-start.36 = (f32[4,128,512]{2,1,0:T(8,128)}, f32[4,128,512]{2,1,0:T(8,128)S(1)}, u32[]{:S(2)}, u32[]{:S(2)}) collective-permute-start(f32[4,128,512]{2,1,0:T(8,128)} %add_momenta.5.refs_8_.refs_0_), channel_id=1, source_target_pairs={{0,2},{2,0},{1,3},{3,1},{4,6},{6,4},{5,7},{7,5},{8,10},{10,8},{9,1... | collective-permute-start | bytes 3145736 | tf_op jit(solution)/shard_map/ppermute | solution.py:407
  44.5 46.7 %collective-permute-start.37 = (f32[4,128,512]{2,1,0:T(8,128)}, f32[4,128,512]{2,1,0:T(8,128)S(1)}, u32[]{:S(2)}, u32[]{:S(2)}) collective-permute-start(f32[4,128,512]{2,1,0:T(8,128)} %add_momenta.7.refs_9_.refs_1_), channel_id=1, source_target_pairs={{0,2},{2,0},{1,3},{3,1},{4,6},{6,4},{5,7},{7,5},{8,10},{10,8},{9,1... | collective-permute-start | bytes 3145736 | tf_op jit(solution)/shard_map/ppermute | solution.py:407
  60.5 36.5 %collective-permute-start.15 = (f32[4,128,512]{2,1,0:T(8,128)}, f32[4,128,512]{2,1,0:T(8,128)S(1)}, u32[]{:S(2)}, u32[]{:S(2)}) collective-permute-start(f32[4,128,512]{2,1,0:T(8,128)} %add_momenta.7.refs_9_.refs_1_), channel_id=1, source_target_pairs={{0,1},{1,0},{2,3},{3,2},{4,5},{5,4},{6,7},{7,6},{8,9},{9,8},{10,11... | collective-permute-start | bytes 3145736 | tf_op jit(solution)/shard_map/ppermute | solution.py:376
  82.5 28.5 %collective-permute-start.16 = (f32[4,128,512]{2,1,0:T(8,128)}, f32[4,128,512]{2,1,0:T(8,128)S(1)}, u32[]{:S(2)}, u32[]{:S(2)}) collective-permute-start(f32[4,128,512]{2,1,0:T(8,128)} %add_momenta.5.refs_8_.refs_0_), channel_id=1, source_target_pairs={{12,8},{8,4},{4,0},{13,9},{9,5},{5,1},{14,10},{10,6},{6,2},{15,11}... | collective-permute-start | bytes 3145736 | tf_op jit(solution)/shard_map/ppermute | solution.py:367
  83.8 48.7 %collective-permute-start.17 = (f32[4,128,512]{2,1,0:T(8,128)}, f32[4,128,512]{2,1,0:T(8,128)}, u32[]{:S(2)}, u32[]{:S(2)}) collective-permute-start(f32[4,128,512]{2,1,0:T(8,128)} %add_momenta.7.refs_9_.refs_1_), channel_id=1, source_target_pairs={{12,8},{8,4},{4,0},{13,9},{9,5},{5,1},{14,10},{10,6},{6,2},{15,11}... | collective-permute-start | bytes 3145736 | tf_op jit(solution)/shard_map/ppermute | solution.py:367
  85.1 49.0 %collective-permute-start.38 = (f32[4,128,512]{2,1,0:T(8,128)S(1)}, f32[4,128,512]{2,1,0:T(8,128)S(1)}, u32[]{:S(2)}, u32[]{:S(2)}) collective-permute-start(f32[4,128,512]{2,1,0:T(8,128)S(1)} %collective-permute-done.36.refs_2_), channel_id=1, source_target_pairs={{0,1},{1,0},{2,3},{3,2},{4,5},{5,4},{6,7},{7,6},{8,9},{9,8},{10,11... | collective-permute-start | bytes 3145736 | tf_op jit(solution)/shard_map/ppermute | solution.py:410
  91.2 43.0 %collective-permute-start.39 = (f32[4,128,512]{2,1,0:T(8,128)S(1)}, f32[4,128,512]{2,1,0:T(8,128)S(1)}, u32[]{:S(2)}, u32[]{:S(2)}) collective-permute-start(f32[4,128,512]{2,1,0:T(8,128)S(1)} %collective-permute-done.37.refs_3_), channel_id=1, source_target_pairs={{0,1},{1,0},{2,3},{3,2},{4,5},{5,4},{6,7},{7,6},{8,9},{9,8},{10,11... | collective-permute-start | bytes 3145736 | tf_op jit(solution)/shard_map/ppermute | solution.py:410
  97.0 54.1 %copy-start.3 = (bf16[3,512,512]{2,1,0:T(8,128)(2,1)}, bf16[3,512,512]{2,1,0:T(8,128)(2,1)S(1)}, u32[]{:S(2)}) copy-start(bf16[3,512,512]{2,1,0:T(8,128)(2,1)S(1)} %get-tuple-element.27.right_high) | copy-start | bytes 4718596
  97.0 54.1 %copy-start.5 = (bf16[3,512,512]{2,1,0:T(8,128)(2,1)}, bf16[3,512,512]{2,1,0:T(8,128)(2,1)S(1)}, u32[]{:S(2)}) copy-start(bf16[3,512,512]{2,1,0:T(8,128)(2,1)S(1)} %get-tuple-element.28.right_low) | copy-start | bytes 4718596
  97.0 54.1 %copy-start.11 = (f32[4,128,512]{2,1,0:T(8,128)}, f32[4,128,512]{2,1,0:T(8,128)S(1)}, u32[]{:S(2)}) copy-start(f32[4,128,512]{2,1,0:T(8,128)S(1)} %collective-permute-done.15.refs_11_.refs_5_) | copy-start | bytes 3145732
  97.0 54.8 %collective-permute-start.6 = (f32[4,128,512]{2,1,0:T(8,128)}, f32[4,128,512]{2,1,0:T(8,128)}, u32[]{:S(2)}, u32[]{:S(2)}) collective-permute-start(f32[4,128,512]{2,1,0:T(8,128)} %collective-permute-done.5.refs_4_), channel_id=1, source_target_pairs={{4,8},{8,12},{5,9},{9,13},{6,10},{10,14},{7,11},{11,15},{20,24},{2... | collective-permute-start | bytes 3145736 | tf_op jit(solution)/shard_map/ppermute | solution.py:366
  111.0 43.4 %collective-permute-start.12 = (f32[4,128,512]{2,1,0:T(8,128)}, f32[4,128,512]{2,1,0:T(8,128)S(1)}, u32[]{:S(2)}, u32[]{:S(2)}) collective-permute-start(f32[4,128,512]{2,1,0:T(8,128)} %collective-permute-done.5.refs_4_), channel_id=1, source_target_pairs={{0,1},{1,0},{2,3},{3,2},{4,5},{5,4},{6,7},{7,6},{8,9},{9,8},{10,11... | collective-permute-start | bytes 3145736 | tf_op jit(solution)/shard_map/ppermute | solution.py:376
  132.5 20.6 %collective-permute-start.9 = (f32[4,128,512]{2,1,0:T(8,128)S(1)}, f32[4,128,512]{2,1,0:T(8,128)}, u32[]{:S(2)}, u32[]{:S(2)}) collective-permute-start(f32[4,128,512]{2,1,0:T(8,128)S(1)} %collective-permute-done.8.refs_5_), channel_id=1, source_target_pairs={{4,8},{8,12},{5,9},{9,13},{6,10},{10,14},{7,11},{11,15},{20,24},{2... | collective-permute-start | bytes 3145736 | tf_op jit(solution)/shard_map/ppermute | solution.py:366
  134.2 21.3 %collective-permute-start.13 = (f32[4,128,512]{2,1,0:T(8,128)S(1)}, f32[4,128,512]{2,1,0:T(8,128)S(1)}, u32[]{:S(2)}, u32[]{:S(2)}) collective-permute-start(f32[4,128,512]{2,1,0:T(8,128)S(1)} %collective-permute-done.8.refs_5_), channel_id=1, source_target_pairs={{0,1},{1,0},{2,3},{3,2},{4,5},{5,4},{6,7},{7,6},{8,9},{9,8},{10,11... | collective-permute-start | bytes 3145736 | tf_op jit(solution)/shard_map/ppermute | solution.py:376
  134.2 22.7 %collective-permute-start.18 = (f32[4,128,512]{2,1,0:T(8,128)S(1)}, f32[4,128,512]{2,1,0:T(8,128)S(1)}, u32[]{:S(2)}, u32[]{:S(2)}) collective-permute-start(f32[4,128,512]{2,1,0:T(8,128)S(1)} %collective-permute-done.16.refs_12_), channel_id=1, source_target_pairs={{0,1},{1,0},{2,3},{3,2},{4,5},{5,4},{6,7},{7,6},{8,9},{9,8},{10,11... | collective-permute-start | bytes 3145736 | tf_op jit(solution)/shard_map/ppermute | solution.py:376
  151.8 30.6 %collective-permute-start.20 = (f32[4,128,512]{2,1,0:T(8,128)S(1)}, f32[4,128,512]{2,1,0:T(8,128)}, u32[]{:S(2)}, u32[]{:S(2)}) collective-permute-start(f32[4,128,512]{2,1,0:T(8,128)S(1)} %collective-permute-done.16.refs_12_), channel_id=1, source_target_pairs={{8,4},{4,0},{9,5},{5,1},{10,6},{6,2},{11,7},{7,3},{24,20},{20,16},... | collective-permute-start | bytes 3145736 | tf_op jit(solution)/shard_map/ppermute | solution.py:367
  153.1 51.1 %collective-permute-start.21 = (f32[4,128,512]{2,1,0:T(8,128)}, f32[4,128,512]{2,1,0:T(8,128)}, u32[]{:S(2)}, u32[]{:S(2)}) collective-permute-start(f32[4,128,512]{2,1,0:T(8,128)} %collective-permute-done.17.refs_13_), channel_id=1, source_target_pairs={{8,4},{4,0},{9,5},{5,1},{10,6},{6,2},{11,7},{7,3},{24,20},{20,16},... | collective-permute-start | bytes 3145736 | tf_op jit(solution)/shard_map/ppermute | solution.py:367
  155.4 50.7 %collective-permute-start.40 = (f32[4,128,512]{2,0,1:T(4,128)S(1)}, f32[4,128,512]{2,0,1:T(4,128)}, u32[]{:S(2)}, u32[]{:S(2)}) collective-permute-start(f32[4,128,512]{2,0,1:T(4,128)S(1)} %copy.6), channel_id=1, source_target_pairs={{0,1},{1,0},{2,3},{3,2},{4,5},{5,4},{6,7},{7,6},{8,9},{9,8},{10,11... | collective-permute-start | bytes 3145736 | tf_op jit(solution)/shard_map/ppermute | solution.py:424
  156.5 55.2 %collective-permute-start.19 = (f32[4,128,512]{2,1,0:T(8,128)}, f32[4,128,512]{2,1,0:T(8,128)}, u32[]{:S(2)}, u32[]{:S(2)}) collective-permute-start(f32[4,128,512]{2,1,0:T(8,128)} %collective-permute-done.17.refs_13_), channel_id=1, source_target_pairs={{0,1},{1,0},{2,3},{3,2},{4,5},{5,4},{6,7},{7,6},{8,9},{9,8},{10,11... | collective-permute-start | bytes 3145736 | tf_op jit(solution)/shard_map/ppermute | solution.py:376
  157.9 55.3 %collective-permute-start.10 = (f32[4,128,512]{2,1,0:T(8,128)}, f32[4,128,512]{2,1,0:T(8,128)}, u32[]{:S(2)}, u32[]{:S(2)}) collective-permute-start(f32[4,128,512]{2,1,0:T(8,128)} %collective-permute-done.6.refs_0_), channel_id=1, source_target_pairs={{8,9},{9,8},{12,13},{13,12},{10,11},{11,10},{14,15},{15,14},{24,25... | collective-permute-start | bytes 3145736 | tf_op jit(solution)/shard_map/ppermute | solution.py:376
  182.4 32.2 %collective-permute-start.11 = (f32[4,128,512]{2,1,0:T(8,128)}, f32[4,128,512]{2,1,0:T(8,128)}, u32[]{:S(2)}, u32[]{:S(2)}) collective-permute-start(f32[4,128,512]{2,1,0:T(8,128)} %collective-permute-done.9.refs_1_), channel_id=1, source_target_pairs={{8,9},{9,8},{12,13},{13,12},{10,11},{11,10},{14,15},{15,14},{24,25... | collective-permute-start | bytes 3145736 | tf_op jit(solution)/shard_map/ppermute | solution.py:376
  204.2 10.3 %collective-permute-start.22 = (f32[4,128,512]{2,1,0:T(8,128)}, f32[4,128,512]{2,1,0:T(8,128)}, u32[]{:S(2)}, u32[]{:S(2)}) collective-permute-start(f32[4,128,512]{2,1,0:T(8,128)} %collective-permute-done.20.refs_16_), channel_id=1, source_target_pairs={{0,1},{1,0},{4,5},{5,4},{2,3},{3,2},{6,7},{7,6},{16,17},{17,16},{2... | collective-permute-start | bytes 3145736 | tf_op jit(solution)/shard_map/ppermute | solution.py:376
  206.2 8.4 %collective-permute-start.23 = (f32[4,128,512]{2,1,0:T(8,128)}, f32[4,128,512]{2,1,0:T(8,128)}, u32[]{:S(2)}, u32[]{:S(2)}) collective-permute-start(f32[4,128,512]{2,1,0:T(8,128)} %collective-permute-done.21.refs_17_), channel_id=1, source_target_pairs={{0,1},{1,0},{4,5},{5,4},{2,3},{3,2},{6,7},{7,6},{16,17},{17,16},{2... | collective-permute-start | bytes 3145736 | tf_op jit(solution)/shard_map/ppermute | solution.py:376
  211.7 68.6 %collective-permute-start.41 = (f32[128,8,512]{2,1,0:T(8,128)S(1)}, f32[128,8,512]{2,1,0:T(8,128)S(1)}, u32[]{:S(2)}, u32[]{:S(2)}) collective-permute-start(f32[128,8,512]{2,1,0:T(8,128)S(1)} %maximum_bitcast_fusion), channel_id=1, source_target_pairs={{0,12},{1,13},{2,14},{3,15},{16,28},{17,29},{18,30},{19,31}} | collective-permute-start | bytes 6291464 | tf_op jit(solution)/shard_map/ppermute | solution.py:428
  213.3 67.1 %collective-permute-start.42 = (f32[128,8,512]{2,1,0:T(8,128)S(1)}, f32[128,8,512]{2,1,0:T(8,128)S(1)}, u32[]{:S(2)}, u32[]{:S(2)}) collective-permute-start(f32[128,8,512]{2,1,0:T(8,128)S(1)} %maximum_bitcast_fusion), channel_id=1, source_target_pairs={{12,0},{13,1},{14,2},{15,3},{28,16},{29,17},{30,18},{31,19}} | collective-permute-start | bytes 6291464 | tf_op jit(solution)/shard_map/ppermute | solution.py:429
  223.4 14.0 %collective-permute-start.26 = (f32[1,128,512]{2,1,0:T(8,128)S(1)}, f32[1,128,512]{2,1,0:T(8,128)S(1)}, u32[]{:S(2)}, u32[]{:S(2)}) collective-permute-start(f32[1,128,512]{2,1,0:T(8,128)S(1)} %get-tuple-element.36), channel_id=1, source_target_pairs={{0,2},{1,3},{2,0},{3,1},{4,6},{5,7},{6,4},{7,5},{8,10},{9,11},{10,... | collective-permute-start | bytes 786440 | tf_op jit(solution)/shard_map/ppermute | solution.py:447
  230.0 8.1 %collective-permute-start.27 = (f32[1,128,512]{2,1,0:T(8,128)S(1)}, f32[1,128,512]{2,1,0:T(8,128)S(1)}, u32[]{:S(2)}, u32[]{:S(2)}) collective-permute-start(f32[1,128,512]{2,1,0:T(8,128)S(1)} %get-tuple-element.37), channel_id=1, source_target_pairs={{0,2},{1,3},{2,0},{3,1},{4,6},{5,7},{6,4},{7,5},{8,10},{9,11},{10,... | collective-permute-start | bytes 786440 | tf_op jit(solution)/shard_map/ppermute | solution.py:447
  235.9 7.9 %collective-permute-start.28 = (f32[1,128,512]{2,1,0:T(8,128)S(1)}, f32[1,128,512]{2,1,0:T(8,128)S(1)}, u32[]{:S(2)}, u32[]{:S(2)}) collective-permute-start(f32[1,128,512]{2,1,0:T(8,128)S(1)} %get-tuple-element.38), channel_id=1, source_target_pairs={{0,2},{1,3},{2,0},{3,1},{4,6},{5,7},{6,4},{7,5},{8,10},{9,11},{10,... | collective-permute-start | bytes 786440 | tf_op jit(solution)/shard_map/ppermute | solution.py:447
  237.4 11.4 %collective-permute-start.29 = (f32[1,128,512]{2,1,0:T(8,128)S(1)}, f32[1,128,512]{2,1,0:T(8,128)S(1)}, u32[]{:S(2)}, u32[]{:S(2)}) collective-permute-start(f32[1,128,512]{2,1,0:T(8,128)S(1)} %get-tuple-element.39), channel_id=1, source_target_pairs={{0,1},{1,0},{2,3},{3,2},{4,5},{5,4},{6,7},{7,6},{8,9},{9,8},{10,11... | collective-permute-start | bytes 786440 | tf_op jit(solution)/shard_map/ppermute | solution.py:447
  238.2 11.4 %collective-permute-start.30 = (f32[1,128,512]{2,1,0:T(8,128)S(1)}, f32[1,128,512]{2,1,0:T(8,128)S(1)}, u32[]{:S(2)}, u32[]{:S(2)}) collective-permute-start(f32[1,128,512]{2,1,0:T(8,128)S(1)} %get-tuple-element.40), channel_id=1, source_target_pairs={{0,1},{1,0},{2,3},{3,2},{4,5},{5,4},{6,7},{7,6},{8,9},{9,8},{10,11... | collective-permute-start | bytes 786440 | tf_op jit(solution)/shard_map/ppermute | solution.py:447
  243.8 6.9 %collective-permute-start.31 = (f32[1,128,512]{2,1,0:T(8,128)S(1)}, f32[1,128,512]{2,1,0:T(8,128)S(1)}, u32[]{:S(2)}, u32[]{:S(2)}) collective-permute-start(f32[1,128,512]{2,1,0:T(8,128)S(1)} %get-tuple-element.41), channel_id=1, source_target_pairs={{0,1},{1,0},{2,3},{3,2},{4,5},{5,4},{6,7},{7,6},{8,9},{9,8},{10,11... | collective-permute-start | bytes 786440 | tf_op jit(solution)/shard_map/ppermute | solution.py:447
  248.9 2.4 collective-permute-start.32
  249.5 8.3 %collective-permute-start.33 = (f32[1,128,512]{2,1,0:T(8,128)S(1)}, f32[1,128,512]{2,1,0:T(8,128)S(1)}, u32[]{:S(2)}, u32[]{:S(2)}) collective-permute-start(f32[1,128,512]{2,1,0:T(8,128)S(1)} %get-tuple-element.43), channel_id=1, source_target_pairs={{0,3},{1,2},{2,1},{3,0},{4,7},{5,6},{6,5},{7,4},{8,11},{9,10},{10,... | collective-permute-start | bytes 786440 | tf_op jit(solution)/shard_map/ppermute | solution.py:447
  250.7 12.8 %collective-permute-start.34 = (f32[1,128,512]{2,1,0:T(8,128)S(1)}, f32[1,128,512]{2,1,0:T(8,128)S(1)}, u32[]{:S(2)}, u32[]{:S(2)}) collective-permute-start(f32[1,128,512]{2,1,0:T(8,128)S(1)} %get-tuple-element.44), channel_id=1, source_target_pairs={{0,3},{1,2},{2,1},{3,0},{4,7},{5,6},{6,5},{7,4},{8,11},{9,10},{10,... | collective-permute-start | bytes 786440 | tf_op jit(solution)/shard_map/ppermute | solution.py:447
  251.3 17.8 %collective-permute-start.35 = (f32[1,128,512]{2,1,0:T(8,128)S(1)}, f32[1,128,512]{2,1,0:T(8,128)S(1)}, u32[]{:S(2)}, u32[]{:S(2)}) collective-permute-start(f32[1,128,512]{2,1,0:T(8,128)S(1)} %get-tuple-element.45), channel_id=1, source_target_pairs={{0,3},{1,2},{2,1},{3,0},{4,7},{5,6},{6,5},{7,4},{8,11},{9,10},{10,... | collective-permute-start | bytes 786440 | tf_op jit(solution)/shard_map/ppermute | solution.py:447
  257.8 17.4 %collective-permute-start.24 = (f32[1,128,512]{2,1,0:T(8,128)S(1)}, f32[1,128,512]{2,1,0:T(8,128)S(1)}, u32[]{:S(2)}, u32[]{:S(2)}) collective-permute-start(f32[1,128,512]{2,1,0:T(8,128)S(1)} %get-tuple-element.30), channel_id=1, source_target_pairs={{0,2},{1,3},{2,0},{3,1},{4,6},{5,7},{6,4},{7,5},{8,10},{9,11},{10,... | collective-permute-start | bytes 786440 | tf_op jit(solution)/shard_map/ppermute | solution.py:447
  263.5 16.9 %collective-permute-start.25 = (f32[1,128,512]{2,1,0:T(8,128)S(1)}, f32[1,128,512]{2,1,0:T(8,128)S(1)}, u32[]{:S(2)}, u32[]{:S(2)}) collective-permute-start(f32[1,128,512]{2,1,0:T(8,128)S(1)} %get-tuple-element.31), channel_id=1, source_target_pairs={{0,3},{1,2},{2,1},{3,0},{4,7},{5,6},{6,5},{7,4},{8,11},{9,10},{10,... | collective-permute-start | bytes 786440 | tf_op jit(solution)/shard_map/ppermute | solution.py:447
  (21 other events, 339.5 us)

commit v9 on v8

--- a/solution.py
+++ b/solution.py
@@ -13,8 +13,9 @@
 PIECES = 2
 
 
-def chunks_of(half):
-    return [1] * half
+def chunks_of(half, order):
+    middle = order // 2
+    return [(0, 1, 0, middle), (0, 1, middle, order - middle)] + [(e, 1, 0, order) for e in range(1, half)]
 
 
 def halves(x):
@@ -94,7 +95,7 @@
         pltpu.make_async_copy(total.at[e], out.at[e], left.at[e]).wait()
 
 
-def split_dot(n_groups, n_parts, n_atoms, momenta, base, grid_total, edev, far, line, steps, occupation, right_high, right_low, left, *refs):
+def split_dot(n_groups, n_parts, n_atoms, momenta, base, columns, grid_total, edev, far, line, steps, occupation, right_high, right_low, left, *refs):
     sources = [
         [refs[(g * 2 + h) * n_parts : (g * 2 + h + 1) * n_parts] for h in range(2)]
         for g in range(n_groups)
@@ -183,7 +184,8 @@
                 continue
             high = combined.astype(jnp.bfloat16)
             low = (combined - high.astype(jnp.float32)).astype(jnp.bfloat16)
-            product = dot(high, right_high[mode]) + dot(low, right_high[mode]) + dot(high, right_low[mode])
+            first, second = right_high[mode, :, columns], right_low[mode, :, columns]
+            product = dot(high, first) + dot(low, first) + dot(high, second)
             high = product.astype(jnp.bfloat16)
             low = (product - high.astype(jnp.float32)).astype(jnp.bfloat16)
             inner[mode, pl.ds(0, rows)] = high
@@ -203,25 +205,26 @@
             out[energy] = result
 
 
-def sandwich(steps, occupation, right, left, groups, n_atoms, momenta, base, grid_total, edev, far, line, out_rows, count):
+def sandwich(steps, occupation, right, left, groups, n_atoms, momenta, base, grid_total, edev, far, line, out_rows, count, first=0, width=None):
     order = right[0].shape[-1]
+    width = width or order
     flat = [part for group in groups for half in group for part in half]
     rows = sum(part.shape[1] for part in groups[0][0])
     n_out = left.shape[1] // out_rows
     buffers = min(count, 2)
     held = 4 * (2 * MODES * buffers + 6) * rows * order + 2 * 3 * MODES * rows * order + (6 << 20)
     held += 4 * left.shape[1] * order * (count + 3) + 4 * MODES * order * order + 2 * left.size
-    flops = count * 2 * 3 * MODES * (rows * order * order + left.shape[1] * rows * order)
+    flops = count * 2 * 3 * MODES * (rows * order * width + left.shape[1] * rows * width)
     return pl.pallas_call(
-        functools.partial(split_dot, len(groups), len(groups[0][0]), n_atoms, momenta, base, grid_total, edev, far, line),
-        out_shape=[jax.ShapeDtypeStruct((count, out_rows, order), jnp.float32)] * n_out,
+        functools.partial(split_dot, len(groups), len(groups[0][0]), n_atoms, momenta, base, pl.ds(first, width), grid_total, edev, far, line),
+        out_shape=[jax.ShapeDtypeStruct((count, out_rows, width), jnp.float32)] * n_out,
         in_specs=[pl.BlockSpec(memory_space=pltpu.SMEM)] * 2
         + [pl.BlockSpec(memory_space=pltpu.VMEM)] * 3
         + [pl.BlockSpec(memory_space=pltpu.HBM)] * len(flat),
         out_specs=[pl.BlockSpec(memory_space=pltpu.VMEM)] * n_out,
         scratch_shapes=[
             pltpu.VMEM((buffers, 2 * MODES, rows, order), jnp.float32),
-            pltpu.VMEM((MODES, 3 * rows, order), jnp.bfloat16),
+            pltpu.VMEM((MODES, 3 * rows, width), jnp.bfloat16),
             pltpu.VMEM((left.shape[1] if far else 8, order), jnp.float32),
             pltpu.SemaphoreType.DMA((2, 2 * MODES)),
         ],
@@ -235,6 +238,10 @@
     )(steps, occupation, right[0], right[1], left, *flat)
 
 
+def beside(refs, term, rows):
+    return jnp.concatenate([refs[ref][row, rows] for ref, row in term], axis=1)
+
+
 def gather_early(layout, count, *refs):
     out = refs[-1]
     core = lax.axis_index("kz")
@@ -250,8 +257,9 @@
                     where = (own if half == 0 else 1 - own) * count
                     for j, terms in enumerate(energies):
                         total = None
-                        for ref, row in terms:
-                            total = refs[ref][row, rows] if total is None else total + refs[ref][row, rows]
+                        for term in terms:
+                            value = beside(refs, term, rows)
+                            total = value if total is None else total + value
                         out[rows, where + j, :] = total
 
 
@@ -277,8 +285,8 @@
                     for j, terms in enumerate(energies):
                         if terms:
                             value = total[rows, where + j, :]
-                            for ref, row in terms:
-                                value = value + refs[ref][row, rows]
+                            for term in terms:
+                                value = value + beside(refs, term, rows)
                             total[rows, where + j, :] = value
 
         pltpu.make_async_copy(total.at[rows], out.at[rows], sem).start()
@@ -286,9 +294,11 @@
     pltpu.make_async_copy(total, out, sem).wait()
 
 
-def gathered(layout, count, arrays, before=()):
-    terms = [[[(arrays.index(x), row) for x, row in entry] for entry in energies] for energies in layout]
-    out_rows, order = arrays[0].shape[1:]
+def gathered(layout, count, order, arrays, before=()):
+    terms = [
+        [[[(arrays.index(x), row) for x, row in term] for term in entry] for entry in energies] for energies in layout
+    ]
+    out_rows = arrays[0].shape[1]
     arrays = list(arrays) + list(before)
     shape = (out_rows, 2 * count, order)
     size = 4 * sum(x.size for x in arrays) + 4 * 2 * count * out_rows * order
@@ -428,13 +438,14 @@
         beyond.append(lax.ppermute(both, "energy", [(0, n - 1)]))
         beyond.append(lax.ppermute(both, "energy", [(n - 1, 0)]))
 
-    terms = [[[] for _ in range(atoms)] for _ in range(cores)]
-    base = 0
-    for count in chunks_of(half):
+    chunks = chunks_of(half, order)
+    entries = [[[[] for _ in range(atoms)] for _ in range(half)] for _ in range(cores)]
+    early, last = Terms(), Terms()
+    for chunk, (energy, count, first, width) in enumerate(chunks):
         sums = sandwich(
-            offsets, occupation, right, left_near, groups, atoms, momenta, base, grid_total, edev, False, line, out_rows, count
+            offsets, occupation, right, left_near, groups, atoms, momenta, energy, grid_total, edev, False, line, out_rows,
+            count, first, width,
         )
-        base += count
         for s in range(atoms - 1, -1, -1):
             for t in range(cores):
                 block = sums[s * cores + t]
@@ -445,22 +456,18 @@
                         for k in range(cores)
                     ]
                     block = lax.ppermute(block, ("atom", "kz"), pairs)
-                terms[t][s].append(block)
-    chunks = chunks_of(half)
-    entries = [[[] for _ in range(half)] for _ in range(cores)]
-    late = [[[] for _ in range(half)] for _ in range(cores)]
-    early, last = Terms(), Terms()
-    for t in range(cores):
-        for s in range(atoms):
-            first = 0
-            for chunk, block in enumerate(terms[t][s]):
-                held = (last, late) if s and chunk == len(chunks) - 1 else (early, entries)
-                held[0].append(block)
-                for row in range(chunks[chunk]):
-                    held[1][t][first + row].append((block, row))
-                first += chunks[chunk]
-    total = gathered(entries, half, early)
-    return gathered(late, half, last, [total] + beyond)
+                (last if s and chunk == len(chunks) - 1 else early).append(block)
+                for row in range(count):
+                    entries[t][energy + row][s].append((block, row))
+    final = {id(x) for x in last}
+
+    def chosen(late):
+        return [
+            [[term for term in terms if (id(term[-1][0]) in final) == late] for terms in energies] for energies in entries
+        ]
+
+    total = gathered(chosen(False), half, order, early)
+    return gathered(chosen(True), half, order, last, [total] + beyond)
 
 
 def solution(mesh):

time: 283 us -> 279 us (0.986)
  waiting for transfers between devices: 169 us -> 161 us
  Pallas kernels: 52.8 us -> 56.1 us
    ppermute x12 -> x15, waiting for transfers between devices: 30.4 us -> 21.4 us  [shards(): block = lax.ppermute(block, ('atom', 'kz'), pairs)]
    pallas_call x5 -> x6, Pallas kernels: 36.8 us -> 40 us  [sandwich(): pl.pallas_call(functools.partial(split_dot, len(groups), len(groups[0][0]...]
    ppermute x12 -> x15, starting transfers between devices: 10.5 us -> 12 us  [shards(): block = lax.ppermute(block, ('atom', 'kz'), pairs)]
    unnamed x52 -> x48, local copies, waits for them, and re-layouts: 8.32 us -> 7.06 us
  transfers between devices with their start and end apart: 43 -> 46, of which waited for: 16 -> 14; matrix products, arithmetic and copies ran while one was open for 1% -> 2% of each run, Pallas kernels for 18% -> 20%
where the time goes in v9:
time: 279 us; the launch traced here: 278 us
  waiting for transfers between devices  161 us (58%)
  Pallas kernels  56.1 us (20%)
  starting transfers between devices  46.3 us (17%)
  local copies, waits for them, and re-layouts  10.6 us (4%)
  other arithmetic  2.98 us (1%)
    ppermute x4, waiting for transfers between devices, shards(): lax.ppermute(x, 'energy', down[d - 1])  77.6 us
    pallas_call x6, Pallas kernels, sandwich(): pl.pallas_call(functools.partial(split_dot, len(groups), len(groups[0][0]...  40 us
    ppermute x4, waiting for transfers between devices, shards(): streams[-d] = [lax.ppermute(x, 'energy', up[d - 1]) for x in streams[1 - d]]  37.5 us
    ppermute x15, waiting for transfers between devices, shards(): block = lax.ppermute(block, ('atom', 'kz'), pairs)  21.4 us
    ppermute x15, starting transfers between devices, shards(): block = lax.ppermute(block, ('atom', 'kz'), pairs)  12 us
    ppermute x1, waiting for transfers between devices, shards(): lax.ppermute(got, 'grp', [(i, (i + d) % parts) for i in range(parts)])  11.6 us
    ppermute x4, starting transfers between devices, shards(): streams[-d] = [lax.ppermute(x, 'energy', up[d - 1]) for x in streams[1 - d]]  10.9 us
    pallas_call x4, Pallas kernels, summed(): pl.pallas_call(functools.partial(add_momenta, theirs, piece * size), out_...  9.89 us
  transfers between devices with their start and end apart: 46, of which 14 were waited for; matrix products, arithmetic and copies ran while one was open for 2% of the time, Pallas kernels for 20%

profile of v9, /device:TPU:0, one launch (start us, length us, event | category | flops | bytes accessed | tf_op | source)
XLA Modules:
  0.0 277.9 jit_solution(11683497265262467251)
XLA Ops:
  0.0 1.9 constant_dynamic-slice_fusion
  1.9 3.0 %collective-permute-start = (f32[2,128,512]{2,1,0:T(8,128)}, f32[2,128,512]{2,1,0:T(8,128)}, u32[]{:S(2)}, u32[]{:S(2)}) collective-permute-start(f32[2,128,512]{2,1,0:T(8,128)} %constant_dynamic-slice_fusion), channel_id=1, source_target_pairs={{0,2},{2,0},{1,3},{3,1},{4,6},{6,4},{5,7},{7,5},{8,10},{10,8},{9,1... | collective-permute-start | bytes 1572872 | tf_op jit(solution)/shard_map/ppermute | solution.py:393
  4.9 2.3 add_momenta.4
  7.2 2.3 add_momenta.6
  10.1 7.0 %collective-permute-done.refs_0_ = f32[2,128,512]{2,1,0:T(8,128)} collective-permute-done((f32[2,128,512]{2,1,0:T(8,128)}, f32[2,128,512]{2,1,0:T(8,128)}, u32[]{:S(2)}, u32[]{:S(2)}) %collective-permute-start) | collective-permute-done | bytes 524320 | tf_op jit(solution)/shard_map/ppermute | solution.py:393
  17.1 1.8 collective-permute-start.2
  18.9 11.6 %collective-permute-done.2.refs_2_ = f32[2,128,512]{2,1,0:T(8,128)} collective-permute-done((f32[2,128,512]{2,1,0:T(8,128)}, f32[2,128,512]{2,1,0:T(8,128)}, u32[]{:S(2)}, u32[]{:S(2)}) %collective-permute-start.2) | collective-permute-done | bytes 524320 | tf_op jit(solution)/shard_map/ppermute | solution.py:395
  30.5 2.6 add_momenta.5.refs_8_.refs_0_
  33.2 4.4 %collective-permute-start.5 = (f32[4,128,512]{2,1,0:T(8,128)}, f32[4,128,512]{2,1,0:T(8,128)}, u32[]{:S(2)}, u32[]{:S(2)}) collective-permute-start(f32[4,128,512]{2,1,0:T(8,128)} %add_momenta.5.refs_8_.refs_0_), channel_id=1, source_target_pairs={{0,4},{4,8},{8,12},{1,5},{5,9},{9,13},{2,6},{6,10},{10,14},{3,7},{... | collective-permute-start | bytes 3145736 | tf_op jit(solution)/shard_map/ppermute | solution.py:376
  37.6 2.6 add_momenta.7.refs_9_.refs_1_
  40.3 2.6 collective-permute-start.8
  42.9 1.6 collective-permute-start.39
  45.0 15.4 %collective-permute-done.5.refs_4_ = f32[4,128,512]{2,1,0:T(8,128)} collective-permute-done((f32[4,128,512]{2,1,0:T(8,128)}, f32[4,128,512]{2,1,0:T(8,128)}, u32[]{:S(2)}, u32[]{:S(2)}) %collective-permute-start.5) | collective-permute-done | bytes 1048608 | tf_op jit(solution)/shard_map/ppermute | solution.py:376
  60.5 22.0 %collective-permute-done.8.refs_5_ = f32[4,128,512]{2,1,0:T(8,128)S(1)} collective-permute-done((f32[4,128,512]{2,1,0:T(8,128)}, f32[4,128,512]{2,1,0:T(8,128)S(1)}, u32[]{:S(2)}, u32[]{:S(2)}) %collective-permute-start.8) | collective-permute-done | bytes 1048608 | tf_op jit(solution)/shard_map/ppermute | solution.py:376
  83.8 1.3 collective-permute-start.17
  85.2 6.0 %collective-permute-done.40.refs_3_ = f32[4,128,512]{2,1,0:T(8,128)S(1)} collective-permute-done((f32[4,128,512]{2,1,0:T(8,128)}, f32[4,128,512]{2,1,0:T(8,128)S(1)}, u32[]{:S(2)}, u32[]{:S(2)}) %collective-permute-start.40) | collective-permute-done | bytes 1048608 | tf_op jit(solution)/shard_map/ppermute | solution.py:417
  92.4 1.6 copy-done.19
  93.9 3.0 %prepare.1 = (bf16[3,512,512]{2,1,0:T(8,128)(2,1)S(1)}, bf16[3,512,512]{2,1,0:T(8,128)(2,1)S(1)}, bf16[3,256,1536]{2,1,0:T(8,128)(2,1)S(1)}, bf16[3,512,768]{2,1,0:T(8,128)(2,1)S(1)}) custom-call(s32[3]{0:T(128)S(1)} %copy-done.23, f32[2,512,512]{2,1,0:T(8,128)S(1)} %copy-done.19, f32[2,128,512]{2,1,0:T(8,128)} %collective-permute-done.refs_0_, ...), custom_call_target="tpu_custom_call" | custom-call | flops 6291456 | bytes 7864320 | tf_op jit(solution)/shard_map/prepare/pallas_call | solution.py:402
  97.0 2.1 collective-permute-start.6
  99.1 12.0 %collective-permute-done.16.refs_12_ = f32[4,128,512]{2,1,0:T(8,128)} collective-permute-done((f32[4,128,512]{2,1,0:T(8,128)}, f32[4,128,512]{2,1,0:T(8,128)}, u32[]{:S(2)}, u32[]{:S(2)}) %collective-permute-start.16) | collective-permute-done | bytes 1048608 | tf_op jit(solution)/shard_map/ppermute | solution.py:377
  111.1 21.4 %collective-permute-done.17.refs_13_ = f32[4,128,512]{2,1,0:T(8,128)} collective-permute-done((f32[4,128,512]{2,1,0:T(8,128)}, f32[4,128,512]{2,1,0:T(8,128)}, u32[]{:S(2)}, u32[]{:S(2)}) %collective-permute-start.17) | collective-permute-done | bytes 1048608 | tf_op jit(solution)/shard_map/ppermute | solution.py:377
  132.5 1.7 collective-permute-start.9
  134.8 16.0 %far_sandwich.1 = (f32[4,128,512]{2,1,0:T(8,128)S(1)}, f32[4,128,512]{2,1,0:T(8,128)S(1)}) custom-call(s32[3]{0:T(128)S(1)} %guard.1.steps, f32[3]{0:T(128)S(1)} %copy-done.22, bf16[3,512,512]{2,1,0:T(8,128)(2,1)S(1)} %get-tuple-element.31.right_high, bf16[3,512,512]{2,1,0:T(8,128)(2,1)S(1)} %get-tuple-element.32.right_low, ...), custom_call_target="tpu_custom_call" | custom-call | flops 14495514624 | bytes 27262976 | tf_op jit(solution)/shard_map/far_sandwich/pallas_call | solution.py:218
  150.8 1.7 copy.6
  153.8 1.3 collective-permute-start.21
  158.6 1.6 collective-permute-start.10
  160.2 23.1 %collective-permute-done.20.refs_16_ = f32[4,128,512]{2,1,0:T(8,128)} collective-permute-done((f32[4,128,512]{2,1,0:T(8,128)}, f32[4,128,512]{2,1,0:T(8,128)}, u32[]{:S(2)}, u32[]{:S(2)}) %collective-permute-start.20) | collective-permute-done | bytes 1048608 | tf_op jit(solution)/shard_map/ppermute | solution.py:377
  184.0 21.1 %collective-permute-done.21.refs_17_ = f32[4,128,512]{2,1,0:T(8,128)} collective-permute-done((f32[4,128,512]{2,1,0:T(8,128)}, f32[4,128,512]{2,1,0:T(8,128)}, u32[]{:S(2)}, u32[]{:S(2)}) %collective-permute-start.21) | collective-permute-done | bytes 1048608 | tf_op jit(solution)/shard_map/ppermute | solution.py:377
  205.1 1.9 collective-permute-start.22
  207.0 2.4 collective-permute-start.23
  209.5 2.6 copy_select_fusion.1
  212.5 1.7 collective-permute-start.44
  214.2 1.3 collective-permute-start.45
  218.1 4.4 %near_sandwich.6 = (f32[1,128,256]{2,1,0:T(8,128)S(1)}, f32[1,128,256]{2,1,0:T(8,128)S(1)}, f32[1,128,256]{2,1,0:T(8,128)S(1)}, f32[1,128,256]{2,1,0:T(8,128)S(1)}) custom-call(s32[3]{0:T(128)S(1)} %copy-done.21, f32[3]{0:T(128)S(1)} %copy-done.22, bf16[3,512,512]{2,1,0:T(8,128)(2,1)S(1)} %copy-done.1, bf16[3,512,512]{2,1,0:T(8,128)(2,1)S(1)} %copy-done.3, ...), custom_call_target="tpu_custom_call" | custom-call | flops 1207959552 | bytes 4194304 | tf_op jit(solution)/shard_map/near_sandwich/pallas_call | solution.py:218
  222.5 1.6 collective-permute-start.26
  224.7 4.5 %near_sandwich.7 = (f32[1,128,256]{2,1,0:T(8,128)S(1)}, f32[1,128,256]{2,1,0:T(8,128)S(1)}, f32[1,128,256]{2,1,0:T(8,128)S(1)}, f32[1,128,256]{2,1,0:T(8,128)S(1)}) custom-call(s32[3]{0:T(128)S(1)} %copy-done.21, f32[3]{0:T(128)S(1)} %copy-done.22, bf16[3,512,512]{2,1,0:T(8,128)(2,1)S(1)} %copy-done.1, bf16[3,512,512]{2,1,0:T(8,128)(2,1)S(1)} %copy-done.3, ...), custom_call_target="tpu_custom_call" | custom-call | flops 1207959552 | bytes 4194304 | tf_op jit(solution)/shard_map/near_sandwich/pallas_call | solution.py:218
  229.2 1.6 collective-permute-start.29
  232.0 5.0 %near_sandwich.8 = (f32[1,128,512]{2,1,0:T(8,128)S(1)}, f32[1,128,512]{2,1,0:T(8,128)S(1)}, f32[1,128,512]{2,1,0:T(8,128)S(1)}, f32[1,128,512]{2,1,0:T(8,128)S(1)}) custom-call(s32[3]{0:T(128)S(1)} %copy-done.21, f32[3]{0:T(128)S(1)} %copy-done.22, bf16[3,512,512]{2,1,0:T(8,128)(2,1)S(1)} %copy-done.1, bf16[3,512,512]{2,1,0:T(8,128)(2,1)S(1)} %copy-done.3, ...), custom_call_target="tpu_custom_call" | custom-call | flops 2415919104 | bytes 4194304 | tf_op jit(solution)/shard_map/near_sandwich/pallas_call | solution.py:218
  239.3 5.1 %near_sandwich.9 = (f32[1,128,512]{2,1,0:T(8,128)S(1)}, f32[1,128,512]{2,1,0:T(8,128)S(1)}, f32[1,128,512]{2,1,0:T(8,128)S(1)}, f32[1,128,512]{2,1,0:T(8,128)S(1)}) custom-call(s32[3]{0:T(128)S(1)} %copy-done.21, f32[3]{0:T(128)S(1)} %copy-done.22, bf16[3,512,512]{2,1,0:T(8,128)(2,1)S(1)} %copy-done.1, bf16[3,512,512]{2,1,0:T(8,128)(2,1)S(1)} %copy-done.3, ...), custom_call_target="tpu_custom_call" | custom-call | flops 2415919104 | bytes 4194304 | tf_op jit(solution)/shard_map/near_sandwich/pallas_call | solution.py:218
  244.3 2.0 collective-permute-done.32.refs_8_
  247.2 4.0 %collective-permute-done.33.refs_9_ = f32[1,128,512]{2,1,0:T(8,128)S(1)} collective-permute-done((f32[1,128,512]{2,1,0:T(8,128)S(1)}, f32[1,128,512]{2,1,0:T(8,128)S(1)}, u32[]{:S(2)}, u32[]{:S(2)}) %collective-permute-start.33) | collective-permute-done | bytes 262176 | tf_op jit(solution)/shard_map/ppermute | solution.py:458
  251.2 1.4 collective-permute-start.36
  252.5 5.1 %near_sandwich.5 = (f32[1,128,512]{2,1,0:T(8,128)S(1)}, f32[1,128,512]{2,1,0:T(8,128)S(1)}, f32[1,128,512]{2,1,0:T(8,128)S(1)}, f32[1,128,512]{2,1,0:T(8,128)S(1)}) custom-call(s32[3]{0:T(128)S(1)} %copy-done.21, f32[3]{0:T(128)S(1)} %copy-done.22, bf16[3,512,512]{2,1,0:T(8,128)(2,1)S(1)} %copy-done.1, bf16[3,512,512]{2,1,0:T(8,128)(2,1)S(1)} %copy-done.3, ...), custom_call_target="tpu_custom_call" | custom-call | flops 2415919104 | bytes 4194304 | tf_op jit(solution)/shard_map/near_sandwich/pallas_call | solution.py:218
  258.3 4.1 %collective-permute-done.36.refs_13_ = f32[1,128,512]{2,1,0:T(8,128)S(1)} collective-permute-done((f32[1,128,512]{2,1,0:T(8,128)S(1)}, f32[1,128,512]{2,1,0:T(8,128)S(1)}, u32[]{:S(2)}, u32[]{:S(2)}) %collective-permute-start.36) | collective-permute-done | bytes 262176 | tf_op jit(solution)/shard_map/ppermute | solution.py:458
  262.6 1.7 collective-permute-start.25
  264.9 6.7 %collective-permute-done.24.refs_0_ = f32[1,128,512]{2,1,0:T(8,128)S(1)} collective-permute-done((f32[1,128,512]{2,1,0:T(8,128)S(1)}, f32[1,128,512]{2,1,0:T(8,128)S(1)}, u32[]{:S(2)}, u32[]{:S(2)}) %collective-permute-start.24) | collective-permute-done | bytes 262176 | tf_op jit(solution)/shard_map/ppermute | solution.py:458
  271.6 4.7 %collective-permute-done.25.refs_1_ = f32[1,128,512]{2,1,0:T(8,128)S(1)} collective-permute-done((f32[1,128,512]{2,1,0:T(8,128)S(1)}, f32[1,128,512]{2,1,0:T(8,128)S(1)}, u32[]{:S(2)}, u32[]{:S(2)}) %collective-permute-start.25) | collective-permute-done | bytes 262176 | tf_op jit(solution)/shard_map/ppermute | solution.py:458
  276.3 1.4 shard_map.56
  (110 shorter events, 19.2 us)
Async XLA Ops:
  1.9 15.2 %collective-permute-start = (f32[2,128,512]{2,1,0:T(8,128)}, f32[2,128,512]{2,1,0:T(8,128)}, u32[]{:S(2)}, u32[]{:S(2)}) collective-permute-start(f32[2,128,512]{2,1,0:T(8,128)} %constant_dynamic-slice_fusion), channel_id=1, source_target_pairs={{0,2},{2,0},{1,3},{3,1},{4,6},{6,4},{5,7},{7,5},{8,10},{10,8},{9,1... | collective-permute-start | bytes 1572872 | tf_op jit(solution)/shard_map/ppermute | solution.py:393
  7.2 23.3 %collective-permute-start.4 = (f32[4,128,512]{2,1,0:T(8,128)}, f32[4,128,512]{2,1,0:T(8,128)}, u32[]{:S(2)}, u32[]{:S(2)}) collective-permute-start(f32[4,128,512]{2,1,0:T(8,128)} %add_momenta.4), channel_id=1, source_target_pairs={{0,1},{1,0},{2,3},{3,2},{4,5},{5,4},{6,7},{7,6},{8,9},{9,8},{10,11... | collective-permute-start | bytes 3145736 | tf_op jit(solution)/shard_map/ppermute | solution.py:365
  9.6 28.0 %collective-permute-start.7 = (f32[4,128,512]{2,1,0:T(8,128)}, f32[4,128,512]{2,1,0:T(8,128)}, u32[]{:S(2)}, u32[]{:S(2)}) collective-permute-start(f32[4,128,512]{2,1,0:T(8,128)} %add_momenta.6), channel_id=1, source_target_pairs={{0,1},{1,0},{2,3},{3,2},{4,5},{5,4},{6,7},{7,6},{8,9},{9,8},{10,11... | collective-permute-start | bytes 3145736 | tf_op jit(solution)/shard_map/ppermute | solution.py:365
  17.1 13.4 %collective-permute-start.2 = (f32[2,128,512]{2,1,0:T(8,128)}, f32[2,128,512]{2,1,0:T(8,128)}, u32[]{:S(2)}, u32[]{:S(2)}) collective-permute-start(f32[2,128,512]{2,1,0:T(8,128)} %collective-permute-done.refs_0_), channel_id=1, source_target_pairs={{0,16},{16,0},{1,17},{17,1},{2,18},{18,2},{3,19},{19,3},{4,20},{20... | collective-permute-start | bytes 1572872 | tf_op jit(solution)/shard_map/ppermute | solution.py:395
  18.9 24.1 %collective-permute-start.1 = (f32[2,128,512]{2,1,0:T(8,128)}, f32[2,128,512]{2,1,0:T(8,128)}, u32[]{:S(2)}, u32[]{:S(2)}) collective-permute-start(f32[2,128,512]{2,1,0:T(8,128)} %collective-permute-done.refs_0_), channel_id=1, source_target_pairs={{0,1},{1,0},{2,3},{3,2},{4,5},{5,4},{6,7},{7,6},{8,9},{9,8},{10,11... | collective-permute-start | bytes 1572872 | tf_op jit(solution)/shard_map/ppermute | solution.py:397
  30.5 14.0 %collective-permute-start.3 = (f32[2,128,512]{2,1,0:T(8,128)}, f32[2,128,512]{2,1,0:T(8,128)}, u32[]{:S(2)}, u32[]{:S(2)}) collective-permute-start(f32[2,128,512]{2,1,0:T(8,128)} %collective-permute-done.2.refs_2_), channel_id=1, source_target_pairs={{0,1},{1,0},{2,3},{3,2},{4,5},{5,4},{6,7},{7,6},{8,9},{9,8},{10,11... | collective-permute-start | bytes 1572872 | tf_op jit(solution)/shard_map/ppermute | solution.py:397
  33.1 58.0 %copy-start.21 = (s32[3]{0:T(128)S(1)}, s32[3]{0:T(128)}, u32[]{:S(2)}) copy-start(s32[3]{0:T(128)} %steps.11) | copy-start | bytes 40
  33.2 59.2 %copy-start.23 = (s32[3]{0:T(128)S(1)}, s32[3]{0:T(128)}, u32[]{:S(2)}) copy-start(s32[3]{0:T(128)} %owners.1) | copy-start | bytes 40
  33.2 27.3 %collective-permute-start.5 = (f32[4,128,512]{2,1,0:T(8,128)}, f32[4,128,512]{2,1,0:T(8,128)}, u32[]{:S(2)}, u32[]{:S(2)}) collective-permute-start(f32[4,128,512]{2,1,0:T(8,128)} %add_momenta.5.refs_8_.refs_0_), channel_id=1, source_target_pairs={{0,4},{4,8},{8,12},{1,5},{5,9},{9,13},{2,6},{6,10},{10,14},{3,7},{... | collective-permute-start | bytes 3145736 | tf_op jit(solution)/shard_map/ppermute | solution.py:376
  40.3 42.2 %collective-permute-start.8 = (f32[4,128,512]{2,1,0:T(8,128)}, f32[4,128,512]{2,1,0:T(8,128)S(1)}, u32[]{:S(2)}, u32[]{:S(2)}) collective-permute-start(f32[4,128,512]{2,1,0:T(8,128)} %add_momenta.7.refs_9_.refs_1_), channel_id=1, source_target_pairs={{0,4},{4,8},{8,12},{1,5},{5,9},{9,13},{2,6},{6,10},{10,14},{3,7},{... | collective-permute-start | bytes 3145736 | tf_op jit(solution)/shard_map/ppermute | solution.py:376
  42.9 40.9 %collective-permute-start.14 = (f32[4,128,512]{2,1,0:T(8,128)}, f32[4,128,512]{2,1,0:T(8,128)S(1)}, u32[]{:S(2)}, u32[]{:S(2)}) collective-permute-start(f32[4,128,512]{2,1,0:T(8,128)} %add_momenta.5.refs_8_.refs_0_), channel_id=1, source_target_pairs={{0,1},{1,0},{2,3},{3,2},{4,5},{5,4},{6,7},{7,6},{8,9},{9,8},{10,11... | collective-permute-start | bytes 3145736 | tf_op jit(solution)/shard_map/ppermute | solution.py:386
  42.9 42.2 %collective-permute-start.39 = (f32[4,128,512]{2,1,0:T(8,128)}, f32[4,128,512]{2,1,0:T(8,128)S(1)}, u32[]{:S(2)}, u32[]{:S(2)}) collective-permute-start(f32[4,128,512]{2,1,0:T(8,128)} %add_momenta.5.refs_8_.refs_0_), channel_id=1, source_target_pairs={{0,2},{2,0},{1,3},{3,1},{4,6},{6,4},{5,7},{7,5},{8,10},{10,8},{9,1... | collective-permute-start | bytes 3145736 | tf_op jit(solution)/shard_map/ppermute | solution.py:417
  44.5 46.7 %collective-permute-start.40 = (f32[4,128,512]{2,1,0:T(8,128)}, f32[4,128,512]{2,1,0:T(8,128)S(1)}, u32[]{:S(2)}, u32[]{:S(2)}) collective-permute-start(f32[4,128,512]{2,1,0:T(8,128)} %add_momenta.7.refs_9_.refs_1_), channel_id=1, source_target_pairs={{0,2},{2,0},{1,3},{3,1},{4,6},{6,4},{5,7},{7,5},{8,10},{10,8},{9,1... | collective-permute-start | bytes 3145736 | tf_op jit(solution)/shard_map/ppermute | solution.py:417
  60.5 36.5 %collective-permute-start.15 = (f32[4,128,512]{2,1,0:T(8,128)}, f32[4,128,512]{2,1,0:T(8,128)S(1)}, u32[]{:S(2)}, u32[]{:S(2)}) collective-permute-start(f32[4,128,512]{2,1,0:T(8,128)} %add_momenta.7.refs_9_.refs_1_), channel_id=1, source_target_pairs={{0,1},{1,0},{2,3},{3,2},{4,5},{5,4},{6,7},{7,6},{8,9},{9,8},{10,11... | collective-permute-start | bytes 3145736 | tf_op jit(solution)/shard_map/ppermute | solution.py:386
  82.5 28.6 %collective-permute-start.16 = (f32[4,128,512]{2,1,0:T(8,128)}, f32[4,128,512]{2,1,0:T(8,128)}, u32[]{:S(2)}, u32[]{:S(2)}) collective-permute-start(f32[4,128,512]{2,1,0:T(8,128)} %add_momenta.5.refs_8_.refs_0_), channel_id=1, source_target_pairs={{12,8},{8,4},{4,0},{13,9},{9,5},{5,1},{14,10},{10,6},{6,2},{15,11}... | collective-permute-start | bytes 3145736 | tf_op jit(solution)/shard_map/ppermute | solution.py:377
  83.8 48.7 %collective-permute-start.17 = (f32[4,128,512]{2,1,0:T(8,128)}, f32[4,128,512]{2,1,0:T(8,128)}, u32[]{:S(2)}, u32[]{:S(2)}) collective-permute-start(f32[4,128,512]{2,1,0:T(8,128)} %add_momenta.7.refs_9_.refs_1_), channel_id=1, source_target_pairs={{12,8},{8,4},{4,0},{13,9},{9,5},{5,1},{14,10},{10,6},{6,2},{15,11}... | collective-permute-start | bytes 3145736 | tf_op jit(solution)/shard_map/ppermute | solution.py:377
  85.1 49.1 %collective-permute-start.41 = (f32[4,128,512]{2,1,0:T(8,128)S(1)}, f32[4,128,512]{2,1,0:T(8,128)S(1)}, u32[]{:S(2)}, u32[]{:S(2)}) collective-permute-start(f32[4,128,512]{2,1,0:T(8,128)S(1)} %collective-permute-done.39.refs_2_), channel_id=1, source_target_pairs={{0,1},{1,0},{2,3},{3,2},{4,5},{5,4},{6,7},{7,6},{8,9},{9,8},{10,11... | collective-permute-start | bytes 3145736 | tf_op jit(solution)/shard_map/ppermute | solution.py:420
  91.2 43.1 %collective-permute-start.42 = (f32[4,128,512]{2,1,0:T(8,128)S(1)}, f32[4,128,512]{2,1,0:T(8,128)S(1)}, u32[]{:S(2)}, u32[]{:S(2)}) collective-permute-start(f32[4,128,512]{2,1,0:T(8,128)S(1)} %collective-permute-done.40.refs_3_), channel_id=1, source_target_pairs={{0,1},{1,0},{2,3},{3,2},{4,5},{5,4},{6,7},{7,6},{8,9},{9,8},{10,11... | collective-permute-start | bytes 3145736 | tf_op jit(solution)/shard_map/ppermute | solution.py:420
  97.0 55.5 %collective-permute-start.6 = (f32[4,128,512]{2,1,0:T(8,128)}, f32[4,128,512]{2,1,0:T(8,128)}, u32[]{:S(2)}, u32[]{:S(2)}) collective-permute-start(f32[4,128,512]{2,1,0:T(8,128)} %collective-permute-done.5.refs_4_), channel_id=1, source_target_pairs={{4,8},{8,12},{5,9},{9,13},{6,10},{10,14},{7,11},{11,15},{20,24},{2... | collective-permute-start | bytes 3145736 | tf_op jit(solution)/shard_map/ppermute | solution.py:376
  111.1 44.0 %collective-permute-start.12 = (f32[4,128,512]{2,1,0:T(8,128)}, f32[4,128,512]{2,1,0:T(8,128)S(1)}, u32[]{:S(2)}, u32[]{:S(2)}) collective-permute-start(f32[4,128,512]{2,1,0:T(8,128)} %collective-permute-done.5.refs_4_), channel_id=1, source_target_pairs={{0,1},{1,0},{2,3},{3,2},{4,5},{5,4},{6,7},{7,6},{8,9},{9,8},{10,11... | collective-permute-start | bytes 3145736 | tf_op jit(solution)/shard_map/ppermute | solution.py:386
  132.5 21.3 %collective-permute-start.9 = (f32[4,128,512]{2,1,0:T(8,128)S(1)}, f32[4,128,512]{2,1,0:T(8,128)}, u32[]{:S(2)}, u32[]{:S(2)}) collective-permute-start(f32[4,128,512]{2,1,0:T(8,128)S(1)} %collective-permute-done.8.refs_5_), channel_id=1, source_target_pairs={{4,8},{8,12},{5,9},{9,13},{6,10},{10,14},{7,11},{11,15},{20,24},{2... | collective-permute-start | bytes 3145736 | tf_op jit(solution)/shard_map/ppermute | solution.py:376
  134.2 21.9 %collective-permute-start.13 = (f32[4,128,512]{2,1,0:T(8,128)S(1)}, f32[4,128,512]{2,1,0:T(8,128)S(1)}, u32[]{:S(2)}, u32[]{:S(2)}) collective-permute-start(f32[4,128,512]{2,1,0:T(8,128)S(1)} %collective-permute-done.8.refs_5_), channel_id=1, source_target_pairs={{0,1},{1,0},{2,3},{3,2},{4,5},{5,4},{6,7},{7,6},{8,9},{9,8},{10,11... | collective-permute-start | bytes 3145736 | tf_op jit(solution)/shard_map/ppermute | solution.py:386
  134.3 23.3 %collective-permute-start.18 = (f32[4,128,512]{2,1,0:T(8,128)}, f32[4,128,512]{2,1,0:T(8,128)S(1)}, u32[]{:S(2)}, u32[]{:S(2)}) collective-permute-start(f32[4,128,512]{2,1,0:T(8,128)} %collective-permute-done.16.refs_12_), channel_id=1, source_target_pairs={{0,1},{1,0},{2,3},{3,2},{4,5},{5,4},{6,7},{7,6},{8,9},{9,8},{10,11... | collective-permute-start | bytes 3145736 | tf_op jit(solution)/shard_map/ppermute | solution.py:386
  152.5 30.8 %collective-permute-start.20 = (f32[4,128,512]{2,1,0:T(8,128)}, f32[4,128,512]{2,1,0:T(8,128)}, u32[]{:S(2)}, u32[]{:S(2)}) collective-permute-start(f32[4,128,512]{2,1,0:T(8,128)} %collective-permute-done.16.refs_12_), channel_id=1, source_target_pairs={{8,4},{4,0},{9,5},{5,1},{10,6},{6,2},{11,7},{7,3},{24,20},{20,16},... | collective-permute-start | bytes 3145736 | tf_op jit(solution)/shard_map/ppermute | solution.py:377
  153.8 51.3 %collective-permute-start.21 = (f32[4,128,512]{2,1,0:T(8,128)}, f32[4,128,512]{2,1,0:T(8,128)}, u32[]{:S(2)}, u32[]{:S(2)}) collective-permute-start(f32[4,128,512]{2,1,0:T(8,128)} %collective-permute-done.17.refs_13_), channel_id=1, source_target_pairs={{8,4},{4,0},{9,5},{5,1},{10,6},{6,2},{11,7},{7,3},{24,20},{20,16},... | collective-permute-start | bytes 3145736 | tf_op jit(solution)/shard_map/ppermute | solution.py:377
  156.1 50.9 %collective-permute-start.43 = (f32[4,128,512]{2,0,1:T(4,128)}, f32[4,128,512]{2,0,1:T(4,128)}, u32[]{:S(2)}, u32[]{:S(2)}) collective-permute-start(f32[4,128,512]{2,0,1:T(4,128)} %copy.6), channel_id=1, source_target_pairs={{0,1},{1,0},{2,3},{3,2},{4,5},{5,4},{6,7},{7,6},{8,9},{9,8},{10,11... | collective-permute-start | bytes 3145736 | tf_op jit(solution)/shard_map/ppermute | solution.py:434
  157.2 55.4 %collective-permute-start.19 = (f32[4,128,512]{2,1,0:T(8,128)}, f32[4,128,512]{2,1,0:T(8,128)}, u32[]{:S(2)}, u32[]{:S(2)}) collective-permute-start(f32[4,128,512]{2,1,0:T(8,128)} %collective-permute-done.17.refs_13_), channel_id=1, source_target_pairs={{0,1},{1,0},{2,3},{3,2},{4,5},{5,4},{6,7},{7,6},{8,9},{9,8},{10,11... | collective-permute-start | bytes 3145736 | tf_op jit(solution)/shard_map/ppermute | solution.py:386
  158.6 55.7 %collective-permute-start.10 = (f32[4,128,512]{2,1,0:T(8,128)}, f32[4,128,512]{2,1,0:T(8,128)}, u32[]{:S(2)}, u32[]{:S(2)}) collective-permute-start(f32[4,128,512]{2,1,0:T(8,128)} %collective-permute-done.6.refs_0_), channel_id=1, source_target_pairs={{8,9},{9,8},{12,13},{13,12},{10,11},{11,10},{14,15},{15,14},{24,25... | collective-permute-start | bytes 3145736 | tf_op jit(solution)/shard_map/ppermute | solution.py:386
  183.3 32.3 %collective-permute-start.11 = (f32[4,128,512]{2,1,0:T(8,128)}, f32[4,128,512]{2,1,0:T(8,128)S(1)}, u32[]{:S(2)}, u32[]{:S(2)}) collective-permute-start(f32[4,128,512]{2,1,0:T(8,128)} %collective-permute-done.9.refs_1_), channel_id=1, source_target_pairs={{8,9},{9,8},{12,13},{13,12},{10,11},{11,10},{14,15},{15,14},{24,25... | collective-permute-start | bytes 3145736 | tf_op jit(solution)/shard_map/ppermute | solution.py:386
  205.1 10.4 %collective-permute-start.22 = (f32[4,128,512]{2,1,0:T(8,128)}, f32[4,128,512]{2,1,0:T(8,128)S(1)}, u32[]{:S(2)}, u32[]{:S(2)}) collective-permute-start(f32[4,128,512]{2,1,0:T(8,128)} %collective-permute-done.20.refs_16_), channel_id=1, source_target_pairs={{0,1},{1,0},{4,5},{5,4},{2,3},{3,2},{6,7},{7,6},{16,17},{17,16},{2... | collective-permute-start | bytes 3145736 | tf_op jit(solution)/shard_map/ppermute | solution.py:386
  207.0 8.5 %collective-permute-start.23 = (f32[4,128,512]{2,1,0:T(8,128)}, f32[4,128,512]{2,1,0:T(8,128)S(1)}, u32[]{:S(2)}, u32[]{:S(2)}) collective-permute-start(f32[4,128,512]{2,1,0:T(8,128)} %collective-permute-done.21.refs_17_), channel_id=1, source_target_pairs={{0,1},{1,0},{4,5},{5,4},{2,3},{3,2},{6,7},{7,6},{16,17},{17,16},{2... | collective-permute-start | bytes 3145736 | tf_op jit(solution)/shard_map/ppermute | solution.py:386
  212.5 63.7 %collective-permute-start.44 = (f32[128,8,512]{2,1,0:T(8,128)S(1)}, f32[128,8,512]{2,1,0:T(8,128)S(1)}, u32[]{:S(2)}, u32[]{:S(2)}) collective-permute-start(f32[128,8,512]{2,1,0:T(8,128)S(1)} %maximum_bitcast_fusion), channel_id=1, source_target_pairs={{0,12},{1,13},{2,14},{3,15},{16,28},{17,29},{18,30},{19,31}} | collective-permute-start | bytes 6291464 | tf_op jit(solution)/shard_map/ppermute | solution.py:438
  214.2 62.0 %collective-permute-start.45 = (f32[128,8,512]{2,1,0:T(8,128)S(1)}, f32[128,8,512]{2,1,0:T(8,128)S(1)}, u32[]{:S(2)}, u32[]{:S(2)}) collective-permute-start(f32[128,8,512]{2,1,0:T(8,128)S(1)} %maximum_bitcast_fusion), channel_id=1, source_target_pairs={{12,0},{13,1},{14,2},{15,3},{28,16},{29,17},{30,18},{31,19}} | collective-permute-start | bytes 6291464 | tf_op jit(solution)/shard_map/ppermute | solution.py:439
  222.5 6.7 %collective-permute-start.26 = (f32[1,128,256]{2,1,0:T(8,128)S(1)}, f32[1,128,256]{2,1,0:T(8,128)S(1)}, u32[]{:S(2)}, u32[]{:S(2)}) collective-permute-start(f32[1,128,256]{2,1,0:T(8,128)S(1)} %get-tuple-element.36), channel_id=1, source_target_pairs={{0,2},{1,3},{2,0},{3,1},{4,6},{5,7},{6,4},{7,5},{8,10},{9,11},{10,... | collective-permute-start | bytes 393224 | tf_op jit(solution)/shard_map/ppermute | solution.py:458
  224.1 6.7 %collective-permute-start.27 = (f32[1,128,256]{2,1,0:T(8,128)S(1)}, f32[1,128,256]{2,1,0:T(8,128)S(1)}, u32[]{:S(2)}, u32[]{:S(2)}) collective-permute-start(f32[1,128,256]{2,1,0:T(8,128)S(1)} %get-tuple-element.37), channel_id=1, source_target_pairs={{0,3},{1,2},{2,1},{3,0},{4,7},{5,6},{6,5},{7,4},{8,11},{9,10},{10,... | collective-permute-start | bytes 393224 | tf_op jit(solution)/shard_map/ppermute | solution.py:458
  224.1 7.9 %collective-permute-start.28 = (f32[1,128,256]{2,1,0:T(8,128)S(1)}, f32[1,128,256]{2,1,0:T(8,128)S(1)}, u32[]{:S(2)}, u32[]{:S(2)}) collective-permute-start(f32[1,128,256]{2,1,0:T(8,128)S(1)} %get-tuple-element.39), channel_id=1, source_target_pairs={{0,1},{1,0},{2,3},{3,2},{4,5},{5,4},{6,7},{7,6},{8,9},{9,8},{10,11... | collective-permute-start | bytes 393224 | tf_op jit(solution)/shard_map/ppermute | solution.py:458
  229.2 7.9 %collective-permute-start.29 = (f32[1,128,256]{2,1,0:T(8,128)S(1)}, f32[1,128,256]{2,1,0:T(8,128)S(1)}, u32[]{:S(2)}, u32[]{:S(2)}) collective-permute-start(f32[1,128,256]{2,1,0:T(8,128)S(1)} %get-tuple-element.40), channel_id=1, source_target_pairs={{0,2},{1,3},{2,0},{3,1},{4,6},{5,7},{6,4},{7,5},{8,10},{9,11},{10,... | collective-permute-start | bytes 393224 | tf_op jit(solution)/shard_map/ppermute | solution.py:458
  230.8 7.3 %collective-permute-start.30 = (f32[1,128,256]{2,1,0:T(8,128)S(1)}, f32[1,128,256]{2,1,0:T(8,128)S(1)}, u32[]{:S(2)}, u32[]{:S(2)}) collective-permute-start(f32[1,128,256]{2,1,0:T(8,128)S(1)} %get-tuple-element.41), channel_id=1, source_target_pairs={{0,3},{1,2},{2,1},{3,0},{4,7},{5,6},{6,5},{7,4},{8,11},{9,10},{10,... | collective-permute-start | bytes 393224 | tf_op jit(solution)/shard_map/ppermute | solution.py:458
  232.0 7.1 %collective-permute-start.31 = (f32[1,128,256]{2,1,0:T(8,128)S(1)}, f32[1,128,256]{2,1,0:T(8,128)S(1)}, u32[]{:S(2)}, u32[]{:S(2)}) collective-permute-start(f32[1,128,256]{2,1,0:T(8,128)S(1)} %get-tuple-element.43), channel_id=1, source_target_pairs={{0,1},{1,0},{2,3},{3,2},{4,5},{5,4},{6,7},{7,6},{8,9},{9,8},{10,11... | collective-permute-start | bytes 393224 | tf_op jit(solution)/shard_map/ppermute | solution.py:458
  237.1 9.2 %collective-permute-start.32 = (f32[1,128,512]{2,1,0:T(8,128)S(1)}, f32[1,128,512]{2,1,0:T(8,128)S(1)}, u32[]{:S(2)}, u32[]{:S(2)}) collective-permute-start(f32[1,128,512]{2,1,0:T(8,128)S(1)} %get-tuple-element.44), channel_id=1, source_target_pairs={{0,2},{1,3},{2,0},{3,1},{4,6},{5,7},{6,4},{7,5},{8,10},{9,11},{10,... | collective-permute-start | bytes 786440 | tf_op jit(solution)/shard_map/ppermute | solution.py:458
  238.0 13.1 %collective-permute-start.33 = (f32[1,128,512]{2,1,0:T(8,128)S(1)}, f32[1,128,512]{2,1,0:T(8,128)S(1)}, u32[]{:S(2)}, u32[]{:S(2)}) collective-permute-start(f32[1,128,512]{2,1,0:T(8,128)S(1)} %get-tuple-element.45), channel_id=1, source_target_pairs={{0,3},{1,2},{2,1},{3,0},{4,7},{5,6},{6,5},{7,4},{8,11},{9,10},{10,... | collective-permute-start | bytes 786440 | tf_op jit(solution)/shard_map/ppermute | solution.py:458
  239.1 13.5 %collective-permute-start.34 = (f32[1,128,512]{2,1,0:T(8,128)S(1)}, f32[1,128,512]{2,1,0:T(8,128)S(1)}, u32[]{:S(2)}, u32[]{:S(2)}) collective-permute-start(f32[1,128,512]{2,1,0:T(8,128)S(1)} %get-tuple-element.47), channel_id=1, source_target_pairs={{0,1},{1,0},{2,3},{3,2},{4,5},{5,4},{6,7},{7,6},{8,9},{9,8},{10,11... | collective-permute-start | bytes 786440 | tf_op jit(solution)/shard_map/ppermute | solution.py:458
  246.3 11.3 %collective-permute-start.35 = (f32[1,128,512]{2,1,0:T(8,128)S(1)}, f32[1,128,512]{2,1,0:T(8,128)S(1)}, u32[]{:S(2)}, u32[]{:S(2)}) collective-permute-start(f32[1,128,512]{2,1,0:T(8,128)S(1)} %get-tuple-element.48), channel_id=1, source_target_pairs={{0,2},{1,3},{2,0},{3,1},{4,6},{5,7},{6,4},{7,5},{8,10},{9,11},{10,... | collective-permute-start | bytes 786440 | tf_op jit(solution)/shard_map/ppermute | solution.py:458
  251.2 11.2 %collective-permute-start.36 = (f32[1,128,512]{2,1,0:T(8,128)S(1)}, f32[1,128,512]{2,1,0:T(8,128)S(1)}, u32[]{:S(2)}, u32[]{:S(2)}) collective-permute-start(f32[1,128,512]{2,1,0:T(8,128)S(1)} %get-tuple-element.49), channel_id=1, source_target_pairs={{0,3},{1,2},{2,1},{3,0},{4,7},{5,6},{6,5},{7,4},{8,11},{9,10},{10,... | collective-permute-start | bytes 786440 | tf_op jit(solution)/shard_map/ppermute | solution.py:458
  252.5 10.1 %collective-permute-start.37 = (f32[1,128,512]{2,1,0:T(8,128)S(1)}, f32[1,128,512]{2,1,0:T(8,128)S(1)}, u32[]{:S(2)}, u32[]{:S(2)}) collective-permute-start(f32[1,128,512]{2,1,0:T(8,128)S(1)} %get-tuple-element.51), channel_id=1, source_target_pairs={{0,1},{1,0},{2,3},{3,2},{4,5},{5,4},{6,7},{7,6},{8,9},{9,8},{10,11... | collective-permute-start | bytes 786440 | tf_op jit(solution)/shard_map/ppermute | solution.py:458
  257.6 6.6 %collective-permute-start.38 = (f32[1,128,512]{2,1,0:T(8,128)S(1)}, f32[1,128,512]{2,1,0:T(8,128)S(1)}, u32[]{:S(2)}, u32[]{:S(2)}) collective-permute-start(f32[1,128,512]{2,1,0:T(8,128)S(1)} %get-tuple-element.53), channel_id=1, source_target_pairs={{0,1},{1,0},{2,3},{3,2},{4,5},{5,4},{6,7},{7,6},{8,9},{9,8},{10,11... | collective-permute-start | bytes 786440 | tf_op jit(solution)/shard_map/ppermute | solution.py:458
  262.4 9.2 %collective-permute-start.24 = (f32[1,128,512]{2,1,0:T(8,128)S(1)}, f32[1,128,512]{2,1,0:T(8,128)S(1)}, u32[]{:S(2)}, u32[]{:S(2)}) collective-permute-start(f32[1,128,512]{2,1,0:T(8,128)S(1)} %get-tuple-element.34), channel_id=1, source_target_pairs={{0,2},{1,3},{2,0},{3,1},{4,6},{5,7},{6,4},{7,5},{8,10},{9,11},{10,... | collective-permute-start | bytes 786440 | tf_op jit(solution)/shard_map/ppermute | solution.py:458
  262.6 13.7 %collective-permute-start.25 = (f32[1,128,512]{2,1,0:T(8,128)S(1)}, f32[1,128,512]{2,1,0:T(8,128)S(1)}, u32[]{:S(2)}, u32[]{:S(2)}) collective-permute-start(f32[1,128,512]{2,1,0:T(8,128)S(1)} %get-tuple-element.35), channel_id=1, source_target_pairs={{0,3},{1,2},{2,1},{3,0},{4,7},{5,6},{6,5},{7,4},{8,11},{9,10},{10,... | collective-permute-start | bytes 786440 | tf_op jit(solution)/shard_map/ppermute | solution.py:458
  (22 other events, 435.6 us)

commit v10 on v8

--- a/solution.py
+++ b/solution.py
@@ -15,6 +15,14 @@
 
 def chunks_of(half):
     return [1] * half
+
+
+def quotient(x, n):
+    return lax.shift_right_logical(x, jnp.int32(n.bit_length() - 1)) if n & (n - 1) == 0 else lax.div(x, n)
+
+
+def remainder(x, n):
+    return x & (n - 1) if n & (n - 1) == 0 else lax.rem(x, n)
 
 
 def halves(x):
@@ -111,24 +119,24 @@
 
     def source_of(energy, mode, side):
         step = steps[mode] if side == 0 else -steps[mode]
-        source = lax.rem(target * edev + base + energy + step + grid_total, grid_total)
-        rel = lax.div(source, edev) - place
+        source = remainder(target * edev + base + energy + step + grid_total, grid_total)
+        rel = quotient(source, edev) - place
         if far:
             valid = rel == 0
         elif line:
             valid = jnp.abs(rel) <= REACH
         else:
-            rel = lax.rem(rel + REACH + blocks, blocks) - REACH
+            rel = remainder(rel + REACH + blocks, blocks) - REACH
             valid = rel <= REACH
         group = jnp.where(valid, rel + n_groups // 2, n_groups // 2)
-        return valid, group, lax.rem(source, edev)
+        return valid, group, remainder(source, edev)
 
     def fetch(energy, buffer):
         for mode in range(MODES):
             for side in range(2):
                 _, group, plane = source_of(energy, mode, side)
-                other = jnp.where(lax.div(plane, half_planes) == core, 0, 1)
-                at = lax.rem(plane, half_planes)
+                other = jnp.where(quotient(plane, half_planes) == core, 0, 1)
+                at = remainder(plane, half_planes)
                 slot = mode * 2 + side
                 for g in range(n_groups):
 
@@ -155,7 +163,7 @@
 
     @pl.loop(0, count)
     def _(energy):
-        buffer = lax.rem(energy, 2)
+        buffer = energy & 1
 
         if count > 1:
 
@@ -164,14 +172,16 @@
                 fetch(energy + 1, 1 - buffer)
 
         dot = functools.partial(jnp.dot, preferred_element_type=jnp.float32)
+        scales = [
+            jnp.where(source_of(energy, mode, side)[0], (occupation[mode] + (1.0 - side)) * (1.0 / momenta), 0.0)
+            for mode in range(MODES)
+            for side in range(2)
+        ]
         for mode in range(MODES):
-            scales = []
-            for side in range(2):
-                slot = mode * 2 + side
+            for slot in (2 * mode, 2 * mode + 1):
                 held = planes.at[buffer, slot]
                 pltpu.make_async_copy(held, held, sems.at[buffer, slot]).wait()
-                scales.append(jnp.where(source_of(energy, mode, side)[0], (occupation[mode] + (1.0 - side)) * (1.0 / momenta), 0.0))
-            combined = scales[0] * planes[buffer, 2 * mode] + scales[1] * planes[buffer, 2 * mode + 1]
+            combined = scales[2 * mode] * planes[buffer, 2 * mode] + scales[2 * mode + 1] * planes[buffer, 2 * mode + 1]
             if far:
                 high, low = halves(combined)
                 inner[mode, pl.ds(0, rows)] = high
@@ -353,7 +363,8 @@
     for piece in range(PIECES):
         given = summed(True, piece)
         given = lax.ppermute(given, "kz", swap)
-        own.append(summed(False, piece, given))
+        kept = summed(False, piece)
+        own.append(kept + given)
 
     if line:
         up = [[(i, i + 1) for i in range(d, n - 1)] for d in range(REACH)]

time: 283 us -> 287 us (1.014)
  other arithmetic: 3.01 us -> 6.38 us
  waiting for transfers between devices: 169 us -> 172 us
    add x0 -> x2, other arithmetic: none -> 3.27 us  [shards(): own.append(kept + given)]
    unnamed x52 -> x56, local copies, waits for them, and re-layouts: 8.32 us -> 7.95 us
  transfers between devices with their start and end apart: 43 -> 43, of which waited for: 16 -> 16; matrix products, arithmetic and copies ran while one was open for 1% -> 2% of each run, Pallas kernels for 18% -> 17%
where the time goes in v10:
time: 287 us; the launch traced here: 286 us
  waiting for transfers between devices  172 us (60%)
  Pallas kernels  51.4 us (18%)
  starting transfers between devices  45.1 us (16%)
  local copies, waits for them, and re-layouts  10.5 us (4%)
  other arithmetic  6.38 us (2%)
    ppermute x4, waiting for transfers between devices, shards(): lax.ppermute(x, 'energy', down[d - 1])  79 us
    ppermute x4, waiting for transfers between devices, shards(): streams[-d] = [lax.ppermute(x, 'energy', up[d - 1]) for x in streams[1 - d]]  38.3 us
    pallas_call x5, Pallas kernels, sandwich(): pl.pallas_call(functools.partial(split_dot, len(groups), len(groups[0][0]...  35.9 us
    ppermute x12, waiting for transfers between devices, shards(): block = lax.ppermute(block, ('atom', 'kz'), pairs)  31 us
    ppermute x1, waiting for transfers between devices, shards(): lax.ppermute(got, 'grp', [(i, (i + d) % parts) for i in range(parts)])  11.6 us
    ppermute x4, starting transfers between devices, shards(): streams[-d] = [lax.ppermute(x, 'energy', up[d - 1]) for x in streams[1 - d]]  10.9 us
    ppermute x12, starting transfers between devices, shards(): block = lax.ppermute(block, ('atom', 'kz'), pairs)  10 us
    pallas_call x4, Pallas kernels, summed(): pl.pallas_call(functools.partial(add_momenta, theirs, piece * size), out_...  9.23 us
  transfers between devices with their start and end apart: 43, of which 16 were waited for; matrix products, arithmetic and copies ran while one was open for 2% of the time, Pallas kernels for 17%

profile of v10, /device:TPU:0, one launch (start us, length us, event | category | flops | bytes accessed | tf_op | source)
XLA Modules:
  0.0 286.1 jit_solution(4482246115556173599)
XLA Ops:
  0.0 1.9 constant_dynamic-slice_fusion
  1.9 3.0 %collective-permute-start = (f32[2,128,512]{2,1,0:T(8,128)}, f32[2,128,512]{2,1,0:T(8,128)}, u32[]{:S(2)}, u32[]{:S(2)}) collective-permute-start(f32[2,128,512]{2,1,0:T(8,128)} %constant_dynamic-slice_fusion), channel_id=1, source_target_pairs={{0,2},{2,0},{1,3},{3,1},{4,6},{6,4},{5,7},{7,5},{8,10},{10,8},{9,1... | collective-permute-start | bytes 1572872 | tf_op jit(solution)/shard_map/ppermute | solution.py:394
  4.8 2.3 add_momenta.5
  7.2 2.3 add_momenta.7
  10.1 7.0 %collective-permute-done.refs_0_ = f32[2,128,512]{2,1,0:T(8,128)} collective-permute-done((f32[2,128,512]{2,1,0:T(8,128)}, f32[2,128,512]{2,1,0:T(8,128)}, u32[]{:S(2)}, u32[]{:S(2)}) %collective-permute-start) | collective-permute-done | bytes 524320 | tf_op jit(solution)/shard_map/ppermute | solution.py:394
  17.1 1.8 collective-permute-start.2
  18.8 11.6 %collective-permute-done.2.refs_2_ = f32[2,128,512]{2,1,0:T(8,128)} collective-permute-done((f32[2,128,512]{2,1,0:T(8,128)}, f32[2,128,512]{2,1,0:T(8,128)}, u32[]{:S(2)}, u32[]{:S(2)}) %collective-permute-start.2) | collective-permute-done | bytes 524320 | tf_op jit(solution)/shard_map/ppermute | solution.py:396
  30.5 2.3 add_momenta.4
  32.8 2.3 add_momenta.6
  35.1 1.8 add.14.refs_8_.refs_0_
  37.0 3.7 %collective-permute-start.5 = (f32[4,128,512]{2,1,0:T(8,128)S(1)}, f32[4,128,512]{2,1,0:T(8,128)S(1)}, u32[]{:S(2)}, u32[]{:S(2)}) collective-permute-start(f32[4,128,512]{2,1,0:T(8,128)S(1)} %add.14.refs_8_.refs_0_), channel_id=1, source_target_pairs={{0,4},{4,8},{8,12},{1,5},{5,9},{9,13},{2,6},{6,10},{10,14},{3,7},{... | collective-permute-start | bytes 3145736 | tf_op jit(solution)/shard_map/ppermute | solution.py:377
  40.7 1.4 add.15.refs_9_.refs_1_
  42.1 3.5 %collective-permute-start.8 = (f32[4,128,512]{2,1,0:T(8,128)S(1)}, f32[4,128,512]{2,1,0:T(8,128)S(1)}, u32[]{:S(2)}, u32[]{:S(2)}) collective-permute-start(f32[4,128,512]{2,1,0:T(8,128)S(1)} %add.15.refs_9_.refs_1_), channel_id=1, source_target_pairs={{0,4},{4,8},{8,12},{1,5},{5,9},{9,13},{2,6},{6,10},{10,14},{3,7},{... | collective-permute-start | bytes 3145736 | tf_op jit(solution)/shard_map/ppermute | solution.py:377
  45.7 1.6 collective-permute-start.36
  47.8 16.3 %collective-permute-done.5.refs_4_ = f32[4,128,512]{2,1,0:T(8,128)S(1)} collective-permute-done((f32[4,128,512]{2,1,0:T(8,128)S(1)}, f32[4,128,512]{2,1,0:T(8,128)S(1)}, u32[]{:S(2)}, u32[]{:S(2)}) %collective-permute-start.5) | collective-permute-done | bytes 1048608 | tf_op jit(solution)/shard_map/ppermute | solution.py:377
  64.1 22.0 %collective-permute-done.8.refs_5_ = f32[4,128,512]{2,1,0:T(8,128)S(1)} collective-permute-done((f32[4,128,512]{2,1,0:T(8,128)S(1)}, f32[4,128,512]{2,1,0:T(8,128)S(1)}, u32[]{:S(2)}, u32[]{:S(2)}) %collective-permute-start.8) | collective-permute-done | bytes 1048608 | tf_op jit(solution)/shard_map/ppermute | solution.py:377
  87.4 1.3 collective-permute-start.17
  88.8 4.9 %collective-permute-done.37.refs_3_ = f32[4,128,512]{2,1,0:T(8,128)S(1)} collective-permute-done((f32[4,128,512]{2,1,0:T(8,128)S(1)}, f32[4,128,512]{2,1,0:T(8,128)S(1)}, u32[]{:S(2)}, u32[]{:S(2)}) %collective-permute-start.37) | collective-permute-done | bytes 1048608 | tf_op jit(solution)/shard_map/ppermute | solution.py:418
  94.9 3.0 %prepare.1 = (bf16[3,512,512]{2,1,0:T(8,128)(2,1)S(1)}, bf16[3,512,512]{2,1,0:T(8,128)(2,1)S(1)}, bf16[3,256,1536]{2,1,0:T(8,128)(2,1)S(1)}, bf16[3,512,768]{2,1,0:T(8,128)(2,1)S(1)}) custom-call(s32[3]{0:T(128)S(1)} %copy-done.26, f32[2,512,512]{2,1,0:T(8,128)S(1)} %copy-done.22, f32[2,128,512]{2,1,0:T(8,128)} %collective-permute-done.refs_0_, ...), custom_call_target="tpu_custom_call" | custom-call | flops 6291456 | bytes 7864320 | tf_op jit(solution)/shard_map/prepare/pallas_call | solution.py:403
  97.9 2.1 collective-permute-start.6
  100.1 14.4 %collective-permute-done.16.refs_12_ = f32[4,128,512]{2,1,0:T(8,128)S(1)} collective-permute-done((f32[4,128,512]{2,1,0:T(8,128)S(1)}, f32[4,128,512]{2,1,0:T(8,128)S(1)}, u32[]{:S(2)}, u32[]{:S(2)}) %collective-permute-start.16) | collective-permute-done | bytes 1048608 | tf_op jit(solution)/shard_map/ppermute | solution.py:378
  114.5 21.5 %collective-permute-done.17.refs_13_ = f32[4,128,512]{2,1,0:T(8,128)} collective-permute-done((f32[4,128,512]{2,1,0:T(8,128)S(1)}, f32[4,128,512]{2,1,0:T(8,128)}, u32[]{:S(2)}, u32[]{:S(2)}) %collective-permute-start.17) | collective-permute-done | bytes 1048608 | tf_op jit(solution)/shard_map/ppermute | solution.py:378
  136.0 1.6 collective-permute-start.9
  138.2 15.8 %far_sandwich.1 = (f32[4,128,512]{2,1,0:T(8,128)S(1)}, f32[4,128,512]{2,1,0:T(8,128)S(1)}) custom-call(s32[3]{0:T(128)S(1)} %guard.1.steps, f32[3]{0:T(128)S(1)} %copy-done.25, bf16[3,512,512]{2,1,0:T(8,128)(2,1)S(1)} %get-tuple-element.27.right_high, bf16[3,512,512]{2,1,0:T(8,128)(2,1)S(1)} %get-tuple-element.28.right_low, ...), custom_call_target="tpu_custom_call" | custom-call | flops 14495514624 | bytes 27262976 | tf_op jit(solution)/shard_map/far_sandwich/pallas_call | solution.py:225
  154.8 1.3 collective-permute-start.20
  160.9 1.6 collective-permute-start.10
  162.5 22.8 %collective-permute-done.20.refs_16_ = f32[4,128,512]{2,1,0:T(8,128)} collective-permute-done((f32[4,128,512]{2,1,0:T(8,128)S(1)}, f32[4,128,512]{2,1,0:T(8,128)}, u32[]{:S(2)}, u32[]{:S(2)}) %collective-permute-start.20) | collective-permute-done | bytes 1048608 | tf_op jit(solution)/shard_map/ppermute | solution.py:378
  185.4 1.6 collective-permute-start.11
  187.0 20.2 %collective-permute-done.21.refs_17_ = f32[4,128,512]{2,1,0:T(8,128)} collective-permute-done((f32[4,128,512]{2,1,0:T(8,128)}, f32[4,128,512]{2,1,0:T(8,128)}, u32[]{:S(2)}, u32[]{:S(2)}) %collective-permute-start.21) | collective-permute-done | bytes 1048608 | tf_op jit(solution)/shard_map/ppermute | solution.py:378
  207.2 1.9 collective-permute-start.22
  209.1 2.4 collective-permute-start.23
  211.6 2.6 copy_select_fusion.1
  214.8 1.6 collective-permute-start.41
  222.6 5.2 %near_sandwich.5 = (f32[1,128,512]{2,1,0:T(8,128)S(1)}, f32[1,128,512]{2,1,0:T(8,128)S(1)}, f32[1,128,512]{2,1,0:T(8,128)S(1)}, f32[1,128,512]{2,1,0:T(8,128)S(1)}) custom-call(s32[3]{0:T(128)S(1)} %copy-done.24, f32[3]{0:T(128)S(1)} %copy-done.25, bf16[3,512,512]{2,1,0:T(8,128)(2,1)S(1)} %copy-done.3, bf16[3,512,512]{2,1,0:T(8,128)(2,1)S(1)} %copy-done.5, ...), custom_call_target="tpu_custom_call" | custom-call | flops 2415919104 | bytes 4194304 | tf_op jit(solution)/shard_map/near_sandwich/pallas_call | solution.py:225
  227.8 1.6 collective-permute-start.26
  229.4 4.9 %near_sandwich.6 = (f32[1,128,512]{2,1,0:T(8,128)S(1)}, f32[1,128,512]{2,1,0:T(8,128)S(1)}, f32[1,128,512]{2,1,0:T(8,128)S(1)}, f32[1,128,512]{2,1,0:T(8,128)S(1)}) custom-call(s32[3]{0:T(128)S(1)} %copy-done.24, f32[3]{0:T(128)S(1)} %copy-done.25, bf16[3,512,512]{2,1,0:T(8,128)(2,1)S(1)} %copy-done.3, bf16[3,512,512]{2,1,0:T(8,128)(2,1)S(1)} %copy-done.5, ...), custom_call_target="tpu_custom_call" | custom-call | flops 2415919104 | bytes 4194304 | tf_op jit(solution)/shard_map/near_sandwich/pallas_call | solution.py:225
  234.9 5.1 %near_sandwich.7 = (f32[1,128,512]{2,1,0:T(8,128)S(1)}, f32[1,128,512]{2,1,0:T(8,128)S(1)}, f32[1,128,512]{2,1,0:T(8,128)S(1)}, f32[1,128,512]{2,1,0:T(8,128)S(1)}) custom-call(s32[3]{0:T(128)S(1)} %copy-done.24, f32[3]{0:T(128)S(1)} %copy-done.25, bf16[3,512,512]{2,1,0:T(8,128)(2,1)S(1)} %copy-done.3, bf16[3,512,512]{2,1,0:T(8,128)(2,1)S(1)} %copy-done.5, ...), custom_call_target="tpu_custom_call" | custom-call | flops 2415919104 | bytes 4194304 | tf_op jit(solution)/shard_map/near_sandwich/pallas_call | solution.py:225
  240.0 1.5 collective-permute-start.28
  242.6 5.4 %collective-permute-done.28.refs_6_ = f32[1,128,512]{2,1,0:T(8,128)S(1)} collective-permute-done((f32[1,128,512]{2,1,0:T(8,128)S(1)}, f32[1,128,512]{2,1,0:T(8,128)S(1)}, u32[]{:S(2)}, u32[]{:S(2)}) %collective-permute-start.28) | collective-permute-done | bytes 262176 | tf_op jit(solution)/shard_map/ppermute | solution.py:458
  248.0 5.0 %near_sandwich.4 = (f32[1,128,512]{2,1,0:T(8,128)S(1)}, f32[1,128,512]{2,1,0:T(8,128)S(1)}, f32[1,128,512]{2,1,0:T(8,128)S(1)}, f32[1,128,512]{2,1,0:T(8,128)S(1)}) custom-call(s32[3]{0:T(128)S(1)} %copy-done.24, f32[3]{0:T(128)S(1)} %copy-done.25, bf16[3,512,512]{2,1,0:T(8,128)(2,1)S(1)} %copy-done.3, bf16[3,512,512]{2,1,0:T(8,128)(2,1)S(1)} %copy-done.5, ...), custom_call_target="tpu_custom_call" | custom-call | flops 2415919104 | bytes 4194304 | tf_op jit(solution)/shard_map/near_sandwich/pallas_call | solution.py:225
  256.4 5.6 %collective-permute-done.33.refs_11_ = f32[1,128,512]{2,1,0:T(8,128)S(1)} collective-permute-done((f32[1,128,512]{2,1,0:T(8,128)S(1)}, f32[1,128,512]{2,1,0:T(8,128)S(1)}, u32[]{:S(2)}, u32[]{:S(2)}) %collective-permute-start.33) | collective-permute-done | bytes 262176 | tf_op jit(solution)/shard_map/ppermute | solution.py:458
  262.0 1.3 collective-permute-start.24
  263.3 4.3 %collective-permute-done.34.refs_12_ = f32[1,128,512]{2,1,0:T(8,128)S(1)} collective-permute-done((f32[1,128,512]{2,1,0:T(8,128)S(1)}, f32[1,128,512]{2,1,0:T(8,128)S(1)}, u32[]{:S(2)}, u32[]{:S(2)}) %collective-permute-start.34) | collective-permute-done | bytes 262176 | tf_op jit(solution)/shard_map/ppermute | solution.py:458
  267.6 1.6 collective-permute-start.25
  269.2 4.0 %collective-permute-done.35.refs_13_ = f32[1,128,512]{2,1,0:T(8,128)S(1)} collective-permute-done((f32[1,128,512]{2,1,0:T(8,128)S(1)}, f32[1,128,512]{2,1,0:T(8,128)S(1)}, u32[]{:S(2)}, u32[]{:S(2)}) %collective-permute-start.35) | collective-permute-done | bytes 262176 | tf_op jit(solution)/shard_map/ppermute | solution.py:458
  273.9 5.5 %collective-permute-done.24.refs_0_ = f32[1,128,512]{2,1,0:T(8,128)S(1)} collective-permute-done((f32[1,128,512]{2,1,0:T(8,128)S(1)}, f32[1,128,512]{2,1,0:T(8,128)S(1)}, u32[]{:S(2)}, u32[]{:S(2)}) %collective-permute-start.24) | collective-permute-done | bytes 262176 | tf_op jit(solution)/shard_map/ppermute | solution.py:458
  279.4 5.1 %collective-permute-done.25.refs_1_ = f32[1,128,512]{2,1,0:T(8,128)S(1)} collective-permute-done((f32[1,128,512]{2,1,0:T(8,128)S(1)}, f32[1,128,512]{2,1,0:T(8,128)S(1)}, u32[]{:S(2)}, u32[]{:S(2)}) %collective-permute-start.25) | collective-permute-done | bytes 262176 | tf_op jit(solution)/shard_map/ppermute | solution.py:458
  284.5 1.4 shard_map.56
  (113 shorter events, 22.3 us)
Async XLA Ops:
  1.9 15.2 %collective-permute-start = (f32[2,128,512]{2,1,0:T(8,128)}, f32[2,128,512]{2,1,0:T(8,128)}, u32[]{:S(2)}, u32[]{:S(2)}) collective-permute-start(f32[2,128,512]{2,1,0:T(8,128)} %constant_dynamic-slice_fusion), channel_id=1, source_target_pairs={{0,2},{2,0},{1,3},{3,1},{4,6},{6,4},{5,7},{7,5},{8,10},{10,8},{9,1... | collective-permute-start | bytes 1572872 | tf_op jit(solution)/shard_map/ppermute | solution.py:394
  7.2 28.0 %collective-permute-start.4 = (f32[4,128,512]{2,1,0:T(8,128)}, f32[4,128,512]{2,1,0:T(8,128)}, u32[]{:S(2)}, u32[]{:S(2)}) collective-permute-start(f32[4,128,512]{2,1,0:T(8,128)} %add_momenta.5), channel_id=1, source_target_pairs={{0,1},{1,0},{2,3},{3,2},{4,5},{5,4},{6,7},{7,6},{8,9},{9,8},{10,11... | collective-permute-start | bytes 3145736 | tf_op jit(solution)/shard_map/ppermute | solution.py:365
  9.6 31.1 %collective-permute-start.7 = (f32[4,128,512]{2,1,0:T(8,128)}, f32[4,128,512]{2,1,0:T(8,128)}, u32[]{:S(2)}, u32[]{:S(2)}) collective-permute-start(f32[4,128,512]{2,1,0:T(8,128)} %add_momenta.7), channel_id=1, source_target_pairs={{0,1},{1,0},{2,3},{3,2},{4,5},{5,4},{6,7},{7,6},{8,9},{9,8},{10,11... | collective-permute-start | bytes 3145736 | tf_op jit(solution)/shard_map/ppermute | solution.py:365
  17.1 13.4 %collective-permute-start.2 = (f32[2,128,512]{2,1,0:T(8,128)}, f32[2,128,512]{2,1,0:T(8,128)}, u32[]{:S(2)}, u32[]{:S(2)}) collective-permute-start(f32[2,128,512]{2,1,0:T(8,128)} %collective-permute-done.refs_0_), channel_id=1, source_target_pairs={{0,16},{16,0},{1,17},{17,1},{2,18},{18,2},{3,19},{19,3},{4,20},{20... | collective-permute-start | bytes 1572872 | tf_op jit(solution)/shard_map/ppermute | solution.py:396
  18.8 26.9 %collective-permute-start.1 = (f32[2,128,512]{2,1,0:T(8,128)}, f32[2,128,512]{2,1,0:T(8,128)}, u32[]{:S(2)}, u32[]{:S(2)}) collective-permute-start(f32[2,128,512]{2,1,0:T(8,128)} %collective-permute-done.refs_0_), channel_id=1, source_target_pairs={{0,1},{1,0},{2,3},{3,2},{4,5},{5,4},{6,7},{7,6},{8,9},{9,8},{10,11... | collective-permute-start | bytes 1572872 | tf_op jit(solution)/shard_map/ppermute | solution.py:398
  30.5 16.8 %collective-permute-start.3 = (f32[2,128,512]{2,1,0:T(8,128)}, f32[2,128,512]{2,1,0:T(8,128)}, u32[]{:S(2)}, u32[]{:S(2)}) collective-permute-start(f32[2,128,512]{2,1,0:T(8,128)} %collective-permute-done.2.refs_2_), channel_id=1, source_target_pairs={{0,1},{1,0},{2,3},{3,2},{4,5},{5,4},{6,7},{7,6},{8,9},{9,8},{10,11... | collective-permute-start | bytes 1572872 | tf_op jit(solution)/shard_map/ppermute | solution.py:398
  37.0 56.8 %copy-start.24 = (s32[3]{0:T(128)S(1)}, s32[3]{0:T(128)}, u32[]{:S(2)}) copy-start(s32[3]{0:T(128)} %steps.9) | copy-start | bytes 40
  37.0 57.9 %copy-start.22 = (f32[2,512,512]{2,1,0:T(8,128)S(1)}, f32[2,512,512]{2,1,0:T(8,128)}, u32[]{:S(2)}) copy-start(f32[2,512,512]{2,1,0:T(8,128)} %couplings.1) | copy-start | bytes 6291460
  37.0 57.9 %copy-start.26 = (s32[3]{0:T(128)S(1)}, s32[3]{0:T(128)}, u32[]{:S(2)}) copy-start(s32[3]{0:T(128)} %owners.1) | copy-start | bytes 40
  37.0 27.1 %collective-permute-start.5 = (f32[4,128,512]{2,1,0:T(8,128)S(1)}, f32[4,128,512]{2,1,0:T(8,128)S(1)}, u32[]{:S(2)}, u32[]{:S(2)}) collective-permute-start(f32[4,128,512]{2,1,0:T(8,128)S(1)} %add.14.refs_8_.refs_0_), channel_id=1, source_target_pairs={{0,4},{4,8},{8,12},{1,5},{5,9},{9,13},{2,6},{6,10},{10,14},{3,7},{... | collective-permute-start | bytes 3145736 | tf_op jit(solution)/shard_map/ppermute | solution.py:377
  42.1 96.1 %copy-start = (f32[4,128,512]{2,1,0:T(8,128)}, f32[4,128,512]{2,1,0:T(8,128)S(1)}, u32[]{:S(2)}) copy-start(f32[4,128,512]{2,1,0:T(8,128)S(1)} %add.15.refs_9_.refs_1_) | copy-start | bytes 3145732
  42.1 44.0 %collective-permute-start.8 = (f32[4,128,512]{2,1,0:T(8,128)S(1)}, f32[4,128,512]{2,1,0:T(8,128)S(1)}, u32[]{:S(2)}, u32[]{:S(2)}) collective-permute-start(f32[4,128,512]{2,1,0:T(8,128)S(1)} %add.15.refs_9_.refs_1_), channel_id=1, source_target_pairs={{0,4},{4,8},{8,12},{1,5},{5,9},{9,13},{2,6},{6,10},{10,14},{3,7},{... | collective-permute-start | bytes 3145736 | tf_op jit(solution)/shard_map/ppermute | solution.py:377
  45.6 41.8 %collective-permute-start.14 = (f32[4,128,512]{2,1,0:T(8,128)S(1)}, f32[4,128,512]{2,1,0:T(8,128)S(1)}, u32[]{:S(2)}, u32[]{:S(2)}) collective-permute-start(f32[4,128,512]{2,1,0:T(8,128)S(1)} %add.14.refs_8_.refs_0_), channel_id=1, source_target_pairs={{0,1},{1,0},{2,3},{3,2},{4,5},{5,4},{6,7},{7,6},{8,9},{9,8},{10,11... | collective-permute-start | bytes 3145736 | tf_op jit(solution)/shard_map/ppermute | solution.py:387
  45.7 43.0 %collective-permute-start.36 = (f32[4,128,512]{2,1,0:T(8,128)S(1)}, f32[4,128,512]{2,1,0:T(8,128)S(1)}, u32[]{:S(2)}, u32[]{:S(2)}) collective-permute-start(f32[4,128,512]{2,1,0:T(8,128)S(1)} %add.14.refs_8_.refs_0_), channel_id=1, source_target_pairs={{0,2},{2,0},{1,3},{3,1},{4,6},{6,4},{5,7},{7,5},{8,10},{10,8},{9,1... | collective-permute-start | bytes 3145736 | tf_op jit(solution)/shard_map/ppermute | solution.py:418
  47.3 46.5 %collective-permute-start.37 = (f32[4,128,512]{2,1,0:T(8,128)S(1)}, f32[4,128,512]{2,1,0:T(8,128)S(1)}, u32[]{:S(2)}, u32[]{:S(2)}) collective-permute-start(f32[4,128,512]{2,1,0:T(8,128)S(1)} %add.15.refs_9_.refs_1_), channel_id=1, source_target_pairs={{0,2},{2,0},{1,3},{3,1},{4,6},{6,4},{5,7},{7,5},{8,10},{10,8},{9,1... | collective-permute-start | bytes 3145736 | tf_op jit(solution)/shard_map/ppermute | solution.py:418
  64.1 33.8 %collective-permute-start.15 = (f32[4,128,512]{2,1,0:T(8,128)S(1)}, f32[4,128,512]{2,1,0:T(8,128)S(1)}, u32[]{:S(2)}, u32[]{:S(2)}) collective-permute-start(f32[4,128,512]{2,1,0:T(8,128)S(1)} %add.15.refs_9_.refs_1_), channel_id=1, source_target_pairs={{0,1},{1,0},{2,3},{3,2},{4,5},{5,4},{6,7},{7,6},{8,9},{9,8},{10,11... | collective-permute-start | bytes 3145736 | tf_op jit(solution)/shard_map/ppermute | solution.py:387
  86.1 28.4 %collective-permute-start.16 = (f32[4,128,512]{2,1,0:T(8,128)S(1)}, f32[4,128,512]{2,1,0:T(8,128)S(1)}, u32[]{:S(2)}, u32[]{:S(2)}) collective-permute-start(f32[4,128,512]{2,1,0:T(8,128)S(1)} %add.14.refs_8_.refs_0_), channel_id=1, source_target_pairs={{12,8},{8,4},{4,0},{13,9},{9,5},{5,1},{14,10},{10,6},{6,2},{15,11}... | collective-permute-start | bytes 3145736 | tf_op jit(solution)/shard_map/ppermute | solution.py:378
  87.4 48.6 %collective-permute-start.17 = (f32[4,128,512]{2,1,0:T(8,128)S(1)}, f32[4,128,512]{2,1,0:T(8,128)}, u32[]{:S(2)}, u32[]{:S(2)}) collective-permute-start(f32[4,128,512]{2,1,0:T(8,128)S(1)} %add.15.refs_9_.refs_1_), channel_id=1, source_target_pairs={{12,8},{8,4},{4,0},{13,9},{9,5},{5,1},{14,10},{10,6},{6,2},{15,11}... | collective-permute-start | bytes 3145736 | tf_op jit(solution)/shard_map/ppermute | solution.py:378
  88.7 48.9 %collective-permute-start.38 = (f32[4,128,512]{2,1,0:T(8,128)S(1)}, f32[4,128,512]{2,1,0:T(8,128)S(1)}, u32[]{:S(2)}, u32[]{:S(2)}) collective-permute-start(f32[4,128,512]{2,1,0:T(8,128)S(1)} %collective-permute-done.36.refs_2_), channel_id=1, source_target_pairs={{0,1},{1,0},{2,3},{3,2},{4,5},{5,4},{6,7},{7,6},{8,9},{9,8},{10,11... | collective-permute-start | bytes 3145736 | tf_op jit(solution)/shard_map/ppermute | solution.py:421
  93.7 44.0 %collective-permute-start.39 = (f32[4,128,512]{2,1,0:T(8,128)S(1)}, f32[4,128,512]{2,1,0:T(8,128)S(1)}, u32[]{:S(2)}, u32[]{:S(2)}) collective-permute-start(f32[4,128,512]{2,1,0:T(8,128)S(1)} %collective-permute-done.37.refs_3_), channel_id=1, source_target_pairs={{0,1},{1,0},{2,3},{3,2},{4,5},{5,4},{6,7},{7,6},{8,9},{9,8},{10,11... | collective-permute-start | bytes 3145736 | tf_op jit(solution)/shard_map/ppermute | solution.py:421
  97.9 56.1 %copy-start.2 = (bf16[3,512,512]{2,1,0:T(8,128)(2,1)}, bf16[3,512,512]{2,1,0:T(8,128)(2,1)S(1)}, u32[]{:S(2)}) copy-start(bf16[3,512,512]{2,1,0:T(8,128)(2,1)S(1)} %get-tuple-element.27.right_high) | copy-start | bytes 4718596
  97.9 56.8 %collective-permute-start.6 = (f32[4,128,512]{2,1,0:T(8,128)S(1)}, f32[4,128,512]{2,1,0:T(8,128)}, u32[]{:S(2)}, u32[]{:S(2)}) collective-permute-start(f32[4,128,512]{2,1,0:T(8,128)S(1)} %collective-permute-done.5.refs_4_), channel_id=1, source_target_pairs={{4,8},{8,12},{5,9},{9,13},{6,10},{10,14},{7,11},{11,15},{20,24},{2... | collective-permute-start | bytes 3145736 | tf_op jit(solution)/shard_map/ppermute | solution.py:377
  114.5 42.9 %collective-permute-start.12 = (f32[4,128,512]{2,1,0:T(8,128)S(1)}, f32[4,128,512]{2,1,0:T(8,128)S(1)}, u32[]{:S(2)}, u32[]{:S(2)}) collective-permute-start(f32[4,128,512]{2,1,0:T(8,128)S(1)} %collective-permute-done.5.refs_4_), channel_id=1, source_target_pairs={{0,1},{1,0},{2,3},{3,2},{4,5},{5,4},{6,7},{7,6},{8,9},{9,8},{10,11... | collective-permute-start | bytes 3145736 | tf_op jit(solution)/shard_map/ppermute | solution.py:387
  136.0 20.0 %collective-permute-start.9 = (f32[4,128,512]{2,1,0:T(8,128)S(1)}, f32[4,128,512]{2,1,0:T(8,128)}, u32[]{:S(2)}, u32[]{:S(2)}) collective-permute-start(f32[4,128,512]{2,1,0:T(8,128)S(1)} %collective-permute-done.8.refs_5_), channel_id=1, source_target_pairs={{4,8},{8,12},{5,9},{9,13},{6,10},{10,14},{7,11},{11,15},{20,24},{2... | collective-permute-start | bytes 3145736 | tf_op jit(solution)/shard_map/ppermute | solution.py:377
  137.7 20.8 %collective-permute-start.13 = (f32[4,128,512]{2,1,0:T(8,128)S(1)}, f32[4,128,512]{2,1,0:T(8,128)S(1)}, u32[]{:S(2)}, u32[]{:S(2)}) collective-permute-start(f32[4,128,512]{2,1,0:T(8,128)S(1)} %collective-permute-done.8.refs_5_), channel_id=1, source_target_pairs={{0,1},{1,0},{2,3},{3,2},{4,5},{5,4},{6,7},{7,6},{8,9},{9,8},{10,11... | collective-permute-start | bytes 3145736 | tf_op jit(solution)/shard_map/ppermute | solution.py:387
  137.7 22.2 %collective-permute-start.18 = (f32[4,128,512]{2,1,0:T(8,128)S(1)}, f32[4,128,512]{2,1,0:T(8,128)S(1)}, u32[]{:S(2)}, u32[]{:S(2)}) collective-permute-start(f32[4,128,512]{2,1,0:T(8,128)S(1)} %collective-permute-done.16.refs_12_), channel_id=1, source_target_pairs={{0,1},{1,0},{2,3},{3,2},{4,5},{5,4},{6,7},{7,6},{8,9},{9,8},{10,11... | collective-permute-start | bytes 3145736 | tf_op jit(solution)/shard_map/ppermute | solution.py:387
  154.8 30.6 %collective-permute-start.20 = (f32[4,128,512]{2,1,0:T(8,128)S(1)}, f32[4,128,512]{2,1,0:T(8,128)}, u32[]{:S(2)}, u32[]{:S(2)}) collective-permute-start(f32[4,128,512]{2,1,0:T(8,128)S(1)} %collective-permute-done.16.refs_12_), channel_id=1, source_target_pairs={{8,4},{4,0},{9,5},{5,1},{10,6},{6,2},{11,7},{7,3},{24,20},{20,16},... | collective-permute-start | bytes 3145736 | tf_op jit(solution)/shard_map/ppermute | solution.py:378
  156.1 51.1 %collective-permute-start.21 = (f32[4,128,512]{2,1,0:T(8,128)}, f32[4,128,512]{2,1,0:T(8,128)}, u32[]{:S(2)}, u32[]{:S(2)}) collective-permute-start(f32[4,128,512]{2,1,0:T(8,128)} %collective-permute-done.17.refs_13_), channel_id=1, source_target_pairs={{8,4},{4,0},{9,5},{5,1},{10,6},{6,2},{11,7},{7,3},{24,20},{20,16},... | collective-permute-start | bytes 3145736 | tf_op jit(solution)/shard_map/ppermute | solution.py:378
  158.4 50.7 %collective-permute-start.40 = (f32[4,128,512]{2,0,1:T(4,128)S(1)}, f32[4,128,512]{2,0,1:T(4,128)}, u32[]{:S(2)}, u32[]{:S(2)}) collective-permute-start(f32[4,128,512]{2,0,1:T(4,128)S(1)} %copy.6), channel_id=1, source_target_pairs={{0,1},{1,0},{2,3},{3,2},{4,5},{5,4},{6,7},{7,6},{8,9},{9,8},{10,11... | collective-permute-start | bytes 3145736 | tf_op jit(solution)/shard_map/ppermute | solution.py:435
  159.5 55.3 %collective-permute-start.19 = (f32[4,128,512]{2,1,0:T(8,128)}, f32[4,128,512]{2,1,0:T(8,128)}, u32[]{:S(2)}, u32[]{:S(2)}) collective-permute-start(f32[4,128,512]{2,1,0:T(8,128)} %collective-permute-done.17.refs_13_), channel_id=1, source_target_pairs={{0,1},{1,0},{2,3},{3,2},{4,5},{5,4},{6,7},{7,6},{8,9},{9,8},{10,11... | collective-permute-start | bytes 3145736 | tf_op jit(solution)/shard_map/ppermute | solution.py:387
  160.9 55.4 %collective-permute-start.10 = (f32[4,128,512]{2,1,0:T(8,128)}, f32[4,128,512]{2,1,0:T(8,128)}, u32[]{:S(2)}, u32[]{:S(2)}) collective-permute-start(f32[4,128,512]{2,1,0:T(8,128)} %collective-permute-done.6.refs_0_), channel_id=1, source_target_pairs={{8,9},{9,8},{12,13},{13,12},{10,11},{11,10},{14,15},{15,14},{24,25... | collective-permute-start | bytes 3145736 | tf_op jit(solution)/shard_map/ppermute | solution.py:387
  185.4 32.3 %collective-permute-start.11 = (f32[4,128,512]{2,1,0:T(8,128)}, f32[4,128,512]{2,1,0:T(8,128)}, u32[]{:S(2)}, u32[]{:S(2)}) collective-permute-start(f32[4,128,512]{2,1,0:T(8,128)} %collective-permute-done.9.refs_1_), channel_id=1, source_target_pairs={{8,9},{9,8},{12,13},{13,12},{10,11},{11,10},{14,15},{15,14},{24,25... | collective-permute-start | bytes 3145736 | tf_op jit(solution)/shard_map/ppermute | solution.py:387
  207.2 10.4 %collective-permute-start.22 = (f32[4,128,512]{2,1,0:T(8,128)}, f32[4,128,512]{2,1,0:T(8,128)}, u32[]{:S(2)}, u32[]{:S(2)}) collective-permute-start(f32[4,128,512]{2,1,0:T(8,128)} %collective-permute-done.20.refs_16_), channel_id=1, source_target_pairs={{0,1},{1,0},{4,5},{5,4},{2,3},{3,2},{6,7},{7,6},{16,17},{17,16},{2... | collective-permute-start | bytes 3145736 | tf_op jit(solution)/shard_map/ppermute | solution.py:387
  209.1 8.5 %collective-permute-start.23 = (f32[4,128,512]{2,1,0:T(8,128)}, f32[4,128,512]{2,1,0:T(8,128)}, u32[]{:S(2)}, u32[]{:S(2)}) collective-permute-start(f32[4,128,512]{2,1,0:T(8,128)} %collective-permute-done.21.refs_17_), channel_id=1, source_target_pairs={{0,1},{1,0},{4,5},{5,4},{2,3},{3,2},{6,7},{7,6},{16,17},{17,16},{2... | collective-permute-start | bytes 3145736 | tf_op jit(solution)/shard_map/ppermute | solution.py:387
  214.8 69.7 %collective-permute-start.41 = (f32[128,8,512]{2,1,0:T(8,128)S(1)}, f32[128,8,512]{2,1,0:T(8,128)S(1)}, u32[]{:S(2)}, u32[]{:S(2)}) collective-permute-start(f32[128,8,512]{2,1,0:T(8,128)S(1)} %maximum_bitcast_fusion), channel_id=1, source_target_pairs={{0,12},{1,13},{2,14},{3,15},{16,28},{17,29},{18,30},{19,31}} | collective-permute-start | bytes 6291464 | tf_op jit(solution)/shard_map/ppermute | solution.py:439
  216.3 68.1 %collective-permute-start.42 = (f32[128,8,512]{2,1,0:T(8,128)S(1)}, f32[128,8,512]{2,1,0:T(8,128)S(1)}, u32[]{:S(2)}, u32[]{:S(2)}) collective-permute-start(f32[128,8,512]{2,1,0:T(8,128)S(1)} %maximum_bitcast_fusion), channel_id=1, source_target_pairs={{12,0},{13,1},{14,2},{15,3},{28,16},{29,17},{30,18},{31,19}} | collective-permute-start | bytes 6291464 | tf_op jit(solution)/shard_map/ppermute | solution.py:440
  227.8 13.7 %collective-permute-start.26 = (f32[1,128,512]{2,1,0:T(8,128)S(1)}, f32[1,128,512]{2,1,0:T(8,128)S(1)}, u32[]{:S(2)}, u32[]{:S(2)}) collective-permute-start(f32[1,128,512]{2,1,0:T(8,128)S(1)} %get-tuple-element.36), channel_id=1, source_target_pairs={{0,2},{1,3},{2,0},{3,1},{4,6},{5,7},{6,4},{7,5},{8,10},{9,11},{10,... | collective-permute-start | bytes 786440 | tf_op jit(solution)/shard_map/ppermute | solution.py:458
  234.3 8.2 %collective-permute-start.27 = (f32[1,128,512]{2,1,0:T(8,128)S(1)}, f32[1,128,512]{2,1,0:T(8,128)S(1)}, u32[]{:S(2)}, u32[]{:S(2)}) collective-permute-start(f32[1,128,512]{2,1,0:T(8,128)S(1)} %get-tuple-element.37), channel_id=1, source_target_pairs={{0,2},{1,3},{2,0},{3,1},{4,6},{5,7},{6,4},{7,5},{8,10},{9,11},{10,... | collective-permute-start | bytes 786440 | tf_op jit(solution)/shard_map/ppermute | solution.py:458
  240.0 8.0 %collective-permute-start.28 = (f32[1,128,512]{2,1,0:T(8,128)S(1)}, f32[1,128,512]{2,1,0:T(8,128)S(1)}, u32[]{:S(2)}, u32[]{:S(2)}) collective-permute-start(f32[1,128,512]{2,1,0:T(8,128)S(1)} %get-tuple-element.38), channel_id=1, source_target_pairs={{0,2},{1,3},{2,0},{3,1},{4,6},{5,7},{6,4},{7,5},{8,10},{9,11},{10,... | collective-permute-start | bytes 786440 | tf_op jit(solution)/shard_map/ppermute | solution.py:458
  241.5 11.5 %collective-permute-start.29 = (f32[1,128,512]{2,1,0:T(8,128)S(1)}, f32[1,128,512]{2,1,0:T(8,128)S(1)}, u32[]{:S(2)}, u32[]{:S(2)}) collective-permute-start(f32[1,128,512]{2,1,0:T(8,128)S(1)} %get-tuple-element.39), channel_id=1, source_target_pairs={{0,1},{1,0},{2,3},{3,2},{4,5},{5,4},{6,7},{7,6},{8,9},{9,8},{10,11... | collective-permute-start | bytes 786440 | tf_op jit(solution)/shard_map/ppermute | solution.py:458
  242.6 11.1 %collective-permute-start.30 = (f32[1,128,512]{2,1,0:T(8,128)S(1)}, f32[1,128,512]{2,1,0:T(8,128)S(1)}, u32[]{:S(2)}, u32[]{:S(2)}) collective-permute-start(f32[1,128,512]{2,1,0:T(8,128)S(1)} %get-tuple-element.40), channel_id=1, source_target_pairs={{0,1},{1,0},{2,3},{3,2},{4,5},{5,4},{6,7},{7,6},{8,9},{9,8},{10,11... | collective-permute-start | bytes 786440 | tf_op jit(solution)/shard_map/ppermute | solution.py:458
  248.0 6.7 %collective-permute-start.31 = (f32[1,128,512]{2,1,0:T(8,128)S(1)}, f32[1,128,512]{2,1,0:T(8,128)S(1)}, u32[]{:S(2)}, u32[]{:S(2)}) collective-permute-start(f32[1,128,512]{2,1,0:T(8,128)S(1)} %get-tuple-element.41), channel_id=1, source_target_pairs={{0,1},{1,0},{2,3},{3,2},{4,5},{5,4},{6,7},{7,6},{8,9},{9,8},{10,11... | collective-permute-start | bytes 786440 | tf_op jit(solution)/shard_map/ppermute | solution.py:458
  253.0 2.4 collective-permute-start.32
  253.7 8.3 %collective-permute-start.33 = (f32[1,128,512]{2,1,0:T(8,128)S(1)}, f32[1,128,512]{2,1,0:T(8,128)S(1)}, u32[]{:S(2)}, u32[]{:S(2)}) collective-permute-start(f32[1,128,512]{2,1,0:T(8,128)S(1)} %get-tuple-element.43), channel_id=1, source_target_pairs={{0,3},{1,2},{2,1},{3,0},{4,7},{5,6},{6,5},{7,4},{8,11},{9,10},{10,... | collective-permute-start | bytes 786440 | tf_op jit(solution)/shard_map/ppermute | solution.py:458
  254.7 12.9 %collective-permute-start.34 = (f32[1,128,512]{2,1,0:T(8,128)S(1)}, f32[1,128,512]{2,1,0:T(8,128)S(1)}, u32[]{:S(2)}, u32[]{:S(2)}) collective-permute-start(f32[1,128,512]{2,1,0:T(8,128)S(1)} %get-tuple-element.44), channel_id=1, source_target_pairs={{0,3},{1,2},{2,1},{3,0},{4,7},{5,6},{6,5},{7,4},{8,11},{9,10},{10,... | collective-permute-start | bytes 786440 | tf_op jit(solution)/shard_map/ppermute | solution.py:458
  255.4 17.8 %collective-permute-start.35 = (f32[1,128,512]{2,1,0:T(8,128)S(1)}, f32[1,128,512]{2,1,0:T(8,128)S(1)}, u32[]{:S(2)}, u32[]{:S(2)}) collective-permute-start(f32[1,128,512]{2,1,0:T(8,128)S(1)} %get-tuple-element.45), channel_id=1, source_target_pairs={{0,3},{1,2},{2,1},{3,0},{4,7},{5,6},{6,5},{7,4},{8,11},{9,10},{10,... | collective-permute-start | bytes 786440 | tf_op jit(solution)/shard_map/ppermute | solution.py:458
  262.0 17.4 %collective-permute-start.24 = (f32[1,128,512]{2,1,0:T(8,128)S(1)}, f32[1,128,512]{2,1,0:T(8,128)S(1)}, u32[]{:S(2)}, u32[]{:S(2)}) collective-permute-start(f32[1,128,512]{2,1,0:T(8,128)S(1)} %get-tuple-element.30), channel_id=1, source_target_pairs={{0,2},{1,3},{2,0},{3,1},{4,6},{5,7},{6,4},{7,5},{8,10},{9,11},{10,... | collective-permute-start | bytes 786440 | tf_op jit(solution)/shard_map/ppermute | solution.py:458
  267.6 16.9 %collective-permute-start.25 = (f32[1,128,512]{2,1,0:T(8,128)S(1)}, f32[1,128,512]{2,1,0:T(8,128)S(1)}, u32[]{:S(2)}, u32[]{:S(2)}) collective-permute-start(f32[1,128,512]{2,1,0:T(8,128)S(1)} %get-tuple-element.31), channel_id=1, source_target_pairs={{0,3},{1,2},{2,1},{3,0},{4,7},{5,6},{6,5},{7,4},{8,11},{9,10},{10,... | collective-permute-start | bytes 786440 | tf_op jit(solution)/shard_map/ppermute | solution.py:458
  (23 other events, 428.4 us)

commit v11 on v10

--- a/solution.py
+++ b/solution.py
@@ -141,7 +141,7 @@
                 for g in range(n_groups):
 
                     @pl.when(group == g)
-                    def _(g=g, at=at, slot=slot, other=other):
+                    def _(g=g, at=at, slot=slot, other=other, mode=mode):
                         for h in range(2):
 
                             @pl.when(other == h)
@@ -156,7 +156,7 @@
                                         start = pl.multiple_of(behind * per + first % per, 8)
                                     pltpu.make_async_copy(
                                         ref.at[at], planes.at[buffer, slot, pl.ds(start, depth)], sems.at[buffer, slot]
-                                    ).start()
+                                    ).start(priority=0 if mode == 0 else 1)
                                     first += depth
 
     fetch(0, 0)
@@ -269,7 +269,7 @@
     out, total, sem = refs[-3:]
     full = refs[-3 - whole : -3]
     core = lax.axis_index("kz")
-    group = 16
+    group = 32
 
     @pl.loop(0, total.shape[0] // group)
     def _(at):
@@ -363,8 +363,7 @@
     for piece in range(PIECES):
         given = summed(True, piece)
         given = lax.ppermute(given, "kz", swap)
-        kept = summed(False, piece)
-        own.append(kept + given)
+        own.append(summed(False, piece, given))
 
     if line:
         up = [[(i, i + 1) for i in range(d, n - 1)] for d in range(REACH)]

time: 287 us -> 283 us (0.986)
  other arithmetic: 6.38 us -> 3.01 us
  waiting for transfers between devices: 172 us -> 169 us
    add x2 -> x0, other arithmetic: 3.27 us -> none  [shards(): own.append(kept + given)]
    unnamed x56 -> x52, local copies, waits for them, and re-layouts: 7.95 us -> 8.32 us
  transfers between devices with their start and end apart: 43 -> 43, of which waited for: 16 -> 16; matrix products, arithmetic and copies ran while one was open for 2% -> 1% of each run, Pallas kernels for 17% -> 18%
where the time goes in v11:
time: 283 us; the launch traced here: 282 us
  waiting for transfers between devices  169 us (60%)
  Pallas kernels  52.7 us (19%)
  starting transfers between devices  45.5 us (16%)
  local copies, waits for them, and re-layouts  10.9 us (4%)
  other arithmetic  3.01 us (1%)
    ppermute x4, waiting for transfers between devices, shards(): lax.ppermute(x, 'energy', down[d - 1])  76.4 us
    ppermute x4, waiting for transfers between devices, shards(): streams[-d] = [lax.ppermute(x, 'energy', up[d - 1]) for x in streams[1 - d]]  37.5 us
    pallas_call x5, Pallas kernels, sandwich(): pl.pallas_call(functools.partial(split_dot, len(groups), len(groups[0][0]...  36.6 us
    ppermute x12, waiting for transfers between devices, shards(): block = lax.ppermute(block, ('atom', 'kz'), pairs)  30.3 us
    ppermute x1, waiting for transfers between devices, shards(): lax.ppermute(got, 'grp', [(i, (i + d) % parts) for i in range(parts)])  11.6 us
    ppermute x4, starting transfers between devices, shards(): streams[-d] = [lax.ppermute(x, 'energy', up[d - 1]) for x in streams[1 - d]]  10.8 us
    ppermute x12, starting transfers between devices, shards(): block = lax.ppermute(block, ('atom', 'kz'), pairs)  10.5 us
    pallas_call x4, Pallas kernels, summed(): pl.pallas_call(functools.partial(add_momenta, theirs, piece * size), out_...  9.89 us
  transfers between devices with their start and end apart: 43, of which 16 were waited for; matrix products, arithmetic and copies ran while one was open for 1% of the time, Pallas kernels for 18%

profile of v11, /device:TPU:0, one launch (start us, length us, event | category | flops | bytes accessed | tf_op | source)
XLA Modules:
  0.0 281.8 jit_solution(13024293072599250746)
XLA Ops:
  0.0 1.9 constant_dynamic-slice_fusion
  1.9 3.0 %collective-permute-start = (f32[2,128,512]{2,1,0:T(8,128)}, f32[2,128,512]{2,1,0:T(8,128)}, u32[]{:S(2)}, u32[]{:S(2)}) collective-permute-start(f32[2,128,512]{2,1,0:T(8,128)} %constant_dynamic-slice_fusion), channel_id=1, source_target_pairs={{0,2},{2,0},{1,3},{3,1},{4,6},{6,4},{5,7},{7,5},{8,10},{10,8},{9,1... | collective-permute-start | bytes 1572872 | tf_op jit(solution)/shard_map/ppermute | solution.py:393
  4.9 2.3 add_momenta.4
  7.2 2.3 add_momenta.6
  10.1 7.0 %collective-permute-done.refs_0_ = f32[2,128,512]{2,1,0:T(8,128)} collective-permute-done((f32[2,128,512]{2,1,0:T(8,128)}, f32[2,128,512]{2,1,0:T(8,128)}, u32[]{:S(2)}, u32[]{:S(2)}) %collective-permute-start) | collective-permute-done | bytes 524320 | tf_op jit(solution)/shard_map/ppermute | solution.py:393
  17.1 1.8 collective-permute-start.2
  18.9 11.6 %collective-permute-done.2.refs_2_ = f32[2,128,512]{2,1,0:T(8,128)} collective-permute-done((f32[2,128,512]{2,1,0:T(8,128)}, f32[2,128,512]{2,1,0:T(8,128)}, u32[]{:S(2)}, u32[]{:S(2)}) %collective-permute-start.2) | collective-permute-done | bytes 524320 | tf_op jit(solution)/shard_map/ppermute | solution.py:395
  30.5 2.6 add_momenta.5.refs_8_.refs_0_
  33.2 4.5 %collective-permute-start.5 = (f32[4,128,512]{2,1,0:T(8,128)}, f32[4,128,512]{2,1,0:T(8,128)}, u32[]{:S(2)}, u32[]{:S(2)}) collective-permute-start(f32[4,128,512]{2,1,0:T(8,128)} %add_momenta.5.refs_8_.refs_0_), channel_id=1, source_target_pairs={{0,4},{4,8},{8,12},{1,5},{5,9},{9,13},{2,6},{6,10},{10,14},{3,7},{... | collective-permute-start | bytes 3145736 | tf_op jit(solution)/shard_map/ppermute | solution.py:376
  37.6 2.6 add_momenta.7.refs_9_.refs_1_
  40.3 2.6 collective-permute-start.8
  43.0 1.6 collective-permute-start.36
  45.0 15.4 %collective-permute-done.5.refs_4_ = f32[4,128,512]{2,1,0:T(8,128)} collective-permute-done((f32[4,128,512]{2,1,0:T(8,128)}, f32[4,128,512]{2,1,0:T(8,128)}, u32[]{:S(2)}, u32[]{:S(2)}) %collective-permute-start.5) | collective-permute-done | bytes 1048608 | tf_op jit(solution)/shard_map/ppermute | solution.py:376
  60.5 22.0 %collective-permute-done.8.refs_5_ = f32[4,128,512]{2,1,0:T(8,128)S(1)} collective-permute-done((f32[4,128,512]{2,1,0:T(8,128)}, f32[4,128,512]{2,1,0:T(8,128)S(1)}, u32[]{:S(2)}, u32[]{:S(2)}) %collective-permute-start.8) | collective-permute-done | bytes 1048608 | tf_op jit(solution)/shard_map/ppermute | solution.py:376
  83.8 1.3 collective-permute-start.17
  85.2 6.0 %collective-permute-done.37.refs_3_ = f32[4,128,512]{2,1,0:T(8,128)S(1)} collective-permute-done((f32[4,128,512]{2,1,0:T(8,128)}, f32[4,128,512]{2,1,0:T(8,128)S(1)}, u32[]{:S(2)}, u32[]{:S(2)}) %collective-permute-start.37) | collective-permute-done | bytes 1048608 | tf_op jit(solution)/shard_map/ppermute | solution.py:417
  92.4 1.6 copy-done.21
  94.0 3.0 %prepare.1 = (bf16[3,512,512]{2,1,0:T(8,128)(2,1)S(1)}, bf16[3,512,512]{2,1,0:T(8,128)(2,1)S(1)}, bf16[3,256,1536]{2,1,0:T(8,128)(2,1)S(1)}, bf16[3,512,768]{2,1,0:T(8,128)(2,1)S(1)}) custom-call(s32[3]{0:T(128)S(1)} %copy-done.25, f32[2,512,512]{2,1,0:T(8,128)S(1)} %copy-done.21, f32[2,128,512]{2,1,0:T(8,128)} %collective-permute-done.refs_0_, ...), custom_call_target="tpu_custom_call" | custom-call | flops 6291456 | bytes 7864320 | tf_op jit(solution)/shard_map/prepare/pallas_call | solution.py:402
  97.0 2.1 collective-permute-start.6
  99.1 11.9 %collective-permute-done.16.refs_12_ = f32[4,128,512]{2,1,0:T(8,128)S(1)} collective-permute-done((f32[4,128,512]{2,1,0:T(8,128)}, f32[4,128,512]{2,1,0:T(8,128)S(1)}, u32[]{:S(2)}, u32[]{:S(2)}) %collective-permute-start.16) | collective-permute-done | bytes 1048608 | tf_op jit(solution)/shard_map/ppermute | solution.py:377
  111.0 21.5 %collective-permute-done.17.refs_13_ = f32[4,128,512]{2,1,0:T(8,128)} collective-permute-done((f32[4,128,512]{2,1,0:T(8,128)}, f32[4,128,512]{2,1,0:T(8,128)}, u32[]{:S(2)}, u32[]{:S(2)}) %collective-permute-start.17) | collective-permute-done | bytes 1048608 | tf_op jit(solution)/shard_map/ppermute | solution.py:377
  132.5 1.6 collective-permute-start.9
  134.7 16.1 %far_sandwich.1 = (f32[4,128,512]{2,1,0:T(8,128)S(1)}, f32[4,128,512]{2,1,0:T(8,128)S(1)}) custom-call(s32[3]{0:T(128)S(1)} %guard.1.steps, f32[3]{0:T(128)S(1)} %copy-done.24, bf16[3,512,512]{2,1,0:T(8,128)(2,1)S(1)} %get-tuple-element.27.right_high, bf16[3,512,512]{2,1,0:T(8,128)(2,1)S(1)} %get-tuple-element.28.right_low, ...), custom_call_target="tpu_custom_call" | custom-call | flops 14495514624 | bytes 27262976 | tf_op jit(solution)/shard_map/far_sandwich/pallas_call | solution.py:225
  151.5 1.3 collective-permute-start.20
  152.9 1.3 collective-permute-start.21
  157.7 1.6 collective-permute-start.10
  159.3 22.8 %collective-permute-done.20.refs_16_ = f32[4,128,512]{2,1,0:T(8,128)} collective-permute-done((f32[4,128,512]{2,1,0:T(8,128)S(1)}, f32[4,128,512]{2,1,0:T(8,128)}, u32[]{:S(2)}, u32[]{:S(2)}) %collective-permute-start.20) | collective-permute-done | bytes 1048608 | tf_op jit(solution)/shard_map/ppermute | solution.py:377
  182.2 1.6 collective-permute-start.11
  183.8 20.2 %collective-permute-done.21.refs_17_ = f32[4,128,512]{2,1,0:T(8,128)} collective-permute-done((f32[4,128,512]{2,1,0:T(8,128)}, f32[4,128,512]{2,1,0:T(8,128)}, u32[]{:S(2)}, u32[]{:S(2)}) %collective-permute-start.21) | collective-permute-done | bytes 1048608 | tf_op jit(solution)/shard_map/ppermute | solution.py:377
  204.0 1.9 collective-permute-start.22
  205.9 2.4 collective-permute-start.23
  208.4 2.6 copy_select_fusion.1
  211.4 1.6 collective-permute-start.41
  218.1 5.1 %near_sandwich.5 = (f32[1,128,512]{2,1,0:T(8,128)S(1)}, f32[1,128,512]{2,1,0:T(8,128)S(1)}, f32[1,128,512]{2,1,0:T(8,128)S(1)}, f32[1,128,512]{2,1,0:T(8,128)S(1)}) custom-call(s32[3]{0:T(128)S(1)} %copy-done.23, f32[3]{0:T(128)S(1)} %copy-done.24, bf16[3,512,512]{2,1,0:T(8,128)(2,1)S(1)} %copy-done.4, bf16[3,512,512]{2,1,0:T(8,128)(2,1)S(1)} %copy-done.6, ...), custom_call_target="tpu_custom_call" | custom-call | flops 2415919104 | bytes 4194304 | tf_op jit(solution)/shard_map/near_sandwich/pallas_call | solution.py:225
  223.2 1.6 collective-permute-start.26
  224.7 5.1 %near_sandwich.6 = (f32[1,128,512]{2,1,0:T(8,128)S(1)}, f32[1,128,512]{2,1,0:T(8,128)S(1)}, f32[1,128,512]{2,1,0:T(8,128)S(1)}, f32[1,128,512]{2,1,0:T(8,128)S(1)}) custom-call(s32[3]{0:T(128)S(1)} %copy-done.23, f32[3]{0:T(128)S(1)} %copy-done.24, bf16[3,512,512]{2,1,0:T(8,128)(2,1)S(1)} %copy-done.4, bf16[3,512,512]{2,1,0:T(8,128)(2,1)S(1)} %copy-done.6, ...), custom_call_target="tpu_custom_call" | custom-call | flops 2415919104 | bytes 4194304 | tf_op jit(solution)/shard_map/near_sandwich/pallas_call | solution.py:225
  230.4 5.2 %near_sandwich.7 = (f32[1,128,512]{2,1,0:T(8,128)S(1)}, f32[1,128,512]{2,1,0:T(8,128)S(1)}, f32[1,128,512]{2,1,0:T(8,128)S(1)}, f32[1,128,512]{2,1,0:T(8,128)S(1)}) custom-call(s32[3]{0:T(128)S(1)} %copy-done.23, f32[3]{0:T(128)S(1)} %copy-done.24, bf16[3,512,512]{2,1,0:T(8,128)(2,1)S(1)} %copy-done.4, bf16[3,512,512]{2,1,0:T(8,128)(2,1)S(1)} %copy-done.6, ...), custom_call_target="tpu_custom_call" | custom-call | flops 2415919104 | bytes 4194304 | tf_op jit(solution)/shard_map/near_sandwich/pallas_call | solution.py:225
  235.7 1.6 collective-permute-start.28
  238.0 5.6 %collective-permute-done.28.refs_6_ = f32[1,128,512]{2,1,0:T(8,128)S(1)} collective-permute-done((f32[1,128,512]{2,1,0:T(8,128)S(1)}, f32[1,128,512]{2,1,0:T(8,128)S(1)}, u32[]{:S(2)}, u32[]{:S(2)}) %collective-permute-start.28) | collective-permute-done | bytes 262176 | tf_op jit(solution)/shard_map/ppermute | solution.py:457
  243.6 5.1 %near_sandwich.4 = (f32[1,128,512]{2,1,0:T(8,128)S(1)}, f32[1,128,512]{2,1,0:T(8,128)S(1)}, f32[1,128,512]{2,1,0:T(8,128)S(1)}, f32[1,128,512]{2,1,0:T(8,128)S(1)}) custom-call(s32[3]{0:T(128)S(1)} %copy-done.23, f32[3]{0:T(128)S(1)} %copy-done.24, bf16[3,512,512]{2,1,0:T(8,128)(2,1)S(1)} %copy-done.4, bf16[3,512,512]{2,1,0:T(8,128)(2,1)S(1)} %copy-done.6, ...), custom_call_target="tpu_custom_call" | custom-call | flops 2415919104 | bytes 4194304 | tf_op jit(solution)/shard_map/near_sandwich/pallas_call | solution.py:225
  252.3 5.4 %collective-permute-done.33.refs_11_ = f32[1,128,512]{2,1,0:T(8,128)S(1)} collective-permute-done((f32[1,128,512]{2,1,0:T(8,128)S(1)}, f32[1,128,512]{2,1,0:T(8,128)S(1)}, u32[]{:S(2)}, u32[]{:S(2)}) %collective-permute-start.33) | collective-permute-done | bytes 262176 | tf_op jit(solution)/shard_map/ppermute | solution.py:457
  257.7 1.5 collective-permute-start.24
  259.2 4.1 %collective-permute-done.34.refs_12_ = f32[1,128,512]{2,1,0:T(8,128)S(1)} collective-permute-done((f32[1,128,512]{2,1,0:T(8,128)S(1)}, f32[1,128,512]{2,1,0:T(8,128)S(1)}, u32[]{:S(2)}, u32[]{:S(2)}) %collective-permute-start.34) | collective-permute-done | bytes 262176 | tf_op jit(solution)/shard_map/ppermute | solution.py:457
  263.3 1.7 collective-permute-start.25
  265.1 3.9 %collective-permute-done.35.refs_13_ = f32[1,128,512]{2,1,0:T(8,128)S(1)} collective-permute-done((f32[1,128,512]{2,1,0:T(8,128)S(1)}, f32[1,128,512]{2,1,0:T(8,128)S(1)}, u32[]{:S(2)}, u32[]{:S(2)}) %collective-permute-start.35) | collective-permute-done | bytes 262176 | tf_op jit(solution)/shard_map/ppermute | solution.py:457
  269.6 5.5 %collective-permute-done.24.refs_0_ = f32[1,128,512]{2,1,0:T(8,128)S(1)} collective-permute-done((f32[1,128,512]{2,1,0:T(8,128)S(1)}, f32[1,128,512]{2,1,0:T(8,128)S(1)}, u32[]{:S(2)}, u32[]{:S(2)}) %collective-permute-start.24) | collective-permute-done | bytes 262176 | tf_op jit(solution)/shard_map/ppermute | solution.py:457
  275.1 5.1 %collective-permute-done.25.refs_1_ = f32[1,128,512]{2,1,0:T(8,128)S(1)} collective-permute-done((f32[1,128,512]{2,1,0:T(8,128)S(1)}, f32[1,128,512]{2,1,0:T(8,128)S(1)}, u32[]{:S(2)}, u32[]{:S(2)}) %collective-permute-start.25) | collective-permute-done | bytes 262176 | tf_op jit(solution)/shard_map/ppermute | solution.py:457
  280.2 1.5 shard_map.56
  (107 shorter events, 19.5 us)
Async XLA Ops:
  1.9 15.2 %collective-permute-start = (f32[2,128,512]{2,1,0:T(8,128)}, f32[2,128,512]{2,1,0:T(8,128)}, u32[]{:S(2)}, u32[]{:S(2)}) collective-permute-start(f32[2,128,512]{2,1,0:T(8,128)} %constant_dynamic-slice_fusion), channel_id=1, source_target_pairs={{0,2},{2,0},{1,3},{3,1},{4,6},{6,4},{5,7},{7,5},{8,10},{10,8},{9,1... | collective-permute-start | bytes 1572872 | tf_op jit(solution)/shard_map/ppermute | solution.py:393
  7.2 23.3 %collective-permute-start.4 = (f32[4,128,512]{2,1,0:T(8,128)}, f32[4,128,512]{2,1,0:T(8,128)}, u32[]{:S(2)}, u32[]{:S(2)}) collective-permute-start(f32[4,128,512]{2,1,0:T(8,128)} %add_momenta.4), channel_id=1, source_target_pairs={{0,1},{1,0},{2,3},{3,2},{4,5},{5,4},{6,7},{7,6},{8,9},{9,8},{10,11... | collective-permute-start | bytes 3145736 | tf_op jit(solution)/shard_map/ppermute | solution.py:365
  9.6 28.1 %collective-permute-start.7 = (f32[4,128,512]{2,1,0:T(8,128)}, f32[4,128,512]{2,1,0:T(8,128)}, u32[]{:S(2)}, u32[]{:S(2)}) collective-permute-start(f32[4,128,512]{2,1,0:T(8,128)} %add_momenta.6), channel_id=1, source_target_pairs={{0,1},{1,0},{2,3},{3,2},{4,5},{5,4},{6,7},{7,6},{8,9},{9,8},{10,11... | collective-permute-start | bytes 3145736 | tf_op jit(solution)/shard_map/ppermute | solution.py:365
  17.1 13.4 %collective-permute-start.2 = (f32[2,128,512]{2,1,0:T(8,128)}, f32[2,128,512]{2,1,0:T(8,128)}, u32[]{:S(2)}, u32[]{:S(2)}) collective-permute-start(f32[2,128,512]{2,1,0:T(8,128)} %collective-permute-done.refs_0_), channel_id=1, source_target_pairs={{0,16},{16,0},{1,17},{17,1},{2,18},{18,2},{3,19},{19,3},{4,20},{20... | collective-permute-start | bytes 1572872 | tf_op jit(solution)/shard_map/ppermute | solution.py:395
  18.9 24.1 %collective-permute-start.1 = (f32[2,128,512]{2,1,0:T(8,128)}, f32[2,128,512]{2,1,0:T(8,128)}, u32[]{:S(2)}, u32[]{:S(2)}) collective-permute-start(f32[2,128,512]{2,1,0:T(8,128)} %collective-permute-done.refs_0_), channel_id=1, source_target_pairs={{0,1},{1,0},{2,3},{3,2},{4,5},{5,4},{6,7},{7,6},{8,9},{9,8},{10,11... | collective-permute-start | bytes 1572872 | tf_op jit(solution)/shard_map/ppermute | solution.py:397
  30.5 14.0 %collective-permute-start.3 = (f32[2,128,512]{2,1,0:T(8,128)}, f32[2,128,512]{2,1,0:T(8,128)}, u32[]{:S(2)}, u32[]{:S(2)}) collective-permute-start(f32[2,128,512]{2,1,0:T(8,128)} %collective-permute-done.2.refs_2_), channel_id=1, source_target_pairs={{0,1},{1,0},{2,3},{3,2},{4,5},{5,4},{6,7},{7,6},{8,9},{9,8},{10,11... | collective-permute-start | bytes 1572872 | tf_op jit(solution)/shard_map/ppermute | solution.py:397
  33.2 58.0 %copy-start.23 = (s32[3]{0:T(128)S(1)}, s32[3]{0:T(128)}, u32[]{:S(2)}) copy-start(s32[3]{0:T(128)} %steps.9) | copy-start | bytes 40
  33.2 59.2 %copy-start.25 = (s32[3]{0:T(128)S(1)}, s32[3]{0:T(128)}, u32[]{:S(2)}) copy-start(s32[3]{0:T(128)} %owners.1) | copy-start | bytes 40
  33.2 27.3 %collective-permute-start.5 = (f32[4,128,512]{2,1,0:T(8,128)}, f32[4,128,512]{2,1,0:T(8,128)}, u32[]{:S(2)}, u32[]{:S(2)}) collective-permute-start(f32[4,128,512]{2,1,0:T(8,128)} %add_momenta.5.refs_8_.refs_0_), channel_id=1, source_target_pairs={{0,4},{4,8},{8,12},{1,5},{5,9},{9,13},{2,6},{6,10},{10,14},{3,7},{... | collective-permute-start | bytes 3145736 | tf_op jit(solution)/shard_map/ppermute | solution.py:376
  40.3 42.2 %collective-permute-start.8 = (f32[4,128,512]{2,1,0:T(8,128)}, f32[4,128,512]{2,1,0:T(8,128)S(1)}, u32[]{:S(2)}, u32[]{:S(2)}) collective-permute-start(f32[4,128,512]{2,1,0:T(8,128)} %add_momenta.7.refs_9_.refs_1_), channel_id=1, source_target_pairs={{0,4},{4,8},{8,12},{1,5},{5,9},{9,13},{2,6},{6,10},{10,14},{3,7},{... | collective-permute-start | bytes 3145736 | tf_op jit(solution)/shard_map/ppermute | solution.py:376
  42.9 40.9 %collective-permute-start.14 = (f32[4,128,512]{2,1,0:T(8,128)}, f32[4,128,512]{2,1,0:T(8,128)S(1)}, u32[]{:S(2)}, u32[]{:S(2)}) collective-permute-start(f32[4,128,512]{2,1,0:T(8,128)} %add_momenta.5.refs_8_.refs_0_), channel_id=1, source_target_pairs={{0,1},{1,0},{2,3},{3,2},{4,5},{5,4},{6,7},{7,6},{8,9},{9,8},{10,11... | collective-permute-start | bytes 3145736 | tf_op jit(solution)/shard_map/ppermute | solution.py:386
  43.0 42.2 %collective-permute-start.36 = (f32[4,128,512]{2,1,0:T(8,128)}, f32[4,128,512]{2,1,0:T(8,128)S(1)}, u32[]{:S(2)}, u32[]{:S(2)}) collective-permute-start(f32[4,128,512]{2,1,0:T(8,128)} %add_momenta.5.refs_8_.refs_0_), channel_id=1, source_target_pairs={{0,2},{2,0},{1,3},{3,1},{4,6},{6,4},{5,7},{7,5},{8,10},{10,8},{9,1... | collective-permute-start | bytes 3145736 | tf_op jit(solution)/shard_map/ppermute | solution.py:417
  44.5 46.7 %collective-permute-start.37 = (f32[4,128,512]{2,1,0:T(8,128)}, f32[4,128,512]{2,1,0:T(8,128)S(1)}, u32[]{:S(2)}, u32[]{:S(2)}) collective-permute-start(f32[4,128,512]{2,1,0:T(8,128)} %add_momenta.7.refs_9_.refs_1_), channel_id=1, source_target_pairs={{0,2},{2,0},{1,3},{3,1},{4,6},{6,4},{5,7},{7,5},{8,10},{10,8},{9,1... | collective-permute-start | bytes 3145736 | tf_op jit(solution)/shard_map/ppermute | solution.py:417
  60.5 36.5 %collective-permute-start.15 = (f32[4,128,512]{2,1,0:T(8,128)}, f32[4,128,512]{2,1,0:T(8,128)S(1)}, u32[]{:S(2)}, u32[]{:S(2)}) collective-permute-start(f32[4,128,512]{2,1,0:T(8,128)} %add_momenta.7.refs_9_.refs_1_), channel_id=1, source_target_pairs={{0,1},{1,0},{2,3},{3,2},{4,5},{5,4},{6,7},{7,6},{8,9},{9,8},{10,11... | collective-permute-start | bytes 3145736 | tf_op jit(solution)/shard_map/ppermute | solution.py:386
  82.5 28.5 %collective-permute-start.16 = (f32[4,128,512]{2,1,0:T(8,128)}, f32[4,128,512]{2,1,0:T(8,128)S(1)}, u32[]{:S(2)}, u32[]{:S(2)}) collective-permute-start(f32[4,128,512]{2,1,0:T(8,128)} %add_momenta.5.refs_8_.refs_0_), channel_id=1, source_target_pairs={{12,8},{8,4},{4,0},{13,9},{9,5},{5,1},{14,10},{10,6},{6,2},{15,11}... | collective-permute-start | bytes 3145736 | tf_op jit(solution)/shard_map/ppermute | solution.py:377
  83.8 48.7 %collective-permute-start.17 = (f32[4,128,512]{2,1,0:T(8,128)}, f32[4,128,512]{2,1,0:T(8,128)}, u32[]{:S(2)}, u32[]{:S(2)}) collective-permute-start(f32[4,128,512]{2,1,0:T(8,128)} %add_momenta.7.refs_9_.refs_1_), channel_id=1, source_target_pairs={{12,8},{8,4},{4,0},{13,9},{9,5},{5,1},{14,10},{10,6},{6,2},{15,11}... | collective-permute-start | bytes 3145736 | tf_op jit(solution)/shard_map/ppermute | solution.py:377
  85.1 49.0 %collective-permute-start.38 = (f32[4,128,512]{2,1,0:T(8,128)S(1)}, f32[4,128,512]{2,1,0:T(8,128)S(1)}, u32[]{:S(2)}, u32[]{:S(2)}) collective-permute-start(f32[4,128,512]{2,1,0:T(8,128)S(1)} %collective-permute-done.36.refs_2_), channel_id=1, source_target_pairs={{0,1},{1,0},{2,3},{3,2},{4,5},{5,4},{6,7},{7,6},{8,9},{9,8},{10,11... | collective-permute-start | bytes 3145736 | tf_op jit(solution)/shard_map/ppermute | solution.py:420
  91.2 43.0 %collective-permute-start.39 = (f32[4,128,512]{2,1,0:T(8,128)S(1)}, f32[4,128,512]{2,1,0:T(8,128)S(1)}, u32[]{:S(2)}, u32[]{:S(2)}) collective-permute-start(f32[4,128,512]{2,1,0:T(8,128)S(1)} %collective-permute-done.37.refs_3_), channel_id=1, source_target_pairs={{0,1},{1,0},{2,3},{3,2},{4,5},{5,4},{6,7},{7,6},{8,9},{9,8},{10,11... | collective-permute-start | bytes 3145736 | tf_op jit(solution)/shard_map/ppermute | solution.py:420
  97.0 53.8 %copy-start.3 = (bf16[3,512,512]{2,1,0:T(8,128)(2,1)}, bf16[3,512,512]{2,1,0:T(8,128)(2,1)S(1)}, u32[]{:S(2)}) copy-start(bf16[3,512,512]{2,1,0:T(8,128)(2,1)S(1)} %get-tuple-element.27.right_high) | copy-start | bytes 4718596
  97.0 53.8 %copy-start.5 = (bf16[3,512,512]{2,1,0:T(8,128)(2,1)}, bf16[3,512,512]{2,1,0:T(8,128)(2,1)S(1)}, u32[]{:S(2)}) copy-start(bf16[3,512,512]{2,1,0:T(8,128)(2,1)S(1)} %get-tuple-element.28.right_low) | copy-start | bytes 4718596
  97.0 53.8 %copy-start.11 = (f32[4,128,512]{2,1,0:T(8,128)}, f32[4,128,512]{2,1,0:T(8,128)S(1)}, u32[]{:S(2)}) copy-start(f32[4,128,512]{2,1,0:T(8,128)S(1)} %collective-permute-done.15.refs_11_.refs_5_) | copy-start | bytes 3145732
  97.0 54.5 %collective-permute-start.6 = (f32[4,128,512]{2,1,0:T(8,128)}, f32[4,128,512]{2,1,0:T(8,128)}, u32[]{:S(2)}, u32[]{:S(2)}) collective-permute-start(f32[4,128,512]{2,1,0:T(8,128)} %collective-permute-done.5.refs_4_), channel_id=1, source_target_pairs={{4,8},{8,12},{5,9},{9,13},{6,10},{10,14},{7,11},{11,15},{20,24},{2... | collective-permute-start | bytes 3145736 | tf_op jit(solution)/shard_map/ppermute | solution.py:376
  111.0 43.2 %collective-permute-start.12 = (f32[4,128,512]{2,1,0:T(8,128)}, f32[4,128,512]{2,1,0:T(8,128)S(1)}, u32[]{:S(2)}, u32[]{:S(2)}) collective-permute-start(f32[4,128,512]{2,1,0:T(8,128)} %collective-permute-done.5.refs_4_), channel_id=1, source_target_pairs={{0,1},{1,0},{2,3},{3,2},{4,5},{5,4},{6,7},{7,6},{8,9},{9,8},{10,11... | collective-permute-start | bytes 3145736 | tf_op jit(solution)/shard_map/ppermute | solution.py:386
  132.5 20.3 %collective-permute-start.9 = (f32[4,128,512]{2,1,0:T(8,128)S(1)}, f32[4,128,512]{2,1,0:T(8,128)}, u32[]{:S(2)}, u32[]{:S(2)}) collective-permute-start(f32[4,128,512]{2,1,0:T(8,128)S(1)} %collective-permute-done.8.refs_5_), channel_id=1, source_target_pairs={{4,8},{8,12},{5,9},{9,13},{6,10},{10,14},{7,11},{11,15},{20,24},{2... | collective-permute-start | bytes 3145736 | tf_op jit(solution)/shard_map/ppermute | solution.py:376
  134.2 21.1 %collective-permute-start.13 = (f32[4,128,512]{2,1,0:T(8,128)S(1)}, f32[4,128,512]{2,1,0:T(8,128)S(1)}, u32[]{:S(2)}, u32[]{:S(2)}) collective-permute-start(f32[4,128,512]{2,1,0:T(8,128)S(1)} %collective-permute-done.8.refs_5_), channel_id=1, source_target_pairs={{0,1},{1,0},{2,3},{3,2},{4,5},{5,4},{6,7},{7,6},{8,9},{9,8},{10,11... | collective-permute-start | bytes 3145736 | tf_op jit(solution)/shard_map/ppermute | solution.py:386
  134.2 22.5 %collective-permute-start.18 = (f32[4,128,512]{2,1,0:T(8,128)S(1)}, f32[4,128,512]{2,1,0:T(8,128)S(1)}, u32[]{:S(2)}, u32[]{:S(2)}) collective-permute-start(f32[4,128,512]{2,1,0:T(8,128)S(1)} %collective-permute-done.16.refs_12_), channel_id=1, source_target_pairs={{0,1},{1,0},{2,3},{3,2},{4,5},{5,4},{6,7},{7,6},{8,9},{9,8},{10,11... | collective-permute-start | bytes 3145736 | tf_op jit(solution)/shard_map/ppermute | solution.py:386
  151.5 30.6 %collective-permute-start.20 = (f32[4,128,512]{2,1,0:T(8,128)S(1)}, f32[4,128,512]{2,1,0:T(8,128)}, u32[]{:S(2)}, u32[]{:S(2)}) collective-permute-start(f32[4,128,512]{2,1,0:T(8,128)S(1)} %collective-permute-done.16.refs_12_), channel_id=1, source_target_pairs={{8,4},{4,0},{9,5},{5,1},{10,6},{6,2},{11,7},{7,3},{24,20},{20,16},... | collective-permute-start | bytes 3145736 | tf_op jit(solution)/shard_map/ppermute | solution.py:377
  152.9 51.1 %collective-permute-start.21 = (f32[4,128,512]{2,1,0:T(8,128)}, f32[4,128,512]{2,1,0:T(8,128)}, u32[]{:S(2)}, u32[]{:S(2)}) collective-permute-start(f32[4,128,512]{2,1,0:T(8,128)} %collective-permute-done.17.refs_13_), channel_id=1, source_target_pairs={{8,4},{4,0},{9,5},{5,1},{10,6},{6,2},{11,7},{7,3},{24,20},{20,16},... | collective-permute-start | bytes 3145736 | tf_op jit(solution)/shard_map/ppermute | solution.py:377
  155.2 50.7 %collective-permute-start.40 = (f32[4,128,512]{2,0,1:T(4,128)S(1)}, f32[4,128,512]{2,0,1:T(4,128)}, u32[]{:S(2)}, u32[]{:S(2)}) collective-permute-start(f32[4,128,512]{2,0,1:T(4,128)S(1)} %copy.6), channel_id=1, source_target_pairs={{0,1},{1,0},{2,3},{3,2},{4,5},{5,4},{6,7},{7,6},{8,9},{9,8},{10,11... | collective-permute-start | bytes 3145736 | tf_op jit(solution)/shard_map/ppermute | solution.py:434
  156.2 55.2 %collective-permute-start.19 = (f32[4,128,512]{2,1,0:T(8,128)}, f32[4,128,512]{2,1,0:T(8,128)}, u32[]{:S(2)}, u32[]{:S(2)}) collective-permute-start(f32[4,128,512]{2,1,0:T(8,128)} %collective-permute-done.17.refs_13_), channel_id=1, source_target_pairs={{0,1},{1,0},{2,3},{3,2},{4,5},{5,4},{6,7},{7,6},{8,9},{9,8},{10,11... | collective-permute-start | bytes 3145736 | tf_op jit(solution)/shard_map/ppermute | solution.py:386
  157.7 55.3 %collective-permute-start.10 = (f32[4,128,512]{2,1,0:T(8,128)}, f32[4,128,512]{2,1,0:T(8,128)}, u32[]{:S(2)}, u32[]{:S(2)}) collective-permute-start(f32[4,128,512]{2,1,0:T(8,128)} %collective-permute-done.6.refs_0_), channel_id=1, source_target_pairs={{8,9},{9,8},{12,13},{13,12},{10,11},{11,10},{14,15},{15,14},{24,25... | collective-permute-start | bytes 3145736 | tf_op jit(solution)/shard_map/ppermute | solution.py:386
  182.2 32.1 %collective-permute-start.11 = (f32[4,128,512]{2,1,0:T(8,128)}, f32[4,128,512]{2,1,0:T(8,128)}, u32[]{:S(2)}, u32[]{:S(2)}) collective-permute-start(f32[4,128,512]{2,1,0:T(8,128)} %collective-permute-done.9.refs_1_), channel_id=1, source_target_pairs={{8,9},{9,8},{12,13},{13,12},{10,11},{11,10},{14,15},{15,14},{24,25... | collective-permute-start | bytes 3145736 | tf_op jit(solution)/shard_map/ppermute | solution.py:386
  204.0 10.3 %collective-permute-start.22 = (f32[4,128,512]{2,1,0:T(8,128)}, f32[4,128,512]{2,1,0:T(8,128)}, u32[]{:S(2)}, u32[]{:S(2)}) collective-permute-start(f32[4,128,512]{2,1,0:T(8,128)} %collective-permute-done.20.refs_16_), channel_id=1, source_target_pairs={{0,1},{1,0},{4,5},{5,4},{2,3},{3,2},{6,7},{7,6},{16,17},{17,16},{2... | collective-permute-start | bytes 3145736 | tf_op jit(solution)/shard_map/ppermute | solution.py:386
  205.9 8.4 %collective-permute-start.23 = (f32[4,128,512]{2,1,0:T(8,128)}, f32[4,128,512]{2,1,0:T(8,128)}, u32[]{:S(2)}, u32[]{:S(2)}) collective-permute-start(f32[4,128,512]{2,1,0:T(8,128)} %collective-permute-done.21.refs_17_), channel_id=1, source_target_pairs={{0,1},{1,0},{4,5},{5,4},{2,3},{3,2},{6,7},{7,6},{16,17},{17,16},{2... | collective-permute-start | bytes 3145736 | tf_op jit(solution)/shard_map/ppermute | solution.py:386
  211.4 68.7 %collective-permute-start.41 = (f32[128,8,512]{2,1,0:T(8,128)S(1)}, f32[128,8,512]{2,1,0:T(8,128)S(1)}, u32[]{:S(2)}, u32[]{:S(2)}) collective-permute-start(f32[128,8,512]{2,1,0:T(8,128)S(1)} %maximum_bitcast_fusion), channel_id=1, source_target_pairs={{0,12},{1,13},{2,14},{3,15},{16,28},{17,29},{18,30},{19,31}} | collective-permute-start | bytes 6291464 | tf_op jit(solution)/shard_map/ppermute | solution.py:438
  213.0 67.2 %collective-permute-start.42 = (f32[128,8,512]{2,1,0:T(8,128)S(1)}, f32[128,8,512]{2,1,0:T(8,128)S(1)}, u32[]{:S(2)}, u32[]{:S(2)}) collective-permute-start(f32[128,8,512]{2,1,0:T(8,128)S(1)} %maximum_bitcast_fusion), channel_id=1, source_target_pairs={{12,0},{13,1},{14,2},{15,3},{28,16},{29,17},{30,18},{31,19}} | collective-permute-start | bytes 6291464 | tf_op jit(solution)/shard_map/ppermute | solution.py:439
  223.2 14.1 %collective-permute-start.26 = (f32[1,128,512]{2,1,0:T(8,128)S(1)}, f32[1,128,512]{2,1,0:T(8,128)S(1)}, u32[]{:S(2)}, u32[]{:S(2)}) collective-permute-start(f32[1,128,512]{2,1,0:T(8,128)S(1)} %get-tuple-element.36), channel_id=1, source_target_pairs={{0,2},{1,3},{2,0},{3,1},{4,6},{5,7},{6,4},{7,5},{8,10},{9,11},{10,... | collective-permute-start | bytes 786440 | tf_op jit(solution)/shard_map/ppermute | solution.py:457
  229.9 8.1 %collective-permute-start.27 = (f32[1,128,512]{2,1,0:T(8,128)S(1)}, f32[1,128,512]{2,1,0:T(8,128)S(1)}, u32[]{:S(2)}, u32[]{:S(2)}) collective-permute-start(f32[1,128,512]{2,1,0:T(8,128)S(1)} %get-tuple-element.37), channel_id=1, source_target_pairs={{0,2},{1,3},{2,0},{3,1},{4,6},{5,7},{6,4},{7,5},{8,10},{9,11},{10,... | collective-permute-start | bytes 786440 | tf_op jit(solution)/shard_map/ppermute | solution.py:457
  235.7 7.9 %collective-permute-start.28 = (f32[1,128,512]{2,1,0:T(8,128)S(1)}, f32[1,128,512]{2,1,0:T(8,128)S(1)}, u32[]{:S(2)}, u32[]{:S(2)}) collective-permute-start(f32[1,128,512]{2,1,0:T(8,128)S(1)} %get-tuple-element.38), channel_id=1, source_target_pairs={{0,2},{1,3},{2,0},{3,1},{4,6},{5,7},{6,4},{7,5},{8,10},{9,11},{10,... | collective-permute-start | bytes 786440 | tf_op jit(solution)/shard_map/ppermute | solution.py:457
  237.3 11.5 %collective-permute-start.29 = (f32[1,128,512]{2,1,0:T(8,128)S(1)}, f32[1,128,512]{2,1,0:T(8,128)S(1)}, u32[]{:S(2)}, u32[]{:S(2)}) collective-permute-start(f32[1,128,512]{2,1,0:T(8,128)S(1)} %get-tuple-element.39), channel_id=1, source_target_pairs={{0,1},{1,0},{2,3},{3,2},{4,5},{5,4},{6,7},{7,6},{8,9},{9,8},{10,11... | collective-permute-start | bytes 786440 | tf_op jit(solution)/shard_map/ppermute | solution.py:457
  238.0 11.4 %collective-permute-start.30 = (f32[1,128,512]{2,1,0:T(8,128)S(1)}, f32[1,128,512]{2,1,0:T(8,128)S(1)}, u32[]{:S(2)}, u32[]{:S(2)}) collective-permute-start(f32[1,128,512]{2,1,0:T(8,128)S(1)} %get-tuple-element.40), channel_id=1, source_target_pairs={{0,1},{1,0},{2,3},{3,2},{4,5},{5,4},{6,7},{7,6},{8,9},{9,8},{10,11... | collective-permute-start | bytes 786440 | tf_op jit(solution)/shard_map/ppermute | solution.py:457
  243.6 6.9 %collective-permute-start.31 = (f32[1,128,512]{2,1,0:T(8,128)S(1)}, f32[1,128,512]{2,1,0:T(8,128)S(1)}, u32[]{:S(2)}, u32[]{:S(2)}) collective-permute-start(f32[1,128,512]{2,1,0:T(8,128)S(1)} %get-tuple-element.41), channel_id=1, source_target_pairs={{0,1},{1,0},{2,3},{3,2},{4,5},{5,4},{6,7},{7,6},{8,9},{9,8},{10,11... | collective-permute-start | bytes 786440 | tf_op jit(solution)/shard_map/ppermute | solution.py:457
  248.7 2.4 collective-permute-start.32
  249.4 8.3 %collective-permute-start.33 = (f32[1,128,512]{2,1,0:T(8,128)S(1)}, f32[1,128,512]{2,1,0:T(8,128)S(1)}, u32[]{:S(2)}, u32[]{:S(2)}) collective-permute-start(f32[1,128,512]{2,1,0:T(8,128)S(1)} %get-tuple-element.43), channel_id=1, source_target_pairs={{0,3},{1,2},{2,1},{3,0},{4,7},{5,6},{6,5},{7,4},{8,11},{9,10},{10,... | collective-permute-start | bytes 786440 | tf_op jit(solution)/shard_map/ppermute | solution.py:457
  250.6 12.8 %collective-permute-start.34 = (f32[1,128,512]{2,1,0:T(8,128)S(1)}, f32[1,128,512]{2,1,0:T(8,128)S(1)}, u32[]{:S(2)}, u32[]{:S(2)}) collective-permute-start(f32[1,128,512]{2,1,0:T(8,128)S(1)} %get-tuple-element.44), channel_id=1, source_target_pairs={{0,3},{1,2},{2,1},{3,0},{4,7},{5,6},{6,5},{7,4},{8,11},{9,10},{10,... | collective-permute-start | bytes 786440 | tf_op jit(solution)/shard_map/ppermute | solution.py:457
  251.1 17.8 %collective-permute-start.35 = (f32[1,128,512]{2,1,0:T(8,128)S(1)}, f32[1,128,512]{2,1,0:T(8,128)S(1)}, u32[]{:S(2)}, u32[]{:S(2)}) collective-permute-start(f32[1,128,512]{2,1,0:T(8,128)S(1)} %get-tuple-element.45), channel_id=1, source_target_pairs={{0,3},{1,2},{2,1},{3,0},{4,7},{5,6},{6,5},{7,4},{8,11},{9,10},{10,... | collective-permute-start | bytes 786440 | tf_op jit(solution)/shard_map/ppermute | solution.py:457
  257.7 17.4 %collective-permute-start.24 = (f32[1,128,512]{2,1,0:T(8,128)S(1)}, f32[1,128,512]{2,1,0:T(8,128)S(1)}, u32[]{:S(2)}, u32[]{:S(2)}) collective-permute-start(f32[1,128,512]{2,1,0:T(8,128)S(1)} %get-tuple-element.30), channel_id=1, source_target_pairs={{0,2},{1,3},{2,0},{3,1},{4,6},{5,7},{6,4},{7,5},{8,10},{9,11},{10,... | collective-permute-start | bytes 786440 | tf_op jit(solution)/shard_map/ppermute | solution.py:457
  263.3 16.9 %collective-permute-start.25 = (f32[1,128,512]{2,1,0:T(8,128)S(1)}, f32[1,128,512]{2,1,0:T(8,128)S(1)}, u32[]{:S(2)}, u32[]{:S(2)}) collective-permute-start(f32[1,128,512]{2,1,0:T(8,128)S(1)} %get-tuple-element.31), channel_id=1, source_target_pairs={{0,3},{1,2},{2,1},{3,0},{4,7},{5,6},{6,5},{7,4},{8,11},{9,10},{10,... | collective-permute-start | bytes 786440 | tf_op jit(solution)/shard_map/ppermute | solution.py:457
  (21 other events, 339.2 us)
